TPU v7x, 32 devices: a whole 2x2x4 slice. The times are simulated.
32 devices in a mesh: dp: 8 (over z, y), tensor: 4 (over x, core).
Axes of the slice: x: 2, y: 2, z: 4, core: 2. Of those that a mesh axis runs over, the one named last changes fastest.
Arguments:
- tokens: bfloat16 [8192, 2048], P('dp'), may hold values from -6 to 6
- segment_ids: int32 [8, 1024], P('dp'), may hold values from 0 to 7, never falling along the last dimension, each value on 1 to 512 neighbouring positions
- attn_gain: bfloat16 [2048], P('dp'), may hold values from 0.25 to 1.75
- query_weight: bfloat16 [2048, 2048], P('dp', 'tensor'), may hold values from -0.125 to 0.125
- key_weight: bfloat16 [2048, 512], P('dp', 'tensor'), may hold values from -0.125 to 0.125
- value_weight: bfloat16 [2048, 512], P('dp', 'tensor'), may hold values from -0.125 to 0.125
- output_weight: bfloat16 [2048, 2048], P('tensor', 'dp'), may hold values from -0.5 to 0.5
- ffn_gain: bfloat16 [2048], P('dp'), may hold values from 0.25 to 1.75
- gate_weight: bfloat16 [2048, 8192], P('dp', 'tensor'), may hold values from -0.125 to 0.125
- up_weight: bfloat16 [2048, 8192], P('dp', 'tensor'), may hold values from -0.125 to 0.125
- down_weight: bfloat16 [8192, 2048], P('tensor', 'dp'), may hold values from -0.0625 to 0.0625
- cotangent: bfloat16 [8192, 2048], P('dp'), may hold values from -6 to 6
Outputs:
- layer_output: bfloat16 [8192, 2048], P('dp')
- tokens_grad: float32 [8192, 2048], P('dp')
- attn_gain_grad: float32 [2048], P('dp')
- query_weight_grad: float32 [2048, 2048], P('dp', 'tensor')
- key_weight_grad: float32 [2048, 512], P('dp', 'tensor')
- value_weight_grad: float32 [2048, 512], P('dp', 'tensor')
- output_weight_grad: float32 [2048, 2048], P('tensor', 'dp')
- ffn_gain_grad: float32 [2048], P('dp')
- gate_weight_grad: float32 [2048, 8192], P('dp', 'tensor')
- up_weight_grad: float32 [2048, 8192], P('dp', 'tensor')
- down_weight_grad: float32 [8192, 2048], P('tensor', 'dp')
Inputs may be any that keep to these rules, and one draw needn't show every extreme that they name: In each row of segment_ids the numbers never fall; each document spans 1 to 512 positions, and one spans exactly 512.
All inputs are finite; a program needn't handle non-finite values.
Results may differ from a plain program's by a relative error of at most 0.02.
Values may be sent and summed in bfloat16 or wider, within the bound.
A program may use at most 256 MiB of HBM per device.

v0:
```python
from functools import partial
import math

import jax
import jax.numpy as jnp
from jax import lax
from jax.sharding import PartitionSpec as P

HD = 64


epsilon = 1e-05


def rope_tables(segment_row, head_size):
    length = segment_row.shape[0]
    places = jnp.arange(length, dtype=jnp.int32)
    boundary = jnp.concatenate([jnp.ones((1,), dtype=bool), segment_row[1:] != segment_row[:-1]])
    starts = lax.cummax(jnp.where(boundary, places, 0), axis=0)
    position = (places - starts).astype(jnp.float32)
    half_size = head_size // 2
    exponent = jnp.arange(half_size, dtype=jnp.float32) * 2.0 / head_size
    inverse = 1.0 / 500000.0**exponent
    wavelen = 2.0 * math.pi / inverse
    smooth = (8192.0 / wavelen - 1.0) / 3.0
    scaled = jnp.where(
        wavelen < 2048.0,
        inverse,
        jnp.where(
            wavelen > 8192.0, inverse / 32.0, (1.0 - smooth) * inverse / 32.0 + smooth * inverse
        ),
    )
    angles = position[:, None] * scaled[None, :]
    cosine_table = jnp.cos(angles)
    sine_table = jnp.sin(angles)
    return (
        jnp.concatenate([cosine_table, cosine_table], axis=-1),
        jnp.concatenate([sine_table, sine_table], axis=-1),
    )


def rotate(values, cosine_table, sine_table):
    half_size = values.shape[-1] // 2
    turned = jnp.concatenate([-values[..., half_size:], values[..., :half_size]], axis=-1)
    return values * cosine_table + turned * sine_table


def rms_norm(values, gain_vector):
    factor = lax.rsqrt(jnp.mean(values * values, axis=-1, keepdims=True) + epsilon)
    return values * factor * gain_vector


def swiglu(gate_values, up_values):
    return jax.nn.silu(gate_values) * up_values


def contract_rows(left_side, right_side):
    return lax.dot_general(
        left_side, right_side, (((0,), (0,)), ((), ())), preferred_element_type=jnp.float32
    )


def contract_cols(left_side, right_side):
    return lax.dot_general(
        left_side, right_side, (((1,), (1,)), ((), ())), preferred_element_type=jnp.float32
    )


def block_scores(query_block, key_seq, segment_row, start_row):
    row_count = query_block.shape[0]
    length = key_seq.shape[0]
    score_scale = query_block.shape[-1] ** (-0.5)
    scores = (
        jnp.einsum("qkgd,skd->kgqs", query_block, key_seq, preferred_element_type=jnp.float32)
        * score_scale
    )
    row_ids = start_row + jnp.arange(row_count, dtype=jnp.int32)
    col_ids = jnp.arange(length, dtype=jnp.int32)
    same_doc = segment_row[start_row : start_row + row_count][:, None] == segment_row[None, :]
    allowed = same_doc & (col_ids[None, :] <= row_ids[:, None])
    return jnp.where(allowed, scores, -1000000000.0)


def attend_forward(operands):
    query_seq, key_seq, value_seq, segment_row = operands
    length, kv_local, head_size = key_seq.shape
    grouped = query_seq.reshape(length, kv_local, -1, head_size)
    block_rows = min(512, length)
    mixed_parts = []
    total_parts = []
    for start_row in range(0, length, block_rows):
        scores = block_scores(
            grouped[start_row : start_row + block_rows], key_seq, segment_row, start_row
        )
        row_max = jnp.max(scores, axis=-1, keepdims=True)
        log_total = jnp.log(jnp.sum(jnp.exp(scores - row_max), axis=-1, keepdims=True)) + row_max
        soft_low = jnp.exp(scores - log_total).astype(jnp.bfloat16)
        mixed_block = jnp.einsum(
            "kgqs,skd->qkgd", soft_low, value_seq, preferred_element_type=jnp.float32
        )
        mixed_parts.append(mixed_block.reshape(block_rows, -1).astype(jnp.bfloat16))
        total_parts.append(log_total)
    return (jnp.concatenate(mixed_parts, axis=0), jnp.concatenate(total_parts, axis=2))


def attend_backward(operands):
    query_seq, key_seq, value_seq, log_total, grad_seq, segment_row = operands
    length, kv_local, head_size = key_seq.shape
    grouped = query_seq.reshape(length, kv_local, -1, head_size)
    grad_grouped = grad_seq.reshape(length, kv_local, -1, head_size)
    block_rows = min(512, length)
    score_scale = head_size ** (-0.5)
    query_parts = []
    key_grad = jnp.zeros(key_seq.shape, jnp.float32)
    value_grad = jnp.zeros(value_seq.shape, jnp.float32)
    for start_row in range(0, length, block_rows):
        query_block = grouped[start_row : start_row + block_rows]
        grad_block = grad_grouped[start_row : start_row + block_rows]
        scores = block_scores(query_block, key_seq, segment_row, start_row)
        soft_weights = jnp.exp(scores - log_total[:, :, start_row : start_row + block_rows])
        soft_grad = jnp.einsum(
            "qkgd,skd->kgqs", grad_block, value_seq, preferred_element_type=jnp.float32
        )
        score_grad = (
            soft_weights * (soft_grad - jnp.sum(soft_weights * soft_grad, axis=-1, keepdims=True))
        ).astype(jnp.bfloat16)
        query_parts.append(
            jnp.einsum("kgqs,skd->qkgd", score_grad, key_seq, preferred_element_type=jnp.float32)
            * score_scale
        )
        key_grad = (
            key_grad
            + jnp.einsum(
                "kgqs,qkgd->skd", score_grad, query_block, preferred_element_type=jnp.float32
            )
            * score_scale
        )
        value_grad = value_grad + jnp.einsum(
            "kgqs,qkgd->skd",
            soft_weights.astype(jnp.bfloat16),
            grad_block,
            preferred_element_type=jnp.float32,
        )
    query_grad = jnp.concatenate(query_parts, axis=0).reshape(length, -1, head_size)
    return (query_grad, key_grad, value_grad)


def shards(
    tokens,
    segment_ids,
    attn_gain,
    query_weight,
    key_weight,
    value_weight,
    output_weight,
    ffn_gain,
    gate_weight,
    up_weight,
    down_weight,
    cotangent,
):
    gathered = (
        lax.all_gather(attn_gain, "dp", axis=0, tiled=True),
        lax.all_gather(query_weight, "dp", axis=0, tiled=True),
        lax.all_gather(key_weight, "dp", axis=0, tiled=True),
        lax.all_gather(value_weight, "dp", axis=0, tiled=True),
        lax.all_gather(output_weight, "dp", axis=1, tiled=True),
        lax.all_gather(ffn_gain, "dp", axis=0, tiled=True),
        lax.all_gather(gate_weight, "dp", axis=0, tiled=True),
        lax.all_gather(up_weight, "dp", axis=0, tiled=True),
        lax.all_gather(down_weight, "dp", axis=1, tiled=True),
    )
    seq_count, length = segment_ids.shape
    token_count = tokens.shape[0]
    tokens_float = tokens.astype(jnp.float32)
    cotangent_float = cotangent.astype(jnp.float32)
    attn_scale = gathered[0].astype(jnp.float32)
    ffn_scale = gathered[5].astype(jnp.float32)
    normed = rms_norm(tokens_float, attn_scale).astype(jnp.bfloat16)
    query_raw = jnp.dot(normed, gathered[1], preferred_element_type=jnp.float32)
    key_raw = jnp.dot(normed, gathered[2], preferred_element_type=jnp.float32)
    value_low = jnp.dot(normed, gathered[3], preferred_element_type=jnp.float32).astype(
        jnp.bfloat16
    )
    cosine_table, sine_table = jax.vmap(partial(rope_tables, head_size=HD))(segment_ids)
    cosine_wide = cosine_table[:, :, None, :]
    sine_wide = sine_table[:, :, None, :]
    query_shaped = query_raw.reshape(seq_count, length, -1, HD)
    key_shaped = key_raw.reshape(seq_count, length, -1, HD)
    query_low = rotate(query_shaped, cosine_wide, sine_wide).astype(jnp.bfloat16)
    key_low = rotate(key_shaped, cosine_wide, sine_wide).astype(jnp.bfloat16)
    value_seqs = value_low.reshape(seq_count, length, -1, HD)
    mixed_low, log_total = lax.map(attend_forward, (query_low, key_low, value_seqs, segment_ids))
    mixed_low = mixed_low.reshape(token_count, -1)
    attn_part = jnp.dot(mixed_low, gathered[4], preferred_element_type=jnp.float32)
    hidden_state = tokens_float + lax.psum(attn_part, "tensor")
    normed_two = rms_norm(hidden_state, ffn_scale).astype(jnp.bfloat16)
    gate_values = jnp.dot(normed_two, gathered[6], preferred_element_type=jnp.float32)
    up_values = jnp.dot(normed_two, gathered[7], preferred_element_type=jnp.float32)
    active = swiglu(gate_values, up_values).astype(jnp.bfloat16)
    ffn_part = jnp.dot(active, gathered[8], preferred_element_type=jnp.float32)
    layer_output = (
        hidden_state + lax.psum(ffn_part.astype(jnp.bfloat16), "tensor").astype(jnp.float32)
    ).astype(jnp.bfloat16)
    down_grad = contract_rows(active, cotangent)
    active_grad = contract_cols(cotangent, gathered[8])
    unused_value, swiglu_pull = jax.vjp(swiglu, gate_values, up_values)
    gate_grad, up_grad = swiglu_pull(active_grad)
    gate_low = gate_grad.astype(jnp.bfloat16)
    up_low = up_grad.astype(jnp.bfloat16)
    gate_weight_grad = contract_rows(normed_two, gate_low)
    up_weight_grad = contract_rows(normed_two, up_low)
    mlp_part = contract_cols(gate_low, gathered[6]) + contract_cols(up_low, gathered[7])
    normed_two_grad = lax.psum(mlp_part, "tensor")
    unused_second, second_pull = jax.vjp(rms_norm, hidden_state, ffn_scale)
    hidden_part, ffn_gain_grad = second_pull(normed_two_grad)
    hidden_grad = cotangent_float + hidden_part
    hidden_low = hidden_grad.astype(jnp.bfloat16)
    output_weight_grad = contract_rows(mixed_low, hidden_low)
    mixed_grad = contract_cols(hidden_low, gathered[4]).astype(jnp.bfloat16)
    query_grad, key_grad, value_grad = lax.map(
        attend_backward,
        (
            query_low,
            key_low,
            value_seqs,
            log_total,
            mixed_grad.reshape(seq_count, length, -1, HD),
            segment_ids,
        ),
    )
    unused_query, query_pull = jax.vjp(
        partial(rotate, cosine_table=cosine_wide, sine_table=sine_wide), query_shaped
    )
    unused_key, key_pull = jax.vjp(
        partial(rotate, cosine_table=cosine_wide, sine_table=sine_wide), key_shaped
    )
    query_raw_grad = query_pull(query_grad)[0].reshape(token_count, -1).astype(jnp.bfloat16)
    key_raw_grad = key_pull(key_grad)[0].reshape(token_count, -1).astype(jnp.bfloat16)
    value_raw_grad = value_grad.reshape(token_count, -1).astype(jnp.bfloat16)
    query_weight_grad = contract_rows(normed, query_raw_grad)
    key_weight_grad = contract_rows(normed, key_raw_grad)
    value_weight_grad = contract_rows(normed, value_raw_grad)
    attn_back_part = (
        contract_cols(query_raw_grad, gathered[1])
        + contract_cols(key_raw_grad, gathered[2])
        + contract_cols(value_raw_grad, gathered[3])
    )
    normed_grad = lax.psum(attn_back_part.astype(jnp.bfloat16), "tensor").astype(jnp.float32)
    unused_first, first_pull = jax.vjp(rms_norm, tokens_float, attn_scale)
    token_part, attn_gain_grad = first_pull(normed_grad)
    tokens_grad = hidden_grad + token_part
    summed = (
        lax.psum_scatter(
            attn_gain_grad.astype(jnp.bfloat16), "dp", scatter_dimension=0, tiled=True
        ).astype(jnp.float32),
        lax.psum_scatter(
            query_weight_grad.astype(jnp.bfloat16), "dp", scatter_dimension=0, tiled=True
        ).astype(jnp.float32),
        lax.psum_scatter(
            key_weight_grad.astype(jnp.bfloat16), "dp", scatter_dimension=0, tiled=True
        ).astype(jnp.float32),
        lax.psum_scatter(
            value_weight_grad.astype(jnp.bfloat16), "dp", scatter_dimension=0, tiled=True
        ).astype(jnp.float32),
        lax.psum_scatter(
            output_weight_grad.astype(jnp.bfloat16), "dp", scatter_dimension=1, tiled=True
        ).astype(jnp.float32),
        lax.psum_scatter(
            ffn_gain_grad.astype(jnp.bfloat16), "dp", scatter_dimension=0, tiled=True
        ).astype(jnp.float32),
        lax.psum_scatter(
            gate_weight_grad.astype(jnp.bfloat16), "dp", scatter_dimension=0, tiled=True
        ).astype(jnp.float32),
        lax.psum_scatter(
            up_weight_grad.astype(jnp.bfloat16), "dp", scatter_dimension=0, tiled=True
        ).astype(jnp.float32),
        lax.psum_scatter(
            down_grad.astype(jnp.bfloat16), "dp", scatter_dimension=1, tiled=True
        ).astype(jnp.float32),
    )
    attn_gain_total = summed[0]
    ffn_gain_total = summed[5]
    return (
        layer_output,
        tokens_grad,
        attn_gain_total,
        summed[1],
        summed[2],
        summed[3],
        summed[4],
        ffn_gain_total,
        summed[6],
        summed[7],
        summed[8],
    )


def solution(mesh):
    return jax.shard_map(
        shards,
        mesh=mesh,
        in_specs=(
            P("dp", None),
            P("dp", None),
            P("dp"),
            P("dp", "tensor"),
            P("dp", "tensor"),
            P("dp", "tensor"),
            P("tensor", "dp"),
            P("dp"),
            P("dp", "tensor"),
            P("dp", "tensor"),
            P("tensor", "dp"),
            P("dp", None),
        ),
        out_specs=(
            P("dp", None),
            P("dp", None),
            P("dp"),
            P("dp", "tensor"),
            P("dp", "tensor"),
            P("dp", "tensor"),
            P("tensor", "dp"),
            P("dp"),
            P("dp", "tensor"),
            P("dp", "tensor"),
            P("tensor", "dp"),
        ),
        check_vma=False,
    )
```

profile of v0, /device:TPU:0, one launch (start us, length us, event | category | flops | bytes accessed | tf_op | source)
XLA Modules:
  0.0 1853.1 jit_solution(15969643140244901022)
XLA Ops:
  10.9 3.1 fusion.19
  15.5 22.5 %all-gather = bf16[8,1,256]{2,1,0:T(2,128)(2,1)S(1)} all-gather(bf16[1,1,256]{2,1,0:T(2,128)(2,1)S(1)} %reshape.443), channel_id=1, replica_groups=mesh['dp'=8,'tensor'=4] {'dp'}, dimensions={0}, use_global_device_ids=true | all-gather | bytes 4608 | tf_op jit(solution)/shard_map/all_gather | solution.py:163
  38.7 33.1 %all_gather.29 = bf16[2048,128]{1,0:T(8,128)(2,1)S(1)} all-gather(bf16[256,128]{1,0:T(8,128)(2,1)} %param.16), channel_id=1, replica_groups=mesh['dp'=8,'tensor'=4] {'dp'}, dimensions={0}, use_global_device_ids=true | all-gather | bytes 589824 | tf_op jit(solution)/shard_map/all_gather | solution.py:165
  71.8 32.3 %all_gather.28 = bf16[2048,128]{1,0:T(8,128)(2,1)S(1)} all-gather(bf16[256,128]{1,0:T(8,128)(2,1)} %param.17), channel_id=1, replica_groups=mesh['dp'=8,'tensor'=4] {'dp'}, dimensions={0}, use_global_device_ids=true | all-gather | bytes 589824 | tf_op jit(solution)/shard_map/all_gather | solution.py:166
  104.2 3.4 fusion.12
  112.1 5.3 fusion.64
  118.3 7.5 fusion.11
  125.8 9.2 exponential_reduce_fusion
  135.0 7.3 fusion.10
  142.3 9.2 exponential_reduce_fusion.1
  151.6 8.6 convolution_convert_fusion.8
  160.2 2.1 copy-done
  162.3 4.1 convolution_convert_fusion.9
  166.4 7.5 fusion.41
  175.8 16.3 all-gather.1
  192.1 132.1 %all-reduce.12.cloned.1.call-done = f32[1024,2048]{1,0:T(8,128)} async-done(((f32[1024,2048]{1,0:T(8,128)}), f32[1024,2048]{1,0:T(8,128)}) %all-reduce.12.cloned.1.call-update) | async-done | bytes 8388624 | tf_op jit(solution)/shard_map/psum | solution.py:196
  324.2 5.7 multiply_reduce_fusion.2
  330.0 3.4 copy-done.1
  333.3 2.7 multiply_convert_fusion.2
  336.1 114.8 %all-gather.14.cloned.1.call-done = bf16[2048,2048]{1,0:T(8,128)(2,1)} async-done(((bf16[256,2048]{1,0:T(8,128)(2,1)}), bf16[2048,2048]{1,0:T(8,128)(2,1)}) %all-gather.14.cloned.1.call-update) | async-done | bytes 8388624 | tf_op jit(solution)/shard_map/all_gather | solution.py:170
  450.8 14.7 fusion.66
  465.5 110.0 %all-gather.12.cloned.1.call-done = bf16[2048,2048]{1,0:T(8,128)(2,1)} async-done(((bf16[256,2048]{1,0:T(8,128)(2,1)}), bf16[2048,2048]{1,0:T(8,128)(2,1)}) %all-gather.12.cloned.1.call-update) | async-done | bytes 8388624 | tf_op jit(solution)/shard_map/all_gather | solution.py:169
  575.5 14.6 fusion.65
  590.1 110.5 %all-gather.16.cloned.1.call-done = bf16[2048,2048]{1,0:T(8,128)(2,1)} async-done(((bf16[2048,256]{1,0:T(8,128)(2,1)}), bf16[2048,2048]{1,0:T(8,128)(2,1)}) %all-gather.16.cloned.1.call-update) | async-done | bytes 8388624 | tf_op jit(solution)/shard_map/all_gather | solution.py:171
  700.6 21.7 %multiply_convert_fusion = (bf16[1024,2048]{1,0:T(8,128)(2,1)}, bf16[1024,2048]{1,0:T(8,128)(2,1)}, bf16[1024,2048]{1,0:T(8,128)(2,1)}) fusion(f32[1024,2048]{1,0:T(8,128)} %fusion.65, f32[1024,2048]{1,0:T(8,128)} %fusion.66, bf16[1024,2048]{1,0:T(8,128)(2,1)} %param.23, bf16[2048,2048]{1,0:T(8,128)(2,1)} %all-gather.16.cloned.1.call-done), kind=kOutput, calls=%fused_computation.44 | convolution fusion | flops 8623489024 | bytes 41943040 | tf_op jit(solution)/shard_map/dot_general | solution.py:64
  722.3 12.9 fusion.67
  735.2 13.6 convolution_add_fusion
  750.5 149.5 %all-reduce.14.cloned.1.call-done = f32[1024,2048]{1,0:T(8,128)} async-done(((f32[1024,2048]{1,0:T(8,128)}), f32[1024,2048]{1,0:T(8,128)}) %all-reduce.14.cloned.1.call-update) | async-done | bytes 8388624 | tf_op jit(solution)/shard_map/psum | solution.py:214
  900.1 8.2 multiply_reduce_fusion
  908.3 9.6 fusion.17
  917.9 6.6 fusion.32
  925.2 5.2 convolution_bitcast_fusion
  930.4 9.4 fusion
  939.8 13.8 fusion.3
  953.6 8.4 fusion.40
  962.0 2.1 convolution_convert_fusion.6
  964.2 30.0 %fusion.2 = (bf16[2,4,512,1024]{2,3,1,0:T(8,128)(2,1)}, bf16[2,4,512,1024]{2,3,1,0:T(8,128)(2,1)}) fusion(f32[2,1024,512,4]{2,1,3,0:T(8,128)} %get-tuple-element.98, f32[2,1024,512,4]{2,1,3,0:T(8,128)} %get-tuple-element.94, f32[2,4,512]{2,1,0:T(4,128)S(1)} %copy-done.35, f32[2,4,512]{2,1,0:T(4,128)S(1)} %bitcast.237, ...), kind=kLoop, calls=%fused_computation.4 | loop fusion | flops 50331648 | bytes 85000192 | tf_op jit(solution)/shard_map/while/body/eval_jaxpr/convert_element_type | solution.py:126
  994.2 6.2 convolution_bitcast_fusion.2
  1000.4 2.6 fusion.38
  1003.3 2.1 convolution_convert_fusion.7
  1005.5 7.1 convolution_convert_fusion.4
  1012.9 5.0 fusion.35
  1017.9 5.0 fusion.36
  1025.2 3.8 convolution_convert_fusion.5
  1029.1 13.8 convolution_convert_fusion.3
  1044.6 2.4 fusion.68
  1047.0 3.3 add_convert_fusion
  1050.7 14.1 convolution_convert_fusion
  1064.9 14.1 convolution_convert_fusion.1
  1079.2 14.2 convolution_convert_fusion.2
  1098.3 66.5 %reduce-scatter.14.cloned.1.call-done = bf16[512,256]{1,0:T(8,128)(2,1)} async-done(((bf16[512,2048]{1,0:T(8,128)(2,1)}), bf16[512,256]{1,0:T(8,128)(2,1)}) %reduce-scatter.14.cloned.1.call-update) | async-done | bytes 262160 | tf_op jit(solution)/shard_map/reduce_scatter | solution.py:266
  1166.6 69.8 %reduce-scatter.8.cloned.1.call-done = bf16[256,512]{1,0:T(8,128)(2,1)} async-done(((bf16[2048,512]{1,0:T(8,128)(2,1)}), bf16[256,512]{1,0:T(8,128)(2,1)}) %reduce-scatter.8.cloned.1.call-update) | async-done | bytes 262160 | tf_op jit(solution)/shard_map/reduce_scatter | solution.py:257
  1236.4 1.8 convert_element_type.232
  1238.2 153.2 %all-reduce.16.cloned.1.call-done = (bf16[1024,2048]{1,0:T(8,128)(2,1)}, bf16[1024,2048]{1,0:T(8,128)(2,1)}) async-done(((bf16[1024,2048]{1,0:T(8,128)(2,1)}, bf16[1024,2048]{1,0:T(8,128)(2,1)}), (bf16[1024,2048]{1,0:T(8,128)(2,1)}, bf16[1024,2048]{1,0:T(8,128)(2,1)})) %all-reduce.16.cloned.1.call-update) | async-done | bytes 8388624 | tf_op jit(solution)/shard_map/psum | solution.py:203
  1391.4 5.9 fusion.13
  1397.3 22.9 %all-reduce.6 = (bf16[2048]{0:T(1024)(128)(2,1)S(1)}, bf16[2048]{0:T(1024)(128)(2,1)S(1)}) all-reduce(bf16[2048]{0:T(1024)(128)(2,1)S(1)} %get-tuple-element.54, bf16[2048]{0:T(1024)(128)(2,1)S(1)} %copy-done.41), channel_id=2, replica_groups=mesh['dp'=8,'tensor'=4] {'dp'}, use_global_device_ids=true, to_apply=%region_17.18.clone | all-reduce | flops 4096 | bytes 16384
  1421.6 8.6 add_convert_fusion.1
  1430.1 6.9 fusion.18
  1437.0 106.4 %reduce-scatter.20.cloned.1.call-done = bf16[2048,256]{1,0:T(8,128)(2,1)} async-done(((bf16[2048,2048]{1,0:T(8,128)(2,1)}), bf16[2048,256]{1,0:T(8,128)(2,1)}) %reduce-scatter.20.cloned.1.call-update) | async-done | bytes 1048592 | tf_op jit(solution)/shard_map/reduce_scatter | solution.py:278
  1543.5 2.7 convert_element_type.246
  1546.2 147.4 %reduce-scatter.18.cloned.1.call-done = bf16[256,2048]{1,0:T(8,128)(2,1)} async-done(((bf16[2048,2048]{1,0:T(8,128)(2,1)}), bf16[256,2048]{1,0:T(8,128)(2,1)}) %reduce-scatter.18.cloned.1.call-update) | async-done | bytes 1048592 | tf_op jit(solution)/shard_map/reduce_scatter | solution.py:275
  1693.6 2.8 convert_element_type.244
  1696.3 147.3 %reduce-scatter.16.cloned.1.call-done = bf16[256,2048]{1,0:T(8,128)(2,1)} async-done(((bf16[2048,2048]{1,0:T(8,128)(2,1)}), bf16[256,2048]{1,0:T(8,128)(2,1)}) %reduce-scatter.16.cloned.1.call-update) | async-done | bytes 1048592 | tf_op jit(solution)/shard_map/reduce_scatter | solution.py:272
  1843.6 2.8 convert_element_type.242
  (194 shorter events, 27.8 us)
Async XLA Ops:
  7.2 104.9 %all-gather.8.cloned.1.call-start = ((), (), s32[]{:S(2)}) async-start(), calls=%async_computation.7 | async-start | bytes 2359296 | tf_op jit(solution)/shard_map/all_gather | solution.py:164
  7.9 158.5 %all-gather.10.cloned.1.call-start = ((), (), s32[]{:S(2)}) async-start(), calls=%async_computation.8 | async-start | bytes 2359296 | tf_op jit(solution)/shard_map/all_gather | solution.py:167
  8.7 315.5 %all-reduce.12.cloned.1.call-start = ((), (), s32[]{:S(2)}) async-start(), calls=%async_computation.9 | async-start | bytes 16777216 | tf_op jit(solution)/shard_map/psum | solution.py:196
  14.6 96.5 %copy-start.37 = (f32[1024]{0:T(1024)}, f32[1024]{0:T(1024)S(1)}, u32[]{:S(2)}) copy-start(f32[1024]{0:T(1024)S(1)} %fusion.50) | copy-start | bytes 12292
  38.0 73.1 %copy-start.33 = (f32[8,1,256]{2,1,0:T(1,128)}, f32[8,1,256]{2,1,0:T(1,128)S(1)}, u32[]{:S(2)}) copy-start(f32[8,1,256]{2,1,0:T(1,128)S(1)} %convert_element_type.247) | copy-start | bytes 24580
  38.6 65.6 %copy-start.26 = (f32[1,1024,32]{1,2,0:T(8,128)}, f32[1,1024,32]{1,2,0:T(8,128)S(1)}, u32[]{:S(2)}) copy-start(f32[1,1024,32]{1,2,0:T(8,128)S(1)} %get-tuple-element.87) | copy-start | bytes 393220
  38.6 65.6 %copy-start.28 = (f32[1,1024,32]{1,2,0:T(8,128)}, f32[1,1024,32]{1,2,0:T(8,128)S(1)}, u32[]{:S(2)}) copy-start(f32[1,1024,32]{1,2,0:T(8,128)S(1)} %get-tuple-element.88) | copy-start | bytes 393220
  38.6 79.0 %copy-start.24 = (f32[1024,64]{0,1:T(8,128)}, f32[1024,64]{0,1:T(8,128)S(1)}, u32[]{:S(2)}) copy-start(f32[1024,64]{0,1:T(8,128)S(1)} %maximum_bitcast_fusion) | copy-start | bytes 786436
  38.7 78.9 %copy-start.22 = (f32[1024,64]{0,1:T(8,128)}, f32[1024,64]{0,1:T(8,128)S(1)}, u32[]{:S(2)}) copy-start(f32[1024,64]{0,1:T(8,128)S(1)} %maximum_bitcast_fusion.1) | copy-start | bytes 786436
  71.8 39.3 %copy-start.15 = (bf16[2048,128]{1,0:T(8,128)(2,1)}, bf16[2048,128]{1,0:T(8,128)(2,1)S(1)}, u32[]{:S(2)}) copy-start(bf16[2048,128]{1,0:T(8,128)(2,1)S(1)} %all_gather.29) | copy-start | bytes 1572868
  104.2 7.0 copy-start.13
  104.2 7.1 copy-start.36
  107.6 2.0 copy-start.4
  111.9 48.3 %copy-start.8 = (pred[512,1024]{0,1:T(8,128)(4,1)}, pred[512,1024]{0,1:T(8,128)(4,1)S(1)}, u32[]{:S(2)}) copy-start(pred[512,1024]{0,1:T(8,128)(4,1)S(1)} %get-tuple-element.89) | copy-start | bytes 1572868
  112.0 23.0 %copy-start.11 = (bf16[1024,2,64,1]{0,2,3,1:T(8,128)(2,1)}, bf16[1024,2,64,1]{0,2,3,1:T(8,128)(2,1)S(1)}, u32[]{:S(2)}) copy-start(bf16[1024,2,64,1]{0,2,3,1:T(8,128)(2,1)S(1)} %fusion.46) | copy-start | bytes 786436
  118.3 7.5 copy-start.19
  118.3 16.7 copy-start.17
  151.5 8.7 copy-start.31
  151.5 10.7 copy-start
  160.2 6.2 copy-start.45
  166.4 7.6 copy-start.47
  174.0 276.9 %all-gather.14.cloned.1.call-start = ((), (), s32[]{:S(2)}) async-start(), calls=%async_computation.11 | async-start | bytes 9437184 | tf_op jit(solution)/shard_map/all_gather | solution.py:170
  174.5 401.0 %all-gather.12.cloned.1.call-start = ((), (), s32[]{:S(2)}) async-start(), calls=%async_computation.10 | async-start | bytes 9437184 | tf_op jit(solution)/shard_map/all_gather | solution.py:169
  175.1 525.4 %all-gather.16.cloned.1.call-start = ((), (), s32[]{:S(2)}) async-start(), calls=%async_computation.12 | async-start | bytes 9437184 | tf_op jit(solution)/shard_map/all_gather | solution.py:171
  175.7 724.4 %all-reduce.14.cloned.1.call-start = ((), (), s32[]{:S(2)}) async-start(), calls=%async_computation.13 | async-start | bytes 16777216 | tf_op jit(solution)/shard_map/psum | solution.py:214
  329.9 3.4 copy-start.1
  722.3 12.9 copy-start.51
  748.8 346.5 %reduce-scatter.12.cloned.1.call-start = ((), (), s32[]{:S(2)}) async-start(), calls=%async_computation.16 | async-start | bytes 589824 | tf_op jit(solution)/shard_map/reduce_scatter | solution.py:263
  900.1 8.2 copy-start.21
  908.2 9.6 copy-start.43
  908.3 16.3 slice-start
  908.3 16.3 slice-start.1
  908.3 16.3 slice-start.2
  917.9 7.3 slice-start.3
  930.4 9.4 copy-start.9
  939.8 13.8 copy-start.32
  939.8 13.8 copy-start.50
  953.6 8.4 copy-start.5
  953.6 10.6 copy-start.35
  964.1 132.7 %reduce-scatter.10.cloned.1.call-start = ((), (), s32[]{:S(2)}) async-start(), calls=%async_computation.15 | async-start | bytes 589824 | tf_op jit(solution)/shard_map/reduce_scatter | solution.py:260
  964.2 30.0 %copy-start.20 = (bf16[1,512,8,64]{1,3,2,0:T(8,128)(2,1)S(1)}, bf16[1,512,8,64]{1,3,2,0:T(8,128)(2,1)}, u32[]{:S(2)}) copy-start(bf16[1,512,8,64]{1,3,2,0:T(8,128)(2,1)} %copy-done.19) | copy-start | bytes 1572868
  994.2 6.2 copy-start.3
  994.2 6.2 copy-start.18
  1000.4 2.8 copy-start.30
  1000.4 2.9 copy-start.6
  1000.4 5.1 copy-start.46
  1000.4 5.1 copy-start.48
  1005.4 7.5 copy-start.12
  1005.4 159.4 %reduce-scatter.14.cloned.1.call-start = ((), (), s32[]{:S(2)}) async-start(), calls=%async_computation.17 | async-start | bytes 2359296 | tf_op jit(solution)/shard_map/reduce_scatter | solution.py:266
  1012.6 223.8 %reduce-scatter.8.cloned.1.call-start = ((), (), s32[]{:S(2)}) async-start(), calls=%async_computation.14 | async-start | bytes 2359296 | tf_op jit(solution)/shard_map/reduce_scatter | solution.py:257
  1017.9 5.2 copy-start.23
  1022.9 2.3 copy-start.7
  1029.0 362.3 %all-reduce.16.cloned.1.call-start = ((), (), s32[]{:S(2)}) async-start(), calls=%async_computation.21 | async-start | bytes 16777216 | tf_op jit(solution)/shard_map/psum | solution.py:203
  1029.1 13.9 copy-start.16
  1044.6 2.4 copy-start.14
  1050.3 493.2 %reduce-scatter.20.cloned.1.call-start = ((), (), s32[]{:S(2)}) async-start(), calls=%async_computation.20 | async-start | bytes 9437184 | tf_op jit(solution)/shard_map/reduce_scatter | solution.py:278
  1064.9 628.7 %reduce-scatter.18.cloned.1.call-start = ((), (), s32[]{:S(2)}) async-start(), calls=%async_computation.19 | async-start | bytes 9437184 | tf_op jit(solution)/shard_map/reduce_scatter | solution.py:275
  1079.0 764.6 %reduce-scatter.16.cloned.1.call-start = ((), (), s32[]{:S(2)}) async-start(), calls=%async_computation.18 | async-start | bytes 9437184 | tf_op jit(solution)/shard_map/reduce_scatter | solution.py:272
  1093.4 298.0 %copy-start.34 = (f32[8,1,256]{2,1,0:T(1,128)S(1)}, f32[8,1,256]{2,1,0:T(1,128)}, u32[]{:S(2)}) copy-start(f32[8,1,256]{2,1,0:T(1,128)} %copy-done.33) | copy-start | bytes 24580
  1093.4 298.0 %copy-start.38 = (f32[1024]{0:T(1024)S(1)}, f32[1024]{0:T(1024)}, u32[]{:S(2)}) copy-start(f32[1024]{0:T(1024)} %copy-done.37) | copy-start | bytes 12292
  1093.4 303.9 %copy-start.41 = (bf16[2048]{0:T(1024)(128)(2,1)S(1)}, bf16[2048]{0:T(1024)(128)(2,1)}, u32[]{:S(2)}) copy-start(bf16[2048]{0:T(1024)(128)(2,1)} %get-tuple-element.52) | copy-start | bytes 12292
  1093.4 328.1 %copy-start.40 = (f32[1024]{0:T(1024)S(1)}, f32[1024]{0:T(1024)}, u32[]{:S(2)}) copy-start(f32[1024]{0:T(1024)} %copy-done.39) | copy-start | bytes 12292
  1421.5 8.6 copy-start.2
  1421.5 8.6 copy-start.10
  (7 other events, 7.5 us)
Sparse Core Ops, SparseCore 0:
  10.1 57.9 all-gather.7
  70.1 52.7 all-gather.9
  174.1 150.0 all-reduce.11
  326.2 124.6 all-gather.13
  452.8 122.6 all-gather.11
  577.4 123.1 all-gather.15
  749.0 151.0 all-reduce.13
  964.2 62.8 reduce-scatter.11
  1031.0 61.7 reduce-scatter.9
  1096.7 68.0 reduce-scatter.13
  1169.0 67.3 reduce-scatter.7
  1239.4 151.9 all-reduce.15
  1395.0 148.4 reduce-scatter.19
  1547.0 146.5 reduce-scatter.17
  1697.0 146.5 reduce-scatter.15
where the time goes:
time: 1860 us; the launch traced here: 1850 us
  waiting for transfers between devices  1310 us (70%)
  matrix products  261 us (14%)
  blocking collectives  127 us (7%)
  other arithmetic  124 us (7%)
    psum x1, waiting for transfers between devices, shards(): lax.psum(ffn_part.astype(jnp.bfloat16), 'tensor').astype(jnp.float32)  153 us
    psum x1, waiting for transfers between devices, shards(): normed_two_grad = lax.psum(mlp_part, 'tensor')  150 us
    reduce_scatter x1, waiting for transfers between devices, shards(): lax.psum_scatter(up_weight_grad.astype(jnp.bfloat16), 'dp', scatter_dimen...  147 us
    reduce_scatter x1, waiting for transfers between devices, shards(): lax.psum_scatter(gate_weight_grad.astype(jnp.bfloat16), 'dp', scatter_dim...  147 us
    psum x1, waiting for transfers between devices, shards(): hidden_state = tokens_float + lax.psum(attn_part, 'tensor')  132 us
    all_gather x1, waiting for transfers between devices, shards(): lax.all_gather(up_weight, 'dp', axis=0, tiled=True)  115 us
    all_gather x1, waiting for transfers between devices, shards(): lax.all_gather(down_weight, 'dp', axis=1, tiled=True)  110 us
    all_gather x1, waiting for transfers between devices, shards(): lax.all_gather(gate_weight, 'dp', axis=0, tiled=True)  110 us
  transfers between devices with their start and end apart: 15, of which 11 were waited for; matrix products, arithmetic and copies ran while one was open for 14% of the time, Pallas kernels for 0%

commit v1 on v0

v1 whole, which is shorter than its diff:
```python
from functools import partial
import math

import jax
import jax.numpy as jnp
from jax import lax
from jax.sharding import PartitionSpec as P

HD = 64
GROUP = 4
epsilon = 1e-05
BF = jnp.bfloat16
F32 = jnp.float32


def rope_tables(segment_row, head_size):
    length = segment_row.shape[0]
    places = jnp.arange(length, dtype=jnp.int32)
    boundary = jnp.concatenate([jnp.ones((1,), dtype=bool), segment_row[1:] != segment_row[:-1]])
    starts = lax.cummax(jnp.where(boundary, places, 0), axis=0)
    position = (places - starts).astype(jnp.float32)
    half_size = head_size // 2
    exponent = jnp.arange(half_size, dtype=jnp.float32) * 2.0 / head_size
    inverse = 1.0 / 500000.0**exponent
    wavelen = 2.0 * math.pi / inverse
    smooth = (8192.0 / wavelen - 1.0) / 3.0
    scaled = jnp.where(
        wavelen < 2048.0,
        inverse,
        jnp.where(
            wavelen > 8192.0, inverse / 32.0, (1.0 - smooth) * inverse / 32.0 + smooth * inverse
        ),
    )
    angles = position[:, None] * scaled[None, :]
    cosine_table = jnp.cos(angles)
    sine_table = jnp.sin(angles)
    return (
        jnp.concatenate([cosine_table, cosine_table], axis=-1),
        jnp.concatenate([sine_table, sine_table], axis=-1),
    )


def rotate(values, cosine_table, sine_table):
    half_size = values.shape[-1] // 2
    turned = jnp.concatenate([-values[..., half_size:], values[..., :half_size]], axis=-1)
    return values * cosine_table + turned * sine_table


def dot_rows(left, right, out=F32):
    return lax.dot_general(
        left, right, (((0,), (0,)), ((), ())), preferred_element_type=F32
    ).astype(out)


def dot_cols(left, right, out=F32):
    return lax.dot_general(
        left, right, (((1,), (1,)), ((), ())), preferred_element_type=F32
    ).astype(out)


def dot(left, right, out=F32):
    return jnp.dot(left, right, preferred_element_type=F32).astype(out)


def tie(value, *others):
    return lax.optimization_barrier((value, *others))[0]


def inverse_root(values):
    return lax.rsqrt(jnp.mean(values * values, axis=-1, keepdims=True) + epsilon)


def block_scores(query_block, key_seq, segment_row, start_row):
    row_count = query_block.shape[0]
    length = key_seq.shape[0]
    scores = jnp.einsum("qkgd,skd->kgqs", query_block, key_seq, preferred_element_type=F32)
    row_ids = start_row + jnp.arange(row_count, dtype=jnp.int32)
    col_ids = jnp.arange(length, dtype=jnp.int32)
    same_doc = segment_row[start_row : start_row + row_count][:, None] == segment_row[None, :]
    allowed = same_doc & (col_ids[None, :] <= row_ids[:, None])
    return jnp.where(allowed, scores, -1000000000.0)


def attend_forward(query_seq, key_seq, value_seq, segment_row):
    length, kv_local, head_size = key_seq.shape
    grouped = query_seq.reshape(length, kv_local, -1, head_size)
    block_rows = min(512, length)
    mixed_parts = []
    total_parts = []
    for start_row in range(0, length, block_rows):
        scores = block_scores(
            grouped[start_row : start_row + block_rows], key_seq, segment_row, start_row
        )
        row_max = jnp.max(scores, axis=-1, keepdims=True)
        log_total = jnp.log(jnp.sum(jnp.exp(scores - row_max), axis=-1, keepdims=True)) + row_max
        soft_low = jnp.exp(scores - log_total).astype(BF)
        mixed_block = jnp.einsum("kgqs,skd->qkgd", soft_low, value_seq, preferred_element_type=F32)
        mixed_parts.append(mixed_block.reshape(block_rows, -1).astype(BF))
        total_parts.append(log_total)
    return (jnp.concatenate(mixed_parts, axis=0), jnp.concatenate(total_parts, axis=2))


def attend_backward(query_seq, key_seq, value_seq, log_total, grad_seq, segment_row):
    length, kv_local, head_size = key_seq.shape
    grouped = query_seq.reshape(length, kv_local, -1, head_size)
    grad_grouped = grad_seq.reshape(length, kv_local, -1, head_size)
    block_rows = min(512, length)
    score_scale = head_size ** (-0.5)
    query_parts = []
    key_grad = jnp.zeros(key_seq.shape, F32)
    value_grad = jnp.zeros(value_seq.shape, F32)
    for start_row in range(0, length, block_rows):
        query_block = grouped[start_row : start_row + block_rows]
        grad_block = grad_grouped[start_row : start_row + block_rows]
        scores = block_scores(query_block, key_seq, segment_row, start_row)
        soft_weights = jnp.exp(scores - log_total[:, :, start_row : start_row + block_rows])
        soft_grad = jnp.einsum("qkgd,skd->kgqs", grad_block, value_seq, preferred_element_type=F32)
        score_grad = (
            soft_weights * (soft_grad - jnp.sum(soft_weights * soft_grad, axis=-1, keepdims=True))
        ).astype(BF)
        query_parts.append(
            jnp.einsum("kgqs,skd->qkgd", score_grad, key_seq, preferred_element_type=F32)
            * score_scale
        )
        key_grad = key_grad + jnp.einsum(
            "kgqs,qkgd->skd", score_grad, query_block, preferred_element_type=F32
        )
        value_grad = value_grad + jnp.einsum(
            "kgqs,qkgd->skd", soft_weights.astype(BF), grad_block, preferred_element_type=F32
        )
    query_grad = jnp.concatenate(query_parts, axis=0).reshape(length, -1, head_size)
    return (query_grad, key_grad, value_grad)


def shards(
    dp_size,
    tensor_size,
    tokens,
    segment_ids,
    attn_gain,
    query_weight,
    key_weight,
    value_weight,
    output_weight,
    ffn_gain,
    gate_weight,
    up_weight,
    down_weight,
    cotangent,
):
    groups = dp_size // 2
    dp_index = lax.axis_index("dp")
    z_index, y_index = dp_index // 2, dp_index % 2
    t_index = lax.axis_index("tensor")
    token_count, width = tokens.shape
    rows = query_weight.shape[0]
    quarter = token_count // tensor_size
    half_quarter = quarter // 2

    def swap_y(value):
        return lax.ppermute(value, "dp", [(i, i ^ 1) for i in range(dp_size)])

    def swap_x(value):
        return lax.ppermute(value, "tensor", [(i, i ^ 2) for i in range(tensor_size)])

    def swap_core(value):
        return lax.ppermute(value, "tensor", [(i, i ^ 1) for i in range(tensor_size)])

    def hop(value):
        return lax.ppermute(value, "dp", [(i, (i + 2) % dp_size) for i in range(dp_size)])

    def ring_gather(value):
        pieces = [value]
        for _ in range(groups - 1):
            pieces.append(hop(pieces[-1]))
        return pieces

    def place(pieces, side, axis):
        size = pieces[0][0].shape[axis]
        shape = list(pieces[0][0].shape)
        shape[axis] = size * dp_size
        whole = jnp.zeros(shape, BF)
        for value, step, y_of in pieces:
            block = ((z_index - step) % groups) * 2 + y_of
            start = [0, 0]
            start[axis] = block * size
            whole = lax.dynamic_update_slice(whole, value, tuple(start))
        return whole

    def my_half(value, axis, mine):
        size = value.shape[axis] // 2
        which = y_index if mine else 1 - y_index
        return lax.dynamic_slice_in_dim(value, which * size, size, axis)

    def relative(value):
        return jnp.concatenate(
            [
                lax.dynamic_slice_in_dim(value, (t_index ^ j) * quarter, quarter, 0)
                for j in range(tensor_size)
            ],
            axis=0,
        )

    def absolute(pieces, dtype):
        whole = jnp.zeros((quarter * tensor_size, pieces[0].shape[1]), dtype)
        for j, piece in enumerate(pieces):
            whole = lax.dynamic_update_slice(
                whole, piece.astype(dtype), ((t_index ^ j) * quarter, 0)
            )
        return whole

    attn_scale = attn_gain.astype(F32)[:, None]
    ffn_scale = ffn_gain.astype(F32)[:, None]

    def scaled(weight, scale):
        return (weight.astype(F32) * scale).astype(BF)

    qkv_local = scaled(jnp.concatenate([query_weight, key_weight, value_weight], axis=1), attn_scale)
    qkv_ring = ring_gather(qkv_local)
    qkv_other = [swap_y(v) for v in qkv_ring]
    qkv_full = place(
        [(v, s, y_index) for s, v in enumerate(qkv_ring)]
        + [(v, s, 1 - y_index) for s, v in enumerate(qkv_other)],
        None,
        0,
    )
    out_ring = ring_gather(tie(output_weight, qkv_ring[-2]))
    out_other = [swap_y(v) for v in out_ring]
    out_full = place(
        [(v, s, y_index) for s, v in enumerate(out_ring)]
        + [(v, s, 1 - y_index) for s, v in enumerate(out_other)],
        None,
        1,
    )

    gate_scaled, up_scaled = scaled(gate_weight, ffn_scale), scaled(up_weight, ffn_scale)
    gu_mine = jnp.concatenate([my_half(gate_scaled, 1, True), my_half(up_scaled, 1, True)], axis=1)
    gu_send = jnp.concatenate([my_half(gate_scaled, 1, False), my_half(up_scaled, 1, False)], axis=1)
    gu_got = swap_y(tie(gu_send, qkv_ring[1]))
    gu_ring_a = ring_gather(tie(gu_mine, out_ring[-2]))
    gu_ring_b = ring_gather(tie(gu_got, gu_ring_a[-2]))
    gu_full = place(
        [(v, s, y_index) for s, v in enumerate(gu_ring_a)]
        + [(v, s, 1 - y_index) for s, v in enumerate(gu_ring_b)],
        None,
        0,
    )
    down_got = swap_y(tie(my_half(down_weight, 0, False), gu_got))
    down_ring_a = ring_gather(tie(my_half(down_weight, 0, True), gu_ring_b[-2]))
    down_ring_b = ring_gather(tie(down_got, down_ring_a[-2]))
    down_full = place(
        [(v, s, y_index) for s, v in enumerate(down_ring_a)]
        + [(v, s, 1 - y_index) for s, v in enumerate(down_ring_b)],
        None,
        1,
    )
    cot_rel = relative(cotangent)
    cot_y = swap_y(tie(cot_rel[:quarter], down_got))
    cot_yx = swap_x(cot_y)
    cot_yc = swap_core(jnp.concatenate([cot_y, cot_yx], axis=0))
    cot_all = jnp.concatenate(
        [cot_rel, cot_y, cot_yc[:quarter], cot_yx, cot_yc[quarter:]], axis=0
    )

    tokens_float = tokens.astype(F32)
    token_root = inverse_root(tokens_float)
    normed = (tokens_float * token_root).astype(BF)
    qkv_raw = dot(normed, qkv_full)
    q_cols, kv_cols = query_weight.shape[1], key_weight.shape[1]
    segment_row = segment_ids[0]
    cosine_table, sine_table = rope_tables(segment_row, HD)
    cosine_wide, sine_wide = cosine_table[:, None, :], sine_table[:, None, :]
    query_raw = qkv_raw[:, :q_cols].reshape(token_count, -1, HD)
    key_raw = qkv_raw[:, q_cols : q_cols + kv_cols].reshape(token_count, -1, HD)
    value_seq = qkv_raw[:, q_cols + kv_cols :].astype(BF).reshape(token_count, -1, HD)
    query_low = (rotate(query_raw, cosine_wide, sine_wide) * HD ** (-0.5)).astype(BF)
    key_low = rotate(key_raw, cosine_wide, sine_wide).astype(BF)
    mixed, log_total = attend_forward(query_low, key_low, value_seq, segment_row)
    mixed_rel = relative(mixed)
    attn_part = dot(mixed_rel, out_full, BF)

    def two_way(first, second):
        return first.astype(F32) + second.astype(F32)

    def scatter_tensor(part):
        send = jnp.concatenate([part[quarter : 2 * quarter], part[3 * quarter :]], axis=0)
        got = swap_core(send)
        keep = two_way(part[:quarter], got[:quarter])
        pass_on = two_way(part[2 * quarter : 3 * quarter], got[quarter:]).astype(BF)
        return keep + swap_x(pass_on).astype(F32)

    def gather_tensor(piece):
        from_core = swap_core(piece)
        from_x = swap_x(piece)
        from_both = swap_core(from_x)
        return [piece, from_core, from_x, from_both]

    def my_quarter(value):
        return lax.dynamic_slice_in_dim(value, t_index * quarter, quarter, 0)

    tokens_quarter = my_quarter(tokens).astype(F32)
    hidden = tokens_quarter + scatter_tensor(attn_part)
    hidden_root = inverse_root(hidden)
    n_two = (hidden * hidden_root).astype(BF)

    first, second = n_two[:half_quarter], n_two[half_quarter:]
    first_x, second_y = swap_x(first), swap_y(second)
    first_y = swap_y(jnp.concatenate([first, first_x], axis=0))
    second_x = swap_x(jnp.concatenate([second, second_y], axis=0))
    held = jnp.concatenate(
        [
            first,
            second,
            first_x,
            second_x[:half_quarter],
            first_y[:half_quarter],
            second_y,
            first_y[half_quarter:],
            second_x[half_quarter:],
        ],
        axis=0,
    )
    crossed = swap_core(held)
    n_all = jnp.concatenate(
        [
            piece
            for y_side in range(2)
            for x_side in range(2)
            for piece in (
                held[(2 * y_side + x_side) * quarter : (2 * y_side + x_side + 1) * quarter],
                crossed[(2 * y_side + x_side) * quarter : (2 * y_side + x_side + 1) * quarter],
            )
        ],
        axis=0,
    )
    hidden_units = gate_weight.shape[1] // 2
    gu_values = dot(n_all, gu_full, BF)
    gate_values = gu_values[:, :hidden_units].astype(F32)
    up_values = gu_values[:, hidden_units:].astype(F32)
    sig = jax.nn.sigmoid(gate_values)
    silu = gate_values * sig
    active = (silu * up_values).astype(BF)

    def scatter_pair(part):
        blocks = [part[j * quarter : (j + 1) * quarter] for j in range(8)]
        got = swap_core(jnp.concatenate([blocks[1], blocks[3], blocks[5], blocks[7]], axis=0))
        kept = [
            two_way(blocks[2 * j], got[j * quarter : (j + 1) * quarter]) for j in range(4)
        ]
        top = [v[:half_quarter] for v in kept]
        low = [v[half_quarter:] for v in kept]
        top_got = swap_x(jnp.concatenate([top[1], top[3]], axis=0).astype(BF)).astype(F32)
        low_got = swap_y(jnp.concatenate([low[2], low[3]], axis=0).astype(BF)).astype(F32)
        top_keep = top[0] + top_got[:half_quarter]
        top_pass = (top[2] + top_got[half_quarter:]).astype(BF)
        low_keep = low[0] + low_got[:half_quarter]
        low_pass = (low[1] + low_got[half_quarter:]).astype(BF)
        return jnp.concatenate(
            [
                top_keep + swap_y(top_pass).astype(F32),
                low_keep + swap_x(low_pass).astype(F32),
            ],
            axis=0,
        )

    def ring_scatter(grad, axis):
        size = grad.shape[axis] // groups

        def block(index):
            return lax.dynamic_slice_in_dim(grad, (index % groups) * size, size, axis)

        running = block(z_index - 1)
        for step in range(groups - 1):
            received = hop(running)
            running = (received.astype(F32) + block(z_index - 2 - step).astype(F32)).astype(BF)
        return running

    down_grad = dot_rows(active, cot_all, BF)
    down_block = ring_scatter(down_grad, 1)

    active_grad = dot_cols(cot_all, down_full)
    gate_grad = (active_grad * up_values * (sig * (1.0 + gate_values * (1.0 - sig)))).astype(BF)
    up_grad = (active_grad * silu).astype(BF)
    gu_grad = jnp.concatenate([gate_grad, up_grad], axis=1)
    e_part = dot_cols(gu_grad, gu_full, BF)
    e_two = scatter_pair(e_part)
    n_hidden = hidden * hidden_root
    cot_quarter = my_quarter(cotangent).astype(F32)
    hidden_grad = cot_quarter + hidden_root * (
        e_two - n_hidden * jnp.mean(e_two * n_hidden, axis=-1, keepdims=True)
    )
    hidden_low = jnp.concatenate(gather_tensor(hidden_grad.astype(BF)), axis=0)

    gu_weight_grad = dot_rows(n_all, gu_grad, BF)
    gu_block = ring_scatter(gu_weight_grad, 0)

    ffn_part = dot(active, down_full, BF)
    layer_quarter = (hidden + scatter_pair(ffn_part)).astype(BF)
    layer_output = absolute(gather_tensor(layer_quarter), BF)

    out_weight_grad = dot_rows(mixed_rel, hidden_low, BF)
    mixed_grad_rel = dot_cols(hidden_low, out_full, BF)
    mixed_grad = absolute(
        [mixed_grad_rel[j * quarter : (j + 1) * quarter] for j in range(tensor_size)], BF
    )
    query_grad, key_grad, value_grad = attend_backward(
        query_low,
        key_low,
        value_seq,
        log_total,
        mixed_grad.reshape(token_count, -1, HD),
        segment_row,
    )
    query_raw_grad = rotate(query_grad, cosine_wide, -sine_wide).astype(BF).reshape(token_count, -1)
    key_raw_grad = rotate(key_grad, cosine_wide, -sine_wide).astype(BF).reshape(token_count, -1)
    value_raw_grad = value_grad.astype(BF).reshape(token_count, -1)
    qkv_grad = jnp.concatenate([query_raw_grad, key_raw_grad, value_raw_grad], axis=1)
    e_one_part = dot_cols(relative(qkv_grad), qkv_full, BF)
    e_one = scatter_tensor(e_one_part)
    n_one = tokens_quarter * my_quarter(token_root)
    tokens_grad_quarter = hidden_grad + my_quarter(token_root) * (
        e_one - n_one * jnp.mean(e_one * n_one, axis=-1, keepdims=True)
    )
    tokens_grad = absolute(gather_tensor(tokens_grad_quarter.astype(BF)), F32)
    qkv_weight_grad = dot_rows(normed, qkv_grad, BF)

    def split_y(grad, axis, size):
        shape = grad.shape
        cut = grad.reshape(shape[:axis] + (groups, 2, size) + shape[axis + 1 :])
        mine = lax.dynamic_index_in_dim(cut, y_index, axis + 1, keepdims=False)
        other = lax.dynamic_index_in_dim(cut, 1 - y_index, axis + 1, keepdims=False)
        flat = shape[:axis] + (groups * size,) + shape[axis + 1 :]
        return mine.reshape(flat), other.reshape(flat)

    def scatter_whole(grad, axis, size):
        mine, other = split_y(grad, axis, size)
        got = swap_y(other)
        return ring_scatter((mine.astype(F32) + got.astype(F32)).astype(BF), axis)

    out_grad = scatter_whole(out_weight_grad, 1, output_weight.shape[1]).astype(F32)
    qkv_block = scatter_whole(qkv_weight_grad, 0, rows).astype(F32)

    def trade(block, axis_cut):
        mine = my_half(block, axis_cut, True)
        got = swap_y(my_half(block, axis_cut, False))
        return mine.astype(F32), got.astype(F32)

    def by_y(mine, got, axis):
        return jnp.where(
            y_index == 0,
            jnp.concatenate([mine, got], axis=axis),
            jnp.concatenate([got, mine], axis=axis),
        )

    gu_mine_rows, gu_got_rows = trade(gu_block, 0)
    gate_g = by_y(gu_mine_rows[:, :hidden_units], gu_got_rows[:, :hidden_units], 1)
    up_g = by_y(gu_mine_rows[:, hidden_units:], gu_got_rows[:, hidden_units:], 1)
    down_mine, down_got_cols = trade(down_block, 1)
    down_weight_grad = by_y(down_mine, down_got_cols, 0)

    attn_gain_part = jnp.sum(
        qkv_block * jnp.concatenate([query_weight, key_weight, value_weight], axis=1).astype(F32),
        axis=1,
    )
    ffn_gain_part = jnp.sum(
        gate_g * gate_weight.astype(F32) + up_g * up_weight.astype(F32), axis=1
    )
    gain_grads = lax.psum(jnp.stack([attn_gain_part, ffn_gain_part]), "tensor")
    qkv_out = qkv_block * attn_scale
    return (
        layer_output,
        tokens_grad,
        gain_grads[0],
        qkv_out[:, :q_cols],
        qkv_out[:, q_cols : q_cols + kv_cols],
        qkv_out[:, q_cols + kv_cols :],
        out_grad,
        gain_grads[1],
        gate_g * ffn_scale,
        up_g * ffn_scale,
        down_weight_grad,
    )


def solution(mesh):
    return jax.shard_map(
        partial(shards, mesh.shape["dp"], mesh.shape["tensor"]),
        mesh=mesh,
        in_specs=(
            P("dp", None),
            P("dp", None),
            P("dp"),
            P("dp", "tensor"),
            P("dp", "tensor"),
            P("dp", "tensor"),
            P("tensor", "dp"),
            P("dp"),
            P("dp", "tensor"),
            P("dp", "tensor"),
            P("tensor", "dp"),
            P("dp", None),
        ),
        out_specs=(
            P("dp", None),
            P("dp", None),
            P("dp"),
            P("dp", "tensor"),
            P("dp", "tensor"),
            P("dp", "tensor"),
            P("tensor", "dp"),
            P("dp"),
            P("dp", "tensor"),
            P("dp", "tensor"),
            P("tensor", "dp"),
        ),
        check_vma=False,
    )
```

time: 1860 us -> 1010 us (0.54)
  waiting for transfers between devices: 1310 us -> 470 us
  blocking collectives: 127 us -> 23.5 us
  local copies, waits for them, and re-layouts: 12.5 us -> 96.8 us
  starting transfers between devices: 1.39 us -> 42.8 us
  matrix products: 261 us -> 230 us
    reduce_scatter x7 -> x0, waiting for transfers between devices: 537 us -> none  [the longest x1 147 us: shards(): lax.psum_scatter(up_weight_grad.astype(jnp.bfloat16), 'dp', scatter_dimen...]
    ppermute x0 -> x75, waiting for transfers between devices: none -> 470 us  [the longest x30 276 us: hop(): lax.ppermute(value, 'dp', [(i, (i + 2) % dp_size) for i in range(dp_size)])]
    psum x3 -> x0, waiting for transfers between devices: 435 us -> none  [the longest x1 153 us: shards(): lax.psum(ffn_part.astype(jnp.bfloat16), 'tensor').astype(jnp.float32)]
    all_gather x5 -> x0, waiting for transfers between devices: 335 us -> none  [the longest x1 115 us: shards(): lax.all_gather(up_weight, 'dp', axis=0, tiled=True)]
    all_gather x4 -> x0, blocking collectives: 104 us -> none  [the longest x1 33.1 us: shards(): lax.all_gather(key_weight, 'dp', axis=0, tiled=True)]
    ppermute x0 -> x75, starting transfers between devices: none -> 42.8 us  [the longest x21 23.6 us: swap_y(): return lax.ppermute(value, 'dp', [(i, i ^ 1) for i in range(dp_size)])]
    dot_general x23 -> x14, matrix products: 192 us -> 161 us  [the longest x4 54.7 us: dot_cols(): lax.dot_general(left, right, (((1,), (1,)), ((), ())), preferred_element_...]
    unnamed x115 -> x234, local copies, waits for them, and re-layouts: 11.4 us -> 41.4 us
  transfers between devices with their start and end apart: 15 -> 75, of which waited for: 11 -> 36; matrix products, arithmetic and copies ran while one was open for 14% -> 33% of each run, Pallas kernels for 0% -> 0%
where the time goes in v1:
time: 1010 us; the launch traced here: 1000 us
  waiting for transfers between devices  470 us (47%)
  matrix products  230 us (23%)
  other arithmetic  137 us (14%)
  local copies, waits for them, and re-layouts  96.8 us (10%)
  starting transfers between devices  42.8 us (4%)
  blocking collectives  23.5 us (2%)
    ppermute x30, waiting for transfers between devices, hop(): lax.ppermute(value, 'dp', [(i, (i + 2) % dp_size) for i in range(dp_size)])  276 us
    ppermute x21, waiting for transfers between devices, swap_y(): return lax.ppermute(value, 'dp', [(i, i ^ 1) for i in range(dp_size)])  118 us
    ppermute x12, waiting for transfers between devices, swap_x(): lax.ppermute(value, 'tensor', [(i, i ^ 2) for i in range(tensor_size)])  76.1 us
    dot_general x4, matrix products, dot_cols(): lax.dot_general(left, right, (((1,), (1,)), ((), ())), preferred_element_...  54.7 us
    dot_general x4, matrix products, dot_rows(): lax.dot_general(left, right, (((0,), (0,)), ((), ())), preferred_element_...  46.2 us
    dot_general x4, matrix products, dot(): return jnp.dot(left, right, preferred_element_type=F32).astype(out)  43.5 us
    unnamed x234, local copies, waits for them, and re-layouts  41.4 us
    convert_element_type x1, other arithmetic, attend_backward(): score_grad = (soft_weights * (soft_grad - jnp.sum(soft_weights * soft_gra...  29.7 us
  transfers between devices with their start and end apart: 75, of which 36 were waited for; matrix products, arithmetic and copies ran while one was open for 33% of the time, Pallas kernels for 0%

profile of v1, /device:TPU:0, one launch (start us, length us, event | category | flops | bytes accessed | tf_op | source)
XLA Modules:
  0.0 1004.1 jit_solution(1185002223804355476)
XLA Ops:
  15.1 4.3 collective-permute-done
  21.8 9.9 collective-permute-done.1
  36.8 6.2 collective-permute-done.7
  45.2 3.5 collective-permute-done.2
  53.9 3.3 collective-permute-done.8
  62.3 5.7 fusion.41
  69.4 8.4 fusion.6
  77.8 8.6 exponential_reduce_fusion.1
  86.5 8.3 convolution_convert_fusion.11
  94.9 8.4 fusion.7
  103.2 8.6 exponential_reduce_fusion
  111.9 8.1 convolution_convert_fusion.10
  139.8 19.8 %collective-permute-done.24 = bf16[256,2048]{0,1:T(8,128)(2,1)S(1)} collective-permute-done((bf16[256,2048]{0,1:T(8,128)(2,1)S(1)}, bf16[256,2048]{0,1:T(8,128)(2,1)S(1)}, u32[]{:S(2)}, u32[]{:S(2)}) %collective-permute-start.24) | collective-permute-done | bytes 1048608 | tf_op jit(solution)/shard_map/ppermute | solution.py:161
  161.8 11.4 %collective-permute-done.31 = bf16[1024,256]{1,0:T(8,128)(2,1)S(1)} collective-permute-done((bf16[1024,256]{1,0:T(8,128)(2,1)S(1)}, bf16[1024,256]{1,0:T(8,128)(2,1)S(1)}, u32[]{:S(2)}, u32[]{:S(2)}) %collective-permute-start.31) | collective-permute-done | bytes 524320 | tf_op jit(solution)/shard_map/ppermute | solution.py:161
  182.2 17.1 %collective-permute-done.43 = bf16[256,2048]{1,0:T(8,128)(2,1)} collective-permute-done((bf16[256,2048]{1,0:T(8,128)(2,1)S(1)}, bf16[256,2048]{1,0:T(8,128)(2,1)}, u32[]{:S(2)}, u32[]{:S(2)}) %collective-permute-start.43) | collective-permute-done | bytes 1048608 | tf_op jit(solution)/shard_map/ppermute | solution.py:161
  202.4 5.9 collective-permute-done.17
  211.8 25.0 %collective-permute-done.16 = bf16[128,2048]{1,0:T(8,128)(2,1)S(1)} collective-permute-done((bf16[128,2048]{1,0:T(8,128)(2,1)}, bf16[128,2048]{1,0:T(8,128)(2,1)S(1)}, u32[]{:S(2)}, u32[]{:S(2)}) %collective-permute-start.16) | collective-permute-done | bytes 524320 | tf_op jit(solution)/shard_map/ppermute | solution.py:164
  244.2 10.1 %collective-permute-done.18 = bf16[256,2048]{1,0:T(8,128)(2,1)S(1)} collective-permute-done((bf16[256,2048]{1,0:T(8,128)(2,1)S(1)}, bf16[256,2048]{1,0:T(8,128)(2,1)S(1)}, u32[]{:S(2)}, u32[]{:S(2)}) %collective-permute-start.18) | collective-permute-done | bytes 1048608 | tf_op jit(solution)/shard_map/ppermute | solution.py:164
  258.4 27.3 %collective-permute-done.26 = bf16[256,2048]{0,1:T(8,128)(2,1)S(1)} collective-permute-done((bf16[256,2048]{0,1:T(8,128)(2,1)S(1)}, bf16[256,2048]{0,1:T(8,128)(2,1)S(1)}, u32[]{:S(2)}, u32[]{:S(2)}) %collective-permute-start.26) | collective-permute-done | bytes 1048608 | tf_op jit(solution)/shard_map/ppermute | solution.py:170
  286.2 16.1 %collective-permute-done.28 = bf16[1024,256]{1,0:T(8,128)(2,1)S(1)} collective-permute-done((bf16[1024,256]{1,0:T(8,128)(2,1)S(1)}, bf16[1024,256]{1,0:T(8,128)(2,1)S(1)}, u32[]{:S(2)}, u32[]{:S(2)}) %collective-permute-start.28) | collective-permute-done | bytes 524320 | tf_op jit(solution)/shard_map/ppermute | solution.py:170
  304.2 14.7 %collective-permute-done.29 = bf16[1024,256]{1,0:T(8,128)(2,1)S(1)} collective-permute-done((bf16[1024,256]{1,0:T(8,128)(2,1)S(1)}, bf16[1024,256]{1,0:T(8,128)(2,1)S(1)}, u32[]{:S(2)}, u32[]{:S(2)}) %collective-permute-start.29) | collective-permute-done | bytes 524320 | tf_op jit(solution)/shard_map/ppermute | solution.py:170
  322.3 29.6 %collective-permute-done.32 = bf16[1024,256]{1,0:T(8,128)(2,1)S(1)} collective-permute-done((bf16[1024,256]{1,0:T(8,128)(2,1)S(1)}, bf16[1024,256]{1,0:T(8,128)(2,1)S(1)}, u32[]{:S(2)}, u32[]{:S(2)}) %collective-permute-start.32) | collective-permute-done | bytes 524320 | tf_op jit(solution)/shard_map/ppermute | solution.py:170
  353.1 15.7 %collective-permute-done.33 = bf16[1024,256]{1,0:T(8,128)(2,1)S(1)} collective-permute-done((bf16[1024,256]{1,0:T(8,128)(2,1)S(1)}, bf16[1024,256]{1,0:T(8,128)(2,1)S(1)}, u32[]{:S(2)}, u32[]{:S(2)}) %collective-permute-start.33) | collective-permute-done | bytes 524320 | tf_op jit(solution)/shard_map/ppermute | solution.py:170
  369.2 10.6 %collective-permute-done.34 = bf16[1024,256]{1,0:T(8,128)(2,1)S(1)} collective-permute-done((bf16[1024,256]{1,0:T(8,128)(2,1)S(1)}, bf16[1024,256]{1,0:T(8,128)(2,1)S(1)}, u32[]{:S(2)}, u32[]{:S(2)}) %collective-permute-start.34) | collective-permute-done | bytes 524320 | tf_op jit(solution)/shard_map/ppermute | solution.py:170
  389.6 22.0 %convolution_convert_fusion.3 = bf16[2048,2048]{0,1:T(8,128)(2,1)} fusion(bf16[2048,2048]{1,0:T(8,128)(2,1)} %slice_dynamic-update-slice_fusion.2, bf16[2048,2048]{0,1:T(8,128)(2,1)S(1)} %constant_dynamic-update-slice_fusion.21), kind=kOutput, calls=%fused_computation.42 | convolution fusion | flops 17184063488 | bytes 25165824 | tf_op jit(solution)/shard_map/dot_general | solution.py:62
  411.6 14.5 %convolution_convert_fusion.4 = bf16[1024,2048]{1,0:T(8,128)(2,1)S(1)} fusion(bf16[2048,2048]{1,0:T(8,128)(2,1)} %slice_dynamic-update-slice_fusion, bf16[2048,2048]{0,1:T(8,128)(2,1)} %convolution_convert_fusion.3), kind=kOutput, calls=%fused_computation.49 | convolution fusion | flops 8608808960 | bytes 20971520 | tf_op jit(solution)/shard_map/dot_general | solution.py:50
  426.1 19.3 %fusion.14 = (bf16[2048,1024]{0,1:T(8,128)(2,1)}, bf16[2048,1024]{0,1:T(8,128)(2,1)}) fusion(bf16[2048,2048]{0,1:T(8,128)(2,1)} %convolution_convert_fusion.3, bf16[2048,2048]{1,0:T(8,128)(2,1)} %slice_dynamic-update-slice_fusion, bf16[1024,2048]{1,0:T(8,128)(2,1)S(1)} %constant_dynamic-update-slice_fusion.13), kind=kOutput, calls=%fused_computation.31 | convolution fusion | flops 8621391872 | bytes 29360128 | tf_op jit(solution)/shard_map/dot_general | solution.py:56
  445.4 22.6 %convolution_convert_fusion = bf16[2048,2048]{0,1:T(8,128)(2,1)S(1)} fusion(bf16[2048,2048]{1,0:T(8,128)(2,1)} %slice_dynamic-update-slice_fusion.2, bf16[2048,1024]{0,1:T(8,128)(2,1)} %get-tuple-element.84, bf16[2048,1024]{0,1:T(8,128)(2,1)} %get-tuple-element.83), kind=kOutput, calls=%fused_computation.39 | convolution fusion | flops 17200840704 | bytes 25165824 | tf_op jit(solution)/shard_map/dot_general | solution.py:50
  468.1 23.8 %convolution_convert_fusion.1 = bf16[2048,2048]{1,0:T(8,128)(2,1)} fusion(bf16[2048,2048]{0,1:T(8,128)(2,1)S(1)} %constant_dynamic-update-slice_fusion.21, bf16[2048,1024]{0,1:T(8,128)(2,1)} %get-tuple-element.84, bf16[2048,1024]{0,1:T(8,128)(2,1)} %get-tuple-element.83), kind=kOutput, calls=%fused_computation.40 | convolution fusion | flops 17200840704 | bytes 25165824 | tf_op jit(solution)/shard_map/dot_general | solution.py:56
  493.6 13.4 %convolution_convert_fusion.2 = bf16[2048,2048]{1,0:T(8,128)(2,1)S(1)} fusion(bf16[1024,2048]{1,0:T(8,128)(2,1)} %copy-done.41, bf16[2048,2048]{0,1:T(8,128)(2,1)} %convolution_convert_fusion.3), kind=kOutput, calls=%fused_computation.41 | convolution fusion | flops 8610906112 | bytes 20971520 | tf_op jit(solution)/shard_map/dot_general | solution.py:62
  507.0 12.8 %collective-permute-done.71 = bf16[1024,512]{1,0:T(8,128)(2,1)S(1)} collective-permute-done((bf16[1024,512]{1,0:T(8,128)(2,1)S(1)}, bf16[1024,512]{1,0:T(8,128)(2,1)S(1)}, u32[]{:S(2)}, u32[]{:S(2)}) %collective-permute-start.71) | collective-permute-done | bytes 1048608 | tf_op jit(solution)/shard_map/ppermute | solution.py:170
  525.7 55.4 %collective-permute-done.72 = bf16[1024,512]{1,0:T(8,128)(2,1)S(1)} collective-permute-done((bf16[1024,512]{1,0:T(8,128)(2,1)S(1)}, bf16[1024,512]{1,0:T(8,128)(2,1)S(1)}, u32[]{:S(2)}, u32[]{:S(2)}) %collective-permute-start.72) | collective-permute-done | bytes 1048608 | tf_op jit(solution)/shard_map/ppermute | solution.py:170
  587.2 23.2 %collective-permute-done.73 = bf16[1024,512]{1,0:T(8,128)(2,1)S(1)} collective-permute-done((bf16[1024,512]{1,0:T(8,128)(2,1)}, bf16[1024,512]{1,0:T(8,128)(2,1)S(1)}, u32[]{:S(2)}, u32[]{:S(2)}) %collective-permute-start.73) | collective-permute-done | bytes 1048608 | tf_op jit(solution)/shard_map/ppermute | solution.py:170
  615.2 7.2 collective-permute-done.74
  625.1 21.1 %collective-permute-done.64 = bf16[512,2048]{0,1:T(8,128)(2,1)} collective-permute-done((bf16[512,2048]{0,1:T(8,128)(2,1)S(1)}, bf16[512,2048]{0,1:T(8,128)(2,1)}, u32[]{:S(2)}, u32[]{:S(2)}) %collective-permute-start.64) | collective-permute-done | bytes 2097184 | tf_op jit(solution)/shard_map/ppermute | solution.py:170
  646.2 4.3 add_convert_fusion.1
  650.7 5.4 convert_add_fusion.4
  659.6 4.0 convert_add_fusion.7
  666.3 17.4 %collective-permute-done.49 = bf16[256,2048]{1,0:T(8,128)(2,1)S(1)} collective-permute-done((bf16[256,2048]{1,0:T(8,128)(2,1)}, bf16[256,2048]{1,0:T(8,128)(2,1)S(1)}, u32[]{:S(2)}, u32[]{:S(2)}) %collective-permute-start.49) | collective-permute-done | bytes 1048608 | tf_op jit(solution)/shard_map/ppermute | solution.py:161
  686.5 10.7 %collective-permute-done.38 = bf16[256,2048]{1,0:T(8,128)(2,1)S(1)} collective-permute-done((bf16[256,2048]{1,0:T(8,128)(2,1)S(1)}, bf16[256,2048]{1,0:T(8,128)(2,1)S(1)}, u32[]{:S(2)}, u32[]{:S(2)}) %collective-permute-start.38) | collective-permute-done | bytes 1048608 | tf_op jit(solution)/shard_map/ppermute | solution.py:161
  699.1 8.0 collective-permute-done.36
  708.6 6.1 collective-permute-done.50
  726.0 12.2 %collective-permute-done.52 = bf16[256,2048]{1,0:T(8,128)(2,1)S(1)} collective-permute-done((bf16[256,2048]{1,0:T(8,128)(2,1)S(1)}, bf16[256,2048]{1,0:T(8,128)(2,1)S(1)}, u32[]{:S(2)}, u32[]{:S(2)}) %collective-permute-start.52) | collective-permute-done | bytes 1048608 | tf_op jit(solution)/shard_map/ppermute | solution.py:164
  742.1 12.1 %collective-permute-done.41 = bf16[256,2048]{1,0:T(8,128)(2,1)} collective-permute-done((bf16[256,2048]{1,0:T(8,128)(2,1)S(1)}, bf16[256,2048]{1,0:T(8,128)(2,1)}, u32[]{:S(2)}, u32[]{:S(2)}) %collective-permute-start.41) | collective-permute-done | bytes 1048608 | tf_op jit(solution)/shard_map/ppermute | solution.py:164
  756.7 5.8 convolution_convert_fusion.9
  764.6 8.7 convolution_bitcast_fusion
  773.2 14.0 %fusion = (f32[2,4,512]{2,1,0:T(4,128)}, f32[2,1024,512,4]{2,1,3,0:T(8,128)}) fusion(f32[2,1024,512,4]{2,1,3,0:T(8,128)} %get-tuple-element.174, f32[2,4,512]{2,1,0:T(4,128)} %bitcast.212, pred[512,1024]{0,1:T(8,128)(4,1)} %copy-done.5, bf16[1024,2,64,1]{0,2,3,1:T(8,128)(2,1)} %bitcast.195, bf16[512,2,4,64]{0,3,2,1:T(8,128)(2,1)} %bitcast.200), kind=kOutput, calls=%fused_computation.2 | convolution fusion | flops 553644032 | bytes 34897920 | tf_op jit(solution)/shard_map/qkgd,skd->kgqs/dot_general | solution.py:117
  787.3 10.1 %fusion.3 = (f32[2,4,512]{2,1,0:T(4,128)}, f32[2,1024,512,4]{2,1,3,0:T(8,128)}) fusion(f32[2,1024,512,4]{2,1,3,0:T(8,128)S(1)} %bitcast.177, f32[2,4,512]{2,1,0:T(4,128)S(1)} %bitcast.208, pred[512,1024]{0,1:T(8,128)(4,1)S(1)} %copy-done.4, bf16[1024,2,64,1]{0,2,3,1:T(8,128)(2,1)} %bitcast.196, bf16[512,2,4,64]{0,3,2,1:T(8,128)(2,1)} %bitcast.197), kind=kOutput, calls=%fused_computation.7 | convolution fusion | flops 553644032 | bytes 34897920 | tf_op jit(solution)/shard_map/qkgd,skd->kgqs/dot_general | solution.py:117
  797.4 29.7 %fusion.2 = (bf16[2,4,512,1024]{2,3,1,0:T(8,128)(2,1)}, bf16[2,4,512,1024]{2,3,1,0:T(8,128)(2,1)}) fusion(f32[2,1024,512,4]{2,1,3,0:T(8,128)} %get-tuple-element.176, f32[2,1024,512,4]{2,1,3,0:T(8,128)} %get-tuple-element.174, f32[2,4,512]{2,1,0:T(4,128)} %get-tuple-element.175, f32[2,4,512]{2,1,0:T(4,128)} %bitcast.213, pred[512,1024]{0,1:T(8,128)(4,1)} %copy-done.5, ...), kind=kLoop, calls=%fused_computation.4 | loop fusion | flops 41943040 | bytes 85000192 | tf_op jit(solution)/shard_map/convert_element_type | solution.py:120
  827.2 6.2 convolution_bitcast_fusion.2
  835.0 7.9 fusion.57
  851.3 5.5 convolution_convert_fusion.7
  856.9 3.7 convolution_convert_fusion.8
  860.5 4.1 copy.74
  864.7 3.2 constant_dynamic-slice_fusion.3
  871.9 5.9 convolution_convert_fusion.6
  888.3 5.6 fusion.55
  904.1 23.4 %collective-permute-done.59 = bf16[1024,768]{1,0:T(8,128)(2,1)} collective-permute-done((bf16[1024,768]{1,0:T(8,128)(2,1)}, bf16[1024,768]{1,0:T(8,128)(2,1)}, u32[]{:S(2)}, u32[]{:S(2)}) %collective-permute-start.59) | collective-permute-done | bytes 1572896 | tf_op jit(solution)/shard_map/ppermute | solution.py:161
  933.3 10.3 %collective-permute-done.60 = bf16[256,768]{1,0:T(8,128)(2,1)S(1)} collective-permute-done((bf16[256,768]{1,0:T(8,128)(2,1)S(1)}, bf16[256,768]{1,0:T(8,128)(2,1)S(1)}, u32[]{:S(2)}, u32[]{:S(2)}) %collective-permute-start.60) | collective-permute-done | bytes 393248 | tf_op jit(solution)/shard_map/ppermute | solution.py:170
  946.1 3.1 collective-permute-done.69
  949.4 8.3 collective-permute-done.61
  962.4 4.2 convert_dynamic-update-slice_fusion.3
  966.7 3.4 copy-done.22
  974.4 23.5 %psum.7 = f32[2,256]{1,0:T(2,128)S(1)} all-reduce(f32[2,256]{1,0:T(2,128)S(1)} %pad_maximum_fusion.28), channel_id=1, replica_groups=mesh['dp'=8,'tensor'=4] {'tensor'}, use_global_device_ids=true, to_apply=%region_14.15 | all-reduce | flops 512 | bytes 4096 | tf_op jit(solution)/shard_map/psum | solution.py:468
  (528 shorter events, 212.1 us)
Async XLA Ops:
  5.3 14.2 %collective-permute-start = (bf16[256,768]{1,0:T(8,128)(2,1)S(1)}, bf16[256,768]{1,0:T(8,128)(2,1)S(1)}, u32[]{:S(2)}, u32[]{:S(2)}) collective-permute-start(bf16[256,768]{1,0:T(8,128)(2,1)S(1)} %get-tuple-element.82), channel_id=1, source_target_pairs={{0,8},{4,12},{8,16},{12,20},{16,24},{20,28},{24,0},{28,4},{1,9},{5... | collective-permute-start | bytes 1179656 | tf_op jit(solution)/shard_map/ppermute | solution.py:170
  8.3 41.2 %collective-permute-start.3 = (bf16[256,768]{1,0:T(8,128)(2,1)S(1)}, bf16[256,768]{1,0:T(8,128)(2,1)S(1)}, u32[]{:S(2)}, u32[]{:S(2)}) collective-permute-start(bf16[256,768]{1,0:T(8,128)(2,1)S(1)} %get-tuple-element.82), channel_id=1, source_target_pairs={{0,4},{4,0},{8,12},{12,8},{16,20},{20,16},{24,28},{28,24},{1,5},{5... | collective-permute-start | bytes 1179656 | tf_op jit(solution)/shard_map/ppermute | solution.py:161
  20.2 31.2 %collective-permute-start.4 = (bf16[256,768]{1,0:T(8,128)(2,1)S(1)}, bf16[256,768]{1,0:T(8,128)(2,1)S(1)}, u32[]{:S(2)}, u32[]{:S(2)}) collective-permute-start(bf16[256,768]{1,0:T(8,128)(2,1)S(1)} %collective-permute-done), channel_id=1, source_target_pairs={{0,4},{4,0},{8,12},{12,8},{16,20},{20,16},{24,28},{28,24},{1,5},{5... | collective-permute-start | bytes 1179656 | tf_op jit(solution)/shard_map/ppermute | solution.py:161
  31.7 17.0 %collective-permute-start.2 = (bf16[256,768]{1,0:T(8,128)(2,1)}, bf16[256,768]{1,0:T(8,128)(2,1)S(1)}, u32[]{:S(2)}, u32[]{:S(2)}) collective-permute-start(bf16[256,768]{1,0:T(8,128)(2,1)} %collective-permute-done.1), channel_id=1, source_target_pairs={{0,8},{4,12},{8,16},{12,20},{16,24},{20,28},{24,0},{28,4},{1,9},{5... | collective-permute-start | bytes 1179656 | tf_op jit(solution)/shard_map/ppermute | solution.py:170
  32.4 88.7 %collective-permute-start.10 = (bf16[512,256]{1,0:T(8,128)(2,1)}, bf16[512,256]{1,0:T(8,128)(2,1)}, u32[]{:S(2)}, u32[]{:S(2)}) collective-permute-start(bf16[512,256]{1,0:T(8,128)(2,1)} %param.18), channel_id=1, source_target_pairs={{0,4},{4,0},{8,12},{12,8},{16,20},{20,16},{24,28},{28,24},{1,5},{5... | collective-permute-start | bytes 786440 | tf_op jit(solution)/shard_map/ppermute | solution.py:161
  51.4 70.8 %collective-permute-start.11 = (bf16[512,256]{1,0:T(8,128)(2,1)}, bf16[512,256]{1,0:T(8,128)(2,1)S(1)}, u32[]{:S(2)}, u32[]{:S(2)}) collective-permute-start(bf16[512,256]{1,0:T(8,128)(2,1)} %collective-permute-done.7), channel_id=1, source_target_pairs={{0,4},{4,0},{8,12},{12,8},{16,20},{20,16},{24,28},{28,24},{1,5},{5... | collective-permute-start | bytes 786440 | tf_op jit(solution)/shard_map/ppermute | solution.py:161
  57.2 65.0 %collective-permute-start.12 = (bf16[512,256]{1,0:T(8,128)(2,1)}, bf16[512,256]{1,0:T(8,128)(2,1)}, u32[]{:S(2)}, u32[]{:S(2)}) collective-permute-start(bf16[512,256]{1,0:T(8,128)(2,1)} %collective-permute-done.8), channel_id=1, source_target_pairs={{0,4},{4,0},{8,12},{12,8},{16,20},{20,16},{24,28},{28,24},{1,5},{5... | collective-permute-start | bytes 786440 | tf_op jit(solution)/shard_map/ppermute | solution.py:161
  58.3 61.8 %collective-permute-start.9 = (bf16[512,256]{1,0:T(8,128)(2,1)}, bf16[512,256]{1,0:T(8,128)(2,1)S(1)}, u32[]{:S(2)}, u32[]{:S(2)}) collective-permute-start(bf16[512,256]{1,0:T(8,128)(2,1)} %collective-permute-done.8), channel_id=1, source_target_pairs={{0,8},{4,12},{8,16},{12,20},{16,24},{20,28},{24,0},{28,4},{1,9},{5... | collective-permute-start | bytes 786440 | tf_op jit(solution)/shard_map/ppermute | solution.py:170
  134.0 25.6 %collective-permute-start.24 = (bf16[256,2048]{0,1:T(8,128)(2,1)S(1)}, bf16[256,2048]{0,1:T(8,128)(2,1)S(1)}, u32[]{:S(2)}, u32[]{:S(2)}) collective-permute-start(bf16[256,2048]{0,1:T(8,128)(2,1)S(1)} %pad_maximum_fusion.16), channel_id=1, source_target_pairs={{0,4},{4,0},{8,12},{12,8},{16,20},{20,16},{24,28},{28,24},{1,5},{5... | collective-permute-start | bytes 3145736 | tf_op jit(solution)/shard_map/ppermute | solution.py:161
  135.1 39.1 %collective-permute-start.21 = (bf16[256,2048]{0,1:T(8,128)(2,1)S(1)}, bf16[256,2048]{0,1:T(8,128)(2,1)}, u32[]{:S(2)}, u32[]{:S(2)}) collective-permute-start(bf16[256,2048]{0,1:T(8,128)(2,1)S(1)} %pad_maximum_fusion.15), channel_id=1, source_target_pairs={{0,8},{4,12},{8,16},{12,20},{16,24},{20,28},{24,0},{28,4},{1,9},{5... | collective-permute-start | bytes 3145736 | tf_op jit(solution)/shard_map/ppermute | solution.py:170
  137.9 36.4 %collective-permute-start.15 = (bf16[256,2048]{1,0:T(8,128)(2,1)S(1)}, bf16[256,2048]{1,0:T(8,128)(2,1)S(1)}, u32[]{:S(2)}, u32[]{:S(2)}) collective-permute-start(bf16[256,2048]{1,0:T(8,128)(2,1)S(1)} %add_convert_fusion.9), channel_id=1, source_target_pairs={{0,2},{1,3},{2,0},{3,1},{4,6},{5,7},{6,4},{7,5},{8,10},{9,11},{10,... | collective-permute-start | bytes 3145736 | tf_op jit(solution)/shard_map/ppermute | solution.py:164
  159.6 13.6 %collective-permute-start.31 = (bf16[1024,256]{1,0:T(8,128)(2,1)S(1)}, bf16[1024,256]{1,0:T(8,128)(2,1)S(1)}, u32[]{:S(2)}, u32[]{:S(2)}) collective-permute-start(bf16[1024,256]{1,0:T(8,128)(2,1)S(1)} %get-tuple-element.24), channel_id=1, source_target_pairs={{0,4},{4,0},{8,12},{12,8},{16,20},{20,16},{24,28},{28,24},{1,5},{5... | collective-permute-start | bytes 1572872 | tf_op jit(solution)/shard_map/ppermute | solution.py:161
  173.2 26.1 %collective-permute-start.43 = (bf16[256,2048]{1,0:T(8,128)(2,1)S(1)}, bf16[256,2048]{1,0:T(8,128)(2,1)}, u32[]{:S(2)}, u32[]{:S(2)}) collective-permute-start(bf16[256,2048]{1,0:T(8,128)(2,1)S(1)} %get-tuple-element.26), channel_id=1, source_target_pairs={{0,4},{4,0},{8,12},{12,8},{16,20},{20,16},{24,28},{28,24},{1,5},{5... | collective-permute-start | bytes 3145736 | tf_op jit(solution)/shard_map/ppermute | solution.py:161
  174.3 28.2 %collective-permute-start.22 = (bf16[256,2048]{0,1:T(8,128)(2,1)}, bf16[256,2048]{0,1:T(8,128)(2,1)}, u32[]{:S(2)}, u32[]{:S(2)}) collective-permute-start(bf16[256,2048]{0,1:T(8,128)(2,1)} %collective-permute-done.21), channel_id=1, source_target_pairs={{0,8},{4,12},{8,16},{12,20},{16,24},{20,28},{24,0},{28,4},{1,9},{5... | collective-permute-start | bytes 3145736 | tf_op jit(solution)/shard_map/ppermute | solution.py:170
  179.1 29.2 %collective-permute-start.17 = (bf16[128,2048]{1,0:T(8,128)(2,1)}, bf16[128,2048]{1,0:T(8,128)(2,1)S(1)}, u32[]{:S(2)}, u32[]{:S(2)}) collective-permute-start(bf16[128,2048]{1,0:T(8,128)(2,1)} %get-tuple-element.139), channel_id=1, source_target_pairs={{0,4},{4,0},{8,12},{12,8},{16,20},{20,16},{24,28},{28,24},{1,5},{5... | collective-permute-start | bytes 1572872 | tf_op jit(solution)/shard_map/ppermute | solution.py:161
  199.3 41.2 %collective-permute-start.44 = (bf16[256,2048]{1,0:T(8,128)(2,1)}, bf16[256,2048]{1,0:T(8,128)(2,1)}, u32[]{:S(2)}, u32[]{:S(2)}) collective-permute-start(bf16[256,2048]{1,0:T(8,128)(2,1)} %collective-permute-done.43), channel_id=1, source_target_pairs={{0,2},{1,3},{2,0},{3,1},{4,6},{5,7},{6,4},{7,5},{8,10},{9,11},{10,... | collective-permute-start | bytes 3145736 | tf_op jit(solution)/shard_map/ppermute | solution.py:164
  200.3 36.5 %collective-permute-start.16 = (bf16[128,2048]{1,0:T(8,128)(2,1)}, bf16[128,2048]{1,0:T(8,128)(2,1)S(1)}, u32[]{:S(2)}, u32[]{:S(2)}) collective-permute-start(bf16[128,2048]{1,0:T(8,128)(2,1)} %get-tuple-element.140), channel_id=1, source_target_pairs={{0,2},{1,3},{2,0},{3,1},{4,6},{5,7},{6,4},{7,5},{8,10},{9,11},{10,... | collective-permute-start | bytes 1572872 | tf_op jit(solution)/shard_map/ppermute | solution.py:164
  202.4 39.8 %collective-permute-start.25 = (bf16[256,2048]{0,1:T(8,128)(2,1)}, bf16[256,2048]{0,1:T(8,128)(2,1)S(1)}, u32[]{:S(2)}, u32[]{:S(2)}) collective-permute-start(bf16[256,2048]{0,1:T(8,128)(2,1)} %copy-done.53), channel_id=1, source_target_pairs={{0,8},{4,12},{8,16},{12,20},{16,24},{20,28},{24,0},{28,4},{1,9},{5... | collective-permute-start | bytes 3145736 | tf_op jit(solution)/shard_map/ppermute | solution.py:170
  209.5 44.7 %collective-permute-start.18 = (bf16[256,2048]{1,0:T(8,128)(2,1)S(1)}, bf16[256,2048]{1,0:T(8,128)(2,1)S(1)}, u32[]{:S(2)}, u32[]{:S(2)}) collective-permute-start(bf16[256,2048]{1,0:T(8,128)(2,1)S(1)} %pad_maximum_fusion.13), channel_id=1, source_target_pairs={{0,2},{1,3},{2,0},{3,1},{4,6},{5,7},{6,4},{7,5},{8,10},{9,11},{10,... | collective-permute-start | bytes 3145736 | tf_op jit(solution)/shard_map/ppermute | solution.py:164
  237.9 16.4 %collective-permute-start.19 = (bf16[256,2048]{1,0:T(8,128)(2,1)S(1)}, bf16[256,2048]{1,0:T(8,128)(2,1)S(1)}, u32[]{:S(2)}, u32[]{:S(2)}) collective-permute-start(bf16[256,2048]{1,0:T(8,128)(2,1)S(1)} %pad_maximum_fusion.14), channel_id=1, source_target_pairs={{0,4},{4,0},{8,12},{12,8},{16,20},{20,16},{24,28},{28,24},{1,5},{5... | collective-permute-start | bytes 3145736 | tf_op jit(solution)/shard_map/ppermute | solution.py:161
  240.4 45.3 %collective-permute-start.23 = (bf16[256,2048]{0,1:T(8,128)(2,1)}, bf16[256,2048]{0,1:T(8,128)(2,1)S(1)}, u32[]{:S(2)}, u32[]{:S(2)}) collective-permute-start(bf16[256,2048]{0,1:T(8,128)(2,1)} %collective-permute-done.22), channel_id=1, source_target_pairs={{0,8},{4,12},{8,16},{12,20},{16,24},{20,28},{24,0},{28,4},{1,9},{5... | collective-permute-start | bytes 3145736 | tf_op jit(solution)/shard_map/ppermute | solution.py:170
  242.2 76.7 %collective-permute-start.45 = (bf16[512,2048]{1,0:T(8,128)(2,1)S(1)}, bf16[512,2048]{1,0:T(8,128)(2,1)S(1)}, u32[]{:S(2)}, u32[]{:S(2)}) collective-permute-start(bf16[512,2048]{1,0:T(8,128)(2,1)S(1)} %pad_maximum_fusion.7), channel_id=1, source_target_pairs={{0,1},{1,0},{2,3},{3,2},{4,5},{5,4},{6,7},{7,6},{8,9},{9,8},{10,11... | collective-permute-start | bytes 6291464 | tf_op jit(solution)/shard_map/ppermute | solution.py:167
  242.3 43.4 %collective-permute-start.26 = (bf16[256,2048]{0,1:T(8,128)(2,1)S(1)}, bf16[256,2048]{0,1:T(8,128)(2,1)S(1)}, u32[]{:S(2)}, u32[]{:S(2)}) collective-permute-start(bf16[256,2048]{0,1:T(8,128)(2,1)S(1)} %collective-permute-done.25), channel_id=1, source_target_pairs={{0,8},{4,12},{8,16},{12,20},{16,24},{20,28},{24,0},{28,4},{1,9},{5... | collective-permute-start | bytes 3145736 | tf_op jit(solution)/shard_map/ppermute | solution.py:170
  254.5 125.3 %collective-permute-start.20 = (bf16[1024,2048]{1,0:T(8,128)(2,1)S(1)}, bf16[1024,2048]{1,0:T(8,128)(2,1)S(1)}, u32[]{:S(2)}, u32[]{:S(2)}) collective-permute-start(bf16[1024,2048]{1,0:T(8,128)(2,1)S(1)} %slice_dynamic-update-slice_fusion.7), channel_id=1, source_target_pairs={{0,1},{1,0},{2,3},{3,2},{4,5},{5,4},{6,7},{7,6},{8,9},{9,8},{10,11... | collective-permute-start | bytes 12582920 | tf_op jit(solution)/shard_map/ppermute | solution.py:167
  285.7 16.6 %collective-permute-start.28 = (bf16[1024,256]{1,0:T(8,128)(2,1)S(1)}, bf16[1024,256]{1,0:T(8,128)(2,1)S(1)}, u32[]{:S(2)}, u32[]{:S(2)}) collective-permute-start(bf16[1024,256]{1,0:T(8,128)(2,1)S(1)} %copy-done.51), channel_id=1, source_target_pairs={{0,8},{4,12},{8,16},{12,20},{16,24},{20,28},{24,0},{28,4},{1,9},{5... | collective-permute-start | bytes 1572872 | tf_op jit(solution)/shard_map/ppermute | solution.py:170
  302.3 16.6 %collective-permute-start.29 = (bf16[1024,256]{1,0:T(8,128)(2,1)S(1)}, bf16[1024,256]{1,0:T(8,128)(2,1)S(1)}, u32[]{:S(2)}, u32[]{:S(2)}) collective-permute-start(bf16[1024,256]{1,0:T(8,128)(2,1)S(1)} %collective-permute-done.28), channel_id=1, source_target_pairs={{0,8},{4,12},{8,16},{12,20},{16,24},{20,28},{24,0},{28,4},{1,9},{5... | collective-permute-start | bytes 1572872 | tf_op jit(solution)/shard_map/ppermute | solution.py:170
  303.3 49.6 %collective-permute-start.27 = (bf16[256,2048]{0,1:T(8,128)(2,1)S(1)}, bf16[256,2048]{0,1:T(8,128)(2,1)S(1)}, u32[]{:S(2)}, u32[]{:S(2)}) collective-permute-start(bf16[256,2048]{0,1:T(8,128)(2,1)S(1)} %collective-permute-done.26), channel_id=1, source_target_pairs={{0,8},{4,12},{8,16},{12,20},{16,24},{20,28},{24,0},{28,4},{1,9},{5... | collective-permute-start | bytes 3145736 | tf_op jit(solution)/shard_map/ppermute | solution.py:170
  318.9 33.0 %collective-permute-start.32 = (bf16[1024,256]{1,0:T(8,128)(2,1)S(1)}, bf16[1024,256]{1,0:T(8,128)(2,1)S(1)}, u32[]{:S(2)}, u32[]{:S(2)}) collective-permute-start(bf16[1024,256]{1,0:T(8,128)(2,1)S(1)} %copy-done.61), channel_id=1, source_target_pairs={{0,8},{4,12},{8,16},{12,20},{16,24},{20,28},{24,0},{28,4},{1,9},{5... | collective-permute-start | bytes 1572872 | tf_op jit(solution)/shard_map/ppermute | solution.py:170
  322.3 46.6 %collective-permute-start.30 = (bf16[1024,256]{1,0:T(8,128)(2,1)S(1)}, bf16[1024,256]{1,0:T(8,128)(2,1)S(1)}, u32[]{:S(2)}, u32[]{:S(2)}) collective-permute-start(bf16[1024,256]{1,0:T(8,128)(2,1)S(1)} %collective-permute-done.29), channel_id=1, source_target_pairs={{0,8},{4,12},{8,16},{12,20},{16,24},{20,28},{24,0},{28,4},{1,9},{5... | collective-permute-start | bytes 1572872 | tf_op jit(solution)/shard_map/ppermute | solution.py:170
  351.9 16.9 %collective-permute-start.33 = (bf16[1024,256]{1,0:T(8,128)(2,1)S(1)}, bf16[1024,256]{1,0:T(8,128)(2,1)S(1)}, u32[]{:S(2)}, u32[]{:S(2)}) collective-permute-start(bf16[1024,256]{1,0:T(8,128)(2,1)S(1)} %collective-permute-done.32), channel_id=1, source_target_pairs={{0,8},{4,12},{8,16},{12,20},{16,24},{20,28},{24,0},{28,4},{1,9},{5... | collective-permute-start | bytes 1572872 | tf_op jit(solution)/shard_map/ppermute | solution.py:170
  492.0 27.9 %collective-permute-start.71 = (bf16[1024,512]{1,0:T(8,128)(2,1)S(1)}, bf16[1024,512]{1,0:T(8,128)(2,1)S(1)}, u32[]{:S(2)}, u32[]{:S(2)}) collective-permute-start(bf16[1024,512]{1,0:T(8,128)(2,1)S(1)} %constant_dynamic-slice_fusion.1), channel_id=1, source_target_pairs={{0,8},{4,12},{8,16},{12,20},{16,24},{20,28},{24,0},{28,4},{1,9},{5... | collective-permute-start | bytes 3145736 | tf_op jit(solution)/shard_map/ppermute | solution.py:170
  493.6 88.8 %collective-permute-start.63 = (bf16[512,2048]{0,1:T(8,128)(2,1)}, bf16[512,2048]{0,1:T(8,128)(2,1)}, u32[]{:S(2)}, u32[]{:S(2)}) collective-permute-start(bf16[512,2048]{0,1:T(8,128)(2,1)} %constant_dynamic-slice_fusion.6), channel_id=1, source_target_pairs={{0,8},{4,12},{8,16},{12,20},{16,24},{20,28},{24,0},{28,4},{1,9},{5... | collective-permute-start | bytes 6291464 | tf_op jit(solution)/shard_map/ppermute | solution.py:170
  520.3 60.8 %collective-permute-start.72 = (bf16[1024,512]{1,0:T(8,128)(2,1)S(1)}, bf16[1024,512]{1,0:T(8,128)(2,1)S(1)}, u32[]{:S(2)}, u32[]{:S(2)}) collective-permute-start(bf16[1024,512]{1,0:T(8,128)(2,1)S(1)} %add_convert_fusion.5), channel_id=1, source_target_pairs={{0,8},{4,12},{8,16},{12,20},{16,24},{20,28},{24,0},{28,4},{1,9},{5... | collective-permute-start | bytes 3145736 | tf_op jit(solution)/shard_map/ppermute | solution.py:170
  525.4 125.3 %collective-permute-start.46 = (bf16[1024,2048]{1,0:T(8,128)(2,1)}, bf16[1024,2048]{1,0:T(8,128)(2,1)}, u32[]{:S(2)}, u32[]{:S(2)}) collective-permute-start(bf16[1024,2048]{1,0:T(8,128)(2,1)} %pad_maximum_fusion.4), channel_id=1, source_target_pairs={{0,1},{1,0},{2,3},{3,2},{4,5},{5,4},{6,7},{7,6},{8,9},{9,8},{10,11... | collective-permute-start | bytes 12582920 | tf_op jit(solution)/shard_map/ppermute | solution.py:167
  582.4 28.0 %collective-permute-start.73 = (bf16[1024,512]{1,0:T(8,128)(2,1)}, bf16[1024,512]{1,0:T(8,128)(2,1)S(1)}, u32[]{:S(2)}, u32[]{:S(2)}) collective-permute-start(bf16[1024,512]{1,0:T(8,128)(2,1)} %add_convert_fusion.4), channel_id=1, source_target_pairs={{0,8},{4,12},{8,16},{12,20},{16,24},{20,28},{24,0},{28,4},{1,9},{5... | collective-permute-start | bytes 3145736 | tf_op jit(solution)/shard_map/ppermute | solution.py:170
  584.9 61.3 %collective-permute-start.64 = (bf16[512,2048]{0,1:T(8,128)(2,1)S(1)}, bf16[512,2048]{0,1:T(8,128)(2,1)}, u32[]{:S(2)}, u32[]{:S(2)}) collective-permute-start(bf16[512,2048]{0,1:T(8,128)(2,1)S(1)} %add_convert_fusion.2), channel_id=1, source_target_pairs={{0,8},{4,12},{8,16},{12,20},{16,24},{20,28},{24,0},{28,4},{1,9},{5... | collective-permute-start | bytes 6291464 | tf_op jit(solution)/shard_map/ppermute | solution.py:170
  587.2 72.3 %collective-permute-start.35 = (bf16[1024,2048]{1,0:T(8,128)(2,1)}, bf16[1024,2048]{1,0:T(8,128)(2,1)}, u32[]{:S(2)}, u32[]{:S(2)}) collective-permute-start(bf16[1024,2048]{1,0:T(8,128)(2,1)} %pad_maximum_fusion.3), channel_id=1, source_target_pairs={{0,1},{1,0},{2,3},{3,2},{4,5},{5,4},{6,7},{7,6},{8,9},{9,8},{10,11... | collective-permute-start | bytes 12582920 | tf_op jit(solution)/shard_map/ppermute | solution.py:167
  650.5 72.6 %collective-permute-start.65 = (bf16[512,2048]{0,1:T(8,128)(2,1)}, bf16[512,2048]{0,1:T(8,128)(2,1)}, u32[]{:S(2)}, u32[]{:S(2)}) collective-permute-start(bf16[512,2048]{0,1:T(8,128)(2,1)} %add_convert_fusion.1), channel_id=1, source_target_pairs={{0,8},{4,12},{8,16},{12,20},{16,24},{20,28},{24,0},{28,4},{1,9},{5... | collective-permute-start | bytes 6291464 | tf_op jit(solution)/shard_map/ppermute | solution.py:170
  657.5 26.2 %collective-permute-start.49 = (bf16[256,2048]{1,0:T(8,128)(2,1)}, bf16[256,2048]{1,0:T(8,128)(2,1)S(1)}, u32[]{:S(2)}, u32[]{:S(2)}) collective-permute-start(bf16[256,2048]{1,0:T(8,128)(2,1)} %pad_maximum_fusion.20), channel_id=1, source_target_pairs={{0,4},{4,0},{8,12},{12,8},{16,20},{20,16},{24,28},{28,24},{1,5},{5... | collective-permute-start | bytes 3145736 | tf_op jit(solution)/shard_map/ppermute | solution.py:161
  658.5 27.1 %collective-permute-start.47 = (bf16[256,2048]{1,0:T(8,128)(2,1)S(1)}, bf16[256,2048]{1,0:T(8,128)(2,1)S(1)}, u32[]{:S(2)}, u32[]{:S(2)}) collective-permute-start(bf16[256,2048]{1,0:T(8,128)(2,1)S(1)} %pad_maximum_fusion.19), channel_id=1, source_target_pairs={{0,2},{1,3},{2,0},{3,1},{4,6},{5,7},{6,4},{7,5},{8,10},{9,11},{10,... | collective-permute-start | bytes 3145736 | tf_op jit(solution)/shard_map/ppermute | solution.py:164
  663.9 33.3 %collective-permute-start.38 = (bf16[256,2048]{1,0:T(8,128)(2,1)S(1)}, bf16[256,2048]{1,0:T(8,128)(2,1)S(1)}, u32[]{:S(2)}, u32[]{:S(2)}) collective-permute-start(bf16[256,2048]{1,0:T(8,128)(2,1)S(1)} %pad_maximum_fusion.18), channel_id=1, source_target_pairs={{0,4},{4,0},{8,12},{12,8},{16,20},{20,16},{24,28},{28,24},{1,5},{5... | collective-permute-start | bytes 3145736 | tf_op jit(solution)/shard_map/ppermute | solution.py:161
  665.7 41.4 %collective-permute-start.36 = (bf16[256,2048]{1,0:T(8,128)(2,1)S(1)}, bf16[256,2048]{1,0:T(8,128)(2,1)S(1)}, u32[]{:S(2)}, u32[]{:S(2)}) collective-permute-start(bf16[256,2048]{1,0:T(8,128)(2,1)S(1)} %pad_maximum_fusion.17), channel_id=1, source_target_pairs={{0,2},{1,3},{2,0},{3,1},{4,6},{5,7},{6,4},{7,5},{8,10},{9,11},{10,... | collective-permute-start | bytes 3145736 | tf_op jit(solution)/shard_map/ppermute | solution.py:164
  684.1 30.7 %collective-permute-start.50 = (bf16[128,2048]{1,0:T(8,128)(2,1)S(1)}, bf16[128,2048]{1,0:T(8,128)(2,1)S(1)}, u32[]{:S(2)}, u32[]{:S(2)}) collective-permute-start(bf16[128,2048]{1,0:T(8,128)(2,1)S(1)} %fusion.58), channel_id=1, source_target_pairs={{0,2},{1,3},{2,0},{3,1},{4,6},{5,7},{6,4},{7,5},{8,10},{9,11},{10,... | collective-permute-start | bytes 1572872 | tf_op jit(solution)/shard_map/ppermute | solution.py:164
  686.0 28.8 %collective-permute-start.48 = (bf16[128,2048]{1,0:T(8,128)(2,1)S(1)}, bf16[128,2048]{1,0:T(8,128)(2,1)S(1)}, u32[]{:S(2)}, u32[]{:S(2)}) collective-permute-start(bf16[128,2048]{1,0:T(8,128)(2,1)S(1)} %fusion.60), channel_id=1, source_target_pairs={{0,4},{4,0},{8,12},{12,8},{16,20},{20,16},{24,28},{28,24},{1,5},{5... | collective-permute-start | bytes 1572872 | tf_op jit(solution)/shard_map/ppermute | solution.py:161
  697.6 22.8 %collective-permute-start.39 = (bf16[128,2048]{1,0:T(8,128)(2,1)S(1)}, bf16[128,2048]{1,0:T(8,128)(2,1)S(1)}, u32[]{:S(2)}, u32[]{:S(2)}) collective-permute-start(bf16[128,2048]{1,0:T(8,128)(2,1)S(1)} %fusion.62), channel_id=1, source_target_pairs={{0,2},{1,3},{2,0},{3,1},{4,6},{5,7},{6,4},{7,5},{8,10},{9,11},{10,... | collective-permute-start | bytes 1572872 | tf_op jit(solution)/shard_map/ppermute | solution.py:164
  716.7 21.4 %collective-permute-start.52 = (bf16[256,2048]{1,0:T(8,128)(2,1)S(1)}, bf16[256,2048]{1,0:T(8,128)(2,1)S(1)}, u32[]{:S(2)}, u32[]{:S(2)}) collective-permute-start(bf16[256,2048]{1,0:T(8,128)(2,1)S(1)} %fusion.94), channel_id=1, source_target_pairs={{0,2},{1,3},{2,0},{3,1},{4,6},{5,7},{6,4},{7,5},{8,10},{9,11},{10,... | collective-permute-start | bytes 3145736 | tf_op jit(solution)/shard_map/ppermute | solution.py:164
  721.9 32.3 %collective-permute-start.40 = (bf16[256,2048]{1,0:T(8,128)(2,1)S(1)}, bf16[256,2048]{1,0:T(8,128)(2,1)S(1)}, u32[]{:S(2)}, u32[]{:S(2)}) collective-permute-start(bf16[256,2048]{1,0:T(8,128)(2,1)S(1)} %get-tuple-element.76), channel_id=1, source_target_pairs={{0,1},{1,0},{2,3},{3,2},{4,5},{5,4},{6,7},{7,6},{8,9},{9,8},{10,11... | collective-permute-start | bytes 3145736 | tf_op jit(solution)/shard_map/ppermute | solution.py:167
  721.9 32.2 %collective-permute-start.41 = (bf16[256,2048]{1,0:T(8,128)(2,1)S(1)}, bf16[256,2048]{1,0:T(8,128)(2,1)}, u32[]{:S(2)}, u32[]{:S(2)}) collective-permute-start(bf16[256,2048]{1,0:T(8,128)(2,1)S(1)} %get-tuple-element.76), channel_id=1, source_target_pairs={{0,2},{1,3},{2,0},{3,1},{4,6},{5,7},{6,4},{7,5},{8,10},{9,11},{10,... | collective-permute-start | bytes 3145736 | tf_op jit(solution)/shard_map/ppermute | solution.py:164
  723.0 32.6 %collective-permute-start.51 = (bf16[256,2048]{1,0:T(8,128)(2,1)S(1)}, bf16[256,2048]{1,0:T(8,128)(2,1)S(1)}, u32[]{:S(2)}, u32[]{:S(2)}) collective-permute-start(bf16[256,2048]{1,0:T(8,128)(2,1)S(1)} %fusion.94), channel_id=1, source_target_pairs={{0,1},{1,0},{2,3},{3,2},{4,5},{5,4},{6,7},{7,6},{8,9},{9,8},{10,11... | collective-permute-start | bytes 3145736 | tf_op jit(solution)/shard_map/ppermute | solution.py:167
  738.1 17.5 %collective-permute-start.53 = (bf16[256,2048]{1,0:T(8,128)(2,1)S(1)}, bf16[256,2048]{1,0:T(8,128)(2,1)S(1)}, u32[]{:S(2)}, u32[]{:S(2)}) collective-permute-start(bf16[256,2048]{1,0:T(8,128)(2,1)S(1)} %collective-permute-done.52), channel_id=1, source_target_pairs={{0,1},{1,0},{2,3},{3,2},{4,5},{5,4},{6,7},{7,6},{8,9},{9,8},{10,11... | collective-permute-start | bytes 3145736 | tf_op jit(solution)/shard_map/ppermute | solution.py:167
  739.5 140.9 %collective-permute-start.66 = (bf16[256,2048]{0,1:T(8,128)(2,1)}, bf16[256,2048]{0,1:T(8,128)(2,1)}, u32[]{:S(2)}, u32[]{:S(2)}) collective-permute-start(bf16[256,2048]{0,1:T(8,128)(2,1)} %get-tuple-element.113), channel_id=1, source_target_pairs={{0,4},{4,0},{8,12},{12,8},{16,20},{20,16},{24,28},{28,24},{1,5},{5... | collective-permute-start | bytes 3145736 | tf_op jit(solution)/shard_map/ppermute | solution.py:161
  754.2 189.7 %collective-permute-start.42 = (bf16[256,2048]{1,0:T(8,128)(2,1)}, bf16[256,2048]{1,0:T(8,128)(2,1)}, u32[]{:S(2)}, u32[]{:S(2)}) collective-permute-start(bf16[256,2048]{1,0:T(8,128)(2,1)} %collective-permute-done.41), channel_id=1, source_target_pairs={{0,1},{1,0},{2,3},{3,2},{4,5},{5,4},{6,7},{7,6},{8,9},{9,8},{10,11... | collective-permute-start | bytes 3145736 | tf_op jit(solution)/shard_map/ppermute | solution.py:167
  867.9 33.8 %collective-permute-start.67 = (bf16[512,1024]{0,1:T(8,128)(2,1)}, bf16[512,1024]{0,1:T(8,128)(2,1)}, u32[]{:S(2)}, u32[]{:S(2)}) collective-permute-start(bf16[512,1024]{0,1:T(8,128)(2,1)} %bitcast.53), channel_id=1, source_target_pairs={{0,4},{4,0},{8,12},{12,8},{16,20},{20,16},{24,28},{28,24},{1,5},{5... | collective-permute-start | bytes 3145736 | tf_op jit(solution)/shard_map/ppermute | solution.py:161
  871.0 56.5 %collective-permute-start.59 = (bf16[1024,768]{1,0:T(8,128)(2,1)}, bf16[1024,768]{1,0:T(8,128)(2,1)}, u32[]{:S(2)}, u32[]{:S(2)}) collective-permute-start(bf16[1024,768]{1,0:T(8,128)(2,1)} %bitcast.47), channel_id=1, source_target_pairs={{0,4},{4,0},{8,12},{12,8},{16,20},{20,16},{24,28},{28,24},{1,5},{5... | collective-permute-start | bytes 4718600 | tf_op jit(solution)/shard_map/ppermute | solution.py:161
  880.4 49.4 %collective-permute-start.54 = (bf16[512,2048]{1,0:T(8,128)(2,1)}, bf16[512,2048]{1,0:T(8,128)(2,1)}, u32[]{:S(2)}, u32[]{:S(2)}) collective-permute-start(bf16[512,2048]{1,0:T(8,128)(2,1)} %pad_maximum_fusion.10), channel_id=1, source_target_pairs={{0,1},{1,0},{2,3},{3,2},{4,5},{5,4},{6,7},{7,6},{8,9},{9,8},{10,11... | collective-permute-start | bytes 6291464 | tf_op jit(solution)/shard_map/ppermute | solution.py:167
  904.0 29.1 %collective-permute-start.68 = (bf16[512,256]{0,1:T(8,128)(2,1)S(1)}, bf16[512,256]{0,1:T(8,128)(2,1)S(1)}, u32[]{:S(2)}, u32[]{:S(2)}) collective-permute-start(bf16[512,256]{0,1:T(8,128)(2,1)S(1)} %constant_dynamic-slice_fusion.2), channel_id=1, source_target_pairs={{0,8},{4,12},{8,16},{12,20},{16,24},{20,28},{24,0},{28,4},{1,9},{5... | collective-permute-start | bytes 786440 | tf_op jit(solution)/shard_map/ppermute | solution.py:170
  929.8 13.8 %collective-permute-start.60 = (bf16[256,768]{1,0:T(8,128)(2,1)S(1)}, bf16[256,768]{1,0:T(8,128)(2,1)S(1)}, u32[]{:S(2)}, u32[]{:S(2)}) collective-permute-start(bf16[256,768]{1,0:T(8,128)(2,1)S(1)} %constant_dynamic-slice_fusion.7), channel_id=1, source_target_pairs={{0,8},{4,12},{8,16},{12,20},{16,24},{20,28},{24,0},{28,4},{1,9},{5... | collective-permute-start | bytes 1179656 | tf_op jit(solution)/shard_map/ppermute | solution.py:170
  932.1 26.4 %collective-permute-start.55 = (bf16[256,2048]{1,0:T(8,128)(2,1)S(1)}, bf16[256,2048]{1,0:T(8,128)(2,1)S(1)}, u32[]{:S(2)}, u32[]{:S(2)}) collective-permute-start(bf16[256,2048]{1,0:T(8,128)(2,1)S(1)} %add_convert_fusion.6), channel_id=1, source_target_pairs={{0,2},{1,3},{2,0},{3,1},{4,6},{5,7},{6,4},{7,5},{8,10},{9,11},{10,... | collective-permute-start | bytes 3145736 | tf_op jit(solution)/shard_map/ppermute | solution.py:164
  933.2 16.0 %collective-permute-start.69 = (bf16[512,256]{0,1:T(8,128)(2,1)S(1)}, bf16[512,256]{0,1:T(8,128)(2,1)S(1)}, u32[]{:S(2)}, u32[]{:S(2)}) collective-permute-start(bf16[512,256]{0,1:T(8,128)(2,1)S(1)} %add_convert_fusion.15), channel_id=1, source_target_pairs={{0,8},{4,12},{8,16},{12,20},{16,24},{20,28},{24,0},{28,4},{1,9},{5... | collective-permute-start | bytes 786440 | tf_op jit(solution)/shard_map/ppermute | solution.py:170
  943.7 13.9 %collective-permute-start.61 = (bf16[256,768]{1,0:T(8,128)(2,1)S(1)}, bf16[256,768]{1,0:T(8,128)(2,1)S(1)}, u32[]{:S(2)}, u32[]{:S(2)}) collective-permute-start(bf16[256,768]{1,0:T(8,128)(2,1)S(1)} %add_convert_fusion.12), channel_id=1, source_target_pairs={{0,8},{4,12},{8,16},{12,20},{16,24},{20,28},{24,0},{28,4},{1,9},{5... | collective-permute-start | bytes 1179656 | tf_op jit(solution)/shard_map/ppermute | solution.py:170
  949.3 21.7 %collective-permute-start.70 = (bf16[512,256]{0,1:T(8,128)(2,1)S(1)}, bf16[512,256]{0,1:T(8,128)(2,1)S(1)}, u32[]{:S(2)}, u32[]{:S(2)}) collective-permute-start(bf16[512,256]{0,1:T(8,128)(2,1)S(1)} %add_convert_fusion.14), channel_id=1, source_target_pairs={{0,8},{4,12},{8,16},{12,20},{16,24},{20,28},{24,0},{28,4},{1,9},{5... | collective-permute-start | bytes 786440 | tf_op jit(solution)/shard_map/ppermute | solution.py:170
  958.5 13.6 %collective-permute-start.62 = (bf16[256,768]{1,0:T(8,128)(2,1)}, bf16[256,768]{1,0:T(8,128)(2,1)}, u32[]{:S(2)}, u32[]{:S(2)}) collective-permute-start(bf16[256,768]{1,0:T(8,128)(2,1)} %add_convert_fusion.11), channel_id=1, source_target_pairs={{0,8},{4,12},{8,16},{12,20},{16,24},{20,28},{24,0},{28,4},{1,9},{5... | collective-permute-start | bytes 1179656 | tf_op jit(solution)/shard_map/ppermute | solution.py:170
  970.1 29.1 %collective-permute-start.56 = (bf16[256,2048]{1,0:T(8,128)(2,1)}, bf16[256,2048]{1,0:T(8,128)(2,1)S(1)}, u32[]{:S(2)}, u32[]{:S(2)}) collective-permute-start(bf16[256,2048]{1,0:T(8,128)(2,1)} %get-tuple-element.72), channel_id=1, source_target_pairs={{0,1},{1,0},{2,3},{3,2},{4,5},{5,4},{6,7},{7,6},{8,9},{9,8},{10,11... | collective-permute-start | bytes 3145736 | tf_op jit(solution)/shard_map/ppermute | solution.py:167
  970.1 29.1 %collective-permute-start.57 = (bf16[256,2048]{1,0:T(8,128)(2,1)}, bf16[256,2048]{1,0:T(8,128)(2,1)S(1)}, u32[]{:S(2)}, u32[]{:S(2)}) collective-permute-start(bf16[256,2048]{1,0:T(8,128)(2,1)} %get-tuple-element.72), channel_id=1, source_target_pairs={{0,2},{1,3},{2,0},{3,1},{4,6},{5,7},{6,4},{7,5},{8,10},{9,11},{10,... | collective-permute-start | bytes 3145736 | tf_op jit(solution)/shard_map/ppermute | solution.py:164
  (114 other events, 1632.6 us)

commit v2 on v1

--- a/solution.py
+++ b/solution.py
@@ -70,13 +70,20 @@
     return lax.rsqrt(jnp.mean(values * values, axis=-1, keepdims=True) + epsilon)
 
 
-def block_scores(query_block, key_seq, segment_row, start_row):
-    row_count = query_block.shape[0]
-    length = key_seq.shape[0]
-    scores = jnp.einsum("qkgd,skd->kgqs", query_block, key_seq, preferred_element_type=F32)
-    row_ids = start_row + jnp.arange(row_count, dtype=jnp.int32)
-    col_ids = jnp.arange(length, dtype=jnp.int32)
-    same_doc = segment_row[start_row : start_row + row_count][:, None] == segment_row[None, :]
+def spans(length):
+    rows = length // 4
+    most = length // 2
+    for start in range(0, length, rows):
+        first = max(0, start - most + 1) // rows * rows
+        yield start, rows, first, start + rows
+
+
+def block_scores(query_block, key_block, segment_row, start, first):
+    rows, keys = query_block.shape[0], key_block.shape[0]
+    scores = jnp.einsum("qkgd,skd->kgqs", query_block, key_block, preferred_element_type=F32)
+    row_ids = start + jnp.arange(rows, dtype=jnp.int32)
+    col_ids = first + jnp.arange(keys, dtype=jnp.int32)
+    same_doc = segment_row[start : start + rows][:, None] == segment_row[first : first + keys][None, :]
     allowed = same_doc & (col_ids[None, :] <= row_ids[:, None])
     return jnp.where(allowed, scores, -1000000000.0)
 
@@ -84,49 +91,52 @@
 def attend_forward(query_seq, key_seq, value_seq, segment_row):
     length, kv_local, head_size = key_seq.shape
     grouped = query_seq.reshape(length, kv_local, -1, head_size)
-    block_rows = min(512, length)
     mixed_parts = []
     total_parts = []
-    for start_row in range(0, length, block_rows):
+    for start, rows, first, last in spans(length):
         scores = block_scores(
-            grouped[start_row : start_row + block_rows], key_seq, segment_row, start_row
+            grouped[start : start + rows], key_seq[first:last], segment_row, start, first
         )
         row_max = jnp.max(scores, axis=-1, keepdims=True)
         log_total = jnp.log(jnp.sum(jnp.exp(scores - row_max), axis=-1, keepdims=True)) + row_max
         soft_low = jnp.exp(scores - log_total).astype(BF)
-        mixed_block = jnp.einsum("kgqs,skd->qkgd", soft_low, value_seq, preferred_element_type=F32)
-        mixed_parts.append(mixed_block.reshape(block_rows, -1).astype(BF))
+        mixed_block = jnp.einsum(
+            "kgqs,skd->qkgd", soft_low, value_seq[first:last], preferred_element_type=F32
+        )
+        mixed_parts.append(mixed_block.reshape(rows, -1).astype(BF))
         total_parts.append(log_total)
-    return (jnp.concatenate(mixed_parts, axis=0), jnp.concatenate(total_parts, axis=2))
-
-
-def attend_backward(query_seq, key_seq, value_seq, log_total, grad_seq, segment_row):
+    return (jnp.concatenate(mixed_parts, axis=0), total_parts)
+
+
+def attend_backward(query_seq, key_seq, value_seq, total_parts, grad_seq, segment_row):
     length, kv_local, head_size = key_seq.shape
     grouped = query_seq.reshape(length, kv_local, -1, head_size)
     grad_grouped = grad_seq.reshape(length, kv_local, -1, head_size)
-    block_rows = min(512, length)
     score_scale = head_size ** (-0.5)
     query_parts = []
     key_grad = jnp.zeros(key_seq.shape, F32)
     value_grad = jnp.zeros(value_seq.shape, F32)
-    for start_row in range(0, length, block_rows):
-        query_block = grouped[start_row : start_row + block_rows]
-        grad_block = grad_grouped[start_row : start_row + block_rows]
-        scores = block_scores(query_block, key_seq, segment_row, start_row)
-        soft_weights = jnp.exp(scores - log_total[:, :, start_row : start_row + block_rows])
-        soft_grad = jnp.einsum("qkgd,skd->kgqs", grad_block, value_seq, preferred_element_type=F32)
+    for (start, rows, first, last), log_total in zip(spans(length), total_parts):
+        query_block = grouped[start : start + rows]
+        grad_block = grad_grouped[start : start + rows]
+        key_block, value_block = key_seq[first:last], value_seq[first:last]
+        scores = block_scores(query_block, key_block, segment_row, start, first)
+        soft_weights = jnp.exp(scores - log_total)
+        soft_grad = jnp.einsum("qkgd,skd->kgqs", grad_block, value_block, preferred_element_type=F32)
         score_grad = (
             soft_weights * (soft_grad - jnp.sum(soft_weights * soft_grad, axis=-1, keepdims=True))
         ).astype(BF)
         query_parts.append(
-            jnp.einsum("kgqs,skd->qkgd", score_grad, key_seq, preferred_element_type=F32)
+            jnp.einsum("kgqs,skd->qkgd", score_grad, key_block, preferred_element_type=F32)
             * score_scale
         )
-        key_grad = key_grad + jnp.einsum(
-            "kgqs,qkgd->skd", score_grad, query_block, preferred_element_type=F32
-        )
-        value_grad = value_grad + jnp.einsum(
-            "kgqs,qkgd->skd", soft_weights.astype(BF), grad_block, preferred_element_type=F32
+        key_grad = key_grad.at[first:last].add(
+            jnp.einsum("kgqs,qkgd->skd", score_grad, query_block, preferred_element_type=F32)
+        )
+        value_grad = value_grad.at[first:last].add(
+            jnp.einsum(
+                "kgqs,qkgd->skd", soft_weights.astype(BF), grad_block, preferred_element_type=F32
+            )
         )
     query_grad = jnp.concatenate(query_parts, axis=0).reshape(length, -1, head_size)
     return (query_grad, key_grad, value_grad)
@@ -233,27 +243,31 @@
         1,
     )
 
+    z_groups = [[i for i in range(dp_size) if i % 2 == side] for side in range(2)]
+
+    def gather_z(value):
+        return lax.all_gather(value, "dp", axis_index_groups=z_groups, axis=0, tiled=True)
+
+    def scatter_z(value):
+        return lax.psum_scatter(
+            value, "dp", axis_index_groups=z_groups, scatter_dimension=0, tiled=True
+        )
+
+    def by_y(mine, got, axis):
+        return jnp.where(
+            y_index == 0,
+            jnp.concatenate([mine, got], axis=axis),
+            jnp.concatenate([got, mine], axis=axis),
+        )
+
     gate_scaled, up_scaled = scaled(gate_weight, ffn_scale), scaled(up_weight, ffn_scale)
     gu_mine = jnp.concatenate([my_half(gate_scaled, 1, True), my_half(up_scaled, 1, True)], axis=1)
     gu_send = jnp.concatenate([my_half(gate_scaled, 1, False), my_half(up_scaled, 1, False)], axis=1)
-    gu_got = swap_y(tie(gu_send, qkv_ring[1]))
-    gu_ring_a = ring_gather(tie(gu_mine, out_ring[-2]))
-    gu_ring_b = ring_gather(tie(gu_got, gu_ring_a[-2]))
-    gu_full = place(
-        [(v, s, y_index) for s, v in enumerate(gu_ring_a)]
-        + [(v, s, 1 - y_index) for s, v in enumerate(gu_ring_b)],
-        None,
-        0,
-    )
-    down_got = swap_y(tie(my_half(down_weight, 0, False), gu_got))
-    down_ring_a = ring_gather(tie(my_half(down_weight, 0, True), gu_ring_b[-2]))
-    down_ring_b = ring_gather(tie(down_got, down_ring_a[-2]))
-    down_full = place(
-        [(v, s, y_index) for s, v in enumerate(down_ring_a)]
-        + [(v, s, 1 - y_index) for s, v in enumerate(down_ring_b)],
-        None,
-        1,
-    )
+    gu_got = swap_y(gu_send)
+    gu_full = gather_z(tie(by_y(gu_mine, gu_got, 0), qkv_ring[-1]))
+    down_t = down_weight.T
+    down_got = swap_y(tie(my_half(down_t, 1, False), gu_got))
+    down_full = gather_z(tie(by_y(my_half(down_t, 1, True), down_got, 0), gu_full))
     cot_rel = relative(cotangent)
     cot_y = swap_y(tie(cot_rel[:quarter], down_got))
     cot_yx = swap_x(cot_y)
@@ -363,22 +377,10 @@
             axis=0,
         )
 
-    def ring_scatter(grad, axis):
-        size = grad.shape[axis] // groups
-
-        def block(index):
-            return lax.dynamic_slice_in_dim(grad, (index % groups) * size, size, axis)
-
-        running = block(z_index - 1)
-        for step in range(groups - 1):
-            received = hop(running)
-            running = (received.astype(F32) + block(z_index - 2 - step).astype(F32)).astype(BF)
-        return running
-
-    down_grad = dot_rows(active, cot_all, BF)
-    down_block = ring_scatter(down_grad, 1)
-
-    active_grad = dot_cols(cot_all, down_full)
+    down_grad = dot_rows(cot_all, active, BF)
+    down_block = scatter_z(down_grad)
+
+    active_grad = dot(cot_all, down_full)
     gate_grad = (active_grad * up_values * (sig * (1.0 + gate_values * (1.0 - sig)))).astype(BF)
     up_grad = (active_grad * silu).astype(BF)
     gu_grad = jnp.concatenate([gate_grad, up_grad], axis=1)
@@ -392,13 +394,13 @@
     hidden_low = jnp.concatenate(gather_tensor(hidden_grad.astype(BF)), axis=0)
 
     gu_weight_grad = dot_rows(n_all, gu_grad, BF)
-    gu_block = ring_scatter(gu_weight_grad, 0)
-
-    ffn_part = dot(active, down_full, BF)
+    gu_block = scatter_z(tie(gu_weight_grad, down_block))
+
+    ffn_part = dot_cols(active, down_full, BF)
     layer_quarter = (hidden + scatter_pair(ffn_part)).astype(BF)
     layer_output = absolute(gather_tensor(layer_quarter), BF)
 
-    out_weight_grad = dot_rows(mixed_rel, hidden_low, BF)
+    out_weight_grad = dot_rows(hidden_low, mixed_rel, BF)
     mixed_grad_rel = dot_cols(hidden_low, out_full, BF)
     mixed_grad = absolute(
         [mixed_grad_rel[j * quarter : (j + 1) * quarter] for j in range(tensor_size)], BF
@@ -424,39 +426,26 @@
     tokens_grad = absolute(gather_tensor(tokens_grad_quarter.astype(BF)), F32)
     qkv_weight_grad = dot_rows(normed, qkv_grad, BF)
 
-    def split_y(grad, axis, size):
-        shape = grad.shape
-        cut = grad.reshape(shape[:axis] + (groups, 2, size) + shape[axis + 1 :])
-        mine = lax.dynamic_index_in_dim(cut, y_index, axis + 1, keepdims=False)
-        other = lax.dynamic_index_in_dim(cut, 1 - y_index, axis + 1, keepdims=False)
-        flat = shape[:axis] + (groups * size,) + shape[axis + 1 :]
-        return mine.reshape(flat), other.reshape(flat)
-
-    def scatter_whole(grad, axis, size):
-        mine, other = split_y(grad, axis, size)
-        got = swap_y(other)
-        return ring_scatter((mine.astype(F32) + got.astype(F32)).astype(BF), axis)
-
-    out_grad = scatter_whole(out_weight_grad, 1, output_weight.shape[1]).astype(F32)
-    qkv_block = scatter_whole(qkv_weight_grad, 0, rows).astype(F32)
+    def scatter_whole(grad, size):
+        cut = grad.reshape(groups, 2, size, -1)
+        mine = lax.dynamic_index_in_dim(cut, y_index, 1, keepdims=False)
+        other = lax.dynamic_index_in_dim(cut, 1 - y_index, 1, keepdims=False)
+        got = swap_y(other.reshape(groups * size, -1))
+        both = (mine.reshape(groups * size, -1).astype(F32) + got.astype(F32)).astype(BF)
+        return scatter_z(both).astype(F32)
+
+    out_grad = scatter_whole(out_weight_grad, output_weight.shape[1]).T
+    qkv_block = scatter_whole(qkv_weight_grad, rows)
 
     def trade(block, axis_cut):
         mine = my_half(block, axis_cut, True)
         got = swap_y(my_half(block, axis_cut, False))
         return mine.astype(F32), got.astype(F32)
 
-    def by_y(mine, got, axis):
-        return jnp.where(
-            y_index == 0,
-            jnp.concatenate([mine, got], axis=axis),
-            jnp.concatenate([got, mine], axis=axis),
-        )
-
     gu_mine_rows, gu_got_rows = trade(gu_block, 0)
     gate_g = by_y(gu_mine_rows[:, :hidden_units], gu_got_rows[:, :hidden_units], 1)
     up_g = by_y(gu_mine_rows[:, hidden_units:], gu_got_rows[:, hidden_units:], 1)
-    down_mine, down_got_cols = trade(down_block, 1)
-    down_weight_grad = by_y(down_mine, down_got_cols, 0)
+    down_weight_grad = by_y(*trade(down_block, 0), 1).T
 
     attn_gain_part = jnp.sum(
         qkv_block * jnp.concatenate([query_weight, key_weight, value_weight], axis=1).astype(F32),
@@ -465,17 +454,22 @@
     ffn_gain_part = jnp.sum(
         gate_g * gate_weight.astype(F32) + up_g * up_weight.astype(F32), axis=1
     )
-    gain_grads = lax.psum(jnp.stack([attn_gain_part, ffn_gain_part]), "tensor")
+
+    def sum_tensor(value):
+        value = value + swap_core(value)
+        return value + swap_x(value)
+
+    attn_gain_grad, ffn_gain_grad = sum_tensor(attn_gain_part), sum_tensor(ffn_gain_part)
     qkv_out = qkv_block * attn_scale
     return (
         layer_output,
         tokens_grad,
-        gain_grads[0],
+        attn_gain_grad,
         qkv_out[:, :q_cols],
         qkv_out[:, q_cols : q_cols + kv_cols],
         qkv_out[:, q_cols + kv_cols :],
         out_grad,
-        gain_grads[1],
+        ffn_gain_grad,
         gate_g * ffn_scale,
         up_g * ffn_scale,
         down_weight_grad,

time: 1010 us -> 853 us (0.84)
  waiting for transfers between devices: 470 us -> 411 us
  matrix products: 230 us -> 183 us
  other arithmetic: 137 us -> 98.4 us
  blocking collectives: 23.5 us -> 0 us
  between operations: 3.28 us -> 17 us
  local copies, waits for them, and re-layouts: 96.8 us -> 86.4 us
    ppermute x30 -> x6, waiting for transfers between devices: 276 us -> 31.1 us  [hop(): lax.ppermute(value, 'dp', [(i, (i + 2) % dp_size) for i in range(dp_size)])]
    all_gather x0 -> x2, waiting for transfers between devices: none -> 83.6 us  [gather_z(): lax.all_gather(value, 'dp', axis_index_groups=z_groups, axis=0, tiled=True)]
    ppermute x21, waiting for transfers between devices: 118 us -> 182 us  [swap_y(): return lax.ppermute(value, 'dp', [(i, i ^ 1) for i in range(dp_size)])]
    dot_general x8 -> x16, matrix products: 60.4 us -> 30.5 us  [the longest x4 13.5 us: attend_backward(): jnp.einsum('qkgd,skd->kgqs', grad_block, value_block, preferred_element_t...]
    ppermute x12 -> x14, waiting for transfers between devices: 76.1 us -> 99.9 us  [swap_x(): lax.ppermute(value, 'tensor', [(i, i ^ 2) for i in range(tensor_size)])]
    psum x1 -> x0, blocking collectives: 23.5 us -> none  [shards(): gain_grads = lax.psum(jnp.stack([attn_gain_part, ffn_gain_part]), 'tensor')]
    convert_element_type x1 -> x4, other arithmetic: 29.7 us -> 13.6 us  [attend_backward(): score_grad = (soft_weights * (soft_grad - jnp.sum(soft_weights * soft_gra...]
    reduce_sum x2 -> x4, other arithmetic: 17.3 us -> 3.34 us  [attend_forward(): jnp.sum(jnp.exp(scores - row_max), axis=-1, keepdims=True)]
  transfers between devices with their start and end apart: 75 -> 61, of which waited for: 36 -> 33; matrix products, arithmetic and copies ran while one was open for 33% -> 34% of each run, Pallas kernels for 0% -> 0%
where the time goes in v2:
time: 853 us; the launch traced here: 848 us
  waiting for transfers between devices  411 us (48%)
  matrix products  183 us (21%)
  other arithmetic  98.4 us (12%)
  local copies, waits for them, and re-layouts  86.4 us (10%)
  starting transfers between devices  51.5 us (6%)
  between operations  17 us (2%)
    ppermute x21, waiting for transfers between devices, swap_y(): return lax.ppermute(value, 'dp', [(i, i ^ 1) for i in range(dp_size)])  182 us
    ppermute x14, waiting for transfers between devices, swap_x(): lax.ppermute(value, 'tensor', [(i, i ^ 2) for i in range(tensor_size)])  99.9 us
    all_gather x2, waiting for transfers between devices, gather_z(): lax.all_gather(value, 'dp', axis_index_groups=z_groups, axis=0, tiled=True)  83.6 us
    unnamed x313, local copies, waits for them, and re-layouts  51.8 us
    dot_general x4, matrix products, dot(): return jnp.dot(left, right, preferred_element_type=F32).astype(out)  49.8 us
    dot_general x4, matrix products, dot_rows(): lax.dot_general(left, right, (((0,), (0,)), ((), ())), preferred_element_...  49.1 us
    dot_general x4, matrix products, dot_cols(): lax.dot_general(left, right, (((1,), (1,)), ((), ())), preferred_element_...  45.8 us
    ppermute x6, waiting for transfers between devices, hop(): lax.ppermute(value, 'dp', [(i, (i + 2) % dp_size) for i in range(dp_size)])  31.1 us
  transfers between devices with their start and end apart: 61, of which 33 were waited for; matrix products, arithmetic and copies ran while one was open for 34% of the time, Pallas kernels for 0%

profile of v2, /device:TPU:0, one launch (start us, length us, event | category | flops | bytes accessed | tf_op | source)
XLA Modules:
  0.0 848.0 jit_solution(2744933958402826314)
XLA Ops:
  10.2 3.1 collective-permute-start
  18.0 6.7 collective-permute-done
  28.9 8.2 collective-permute-done.1
  40.8 7.5 collective-permute-done.7
  49.6 4.5 collective-permute-done.2
  58.2 4.1 collective-permute-done.8
  63.7 2.9 collective-permute-done.6
  66.6 3.8 fusion.141
  89.4 4.1 collective-permute-done.13
  93.6 2.4 convolution_convert_fusion.4
  103.0 23.6 %collective-permute-done.21 = bf16[256,2048]{1,0:T(8,128)(2,1)} collective-permute-done((bf16[256,2048]{1,0:T(8,128)(2,1)}, bf16[256,2048]{1,0:T(8,128)(2,1)}, u32[]{:S(2)}, u32[]{:S(2)}) %collective-permute-start.21) | collective-permute-done | bytes 1048608 | tf_op jit(solution)/shard_map/ppermute | solution.py:171
  126.6 10.3 %maximum_select_fusion = bf16[512,2048]{1,0:T(8,128)(2,1)} fusion(bf16[256,2048]{1,0:T(8,128)(2,1)} %collective-permute-done.21, bf16[256,1024]{1,0:T(8,128)(2,1)S(1)} %get-tuple-element.217, bf16[256,1024]{1,0:T(8,128)(2,1)S(1)} %get-tuple-element.269, pred[]{:T(512)S(6)} %eq.138), kind=kLoop, calls=%fused_computation.85 | loop fusion | flops 13631488 | bytes 4194305 | tf_op jit(solution)/shard_map/jit(_where)/select_n | solution.py:257
  137.2 2.4 add_convert_fusion.4
  143.0 20.8 %collective-permute-done.15 = bf16[256,2048]{1,0:T(8,128)(2,1)S(1)} collective-permute-done((bf16[256,2048]{1,0:T(8,128)(2,1)S(1)}, bf16[256,2048]{1,0:T(8,128)(2,1)S(1)}, u32[]{:S(2)}, u32[]{:S(2)}) %collective-permute-start.15) | collective-permute-done | bytes 1048608 | tf_op jit(solution)/shard_map/ppermute | solution.py:174
  163.9 2.7 multiply_reduce_fusion.1
  172.0 10.7 %collective-permute-done.17 = bf16[128,2048]{1,0:T(8,128)(2,1)S(1)} collective-permute-done((bf16[128,2048]{1,0:T(8,128)(2,1)S(1)}, bf16[128,2048]{1,0:T(8,128)(2,1)S(1)}, u32[]{:S(2)}, u32[]{:S(2)}) %collective-permute-start.17) | collective-permute-done | bytes 524320 | tf_op jit(solution)/shard_map/ppermute | solution.py:171
  186.3 18.9 %collective-permute-done.31 = bf16[256,2048]{1,0:T(8,128)(2,1)S(1)} collective-permute-done((bf16[256,2048]{1,0:T(8,128)(2,1)S(1)}, bf16[256,2048]{1,0:T(8,128)(2,1)S(1)}, u32[]{:S(2)}, u32[]{:S(2)}) %collective-permute-start.31) | collective-permute-done | bytes 1048608 | tf_op jit(solution)/shard_map/ppermute | solution.py:171
  208.6 16.4 %collective-permute-done.19 = bf16[256,2048]{1,0:T(8,128)(2,1)S(1)} collective-permute-done((bf16[256,2048]{1,0:T(8,128)(2,1)S(1)}, bf16[256,2048]{1,0:T(8,128)(2,1)S(1)}, u32[]{:S(2)}, u32[]{:S(2)}) %collective-permute-start.19) | collective-permute-done | bytes 1048608 | tf_op jit(solution)/shard_map/ppermute | solution.py:171
  230.9 3.4 copy-done.117
  235.6 2.4 constant_dynamic-update-slice_fusion.7
  239.0 2.4 slice_dynamic-update-slice_fusion.1
  242.5 2.4 slice_dynamic-update-slice_fusion
  251.2 36.3 %all-gather.3.cloned.1.call-done = bf16[2048,2048]{1,0:T(8,128)(2,1)} async-done(((bf16[512,2048]{1,0:T(8,128)(2,1)}), bf16[2048,2048]{1,0:T(8,128)(2,1)}) %all-gather.3.cloned.1.call-update) | async-done | bytes 8388624 | tf_op jit(solution)/shard_map/all_gather | solution.py:249
  294.3 2.4 slice_dynamic-update-slice_fusion.2
  296.8 23.8 %convolution_convert_fusion.3 = bf16[2048,2048]{0,1:T(8,128)(2,1)} fusion(bf16[2048,2048]{1,0:T(8,128)(2,1)} %slice_dynamic-update-slice_fusion.2, bf16[2048,2048]{1,0:T(8,128)(2,1)} %all-gather.3.cloned.1.call-done), kind=kOutput, calls=%fused_computation.22 | convolution fusion | flops 17184063488 | bytes 25165824 | tf_op jit(solution)/shard_map/dot_general | solution.py:62
  320.6 47.4 %all-gather.5.cloned.1.call-done = bf16[2048,1024]{0,1:T(8,128)(2,1)} async-done(((bf16[512,1024]{0,1:T(8,128)(2,1)}), bf16[2048,1024]{0,1:T(8,128)(2,1)}) %all-gather.5.cloned.1.call-update) | async-done | bytes 4194320 | tf_op jit(solution)/shard_map/all_gather | solution.py:249
  367.9 19.8 %fusion.4 = (bf16[2048,1024]{0,1:T(8,128)(2,1)}, bf16[2048,1024]{0,1:T(8,128)(2,1)}) fusion(bf16[2048,2048]{0,1:T(8,128)(2,1)} %convolution_convert_fusion.3, bf16[2048,2048]{1,0:T(8,128)(2,1)} %slice_dynamic-update-slice_fusion, bf16[2048,1024]{0,1:T(8,128)(2,1)} %all-gather.5.cloned.1.call-done), kind=kOutput, calls=%fused_computation.11 | convolution fusion | flops 8621391872 | bytes 29360128 | tf_op jit(solution)/shard_map/dot_general | solution.py:62
  387.8 22.6 %convolution_convert_fusion.1 = bf16[2048,2048]{1,0:T(8,128)(2,1)S(1)} fusion(bf16[2048,2048]{1,0:T(8,128)(2,1)} %all-gather.3.cloned.1.call-done, bf16[2048,1024]{0,1:T(8,128)(2,1)} %get-tuple-element.156, bf16[2048,1024]{0,1:T(8,128)(2,1)} %get-tuple-element.155), kind=kOutput, calls=%fused_computation.20 | convolution fusion | flops 17200840704 | bytes 25165824 | tf_op jit(solution)/shard_map/dot_general | solution.py:56
  411.5 7.1 collective-permute-done.34
  424.1 22.0 %collective-permute-done.37 = bf16[256,2048]{1,0:T(8,128)(2,1)S(1)} collective-permute-done((bf16[256,2048]{1,0:T(8,128)(2,1)S(1)}, bf16[256,2048]{1,0:T(8,128)(2,1)S(1)}, u32[]{:S(2)}, u32[]{:S(2)}) %collective-permute-start.37) | collective-permute-done | bytes 1048608 | tf_op jit(solution)/shard_map/ppermute | solution.py:171
  450.0 9.7 %collective-permute-done.38 = bf16[128,2048]{1,0:T(8,128)(2,1)S(1)} collective-permute-done((bf16[128,2048]{1,0:T(8,128)(2,1)S(1)}, bf16[128,2048]{1,0:T(8,128)(2,1)S(1)}, u32[]{:S(2)}, u32[]{:S(2)}) %collective-permute-start.38) | collective-permute-done | bytes 524320 | tf_op jit(solution)/shard_map/ppermute | solution.py:174
  465.6 22.3 %collective-permute-done.40 = bf16[256,2048]{1,0:T(8,128)(2,1)} collective-permute-done((bf16[256,2048]{1,0:T(8,128)(2,1)S(1)}, bf16[256,2048]{1,0:T(8,128)(2,1)}, u32[]{:S(2)}, u32[]{:S(2)}) %collective-permute-start.40) | collective-permute-done | bytes 1048608 | tf_op jit(solution)/shard_map/ppermute | solution.py:174
  487.9 16.1 %convolution_convert_fusion.6 = bf16[2048,1024]{1,0:T(8,128)(2,1)} fusion(bf16[2048,2048]{1,0:T(8,128)(2,1)} %slice_dynamic-update-slice_fusion, bf16[2048,2048]{0,1:T(8,128)(2,1)} %convolution_convert_fusion.3), kind=kOutput, calls=%fused_computation.56 | convolution fusion | flops 8608808960 | bytes 20971520 | tf_op jit(solution)/shard_map/dot_general | solution.py:50
  505.6 4.2 convolution_convert_fusion.9
  514.8 4.3 convolution_convert_fusion.8
  523.3 3.6 fusion.18
  532.5 4.4 fusion.13
  536.9 6.1 fusion.15
  543.0 3.5 fusion.59
  546.5 5.0 fusion.10
  551.5 5.9 fusion.12
  557.4 2.8 fusion.58
  576.1 2.9 copy.93
  582.1 4.4 convolution_convert_fusion.7
  588.6 2.6 add_convert_fusion
  591.3 15.2 %convolution_convert_fusion.2 = bf16[2048,2048]{1,0:T(8,128)(2,1)} fusion(bf16[2048,1024]{0,1:T(8,128)(2,1)} %all-gather.5.cloned.1.call-done, bf16[2048,2048]{0,1:T(8,128)(2,1)} %convolution_convert_fusion.3), kind=kOutput, calls=%fused_computation.21 | convolution fusion | flops 8610906112 | bytes 20971520 | tf_op jit(solution)/shard_map/dot_general | solution.py:56
  606.5 18.3 %collective-permute-done.47 = bf16[1024,768]{1,0:T(8,128)(2,1)} collective-permute-done((bf16[1024,768]{1,0:T(8,128)(2,1)}, bf16[1024,768]{1,0:T(8,128)(2,1)}, u32[]{:S(2)}, u32[]{:S(2)}) %collective-permute-start.47) | collective-permute-done | bytes 1572896 | tf_op jit(solution)/shard_map/ppermute | solution.py:171
  624.8 2.9 fusion.24
  627.8 24.3 %convolution_convert_fusion = bf16[2048,2048]{1,0:T(8,128)(2,1)} fusion(bf16[2048,2048]{1,0:T(8,128)(2,1)} %slice_dynamic-update-slice_fusion.2, bf16[2048,1024]{0,1:T(8,128)(2,1)} %get-tuple-element.156, bf16[2048,1024]{0,1:T(8,128)(2,1)} %get-tuple-element.155), kind=kOutput, calls=%fused_computation.19 | convolution fusion | flops 17200840704 | bytes 25165824 | tf_op jit(solution)/shard_map/dot_general | solution.py:50
  652.2 2.9 fusion.128
  655.9 7.1 collective-permute-done.23
  666.8 23.7 %collective-permute-done.26 = bf16[256,2048]{1,0:T(8,128)(2,1)S(1)} collective-permute-done((bf16[256,2048]{1,0:T(8,128)(2,1)S(1)}, bf16[256,2048]{1,0:T(8,128)(2,1)S(1)}, u32[]{:S(2)}, u32[]{:S(2)}) %collective-permute-start.26) | collective-permute-done | bytes 1048608 | tf_op jit(solution)/shard_map/ppermute | solution.py:171
  693.7 3.9 convolution_convert_fusion.5
  699.4 4.9 collective-permute-done.27
  704.2 8.4 collective-permute-done.25
  722.5 13.0 %collective-permute-done.54 = bf16[256,1024]{1,0:T(8,128)(2,1)S(1)} collective-permute-done((bf16[256,1024]{1,0:T(8,128)(2,1)S(1)}, bf16[256,1024]{1,0:T(8,128)(2,1)S(1)}, u32[]{:S(2)}, u32[]{:S(2)}) %collective-permute-start.54) | collective-permute-done | bytes 524320 | tf_op jit(solution)/shard_map/ppermute | solution.py:171
  735.7 6.8 collective-permute-done.29
  742.4 21.1 %collective-permute-done.43 = bf16[256,2048]{1,0:T(8,128)(2,1)S(1)} collective-permute-done((bf16[256,2048]{1,0:T(8,128)(2,1)}, bf16[256,2048]{1,0:T(8,128)(2,1)S(1)}, u32[]{:S(2)}, u32[]{:S(2)}) %collective-permute-start.43) | collective-permute-done | bytes 1048608 | tf_op jit(solution)/shard_map/ppermute | solution.py:174
  768.4 4.0 convert_dynamic-update-slice_fusion.3
  772.4 3.4 copy-done.30
  784.2 2.4 constant_dynamic-update-slice_fusion.9
  788.3 13.3 %collective-permute-done.45 = bf16[256,2048]{1,0:T(8,128)(2,1)S(1)} collective-permute-done((bf16[256,2048]{1,0:T(8,128)(2,1)}, bf16[256,2048]{1,0:T(8,128)(2,1)S(1)}, u32[]{:S(2)}, u32[]{:S(2)}) %collective-permute-start.45) | collective-permute-done | bytes 1048608 | tf_op jit(solution)/shard_map/ppermute | solution.py:174
  801.6 2.8 convert_dynamic-update-slice_fusion.2
  815.9 17.3 %collective-permute-done.51 = bf16[256,2048]{1,0:T(8,128)(2,1)S(1)} collective-permute-done((bf16[256,2048]{1,0:T(8,128)(2,1)S(1)}, bf16[256,2048]{1,0:T(8,128)(2,1)S(1)}, u32[]{:S(2)}, u32[]{:S(2)}) %collective-permute-start.51) | collective-permute-done | bytes 1048608 | tf_op jit(solution)/shard_map/ppermute | solution.py:171
  (587 shorter events, 192.4 us)
Async XLA Ops:
  7.2 280.2 %all-gather.3.cloned.1.call-start = ((), (), s32[]{:S(2)}) async-start(), calls=%async_computation.4 | async-start | bytes 10485760 | tf_op jit(solution)/shard_map/all_gather | solution.py:249
  10.2 14.5 %collective-permute-start = (bf16[256,768]{1,0:T(8,128)(2,1)}, bf16[256,768]{1,0:T(8,128)(2,1)}, u32[]{:S(2)}, u32[]{:S(2)}) collective-permute-start(bf16[256,768]{1,0:T(8,128)(2,1)} %get-tuple-element.154), channel_id=1, source_target_pairs={{0,8},{4,12},{8,16},{12,20},{16,24},{20,28},{24,0},{28,4},{1,9},{5... | collective-permute-start | bytes 1179656 | tf_op jit(solution)/shard_map/ppermute | solution.py:180
  13.3 40.9 %collective-permute-start.3 = (bf16[256,768]{1,0:T(8,128)(2,1)}, bf16[256,768]{1,0:T(8,128)(2,1)}, u32[]{:S(2)}, u32[]{:S(2)}) collective-permute-start(bf16[256,768]{1,0:T(8,128)(2,1)} %get-tuple-element.154), channel_id=1, source_target_pairs={{0,4},{4,0},{8,12},{12,8},{16,20},{20,16},{24,28},{28,24},{1,5},{5... | collective-permute-start | bytes 1179656 | tf_op jit(solution)/shard_map/ppermute | solution.py:171
  24.7 12.4 %collective-permute-start.1 = (bf16[256,768]{1,0:T(8,128)(2,1)}, bf16[256,768]{1,0:T(8,128)(2,1)}, u32[]{:S(2)}, u32[]{:S(2)}) collective-permute-start(bf16[256,768]{1,0:T(8,128)(2,1)} %collective-permute-done), channel_id=1, source_target_pairs={{0,8},{4,12},{8,16},{12,20},{16,24},{20,28},{24,0},{28,4},{1,9},{5... | collective-permute-start | bytes 1179656 | tf_op jit(solution)/shard_map/ppermute | solution.py:180
  24.7 74.1 %copy-start.130 = (f32[256]{0:T(256)}, f32[256]{0:T(256)S(1)}, u32[]{:S(2)}) copy-start(f32[256]{0:T(256)S(1)} %convert_element_type.394) | copy-start | bytes 3076
  27.3 29.1 %collective-permute-start.4 = (bf16[256,768]{1,0:T(8,128)(2,1)}, bf16[256,768]{1,0:T(8,128)(2,1)S(1)}, u32[]{:S(2)}, u32[]{:S(2)}) collective-permute-start(bf16[256,768]{1,0:T(8,128)(2,1)} %collective-permute-done), channel_id=1, source_target_pairs={{0,4},{4,0},{8,12},{12,8},{16,20},{20,16},{24,28},{28,24},{1,5},{5... | collective-permute-start | bytes 1179656 | tf_op jit(solution)/shard_map/ppermute | solution.py:171
  37.1 11.2 %collective-permute-start.7 = (bf16[512,256]{1,0:T(8,128)(2,1)}, bf16[512,256]{1,0:T(8,128)(2,1)S(1)}, u32[]{:S(2)}, u32[]{:S(2)}) collective-permute-start(bf16[512,256]{1,0:T(8,128)(2,1)} %param.34), channel_id=1, source_target_pairs={{0,8},{4,12},{8,16},{12,20},{16,24},{20,28},{24,0},{28,4},{1,9},{5... | collective-permute-start | bytes 786440 | tf_op jit(solution)/shard_map/ppermute | solution.py:180
  37.1 17.0 %collective-permute-start.2 = (bf16[256,768]{1,0:T(8,128)(2,1)}, bf16[256,768]{1,0:T(8,128)(2,1)S(1)}, u32[]{:S(2)}, u32[]{:S(2)}) collective-permute-start(bf16[256,768]{1,0:T(8,128)(2,1)} %collective-permute-done.1), channel_id=1, source_target_pairs={{0,8},{4,12},{8,16},{12,20},{16,24},{20,28},{24,0},{28,4},{1,9},{5... | collective-permute-start | bytes 1179656 | tf_op jit(solution)/shard_map/ppermute | solution.py:180
  38.1 50.8 %collective-permute-start.10 = (bf16[512,256]{1,0:T(8,128)(2,1)}, bf16[512,256]{1,0:T(8,128)(2,1)S(1)}, u32[]{:S(2)}, u32[]{:S(2)}) collective-permute-start(bf16[512,256]{1,0:T(8,128)(2,1)} %param.34), channel_id=1, source_target_pairs={{0,4},{4,0},{8,12},{12,8},{16,20},{20,16},{24,28},{28,24},{1,5},{5... | collective-permute-start | bytes 786440 | tf_op jit(solution)/shard_map/ppermute | solution.py:171
  48.3 9.9 %collective-permute-start.5 = (bf16[256,768]{1,0:T(8,128)(2,1)}, bf16[256,768]{1,0:T(8,128)(2,1)S(1)}, u32[]{:S(2)}, u32[]{:S(2)}) collective-permute-start(bf16[256,768]{1,0:T(8,128)(2,1)} %collective-permute-done.1), channel_id=1, source_target_pairs={{0,4},{4,0},{8,12},{12,8},{16,20},{20,16},{24,28},{28,24},{1,5},{5... | collective-permute-start | bytes 1179656 | tf_op jit(solution)/shard_map/ppermute | solution.py:171
  54.2 8.2 collective-permute-start.8
  54.2 12.4 %collective-permute-start.6 = (bf16[256,768]{1,0:T(8,128)(2,1)S(1)}, bf16[256,768]{1,0:T(8,128)(2,1)S(1)}, u32[]{:S(2)}, u32[]{:S(2)}) collective-permute-start(bf16[256,768]{1,0:T(8,128)(2,1)S(1)} %collective-permute-done.2), channel_id=1, source_target_pairs={{0,4},{4,0},{8,12},{12,8},{16,20},{20,16},{24,28},{28,24},{1,5},{5... | collective-permute-start | bytes 1179656 | tf_op jit(solution)/shard_map/ppermute | solution.py:171
  56.4 32.7 %collective-permute-start.11 = (bf16[512,256]{1,0:T(8,128)(2,1)S(1)}, bf16[512,256]{1,0:T(8,128)(2,1)S(1)}, u32[]{:S(2)}, u32[]{:S(2)}) collective-permute-start(bf16[512,256]{1,0:T(8,128)(2,1)S(1)} %collective-permute-done.7), channel_id=1, source_target_pairs={{0,4},{4,0},{8,12},{12,8},{16,20},{20,16},{24,28},{28,24},{1,5},{5... | collective-permute-start | bytes 786440 | tf_op jit(solution)/shard_map/ppermute | solution.py:171
  62.3 24.7 %collective-permute-start.9 = (bf16[512,256]{1,0:T(8,128)(2,1)S(1)}, bf16[512,256]{1,0:T(8,128)(2,1)S(1)}, u32[]{:S(2)}, u32[]{:S(2)}) collective-permute-start(bf16[512,256]{1,0:T(8,128)(2,1)S(1)} %collective-permute-done.8), channel_id=1, source_target_pairs={{0,8},{4,12},{8,16},{12,20},{16,24},{20,28},{24,0},{28,4},{1,9},{5... | collective-permute-start | bytes 786440 | tf_op jit(solution)/shard_map/ppermute | solution.py:180
  62.5 26.6 %collective-permute-start.12 = (bf16[512,256]{1,0:T(8,128)(2,1)S(1)}, bf16[512,256]{1,0:T(8,128)(2,1)S(1)}, u32[]{:S(2)}, u32[]{:S(2)}) collective-permute-start(bf16[512,256]{1,0:T(8,128)(2,1)S(1)} %collective-permute-done.8), channel_id=1, source_target_pairs={{0,4},{4,0},{8,12},{12,8},{16,20},{20,16},{24,28},{28,24},{1,5},{5... | collective-permute-start | bytes 786440 | tf_op jit(solution)/shard_map/ppermute | solution.py:171
  87.1 6.4 collective-permute-start.13
  98.8 38.3 %collective-permute-start.14 = (bf16[512,2048]{1,0:T(8,128)(2,1)}, bf16[512,2048]{1,0:T(8,128)(2,1)S(1)}, u32[]{:S(2)}, u32[]{:S(2)}) collective-permute-start(bf16[512,2048]{1,0:T(8,128)(2,1)} %pad_maximum_fusion.6), channel_id=1, source_target_pairs={{0,1},{1,0},{2,3},{3,2},{4,5},{5,4},{6,7},{7,6},{8,9},{9,8},{10,11... | collective-permute-start | bytes 6291464 | tf_op jit(solution)/shard_map/ppermute | solution.py:177
  101.3 25.4 %collective-permute-start.21 = (bf16[256,2048]{1,0:T(8,128)(2,1)}, bf16[256,2048]{1,0:T(8,128)(2,1)}, u32[]{:S(2)}, u32[]{:S(2)}) collective-permute-start(bf16[256,2048]{1,0:T(8,128)(2,1)} %pad_maximum_fusion.16), channel_id=1, source_target_pairs={{0,4},{4,0},{8,12},{12,8},{16,20},{20,16},{24,28},{28,24},{1,5},{5... | collective-permute-start | bytes 3145736 | tf_op jit(solution)/shard_map/ppermute | solution.py:171
  136.9 231.0 %all-gather.5.cloned.1.call-start = ((), (), s32[]{:S(2)}) async-start(), calls=%async_computation.5 | async-start | bytes 5242880 | tf_op jit(solution)/shard_map/all_gather | solution.py:249
  139.6 24.3 %collective-permute-start.15 = (bf16[256,2048]{1,0:T(8,128)(2,1)S(1)}, bf16[256,2048]{1,0:T(8,128)(2,1)S(1)}, u32[]{:S(2)}, u32[]{:S(2)}) collective-permute-start(bf16[256,2048]{1,0:T(8,128)(2,1)S(1)} %add_convert_fusion.4), channel_id=1, source_target_pairs={{0,2},{1,3},{2,0},{3,1},{4,6},{5,7},{6,4},{7,5},{8,10},{9,11},{10,... | collective-permute-start | bytes 3145736 | tf_op jit(solution)/shard_map/ppermute | solution.py:174
  141.4 29.9 %collective-permute-start.22 = (bf16[256,1024]{0,1:T(8,128)(2,1)S(1)}, bf16[256,1024]{0,1:T(8,128)(2,1)S(1)}, u32[]{:S(2)}, u32[]{:S(2)}) collective-permute-start(bf16[256,1024]{0,1:T(8,128)(2,1)S(1)} %get-tuple-element.115), channel_id=1, source_target_pairs={{0,4},{4,0},{8,12},{12,8},{16,20},{20,16},{24,28},{28,24},{1,5},{5... | collective-permute-start | bytes 1572872 | tf_op jit(solution)/shard_map/ppermute | solution.py:171
  166.6 295.8 %copy-start.2 = (f32[256,2048]{1,0:T(8,128)}, f32[256,2048]{1,0:T(8,128)S(1)}, u32[]{:S(2)}) copy-start(f32[256,2048]{1,0:T(8,128)S(1)} %get-tuple-element.152) | copy-start | bytes 6291460
  166.6 295.8 %copy-start.128 = (f32[256]{0:T(256)}, f32[256]{0:T(256)S(1)}, u32[]{:S(2)}) copy-start(f32[256]{0:T(256)S(1)} %add_rsqrt_fusion.1) | copy-start | bytes 3076
  167.8 14.9 %collective-permute-start.17 = (bf16[128,2048]{1,0:T(8,128)(2,1)S(1)}, bf16[128,2048]{1,0:T(8,128)(2,1)S(1)}, u32[]{:S(2)}, u32[]{:S(2)}) collective-permute-start(bf16[128,2048]{1,0:T(8,128)(2,1)S(1)} %get-tuple-element.213), channel_id=1, source_target_pairs={{0,4},{4,0},{8,12},{12,8},{16,20},{20,16},{24,28},{28,24},{1,5},{5... | collective-permute-start | bytes 1572872 | tf_op jit(solution)/shard_map/ppermute | solution.py:171
  169.6 14.9 %collective-permute-start.16 = (bf16[128,2048]{1,0:T(8,128)(2,1)S(1)}, bf16[128,2048]{1,0:T(8,128)(2,1)S(1)}, u32[]{:S(2)}, u32[]{:S(2)}) collective-permute-start(bf16[128,2048]{1,0:T(8,128)(2,1)S(1)} %get-tuple-element.214), channel_id=1, source_target_pairs={{0,2},{1,3},{2,0},{3,1},{4,6},{5,7},{6,4},{7,5},{8,10},{9,11},{10,... | collective-permute-start | bytes 1572872 | tf_op jit(solution)/shard_map/ppermute | solution.py:174
  171.4 33.8 %collective-permute-start.31 = (bf16[256,2048]{1,0:T(8,128)(2,1)S(1)}, bf16[256,2048]{1,0:T(8,128)(2,1)S(1)}, u32[]{:S(2)}, u32[]{:S(2)}) collective-permute-start(bf16[256,2048]{1,0:T(8,128)(2,1)S(1)} %get-tuple-element.117), channel_id=1, source_target_pairs={{0,4},{4,0},{8,12},{12,8},{16,20},{20,16},{24,28},{28,24},{1,5},{5... | collective-permute-start | bytes 3145736 | tf_op jit(solution)/shard_map/ppermute | solution.py:171
  182.8 24.9 %collective-permute-start.18 = (bf16[256,2048]{1,0:T(8,128)(2,1)S(1)}, bf16[256,2048]{1,0:T(8,128)(2,1)S(1)}, u32[]{:S(2)}, u32[]{:S(2)}) collective-permute-start(bf16[256,2048]{1,0:T(8,128)(2,1)S(1)} %pad_maximum_fusion.14), channel_id=1, source_target_pairs={{0,2},{1,3},{2,0},{3,1},{4,6},{5,7},{6,4},{7,5},{8,10},{9,11},{10,... | collective-permute-start | bytes 3145736 | tf_op jit(solution)/shard_map/ppermute | solution.py:174
  184.7 40.3 %collective-permute-start.19 = (bf16[256,2048]{1,0:T(8,128)(2,1)S(1)}, bf16[256,2048]{1,0:T(8,128)(2,1)S(1)}, u32[]{:S(2)}, u32[]{:S(2)}) collective-permute-start(bf16[256,2048]{1,0:T(8,128)(2,1)S(1)} %pad_maximum_fusion.15), channel_id=1, source_target_pairs={{0,4},{4,0},{8,12},{12,8},{16,20},{20,16},{24,28},{28,24},{1,5},{5... | collective-permute-start | bytes 3145736 | tf_op jit(solution)/shard_map/ppermute | solution.py:171
  205.2 23.2 %collective-permute-start.32 = (bf16[256,2048]{1,0:T(8,128)(2,1)S(1)}, bf16[256,2048]{1,0:T(8,128)(2,1)S(1)}, u32[]{:S(2)}, u32[]{:S(2)}) collective-permute-start(bf16[256,2048]{1,0:T(8,128)(2,1)S(1)} %collective-permute-done.31), channel_id=1, source_target_pairs={{0,2},{1,3},{2,0},{3,1},{4,6},{5,7},{6,4},{7,5},{8,10},{9,11},{10,... | collective-permute-start | bytes 3145736 | tf_op jit(solution)/shard_map/ppermute | solution.py:174
  228.4 16.4 %collective-permute-start.20 = (bf16[1024,2048]{1,0:T(8,128)(2,1)}, bf16[1024,2048]{1,0:T(8,128)(2,1)}, u32[]{:S(2)}, u32[]{:S(2)}) collective-permute-start(bf16[1024,2048]{1,0:T(8,128)(2,1)} %slice_dynamic-update-slice_fusion.7), channel_id=1, source_target_pairs={{0,1},{1,0},{2,3},{3,2},{4,5},{5,4},{6,7},{7,6},{8,9},{9,8},{10,11... | collective-permute-start | bytes 12582920 | tf_op jit(solution)/shard_map/ppermute | solution.py:177
  230.1 9.0 %collective-permute-start.33 = (bf16[512,2048]{1,0:T(8,128)(2,1)}, bf16[512,2048]{1,0:T(8,128)(2,1)}, u32[]{:S(2)}, u32[]{:S(2)}) collective-permute-start(bf16[512,2048]{1,0:T(8,128)(2,1)} %pad_maximum_fusion.7), channel_id=1, source_target_pairs={{0,1},{1,0},{2,3},{3,2},{4,5},{5,4},{6,7},{7,6},{8,9},{9,8},{10,11... | collective-permute-start | bytes 6291464 | tf_op jit(solution)/shard_map/ppermute | solution.py:177
  287.4 364.7 %reduce-scatter.9.cloned.1.call-start = ((), (), s32[]{:S(2)}) async-start(), calls=%async_computation.8 | async-start | bytes 5242880 | tf_op jit(solution)/shard_map/reduce_scatter | solution.py:252
  411.4 7.2 collective-permute-start.34
  420.9 25.3 %collective-permute-start.37 = (bf16[256,2048]{1,0:T(8,128)(2,1)S(1)}, bf16[256,2048]{1,0:T(8,128)(2,1)S(1)}, u32[]{:S(2)}, u32[]{:S(2)}) collective-permute-start(bf16[256,2048]{1,0:T(8,128)(2,1)S(1)} %pad_maximum_fusion.20), channel_id=1, source_target_pairs={{0,4},{4,0},{8,12},{12,8},{16,20},{20,16},{24,28},{28,24},{1,5},{5... | collective-permute-start | bytes 3145736 | tf_op jit(solution)/shard_map/ppermute | solution.py:171
  422.6 25.5 %collective-permute-start.35 = (bf16[256,2048]{1,0:T(8,128)(2,1)S(1)}, bf16[256,2048]{1,0:T(8,128)(2,1)S(1)}, u32[]{:S(2)}, u32[]{:S(2)}) collective-permute-start(bf16[256,2048]{1,0:T(8,128)(2,1)S(1)} %pad_maximum_fusion.19), channel_id=1, source_target_pairs={{0,2},{1,3},{2,0},{3,1},{4,6},{5,7},{6,4},{7,5},{8,10},{9,11},{10,... | collective-permute-start | bytes 3145736 | tf_op jit(solution)/shard_map/ppermute | solution.py:174
  446.5 13.2 %collective-permute-start.38 = (bf16[128,2048]{1,0:T(8,128)(2,1)S(1)}, bf16[128,2048]{1,0:T(8,128)(2,1)S(1)}, u32[]{:S(2)}, u32[]{:S(2)}) collective-permute-start(bf16[128,2048]{1,0:T(8,128)(2,1)S(1)} %fusion.76), channel_id=1, source_target_pairs={{0,2},{1,3},{2,0},{3,1},{4,6},{5,7},{6,4},{7,5},{8,10},{9,11},{10,... | collective-permute-start | bytes 1572872 | tf_op jit(solution)/shard_map/ppermute | solution.py:174
  448.4 12.9 %collective-permute-start.36 = (bf16[128,2048]{1,0:T(8,128)(2,1)S(1)}, bf16[128,2048]{1,0:T(8,128)(2,1)S(1)}, u32[]{:S(2)}, u32[]{:S(2)}) collective-permute-start(bf16[128,2048]{1,0:T(8,128)(2,1)S(1)} %fusion.78), channel_id=1, source_target_pairs={{0,4},{4,0},{8,12},{12,8},{16,20},{20,16},{24,28},{28,24},{1,5},{5... | collective-permute-start | bytes 1572872 | tf_op jit(solution)/shard_map/ppermute | solution.py:171
  464.5 23.4 %collective-permute-start.40 = (bf16[256,2048]{1,0:T(8,128)(2,1)S(1)}, bf16[256,2048]{1,0:T(8,128)(2,1)}, u32[]{:S(2)}, u32[]{:S(2)}) collective-permute-start(bf16[256,2048]{1,0:T(8,128)(2,1)S(1)} %fusion.121), channel_id=1, source_target_pairs={{0,2},{1,3},{2,0},{3,1},{4,6},{5,7},{6,4},{7,5},{8,10},{9,11},{10,... | collective-permute-start | bytes 3145736 | tf_op jit(solution)/shard_map/ppermute | solution.py:174
  465.6 38.5 %collective-permute-start.39 = (bf16[256,2048]{1,0:T(8,128)(2,1)S(1)}, bf16[256,2048]{1,0:T(8,128)(2,1)}, u32[]{:S(2)}, u32[]{:S(2)}) collective-permute-start(bf16[256,2048]{1,0:T(8,128)(2,1)S(1)} %fusion.121), channel_id=1, source_target_pairs={{0,1},{1,0},{2,3},{3,2},{4,5},{5,4},{6,7},{7,6},{8,9},{9,8},{10,11... | collective-permute-start | bytes 3145736 | tf_op jit(solution)/shard_map/ppermute | solution.py:177
  487.9 16.2 %collective-permute-start.41 = (bf16[256,2048]{1,0:T(8,128)(2,1)}, bf16[256,2048]{1,0:T(8,128)(2,1)}, u32[]{:S(2)}, u32[]{:S(2)}) collective-permute-start(bf16[256,2048]{1,0:T(8,128)(2,1)} %collective-permute-done.40), channel_id=1, source_target_pairs={{0,1},{1,0},{2,3},{3,2},{4,5},{5,4},{6,7},{7,6},{8,9},{9,8},{10,11... | collective-permute-start | bytes 3145736 | tf_op jit(solution)/shard_map/ppermute | solution.py:177
  504.1 282.5 %reduce-scatter.7.cloned.1.call-start = ((), (), s32[]{:S(2)}) async-start(), calls=%async_computation.7 | async-start | bytes 1310720 | tf_op jit(solution)/shard_map/reduce_scatter | solution.py:252
  521.7 66.9 %collective-permute-start.50 = (bf16[1024,512]{0,1:T(8,128)(2,1)}, bf16[1024,512]{0,1:T(8,128)(2,1)}, u32[]{:S(2)}, u32[]{:S(2)}) collective-permute-start(bf16[1024,512]{0,1:T(8,128)(2,1)} %copy.94), channel_id=1, source_target_pairs={{0,4},{4,0},{8,12},{12,8},{16,20},{20,16},{24,28},{28,24},{1,5},{5... | collective-permute-start | bytes 3145736 | tf_op jit(solution)/shard_map/ppermute | solution.py:171
  587.8 37.0 %collective-permute-start.47 = (bf16[1024,768]{1,0:T(8,128)(2,1)}, bf16[1024,768]{1,0:T(8,128)(2,1)}, u32[]{:S(2)}, u32[]{:S(2)}) collective-permute-start(bf16[1024,768]{1,0:T(8,128)(2,1)} %bitcast.103), channel_id=1, source_target_pairs={{0,4},{4,0},{8,12},{12,8},{16,20},{20,16},{24,28},{28,24},{1,5},{5... | collective-permute-start | bytes 4718600 | tf_op jit(solution)/shard_map/ppermute | solution.py:171
  591.3 213.2 %reduce-scatter.5.cloned.1.call-start = ((), (), s32[]{:S(2)}) async-start(), calls=%async_computation.6 | async-start | bytes 1966080 | tf_op jit(solution)/shard_map/reduce_scatter | solution.py:252
  627.8 178.9 %reduce-scatter.11.cloned.1.call-start = ((), (), s32[]{:S(2)}) async-start(), calls=%async_computation.9 | async-start | bytes 10485760 | tf_op jit(solution)/shard_map/reduce_scatter | solution.py:252
  655.8 7.2 collective-permute-start.23
  665.3 25.3 %collective-permute-start.26 = (bf16[256,2048]{1,0:T(8,128)(2,1)S(1)}, bf16[256,2048]{1,0:T(8,128)(2,1)S(1)}, u32[]{:S(2)}, u32[]{:S(2)}) collective-permute-start(bf16[256,2048]{1,0:T(8,128)(2,1)S(1)} %pad_maximum_fusion.18), channel_id=1, source_target_pairs={{0,4},{4,0},{8,12},{12,8},{16,20},{20,16},{24,28},{28,24},{1,5},{5... | collective-permute-start | bytes 3145736 | tf_op jit(solution)/shard_map/ppermute | solution.py:171
  665.8 25.5 %collective-permute-start.24 = (bf16[256,2048]{1,0:T(8,128)(2,1)S(1)}, bf16[256,2048]{1,0:T(8,128)(2,1)S(1)}, u32[]{:S(2)}, u32[]{:S(2)}) collective-permute-start(bf16[256,2048]{1,0:T(8,128)(2,1)S(1)} %pad_maximum_fusion.17), channel_id=1, source_target_pairs={{0,2},{1,3},{2,0},{3,1},{4,6},{5,7},{6,4},{7,5},{8,10},{9,11},{10,... | collective-permute-start | bytes 3145736 | tf_op jit(solution)/shard_map/ppermute | solution.py:174
  691.0 13.3 %collective-permute-start.27 = (bf16[128,2048]{1,0:T(8,128)(2,1)S(1)}, bf16[128,2048]{1,0:T(8,128)(2,1)S(1)}, u32[]{:S(2)}, u32[]{:S(2)}) collective-permute-start(bf16[128,2048]{1,0:T(8,128)(2,1)S(1)} %fusion.80), channel_id=1, source_target_pairs={{0,2},{1,3},{2,0},{3,1},{4,6},{5,7},{6,4},{7,5},{8,10},{9,11},{10,... | collective-permute-start | bytes 1572872 | tf_op jit(solution)/shard_map/ppermute | solution.py:174
  698.0 19.5 %collective-permute-start.42 = (bf16[512,2048]{1,0:T(8,128)(2,1)S(1)}, bf16[512,2048]{1,0:T(8,128)(2,1)S(1)}, u32[]{:S(2)}, u32[]{:S(2)}) collective-permute-start(bf16[512,2048]{1,0:T(8,128)(2,1)S(1)} %pad_maximum_fusion.10), channel_id=1, source_target_pairs={{0,1},{1,0},{2,3},{3,2},{4,5},{5,4},{6,7},{7,6},{8,9},{9,8},{10,11... | collective-permute-start | bytes 6291464 | tf_op jit(solution)/shard_map/ppermute | solution.py:177
  698.2 14.4 %collective-permute-start.25 = (bf16[128,2048]{1,0:T(8,128)(2,1)S(1)}, bf16[128,2048]{1,0:T(8,128)(2,1)S(1)}, u32[]{:S(2)}, u32[]{:S(2)}) collective-permute-start(bf16[128,2048]{1,0:T(8,128)(2,1)S(1)} %fusion.82), channel_id=1, source_target_pairs={{0,4},{4,0},{8,12},{12,8},{16,20},{20,16},{24,28},{28,24},{1,5},{5... | collective-permute-start | bytes 1572872 | tf_op jit(solution)/shard_map/ppermute | solution.py:171
  716.1 26.3 %collective-permute-start.29 = (bf16[256,2048]{1,0:T(8,128)(2,1)}, bf16[256,2048]{1,0:T(8,128)(2,1)}, u32[]{:S(2)}, u32[]{:S(2)}) collective-permute-start(bf16[256,2048]{1,0:T(8,128)(2,1)} %get-tuple-element.148), channel_id=1, source_target_pairs={{0,2},{1,3},{2,0},{3,1},{4,6},{5,7},{6,4},{7,5},{8,10},{9,11},{10,... | collective-permute-start | bytes 3145736 | tf_op jit(solution)/shard_map/ppermute | solution.py:174
  719.2 44.3 %collective-permute-start.43 = (bf16[256,2048]{1,0:T(8,128)(2,1)}, bf16[256,2048]{1,0:T(8,128)(2,1)S(1)}, u32[]{:S(2)}, u32[]{:S(2)}) collective-permute-start(bf16[256,2048]{1,0:T(8,128)(2,1)} %add_convert_fusion.1), channel_id=1, source_target_pairs={{0,2},{1,3},{2,0},{3,1},{4,6},{5,7},{6,4},{7,5},{8,10},{9,11},{10,... | collective-permute-start | bytes 3145736 | tf_op jit(solution)/shard_map/ppermute | solution.py:174
  722.1 13.4 %collective-permute-start.54 = (bf16[256,1024]{1,0:T(8,128)(2,1)S(1)}, bf16[256,1024]{1,0:T(8,128)(2,1)S(1)}, u32[]{:S(2)}, u32[]{:S(2)}) collective-permute-start(bf16[256,1024]{1,0:T(8,128)(2,1)S(1)} %get-tuple-element.202), channel_id=1, source_target_pairs={{0,4},{4,0},{8,12},{12,8},{16,20},{20,16},{24,28},{28,24},{1,5},{5... | collective-permute-start | bytes 1572872 | tf_op jit(solution)/shard_map/ppermute | solution.py:171
  735.6 43.9 %collective-permute-start.28 = (bf16[256,2048]{1,0:T(8,128)(2,1)}, bf16[256,2048]{1,0:T(8,128)(2,1)}, u32[]{:S(2)}, u32[]{:S(2)}) collective-permute-start(bf16[256,2048]{1,0:T(8,128)(2,1)} %get-tuple-element.148), channel_id=1, source_target_pairs={{0,1},{1,0},{2,3},{3,2},{4,5},{5,4},{6,7},{7,6},{8,9},{9,8},{10,11... | collective-permute-start | bytes 3145736 | tf_op jit(solution)/shard_map/ppermute | solution.py:177
  742.4 41.8 %collective-permute-start.30 = (bf16[256,2048]{1,0:T(8,128)(2,1)}, bf16[256,2048]{1,0:T(8,128)(2,1)}, u32[]{:S(2)}, u32[]{:S(2)}) collective-permute-start(bf16[256,2048]{1,0:T(8,128)(2,1)} %collective-permute-done.29), channel_id=1, source_target_pairs={{0,1},{1,0},{2,3},{3,2},{4,5},{5,4},{6,7},{7,6},{8,9},{9,8},{10,11... | collective-permute-start | bytes 3145736 | tf_op jit(solution)/shard_map/ppermute | solution.py:177
  775.8 25.8 %collective-permute-start.44 = (bf16[256,2048]{1,0:T(8,128)(2,1)}, bf16[256,2048]{1,0:T(8,128)(2,1)}, u32[]{:S(2)}, u32[]{:S(2)}) collective-permute-start(bf16[256,2048]{1,0:T(8,128)(2,1)} %get-tuple-element.144), channel_id=1, source_target_pairs={{0,1},{1,0},{2,3},{3,2},{4,5},{5,4},{6,7},{7,6},{8,9},{9,8},{10,11... | collective-permute-start | bytes 3145736 | tf_op jit(solution)/shard_map/ppermute | solution.py:177
  775.8 25.8 %collective-permute-start.45 = (bf16[256,2048]{1,0:T(8,128)(2,1)}, bf16[256,2048]{1,0:T(8,128)(2,1)S(1)}, u32[]{:S(2)}, u32[]{:S(2)}) collective-permute-start(bf16[256,2048]{1,0:T(8,128)(2,1)} %get-tuple-element.144), channel_id=1, source_target_pairs={{0,2},{1,3},{2,0},{3,1},{4,6},{5,7},{6,4},{7,5},{8,10},{9,11},{10,... | collective-permute-start | bytes 3145736 | tf_op jit(solution)/shard_map/ppermute | solution.py:174
  801.6 33.7 %collective-permute-start.46 = (bf16[256,2048]{1,0:T(8,128)(2,1)S(1)}, bf16[256,2048]{1,0:T(8,128)(2,1)S(1)}, u32[]{:S(2)}, u32[]{:S(2)}) collective-permute-start(bf16[256,2048]{1,0:T(8,128)(2,1)S(1)} %collective-permute-done.45), channel_id=1, source_target_pairs={{0,1},{1,0},{2,3},{3,2},{4,5},{5,4},{6,7},{7,6},{8,9},{9,8},{10,11... | collective-permute-start | bytes 3145736 | tf_op jit(solution)/shard_map/ppermute | solution.py:177
  805.6 6.0 collective-permute-start.48
  808.5 24.7 %collective-permute-start.51 = (bf16[256,2048]{1,0:T(8,128)(2,1)S(1)}, bf16[256,2048]{1,0:T(8,128)(2,1)S(1)}, u32[]{:S(2)}, u32[]{:S(2)}) collective-permute-start(bf16[256,2048]{1,0:T(8,128)(2,1)S(1)} %get-tuple-element.183), channel_id=1, source_target_pairs={{0,4},{4,0},{8,12},{12,8},{16,20},{20,16},{24,28},{28,24},{1,5},{5... | collective-permute-start | bytes 3145736 | tf_op jit(solution)/shard_map/ppermute | solution.py:171
  811.6 3.6 collective-permute-start.49
  835.3 1.6 collective-permute-start.52
  836.8 3.6 collective-permute-start.53
  (143 other events, 1316.0 us)
Sparse Core Ops, SparseCore 0:
  137.1 150.3 all-gather.2
  289.0 78.9 all-gather.4
  504.2 74.5 reduce-scatter.8
  591.4 25.6 reduce-scatter.6
  627.9 33.0 reduce-scatter.4
  663.2 143.4 reduce-scatter.10

commit v3 on v2

--- a/solution.py
+++ b/solution.py
@@ -88,15 +88,16 @@
     return jnp.where(allowed, scores, -1000000000.0)
 
 
-def attend_forward(query_seq, key_seq, value_seq, segment_row):
+def attend_forward(query_seq, key_seq, value_seq, segment_row, gates):
     length, kv_local, head_size = key_seq.shape
     grouped = query_seq.reshape(length, kv_local, -1, head_size)
     mixed_parts = []
     total_parts = []
-    for start, rows, first, last in spans(length):
-        scores = block_scores(
-            grouped[start : start + rows], key_seq[first:last], segment_row, start, first
-        )
+    for (start, rows, first, last), gate in zip(spans(length), gates):
+        query_block = grouped[start : start + rows]
+        if gate:
+            query_block = tie(query_block, *gate)
+        scores = block_scores(query_block, key_seq[first:last], segment_row, start, first)
         row_max = jnp.max(scores, axis=-1, keepdims=True)
         log_total = jnp.log(jnp.sum(jnp.exp(scores - row_max), axis=-1, keepdims=True)) + row_max
         soft_low = jnp.exp(scores - log_total).astype(BF)
@@ -108,7 +109,7 @@
     return (jnp.concatenate(mixed_parts, axis=0), total_parts)
 
 
-def attend_backward(query_seq, key_seq, value_seq, total_parts, grad_seq, segment_row):
+def attend_backward(query_seq, key_seq, value_seq, total_parts, grad_seq, segment_row, gates):
     length, kv_local, head_size = key_seq.shape
     grouped = query_seq.reshape(length, kv_local, -1, head_size)
     grad_grouped = grad_seq.reshape(length, kv_local, -1, head_size)
@@ -116,9 +117,11 @@
     query_parts = []
     key_grad = jnp.zeros(key_seq.shape, F32)
     value_grad = jnp.zeros(value_seq.shape, F32)
-    for (start, rows, first, last), log_total in zip(spans(length), total_parts):
+    for (start, rows, first, last), log_total, gate in zip(spans(length), total_parts, gates):
         query_block = grouped[start : start + rows]
         grad_block = grad_grouped[start : start + rows]
+        if gate:
+            grad_block = tie(grad_block, *gate)
         key_block, value_block = key_seq[first:last], value_seq[first:last]
         scores = block_scores(query_block, key_block, segment_row, start, first)
         soft_weights = jnp.exp(scores - log_total)
@@ -225,7 +228,11 @@
     def scaled(weight, scale):
         return (weight.astype(F32) * scale).astype(BF)
 
+    gate_scaled, up_scaled = scaled(gate_weight, ffn_scale), scaled(up_weight, ffn_scale)
+    gu_send = jnp.concatenate([my_half(gate_scaled, 1, False), my_half(up_scaled, 1, False)], axis=1)
+    gu_got = swap_y(gu_send)
     qkv_local = scaled(jnp.concatenate([query_weight, key_weight, value_weight], axis=1), attn_scale)
+    qkv_local = tie(qkv_local, gu_send)
     qkv_ring = ring_gather(qkv_local)
     qkv_other = [swap_y(v) for v in qkv_ring]
     qkv_full = place(
@@ -260,14 +267,19 @@
             jnp.concatenate([got, mine], axis=axis),
         )
 
-    gate_scaled, up_scaled = scaled(gate_weight, ffn_scale), scaled(up_weight, ffn_scale)
+    def pair_rows(mine, got):
+        size = mine.shape[0]
+        whole = jnp.zeros((2 * size, mine.shape[1]), BF)
+        whole = lax.dynamic_update_slice(whole, mine, (y_index * size, 0))
+        return lax.dynamic_update_slice(whole, got, ((1 - y_index) * size, 0))
+
     gu_mine = jnp.concatenate([my_half(gate_scaled, 1, True), my_half(up_scaled, 1, True)], axis=1)
-    gu_send = jnp.concatenate([my_half(gate_scaled, 1, False), my_half(up_scaled, 1, False)], axis=1)
-    gu_got = swap_y(gu_send)
-    gu_full = gather_z(tie(by_y(gu_mine, gu_got, 0), qkv_ring[-1]))
+    gu_pair = pair_rows(gu_mine, gu_got)
+    gu_full = gather_z(tie(gu_pair, qkv_ring[-1]))
     down_t = down_weight.T
-    down_got = swap_y(tie(my_half(down_t, 1, False), gu_got))
-    down_full = gather_z(tie(by_y(my_half(down_t, 1, True), down_got, 0), gu_full))
+    down_got = swap_y(tie(my_half(down_t, 1, False), out_other[-1]))
+    down_pair = pair_rows(my_half(down_t, 1, True), down_got)
+    down_full = gather_z(tie(down_pair, gu_pair))
     cot_rel = relative(cotangent)
     cot_y = swap_y(tie(cot_rel[:quarter], down_got))
     cot_yx = swap_x(cot_y)
@@ -279,7 +291,7 @@
     tokens_float = tokens.astype(F32)
     token_root = inverse_root(tokens_float)
     normed = (tokens_float * token_root).astype(BF)
-    qkv_raw = dot(normed, qkv_full)
+    qkv_raw = dot(tie(normed, gu_pair), qkv_full)
     q_cols, kv_cols = query_weight.shape[1], key_weight.shape[1]
     segment_row = segment_ids[0]
     cosine_table, sine_table = rope_tables(segment_row, HD)
@@ -289,9 +301,10 @@
     value_seq = qkv_raw[:, q_cols + kv_cols :].astype(BF).reshape(token_count, -1, HD)
     query_low = (rotate(query_raw, cosine_wide, sine_wide) * HD ** (-0.5)).astype(BF)
     key_low = rotate(key_raw, cosine_wide, sine_wide).astype(BF)
-    mixed, log_total = attend_forward(query_low, key_low, value_seq, segment_row)
+    out_gates = ((), (out_ring[1],), (out_ring[2],), (out_ring[3], out_other[1]))
+    mixed, log_total = attend_forward(query_low, key_low, value_seq, segment_row, out_gates)
     mixed_rel = relative(mixed)
-    attn_part = dot(mixed_rel, out_full, BF)
+    attn_part = dot(tie(mixed_rel, down_pair), out_full, BF)
 
     def two_way(first, second):
         return first.astype(F32) + second.astype(F32)
@@ -355,37 +368,86 @@
     silu = gate_values * sig
     active = (silu * up_values).astype(BF)
 
-    def scatter_pair(part):
-        blocks = [part[j * quarter : (j + 1) * quarter] for j in range(8)]
-        got = swap_core(jnp.concatenate([blocks[1], blocks[3], blocks[5], blocks[7]], axis=0))
+    def pair_core(part):
+        return swap_core(
+            jnp.concatenate([part[j * quarter : (j + 1) * quarter] for j in (1, 3, 5, 7)], axis=0)
+        )
+
+    def pair_kept(part, got):
         kept = [
-            two_way(blocks[2 * j], got[j * quarter : (j + 1) * quarter]) for j in range(4)
+            two_way(
+                part[2 * j * quarter : (2 * j + 1) * quarter], got[j * quarter : (j + 1) * quarter]
+            )
+            for j in range(4)
         ]
         top = [v[:half_quarter] for v in kept]
         low = [v[half_quarter:] for v in kept]
-        top_got = swap_x(jnp.concatenate([top[1], top[3]], axis=0).astype(BF)).astype(F32)
-        low_got = swap_y(jnp.concatenate([low[2], low[3]], axis=0).astype(BF)).astype(F32)
+        sends = (
+            jnp.concatenate([top[1], top[3]], axis=0).astype(BF),
+            jnp.concatenate([low[2], low[3]], axis=0).astype(BF),
+        )
+        return top, low, sends
+
+    def pair_pass(top, low, sends):
+        top_got = swap_x(sends[0]).astype(F32)
+        low_got = swap_y(sends[1]).astype(F32)
         top_keep = top[0] + top_got[:half_quarter]
         top_pass = (top[2] + top_got[half_quarter:]).astype(BF)
         low_keep = low[0] + low_got[:half_quarter]
         low_pass = (low[1] + low_got[half_quarter:]).astype(BF)
+        return top_keep, low_keep, (top_pass, low_pass)
+
+    def pair_sum(top_keep, low_keep, passes):
         return jnp.concatenate(
             [
-                top_keep + swap_y(top_pass).astype(F32),
-                low_keep + swap_x(low_pass).astype(F32),
+                top_keep + swap_y(passes[0]).astype(F32),
+                low_keep + swap_x(passes[1]).astype(F32),
             ],
             axis=0,
         )
 
+    def ring_begin(block):
+        return hop(block(1))
+
+    def ring_step(received, block, step):
+        return hop((received.astype(F32) + block(step + 1)).astype(BF))
+
+    def ring_end(received, block):
+        return received.astype(F32) + block(groups)
+
+    def z_block(grad):
+        size = grad.shape[0] // groups
+
+        def block(back):
+            return lax.dynamic_slice_in_dim(
+                grad, (z_index - back) % groups * size, size, 0
+            )
+
+        return block
+
     down_grad = dot_rows(cot_all, active, BF)
-    down_block = scatter_z(down_grad)
-
-    active_grad = dot(cot_all, down_full)
+    down_part = z_block(down_grad)
+    down_runs = [ring_begin(down_part)]
+    for step in range(1, groups - 1):
+        down_runs.append(ring_step(down_runs[-1], down_part, step))
+    down_block = ring_end(down_runs[-1], down_part).astype(BF)
+
+    active_grad = dot(tie(cot_all, down_grad), down_full)
     gate_grad = (active_grad * up_values * (sig * (1.0 + gate_values * (1.0 - sig)))).astype(BF)
     up_grad = (active_grad * silu).astype(BF)
     gu_grad = jnp.concatenate([gate_grad, up_grad], axis=1)
-    e_part = dot_cols(gu_grad, gu_full, BF)
-    e_two = scatter_pair(e_part)
+    e_part = dot_cols(tie(gu_grad, down_runs[0]), gu_full, BF)
+    e_got = pair_core(e_part)
+    gate_weight_grad = dot_rows(n_all, tie(gu_grad[:, :hidden_units], e_part, down_runs[1]), BF)
+    gate_block = scatter_z(gate_weight_grad)
+    e_kept = pair_kept(tie(e_part, gate_weight_grad), e_got)
+    up_weight_grad = dot_rows(n_all, tie(gu_grad[:, hidden_units:], *e_kept[2]), BF)
+    up_block = scatter_z(up_weight_grad)
+    ffn_part = dot_cols(tie(active, up_weight_grad, down_runs[-1]), down_full, BF)
+    ffn_got = pair_core(ffn_part)
+    e_top, e_low, e_sends = e_kept
+    e_top[2] = tie(e_top[2], ffn_part)
+    e_two = pair_sum(*pair_pass(e_top, e_low, e_sends))
     n_hidden = hidden * hidden_root
     cot_quarter = my_quarter(cotangent).astype(F32)
     hidden_grad = cot_quarter + hidden_root * (
@@ -393,15 +455,34 @@
     )
     hidden_low = jnp.concatenate(gather_tensor(hidden_grad.astype(BF)), axis=0)
 
-    gu_weight_grad = dot_rows(n_all, gu_grad, BF)
-    gu_block = scatter_z(tie(gu_weight_grad, down_block))
-
-    ffn_part = dot_cols(active, down_full, BF)
-    layer_quarter = (hidden + scatter_pair(ffn_part)).astype(BF)
+    ffn_kept = pair_kept(ffn_part, ffn_got)
+    ffn_sends = tuple(tie(v, hidden_low) for v in ffn_kept[2])
+    ffn_passed = pair_pass(ffn_kept[0], ffn_kept[1], ffn_sends)
+    layer_quarter = (hidden + pair_sum(*ffn_passed)).astype(BF)
     layer_output = absolute(gather_tensor(layer_quarter), BF)
 
-    out_weight_grad = dot_rows(hidden_low, mixed_rel, BF)
     mixed_grad_rel = dot_cols(hidden_low, out_full, BF)
+    out_weight_grad = dot_rows(hidden_low, tie(mixed_rel, mixed_grad_rel), BF)
+    def y_parts(grad):
+        cut = grad.reshape(groups, 2, grad.shape[0] // (2 * groups), -1)
+
+        def pick(back, side):
+            start = ((z_index - back) % groups, side, 0, 0)
+            return lax.dynamic_slice(cut, start, (1, 1) + cut.shape[2:])[0, 0]
+
+        return lambda back: pick(back, y_index), lambda back: pick(back, 1 - y_index)
+
+    def with_other(mine, other):
+        return lambda back: mine(back).astype(F32) + other[back - 1].astype(F32)
+
+    out_mine, out_other_y = y_parts(out_weight_grad)
+    out_sent = swap_y(jnp.stack([out_other_y(back) for back in range(1, groups + 1)]))
+    out_part = with_other(out_mine, out_sent)
+    out_runs = [hop(out_part(1).astype(BF))]
+    for step in range(1, groups - 1):
+        out_runs.append(ring_step(out_runs[-1], out_part, step))
+    out_grad = ring_end(out_runs[-1], out_part).T
+
     mixed_grad = absolute(
         [mixed_grad_rel[j * quarter : (j + 1) * quarter] for j in range(tensor_size)], BF
     )
@@ -412,39 +493,41 @@
         log_total,
         mixed_grad.reshape(token_count, -1, HD),
         segment_row,
+        (
+            ffn_sends + (out_weight_grad,),
+            (out_sent,),
+            ffn_passed[2] + (out_runs[0],),
+            (layer_quarter, out_runs[1]),
+        ),
     )
     query_raw_grad = rotate(query_grad, cosine_wide, -sine_wide).astype(BF).reshape(token_count, -1)
     key_raw_grad = rotate(key_grad, cosine_wide, -sine_wide).astype(BF).reshape(token_count, -1)
     value_raw_grad = value_grad.astype(BF).reshape(token_count, -1)
     qkv_grad = jnp.concatenate([query_raw_grad, key_raw_grad, value_raw_grad], axis=1)
-    e_one_part = dot_cols(relative(qkv_grad), qkv_full, BF)
+    qkv_weight_grad = dot_rows(normed, qkv_grad, BF)
+    e_one_part = dot_cols(relative(tie(qkv_grad, qkv_weight_grad)), qkv_full, BF)
     e_one = scatter_tensor(e_one_part)
     n_one = tokens_quarter * my_quarter(token_root)
     tokens_grad_quarter = hidden_grad + my_quarter(token_root) * (
         e_one - n_one * jnp.mean(e_one * n_one, axis=-1, keepdims=True)
     )
     tokens_grad = absolute(gather_tensor(tokens_grad_quarter.astype(BF)), F32)
-    qkv_weight_grad = dot_rows(normed, qkv_grad, BF)
-
-    def scatter_whole(grad, size):
-        cut = grad.reshape(groups, 2, size, -1)
-        mine = lax.dynamic_index_in_dim(cut, y_index, 1, keepdims=False)
-        other = lax.dynamic_index_in_dim(cut, 1 - y_index, 1, keepdims=False)
-        got = swap_y(other.reshape(groups * size, -1))
-        both = (mine.reshape(groups * size, -1).astype(F32) + got.astype(F32)).astype(BF)
-        return scatter_z(both).astype(F32)
-
-    out_grad = scatter_whole(out_weight_grad, output_weight.shape[1]).T
-    qkv_block = scatter_whole(qkv_weight_grad, rows)
+
+    qkv_mine, qkv_other_y = y_parts(qkv_weight_grad)
+    qkv_sent = [swap_y(qkv_other_y(back)) for back in range(1, groups + 1)]
+    qkv_part = with_other(qkv_mine, qkv_sent)
+    qkv_run = hop(qkv_part(1).astype(BF))
+    for step in range(1, groups - 1):
+        qkv_run = ring_step(qkv_run, qkv_part, step)
+    qkv_block = ring_end(qkv_run, qkv_part)
 
     def trade(block, axis_cut):
         mine = my_half(block, axis_cut, True)
         got = swap_y(my_half(block, axis_cut, False))
         return mine.astype(F32), got.astype(F32)
 
-    gu_mine_rows, gu_got_rows = trade(gu_block, 0)
-    gate_g = by_y(gu_mine_rows[:, :hidden_units], gu_got_rows[:, :hidden_units], 1)
-    up_g = by_y(gu_mine_rows[:, hidden_units:], gu_got_rows[:, hidden_units:], 1)
+    gate_g = by_y(*trade(gate_block, 0), 1)
+    up_g = by_y(*trade(up_block, 0), 1)
     down_weight_grad = by_y(*trade(down_block, 0), 1).T
 
     attn_gain_part = jnp.sum(

time: 853 us -> 835 us (0.979)
  waiting for transfers between devices: 411 us -> 260 us
  local copies, waits for them, and re-layouts: 86.4 us -> 140 us
  other arithmetic: 98.4 us -> 137 us
  starting transfers between devices: 51.5 us -> 80.4 us
  matrix products: 183 us -> 192 us
    ppermute x21 -> x25, waiting for transfers between devices: 182 us -> 81.2 us  [swap_y(): return lax.ppermute(value, 'dp', [(i, i ^ 1) for i in range(dp_size)])]
    all_gather x2, waiting for transfers between devices: 83.6 us -> 26.7 us  [gather_z(): lax.all_gather(value, 'dp', axis_index_groups=z_groups, axis=0, tiled=True)]
    ppermute x6 -> x15, waiting for transfers between devices: 31.1 us -> 66.2 us  [hop(): lax.ppermute(value, 'dp', [(i, (i + 2) % dp_size) for i in range(dp_size)])]
    ppermute x6 -> x15, starting transfers between devices: 3.26 us -> 33.6 us  [hop(): lax.ppermute(value, 'dp', [(i, (i + 2) % dp_size) for i in range(dp_size)])]
    convert_element_type x11 -> x19, other arithmetic: 8.68 us -> 27.8 us  [the longest x6 12 us: ring_step(): return hop((received.astype(F32) + block(step + 1)).astype(BF))]
    ppermute x14, waiting for transfers between devices: 99.9 us -> 81.5 us  [swap_x(): lax.ppermute(value, 'tensor', [(i, i ^ 2) for i in range(tensor_size)])]
    dynamic_update_slice x15 -> x16, local copies, waits for them, and re-layouts: 3.39 us -> 21.2 us  [place(): whole = lax.dynamic_update_slice(whole, value, tuple(start))]
    concatenate x6 -> x9, other arithmetic: 1.72 us -> 15.8 us  [the longest x1 8.43 us: shards(): gu_grad = jnp.concatenate([gate_grad, up_grad], axis=1)]
  transfers between devices with their start and end apart: 61 -> 72, of which waited for: 33 -> 25; matrix products, arithmetic and copies ran while one was open for 34% -> 51% of each run, Pallas kernels for 0% -> 0%
where the time goes in v3:
time: 835 us; the launch traced here: 826 us
  waiting for transfers between devices  260 us (31%)
  matrix products  192 us (23%)
  local copies, waits for them, and re-layouts  140 us (17%)
  other arithmetic  137 us (16%)
  starting transfers between devices  80.4 us (10%)
  between operations  16.6 us (2%)
    ppermute x14, waiting for transfers between devices, swap_x(): lax.ppermute(value, 'tensor', [(i, i ^ 2) for i in range(tensor_size)])  81.5 us
    ppermute x25, waiting for transfers between devices, swap_y(): return lax.ppermute(value, 'dp', [(i, i ^ 1) for i in range(dp_size)])  81.2 us
    ppermute x15, waiting for transfers between devices, hop(): lax.ppermute(value, 'dp', [(i, (i + 2) % dp_size) for i in range(dp_size)])  66.2 us
    unnamed x288, local copies, waits for them, and re-layouts  63.7 us
    dot_general x4, matrix products, dot(): return jnp.dot(left, right, preferred_element_type=F32).astype(out)  53.1 us
    dot_general x4, matrix products, dot_cols(): lax.dot_general(left, right, (((1,), (1,)), ((), ())), preferred_element_...  49.4 us
    dot_general x5, matrix products, dot_rows(): lax.dot_general(left, right, (((0,), (0,)), ((), ())), preferred_element_...  47.7 us
    ppermute x15, starting transfers between devices, hop(): lax.ppermute(value, 'dp', [(i, (i + 2) % dp_size) for i in range(dp_size)])  33.6 us
  transfers between devices with their start and end apart: 72, of which 25 were waited for; matrix products, arithmetic and copies ran while one was open for 51% of the time, Pallas kernels for 0%

profile of v3, /device:TPU:0, one launch (start us, length us, event | category | flops | bytes accessed | tf_op | source)
XLA Modules:
  0.0 825.7 jit_solution(2319679555856869795)
XLA Ops:
  14.9 3.1 collective-permute-start.1
  21.0 3.2 fusion
  24.5 2.8 fusion.1
  40.6 5.6 collective-permute-done.2
  62.4 4.3 collective-permute-done.14
  85.5 3.6 collective-permute-done.7
  89.9 6.4 fusion.185
  112.8 3.3 collective-permute-done.12
  120.9 6.4 collective-permute-done.13
  128.3 4.4 convolution_convert_fusion.6
  133.1 4.1 collective-permute-done.16
  139.2 23.7 %collective-permute-done.17 = bf16[256,2048]{1,0:T(8,128)(2,1)S(1)} collective-permute-done((bf16[256,2048]{1,0:T(8,128)(2,1)S(1)}, bf16[256,2048]{1,0:T(8,128)(2,1)S(1)}, u32[]{:S(2)}, u32[]{:S(2)}) %collective-permute-start.17) | collective-permute-done | bytes 1048608 | tf_op jit(solution)/shard_map/ppermute | solution.py:177
  172.5 8.9 %collective-permute-done.19 = bf16[128,2048]{1,0:T(8,128)(2,1)S(1)} collective-permute-done((bf16[128,2048]{1,0:T(8,128)(2,1)S(1)}, bf16[128,2048]{1,0:T(8,128)(2,1)S(1)}, u32[]{:S(2)}, u32[]{:S(2)}) %collective-permute-start.19) | collective-permute-done | bytes 524320 | tf_op jit(solution)/shard_map/ppermute | solution.py:174
  184.7 19.2 %collective-permute-done.23 = bf16[256,2048]{1,0:T(8,128)(2,1)S(1)} collective-permute-done((bf16[256,2048]{1,0:T(8,128)(2,1)S(1)}, bf16[256,2048]{1,0:T(8,128)(2,1)S(1)}, u32[]{:S(2)}, u32[]{:S(2)}) %collective-permute-start.23) | collective-permute-done | bytes 1048608 | tf_op jit(solution)/shard_map/ppermute | solution.py:174
  207.0 17.7 %collective-permute-done.21 = bf16[256,2048]{1,0:T(8,128)(2,1)S(1)} collective-permute-done((bf16[256,2048]{1,0:T(8,128)(2,1)S(1)}, bf16[256,2048]{1,0:T(8,128)(2,1)S(1)}, u32[]{:S(2)}, u32[]{:S(2)}) %collective-permute-start.21) | collective-permute-done | bytes 1048608 | tf_op jit(solution)/shard_map/ppermute | solution.py:174
  261.1 22.4 %convolution_convert_fusion.2 = bf16[2048,2048]{0,1:T(8,128)(2,1)S(1)} fusion(bf16[2048,2048]{1,0:T(8,128)(2,1)} %slice_dynamic-update-slice_fusion.2, bf16[2048,2048]{0,1:T(8,128)(2,1)} %all-gather.3.cloned.1.call-done), kind=kOutput, calls=%fused_computation.21 | convolution fusion | flops 17184063488 | bytes 25165824 | tf_op jit(solution)/shard_map/dot_general | solution.py:62
  283.6 2.9 fusion.2
  287.0 12.8 %convolution_convert_fusion.5 = bf16[2048,1024]{0,1:T(8,128)(2,1)S(1)} fusion(bf16[2048,1024]{0,1:T(8,128)(2,1)S(1)} %fusion.2, bf16[2048,2048]{1,0:T(8,128)(2,1)} %slice_dynamic-update-slice_fusion), kind=kOutput, calls=%fused_computation.64 | convolution fusion | flops 8592031744 | bytes 16777216 | tf_op jit(solution)/shard_map/dot_general | solution.py:50
  303.3 26.7 %all-gather.5.cloned.1.call-done = bf16[2048,1024]{0,1:T(8,128)(2,1)} async-done(((bf16[512,1024]{0,1:T(8,128)(2,1)}), bf16[2048,1024]{0,1:T(8,128)(2,1)}) %all-gather.5.cloned.1.call-update) | async-done | bytes 4194320 | tf_op jit(solution)/shard_map/all_gather | solution.py:256
  330.1 19.9 %fusion.4 = (bf16[2048,1024]{0,1:T(8,128)(2,1)}, bf16[2048,1024]{0,1:T(8,128)(2,1)}) fusion(bf16[2048,2048]{0,1:T(8,128)(2,1)} %copy-done.25, bf16[2048,2048]{1,0:T(8,128)(2,1)} %slice_dynamic-update-slice_fusion, bf16[2048,1024]{0,1:T(8,128)(2,1)} %all-gather.5.cloned.1.call-done), kind=kOutput, calls=%fused_computation.11 | convolution fusion | flops 8621391872 | bytes 29360128 | tf_op jit(solution)/shard_map/dot_general | solution.py:62
  350.0 8.4 %pad_maximum_fusion = bf16[2048,2048]{0,1:T(8,128)(2,1)} fusion(bf16[2048,1024]{0,1:T(8,128)(2,1)} %get-tuple-element.148, bf16[2048,1024]{0,1:T(8,128)(2,1)} %get-tuple-element.146), kind=kLoop, calls=%fused_computation.17 | loop fusion | flops 16777216 | bytes 16777216 | tf_op jit(solution)/shard_map/concatenate | solution.py:438
  358.4 22.4 %convolution_convert_fusion.1 = bf16[2048,2048]{1,0:T(8,128)(2,1)S(1)} fusion(bf16[2048,2048]{0,1:T(8,128)(2,1)} %pad_maximum_fusion, bf16[2048,2048]{0,1:T(8,128)(2,1)} %all-gather.3.cloned.1.call-done), kind=kOutput, calls=%fused_computation.20 | convolution fusion | flops 17184063488 | bytes 25165824 | tf_op jit(solution)/shard_map/dot_general | solution.py:56
  381.1 3.1 copy-done.34
  388.0 27.3 %collective-permute-done.27 = bf16[512,1024]{0,1:T(8,128)(2,1)S(1)} collective-permute-done((bf16[512,1024]{0,1:T(8,128)(2,1)S(1)}, bf16[512,1024]{0,1:T(8,128)(2,1)S(1)}, u32[]{:S(2)}, u32[]{:S(2)}) %collective-permute-start.27) | collective-permute-done | bytes 1048608 | tf_op jit(solution)/shard_map/ppermute | solution.py:183
  415.4 14.0 %convolution_convert_fusion.4 = bf16[2048,1024]{0,1:T(8,128)(2,1)} fusion(bf16[2048,1024]{0,1:T(8,128)(2,1)} %get-tuple-element.146, bf16[2048,2048]{1,0:T(8,128)(2,1)} %slice_dynamic-update-slice_fusion.2), kind=kOutput, calls=%fused_computation.63 | convolution fusion | flops 8592031744 | bytes 16777216 | tf_op jit(solution)/shard_map/dot_general | solution.py:50
  432.0 7.4 convert_add_fusion.3
  445.1 12.6 %convolution_convert_fusion.3 = bf16[2048,1024]{0,1:T(8,128)(2,1)} fusion(bf16[2048,1024]{0,1:T(8,128)(2,1)S(1)} %copy-done.61, bf16[2048,2048]{1,0:T(8,128)(2,1)} %slice_dynamic-update-slice_fusion.2), kind=kOutput, calls=%fused_computation.62 | convolution fusion | flops 8592031744 | bytes 16777216 | tf_op jit(solution)/shard_map/dot_general | solution.py:50
  457.7 23.6 %collective-permute-done.29 = bf16[512,1024]{0,1:T(8,128)(2,1)} collective-permute-done((bf16[512,1024]{0,1:T(8,128)(2,1)}, bf16[512,1024]{0,1:T(8,128)(2,1)}, u32[]{:S(2)}, u32[]{:S(2)}) %collective-permute-start.29) | collective-permute-done | bytes 1048608 | tf_op jit(solution)/shard_map/ppermute | solution.py:183
  481.3 14.0 %convolution_convert_fusion = bf16[2048,2048]{1,0:T(8,128)(2,1)} fusion(bf16[2048,1024]{0,1:T(8,128)(2,1)} %copy-done.42, bf16[2048,1024]{0,1:T(8,128)(2,1)} %all-gather.5.cloned.1.call-done), kind=kOutput, calls=%fused_computation.19 | convolution fusion | flops 8594128896 | bytes 16777216 | tf_op jit(solution)/shard_map/dot_general | solution.py:56
  502.6 5.7 collective-permute-done.34
  508.3 2.8 collective-permute-done.32
  511.9 3.1 fusion.126
  518.6 3.7 fusion.152
  522.9 2.7 pad_maximum_fusion.2
  526.2 12.6 %collective-permute-done.36 = bf16[256,2048]{1,0:T(8,128)(2,1)} collective-permute-done((bf16[256,2048]{1,0:T(8,128)(2,1)}, bf16[256,2048]{1,0:T(8,128)(2,1)}, u32[]{:S(2)}, u32[]{:S(2)}) %collective-permute-start.36) | collective-permute-done | bytes 1048608 | tf_op jit(solution)/shard_map/ppermute | solution.py:177
  538.8 2.8 fusion.156
  541.6 3.7 fusion.154
  549.8 6.3 convolution_convert_fusion.10
  556.1 4.6 convolution_convert_fusion.9
  580.8 5.4 convert_add_fusion.4
  592.9 4.9 collective-permute-done.45
  598.9 7.3 collective-permute-start.46
  611.7 6.0 collective-permute-done.46
  619.7 8.5 %collective-permute-start.47 = (bf16[256,512]{0,1:T(8,128)(2,1)}, bf16[256,512]{0,1:T(8,128)(2,1)}, u32[]{:S(2)}, u32[]{:S(2)}) collective-permute-start(bf16[256,512]{0,1:T(8,128)(2,1)} %fusion.145), channel_id=1, source_target_pairs={{0,8},{4,12},{8,16},{12,20},{16,24},{20,28},{24,0},{28,4},{1,9},{5... | collective-permute-start | bytes 786440 | tf_op jit(solution)/shard_map/ppermute | solution.py:183
  634.2 4.4 fusion.15
  638.7 4.3 fusion.17
  654.1 4.4 fusion.10
  658.5 4.3 fusion.12
  672.0 3.8 convolution_convert_fusion.8
  676.0 6.8 convolution_convert_fusion.7
  692.3 6.6 collective-permute-done.53
  700.8 2.8 collective-permute-start.54
  710.9 3.3 collective-permute-done.54
  724.3 3.4 collective-permute-done.57
  732.2 2.9 add_convert_fusion.1
  737.7 2.9 copy.97
  740.6 9.5 %collective-permute-done.43 = bf16[256,2048]{1,0:T(8,128)(2,1)} collective-permute-done((bf16[256,2048]{1,0:T(8,128)(2,1)}, bf16[256,2048]{1,0:T(8,128)(2,1)}, u32[]{:S(2)}, u32[]{:S(2)}) %collective-permute-start.43) | collective-permute-done | bytes 1048608 | tf_op jit(solution)/shard_map/ppermute | solution.py:177
  752.5 2.9 fusion.148
  757.9 14.2 %collective-permute-done.49 = bf16[256,2048]{1,0:T(8,128)(2,1)} collective-permute-done((bf16[256,2048]{1,0:T(8,128)(2,1)}, bf16[256,2048]{1,0:T(8,128)(2,1)}, u32[]{:S(2)}, u32[]{:S(2)}) %collective-permute-start.49) | collective-permute-done | bytes 1048608 | tf_op jit(solution)/shard_map/ppermute | solution.py:177
  772.1 2.9 fusion.43
  776.5 4.5 convert_dynamic-update-slice_fusion.3
  781.7 5.6 constant_dynamic-update-slice_fusion.10
  791.3 15.7 %collective-permute-done.61 = f32[256]{0:T(256)S(1)} collective-permute-done((f32[256]{0:T(256)S(1)}, f32[256]{0:T(256)S(1)}, u32[]{:S(2)}, u32[]{:S(2)}) %collective-permute-start.61) | collective-permute-done | bytes 1056 | tf_op jit(solution)/shard_map/ppermute | solution.py:177
  814.3 2.8 convert_dynamic-update-slice_fusion.1
  (616 shorter events, 286.7 us)
Async XLA Ops:
  7.2 254.0 %all-gather.3.cloned.1.call-start = ((), (), s32[]{:S(2)}) async-start(), calls=%async_computation.2 | async-start | bytes 10485760 | tf_op jit(solution)/shard_map/all_gather | solution.py:256
  14.9 19.0 %collective-permute-start.1 = (bf16[256,768]{1,0:T(8,128)(2,1)}, bf16[256,768]{1,0:T(8,128)(2,1)}, u32[]{:S(2)}, u32[]{:S(2)}) collective-permute-start(bf16[256,768]{1,0:T(8,128)(2,1)} %fusion.127), channel_id=1, source_target_pairs={{0,8},{4,12},{8,16},{12,20},{16,24},{20,28},{24,0},{28,4},{1,9},{5... | collective-permute-start | bytes 1179656 | tf_op jit(solution)/shard_map/ppermute | solution.py:183
  18.0 55.6 %collective-permute-start.4 = (bf16[256,768]{1,0:T(8,128)(2,1)}, bf16[256,768]{1,0:T(8,128)(2,1)}, u32[]{:S(2)}, u32[]{:S(2)}) collective-permute-start(bf16[256,768]{1,0:T(8,128)(2,1)} %fusion.127), channel_id=1, source_target_pairs={{0,4},{4,0},{8,12},{12,8},{16,20},{20,16},{24,28},{28,24},{1,5},{5... | collective-permute-start | bytes 1179656 | tf_op jit(solution)/shard_map/ppermute | solution.py:174
  19.5 34.7 %collective-permute-start = (bf16[256,2048]{0,1:T(8,128)(2,1)}, bf16[256,2048]{0,1:T(8,128)(2,1)}, u32[]{:S(2)}, u32[]{:S(2)}) collective-permute-start(bf16[256,2048]{0,1:T(8,128)(2,1)} %pad_maximum_fusion.10), channel_id=1, source_target_pairs={{0,4},{4,0},{8,12},{12,8},{16,20},{20,16},{24,28},{28,24},{1,5},{5... | collective-permute-start | bytes 3145736 | tf_op jit(solution)/shard_map/ppermute | solution.py:174
  33.9 12.2 %collective-permute-start.2 = (bf16[256,768]{1,0:T(8,128)(2,1)}, bf16[256,768]{1,0:T(8,128)(2,1)}, u32[]{:S(2)}, u32[]{:S(2)}) collective-permute-start(bf16[256,768]{1,0:T(8,128)(2,1)} %collective-permute-done.1), channel_id=1, source_target_pairs={{0,8},{4,12},{8,16},{12,20},{16,24},{20,28},{24,0},{28,4},{1,9},{5... | collective-permute-start | bytes 1179656 | tf_op jit(solution)/shard_map/ppermute | solution.py:183
  37.1 38.7 %collective-permute-start.5 = (bf16[256,768]{1,0:T(8,128)(2,1)}, bf16[256,768]{1,0:T(8,128)(2,1)}, u32[]{:S(2)}, u32[]{:S(2)}) collective-permute-start(bf16[256,768]{1,0:T(8,128)(2,1)} %collective-permute-done.1), channel_id=1, source_target_pairs={{0,4},{4,0},{8,12},{12,8},{16,20},{20,16},{24,28},{28,24},{1,5},{5... | collective-permute-start | bytes 1179656 | tf_op jit(solution)/shard_map/ppermute | solution.py:174
  46.1 11.3 %collective-permute-start.8 = (bf16[512,256]{1,0:T(8,128)(2,1)}, bf16[512,256]{1,0:T(8,128)(2,1)}, u32[]{:S(2)}, u32[]{:S(2)}) collective-permute-start(bf16[512,256]{1,0:T(8,128)(2,1)} %param.34), channel_id=1, source_target_pairs={{0,8},{4,12},{8,16},{12,20},{16,24},{20,28},{24,0},{28,4},{1,9},{5... | collective-permute-start | bytes 786440 | tf_op jit(solution)/shard_map/ppermute | solution.py:183
  48.0 22.2 %collective-permute-start.3 = (bf16[256,768]{1,0:T(8,128)(2,1)}, bf16[256,768]{1,0:T(8,128)(2,1)}, u32[]{:S(2)}, u32[]{:S(2)}) collective-permute-start(bf16[256,768]{1,0:T(8,128)(2,1)} %collective-permute-done.2), channel_id=1, source_target_pairs={{0,8},{4,12},{8,16},{12,20},{16,24},{20,28},{24,0},{28,4},{1,9},{5... | collective-permute-start | bytes 1179656 | tf_op jit(solution)/shard_map/ppermute | solution.py:183
  54.2 12.6 %collective-permute-start.14 = (bf16[512,256]{1,0:T(8,128)(2,1)}, bf16[512,256]{1,0:T(8,128)(2,1)}, u32[]{:S(2)}, u32[]{:S(2)}) collective-permute-start(bf16[512,256]{1,0:T(8,128)(2,1)} %param.34), channel_id=1, source_target_pairs={{0,4},{4,0},{8,12},{12,8},{16,20},{20,16},{24,28},{28,24},{1,5},{5... | collective-permute-start | bytes 786440 | tf_op jit(solution)/shard_map/ppermute | solution.py:174
  57.4 20.2 %collective-permute-start.6 = (bf16[256,768]{1,0:T(8,128)(2,1)}, bf16[256,768]{1,0:T(8,128)(2,1)}, u32[]{:S(2)}, u32[]{:S(2)}) collective-permute-start(bf16[256,768]{1,0:T(8,128)(2,1)} %collective-permute-done.2), channel_id=1, source_target_pairs={{0,4},{4,0},{8,12},{12,8},{16,20},{20,16},{24,28},{28,24},{1,5},{5... | collective-permute-start | bytes 1179656 | tf_op jit(solution)/shard_map/ppermute | solution.py:174
  66.8 12.7 %collective-permute-start.9 = (bf16[512,256]{1,0:T(8,128)(2,1)}, bf16[512,256]{1,0:T(8,128)(2,1)}, u32[]{:S(2)}, u32[]{:S(2)}) collective-permute-start(bf16[512,256]{1,0:T(8,128)(2,1)} %collective-permute-done.8), channel_id=1, source_target_pairs={{0,8},{4,12},{8,16},{12,20},{16,24},{20,28},{24,0},{28,4},{1,9},{5... | collective-permute-start | bytes 786440 | tf_op jit(solution)/shard_map/ppermute | solution.py:183
  70.1 13.5 %collective-permute-start.11 = (bf16[512,256]{1,0:T(8,128)(2,1)}, bf16[512,256]{1,0:T(8,128)(2,1)}, u32[]{:S(2)}, u32[]{:S(2)}) collective-permute-start(bf16[512,256]{1,0:T(8,128)(2,1)} %collective-permute-done.8), channel_id=1, source_target_pairs={{0,4},{4,0},{8,12},{12,8},{16,20},{20,16},{24,28},{28,24},{1,5},{5... | collective-permute-start | bytes 786440 | tf_op jit(solution)/shard_map/ppermute | solution.py:174
  71.7 258.4 %all-gather.5.cloned.1.call-start = ((), (), s32[]{:S(2)}) async-start(), calls=%async_computation.3 | async-start | bytes 5242880 | tf_op jit(solution)/shard_map/all_gather | solution.py:256
  73.5 15.6 %collective-permute-start.7 = (bf16[256,768]{1,0:T(8,128)(2,1)}, bf16[256,768]{1,0:T(8,128)(2,1)S(1)}, u32[]{:S(2)}, u32[]{:S(2)}) collective-permute-start(bf16[256,768]{1,0:T(8,128)(2,1)} %collective-permute-done.3), channel_id=1, source_target_pairs={{0,4},{4,0},{8,12},{12,8},{16,20},{20,16},{24,28},{28,24},{1,5},{5... | collective-permute-start | bytes 1179656 | tf_op jit(solution)/shard_map/ppermute | solution.py:174
  79.5 18.4 %collective-permute-start.10 = (bf16[512,256]{1,0:T(8,128)(2,1)}, bf16[512,256]{1,0:T(8,128)(2,1)S(1)}, u32[]{:S(2)}, u32[]{:S(2)}) collective-permute-start(bf16[512,256]{1,0:T(8,128)(2,1)} %collective-permute-done.9), channel_id=1, source_target_pairs={{0,8},{4,12},{8,16},{12,20},{16,24},{20,28},{24,0},{28,4},{1,9},{5... | collective-permute-start | bytes 786440 | tf_op jit(solution)/shard_map/ppermute | solution.py:183
  82.2 36.5 %collective-permute-start.15 = (bf16[512,256]{1,0:T(8,128)(2,1)}, bf16[512,256]{1,0:T(8,128)(2,1)S(1)}, u32[]{:S(2)}, u32[]{:S(2)}) collective-permute-start(bf16[512,256]{1,0:T(8,128)(2,1)} %collective-permute-done.9), channel_id=1, source_target_pairs={{0,4},{4,0},{8,12},{12,8},{16,20},{20,16},{24,28},{28,24},{1,5},{5... | collective-permute-start | bytes 786440 | tf_op jit(solution)/shard_map/ppermute | solution.py:174
  116.1 11.2 %collective-permute-start.13 = (bf16[256,1024]{0,1:T(8,128)(2,1)}, bf16[256,1024]{0,1:T(8,128)(2,1)}, u32[]{:S(2)}, u32[]{:S(2)}) collective-permute-start(bf16[256,1024]{0,1:T(8,128)(2,1)} %dynamic-slice_bitcast_fusion), channel_id=1, source_target_pairs={{0,4},{4,0},{8,12},{12,8},{16,20},{20,16},{24,28},{28,24},{1,5},{5... | collective-permute-start | bytes 1572872 | tf_op jit(solution)/shard_map/ppermute | solution.py:174
  137.7 25.3 %collective-permute-start.17 = (bf16[256,2048]{1,0:T(8,128)(2,1)S(1)}, bf16[256,2048]{1,0:T(8,128)(2,1)S(1)}, u32[]{:S(2)}, u32[]{:S(2)}) collective-permute-start(bf16[256,2048]{1,0:T(8,128)(2,1)S(1)} %add_convert_fusion.6), channel_id=1, source_target_pairs={{0,2},{1,3},{2,0},{3,1},{4,6},{5,7},{6,4},{7,5},{8,10},{9,11},{10,... | collective-permute-start | bytes 3145736 | tf_op jit(solution)/shard_map/ppermute | solution.py:177
  166.6 14.8 %collective-permute-start.19 = (bf16[128,2048]{1,0:T(8,128)(2,1)S(1)}, bf16[128,2048]{1,0:T(8,128)(2,1)S(1)}, u32[]{:S(2)}, u32[]{:S(2)}) collective-permute-start(bf16[128,2048]{1,0:T(8,128)(2,1)S(1)} %get-tuple-element.259), channel_id=1, source_target_pairs={{0,4},{4,0},{8,12},{12,8},{16,20},{20,16},{24,28},{28,24},{1,5},{5... | collective-permute-start | bytes 1572872 | tf_op jit(solution)/shard_map/ppermute | solution.py:174
  168.1 14.9 %collective-permute-start.18 = (bf16[128,2048]{1,0:T(8,128)(2,1)S(1)}, bf16[128,2048]{1,0:T(8,128)(2,1)S(1)}, u32[]{:S(2)}, u32[]{:S(2)}) collective-permute-start(bf16[128,2048]{1,0:T(8,128)(2,1)S(1)} %get-tuple-element.260), channel_id=1, source_target_pairs={{0,2},{1,3},{2,0},{3,1},{4,6},{5,7},{6,4},{7,5},{8,10},{9,11},{10,... | collective-permute-start | bytes 1572872 | tf_op jit(solution)/shard_map/ppermute | solution.py:177
  171.9 31.9 %collective-permute-start.23 = (bf16[256,2048]{1,0:T(8,128)(2,1)S(1)}, bf16[256,2048]{1,0:T(8,128)(2,1)S(1)}, u32[]{:S(2)}, u32[]{:S(2)}) collective-permute-start(bf16[256,2048]{1,0:T(8,128)(2,1)S(1)} %get-tuple-element.142), channel_id=1, source_target_pairs={{0,4},{4,0},{8,12},{12,8},{16,20},{20,16},{24,28},{28,24},{1,5},{5... | collective-permute-start | bytes 3145736 | tf_op jit(solution)/shard_map/ppermute | solution.py:174
  181.4 24.7 %collective-permute-start.20 = (bf16[256,2048]{1,0:T(8,128)(2,1)S(1)}, bf16[256,2048]{1,0:T(8,128)(2,1)S(1)}, u32[]{:S(2)}, u32[]{:S(2)}) collective-permute-start(bf16[256,2048]{1,0:T(8,128)(2,1)S(1)} %pad_maximum_fusion.13), channel_id=1, source_target_pairs={{0,2},{1,3},{2,0},{3,1},{4,6},{5,7},{6,4},{7,5},{8,10},{9,11},{10,... | collective-permute-start | bytes 3145736 | tf_op jit(solution)/shard_map/ppermute | solution.py:177
  183.1 41.6 %collective-permute-start.21 = (bf16[256,2048]{1,0:T(8,128)(2,1)S(1)}, bf16[256,2048]{1,0:T(8,128)(2,1)S(1)}, u32[]{:S(2)}, u32[]{:S(2)}) collective-permute-start(bf16[256,2048]{1,0:T(8,128)(2,1)S(1)} %pad_maximum_fusion.14), channel_id=1, source_target_pairs={{0,4},{4,0},{8,12},{12,8},{16,20},{20,16},{24,28},{28,24},{1,5},{5... | collective-permute-start | bytes 3145736 | tf_op jit(solution)/shard_map/ppermute | solution.py:174
  203.8 24.3 %collective-permute-start.24 = (bf16[256,2048]{1,0:T(8,128)(2,1)S(1)}, bf16[256,2048]{1,0:T(8,128)(2,1)S(1)}, u32[]{:S(2)}, u32[]{:S(2)}) collective-permute-start(bf16[256,2048]{1,0:T(8,128)(2,1)S(1)} %collective-permute-done.23), channel_id=1, source_target_pairs={{0,2},{1,3},{2,0},{3,1},{4,6},{5,7},{6,4},{7,5},{8,10},{9,11},{10,... | collective-permute-start | bytes 3145736 | tf_op jit(solution)/shard_map/ppermute | solution.py:177
  228.1 18.6 %collective-permute-start.22 = (bf16[1024,2048]{1,0:T(8,128)(2,1)}, bf16[1024,2048]{1,0:T(8,128)(2,1)}, u32[]{:S(2)}, u32[]{:S(2)}) collective-permute-start(bf16[1024,2048]{1,0:T(8,128)(2,1)} %slice_dynamic-update-slice_fusion.7), channel_id=1, source_target_pairs={{0,1},{1,0},{2,3},{3,2},{4,5},{5,4},{6,7},{7,6},{8,9},{9,8},{10,11... | collective-permute-start | bytes 12582920 | tf_op jit(solution)/shard_map/ppermute | solution.py:180
  237.4 466.3 %reduce-scatter.3.cloned.1.call-start = ((), (), s32[]{:S(2)}) async-start(), calls=%async_computation.4 | async-start | bytes 5242880 | tf_op jit(solution)/shard_map/reduce_scatter | solution.py:259
  301.8 56.6 %collective-permute-start.26 = (bf16[512,1024]{0,1:T(8,128)(2,1)S(1)}, bf16[512,1024]{0,1:T(8,128)(2,1)S(1)}, u32[]{:S(2)}, u32[]{:S(2)}) collective-permute-start(bf16[512,1024]{0,1:T(8,128)(2,1)S(1)} %constant_dynamic-slice_fusion.15), channel_id=1, source_target_pairs={{0,8},{4,12},{8,16},{12,20},{16,24},{20,28},{24,0},{28,4},{1,9},{5... | collective-permute-start | bytes 3145736 | tf_op jit(solution)/shard_map/ppermute | solution.py:183
  386.4 45.6 %collective-permute-start.28 = (bf16[1024,2048]{1,0:T(8,128)(2,1)}, bf16[1024,2048]{1,0:T(8,128)(2,1)}, u32[]{:S(2)}, u32[]{:S(2)}) collective-permute-start(bf16[1024,2048]{1,0:T(8,128)(2,1)} %pad_maximum_fusion.1), channel_id=1, source_target_pairs={{0,1},{1,0},{2,3},{3,2},{4,5},{5,4},{6,7},{7,6},{8,9},{9,8},{10,11... | collective-permute-start | bytes 12582920 | tf_op jit(solution)/shard_map/ppermute | solution.py:180
  388.0 27.4 %collective-permute-start.27 = (bf16[512,1024]{0,1:T(8,128)(2,1)S(1)}, bf16[512,1024]{0,1:T(8,128)(2,1)S(1)}, u32[]{:S(2)}, u32[]{:S(2)}) collective-permute-start(bf16[512,1024]{0,1:T(8,128)(2,1)S(1)} %add_convert_fusion.5), channel_id=1, source_target_pairs={{0,8},{4,12},{8,16},{12,20},{16,24},{20,28},{24,0},{28,4},{1,9},{5... | collective-permute-start | bytes 3145736 | tf_op jit(solution)/shard_map/ppermute | solution.py:183
  429.4 326.5 %reduce-scatter.5.cloned.1.call-start = ((), (), s32[]{:S(2)}) async-start(), calls=%async_computation.5 | async-start | bytes 5242880 | tf_op jit(solution)/shard_map/reduce_scatter | solution.py:259
  432.0 49.3 %collective-permute-start.29 = (bf16[512,1024]{0,1:T(8,128)(2,1)}, bf16[512,1024]{0,1:T(8,128)(2,1)}, u32[]{:S(2)}, u32[]{:S(2)}) collective-permute-start(bf16[512,1024]{0,1:T(8,128)(2,1)} %add_convert_fusion.3), channel_id=1, source_target_pairs={{0,8},{4,12},{8,16},{12,20},{16,24},{20,28},{24,0},{28,4},{1,9},{5... | collective-permute-start | bytes 3145736 | tf_op jit(solution)/shard_map/ppermute | solution.py:183
  441.1 54.3 %collective-permute-start.33 = (bf16[256,2048]{1,0:T(8,128)(2,1)}, bf16[256,2048]{1,0:T(8,128)(2,1)}, u32[]{:S(2)}, u32[]{:S(2)}) collective-permute-start(bf16[256,2048]{1,0:T(8,128)(2,1)} %pad_maximum_fusion.16), channel_id=1, source_target_pairs={{0,4},{4,0},{8,12},{12,8},{16,20},{20,16},{24,28},{28,24},{1,5},{5... | collective-permute-start | bytes 3145736 | tf_op jit(solution)/shard_map/ppermute | solution.py:174
  443.7 55.7 %collective-permute-start.31 = (bf16[256,2048]{1,0:T(8,128)(2,1)}, bf16[256,2048]{1,0:T(8,128)(2,1)S(1)}, u32[]{:S(2)}, u32[]{:S(2)}) collective-permute-start(bf16[256,2048]{1,0:T(8,128)(2,1)} %pad_maximum_fusion.15), channel_id=1, source_target_pairs={{0,2},{1,3},{2,0},{3,1},{4,6},{5,7},{6,4},{7,5},{8,10},{9,11},{10,... | collective-permute-start | bytes 3145736 | tf_op jit(solution)/shard_map/ppermute | solution.py:177
  518.1 20.7 %collective-permute-start.36 = (bf16[256,2048]{1,0:T(8,128)(2,1)}, bf16[256,2048]{1,0:T(8,128)(2,1)}, u32[]{:S(2)}, u32[]{:S(2)}) collective-permute-start(bf16[256,2048]{1,0:T(8,128)(2,1)} %fusion.170), channel_id=1, source_target_pairs={{0,2},{1,3},{2,0},{3,1},{4,6},{5,7},{6,4},{7,5},{8,10},{9,11},{10,... | collective-permute-start | bytes 3145736 | tf_op jit(solution)/shard_map/ppermute | solution.py:177
  525.6 55.2 %collective-permute-start.30 = (bf16[1024,2048]{1,0:T(8,128)(2,1)}, bf16[1024,2048]{1,0:T(8,128)(2,1)}, u32[]{:S(2)}, u32[]{:S(2)}) collective-permute-start(bf16[1024,2048]{1,0:T(8,128)(2,1)} %pad_maximum_fusion.2), channel_id=1, source_target_pairs={{0,1},{1,0},{2,3},{3,2},{4,5},{5,4},{6,7},{7,6},{8,9},{9,8},{10,11... | collective-permute-start | bytes 12582920 | tf_op jit(solution)/shard_map/ppermute | solution.py:180
  525.7 24.1 %collective-permute-start.35 = (bf16[256,2048]{1,0:T(8,128)(2,1)}, bf16[256,2048]{1,0:T(8,128)(2,1)}, u32[]{:S(2)}, u32[]{:S(2)}) collective-permute-start(bf16[256,2048]{1,0:T(8,128)(2,1)} %fusion.170), channel_id=1, source_target_pairs={{0,1},{1,0},{2,3},{3,2},{4,5},{5,4},{6,7},{7,6},{8,9},{9,8},{10,11... | collective-permute-start | bytes 3145736 | tf_op jit(solution)/shard_map/ppermute | solution.py:180
  548.4 139.4 %collective-permute-start.67 = (bf16[256,1024]{0,1:T(8,128)(2,1)}, bf16[256,1024]{0,1:T(8,128)(2,1)}, u32[]{:S(2)}, u32[]{:S(2)}) collective-permute-start(bf16[256,1024]{0,1:T(8,128)(2,1)} %get-tuple-element.246), channel_id=1, source_target_pairs={{0,4},{4,0},{8,12},{12,8},{16,20},{20,16},{24,28},{28,24},{1,5},{5... | collective-permute-start | bytes 1572872 | tf_op jit(solution)/shard_map/ppermute | solution.py:174
  571.5 26.3 %collective-permute-start.45 = (bf16[4,256,512]{1,2,0:T(8,128)(2,1)}, bf16[4,256,512]{1,2,0:T(8,128)(2,1)}, u32[]{:S(2)}, u32[]{:S(2)}) collective-permute-start(bf16[4,256,512]{1,2,0:T(8,128)(2,1)} %pad_maximum_fusion.19), channel_id=1, source_target_pairs={{0,4},{4,0},{8,12},{12,8},{16,20},{20,16},{24,28},{28,24},{1,5},{5... | collective-permute-start | bytes 3145736 | tf_op jit(solution)/shard_map/ppermute | solution.py:174
  586.6 41.5 %collective-permute-start.40 = (bf16[256,2048]{1,0:T(8,128)(2,1)S(1)}, bf16[256,2048]{1,0:T(8,128)(2,1)S(1)}, u32[]{:S(2)}, u32[]{:S(2)}) collective-permute-start(bf16[256,2048]{1,0:T(8,128)(2,1)S(1)} %pad_maximum_fusion.18), channel_id=1, source_target_pairs={{0,4},{4,0},{8,12},{12,8},{16,20},{20,16},{24,28},{28,24},{1,5},{5... | collective-permute-start | bytes 3145736 | tf_op jit(solution)/shard_map/ppermute | solution.py:174
  588.0 42.7 %collective-permute-start.38 = (bf16[256,2048]{1,0:T(8,128)(2,1)S(1)}, bf16[256,2048]{1,0:T(8,128)(2,1)S(1)}, u32[]{:S(2)}, u32[]{:S(2)}) collective-permute-start(bf16[256,2048]{1,0:T(8,128)(2,1)S(1)} %pad_maximum_fusion.17), channel_id=1, source_target_pairs={{0,2},{1,3},{2,0},{3,1},{4,6},{5,7},{6,4},{7,5},{8,10},{9,11},{10,... | collective-permute-start | bytes 3145736 | tf_op jit(solution)/shard_map/ppermute | solution.py:177
  598.9 18.9 %collective-permute-start.46 = (bf16[256,512]{0,1:T(8,128)(2,1)S(1)}, bf16[256,512]{0,1:T(8,128)(2,1)S(1)}, u32[]{:S(2)}, u32[]{:S(2)}) collective-permute-start(bf16[256,512]{0,1:T(8,128)(2,1)S(1)} %fusion.146), channel_id=1, source_target_pairs={{0,8},{4,12},{8,16},{12,20},{16,24},{20,28},{24,0},{28,4},{1,9},{5... | collective-permute-start | bytes 786440 | tf_op jit(solution)/shard_map/ppermute | solution.py:183
  619.7 34.3 %collective-permute-start.47 = (bf16[256,512]{0,1:T(8,128)(2,1)}, bf16[256,512]{0,1:T(8,128)(2,1)}, u32[]{:S(2)}, u32[]{:S(2)}) collective-permute-start(bf16[256,512]{0,1:T(8,128)(2,1)} %fusion.145), channel_id=1, source_target_pairs={{0,8},{4,12},{8,16},{12,20},{16,24},{20,28},{24,0},{28,4},{1,9},{5... | collective-permute-start | bytes 786440 | tf_op jit(solution)/shard_map/ppermute | solution.py:183
  632.0 15.3 %collective-permute-start.41 = (bf16[128,2048]{1,0:T(8,128)(2,1)}, bf16[128,2048]{1,0:T(8,128)(2,1)S(1)}, u32[]{:S(2)}, u32[]{:S(2)}) collective-permute-start(bf16[128,2048]{1,0:T(8,128)(2,1)} %fusion.119), channel_id=1, source_target_pairs={{0,2},{1,3},{2,0},{3,1},{4,6},{5,7},{6,4},{7,5},{8,10},{9,11},{10,... | collective-permute-start | bytes 1572872 | tf_op jit(solution)/shard_map/ppermute | solution.py:177
  632.7 14.6 %collective-permute-start.39 = (bf16[128,2048]{1,0:T(8,128)(2,1)}, bf16[128,2048]{1,0:T(8,128)(2,1)}, u32[]{:S(2)}, u32[]{:S(2)}) collective-permute-start(bf16[128,2048]{1,0:T(8,128)(2,1)} %fusion.121), channel_id=1, source_target_pairs={{0,4},{4,0},{8,12},{12,8},{16,20},{20,16},{24,28},{28,24},{1,5},{5... | collective-permute-start | bytes 1572872 | tf_op jit(solution)/shard_map/ppermute | solution.py:174
  685.4 46.8 %collective-permute-start.48 = (bf16[512,2048]{1,0:T(8,128)(2,1)}, bf16[512,2048]{1,0:T(8,128)(2,1)}, u32[]{:S(2)}, u32[]{:S(2)}) collective-permute-start(bf16[512,2048]{1,0:T(8,128)(2,1)} %pad_maximum_fusion.8), channel_id=1, source_target_pairs={{0,1},{1,0},{2,3},{3,2},{4,5},{5,4},{6,7},{7,6},{8,9},{9,8},{10,11... | collective-permute-start | bytes 6291464 | tf_op jit(solution)/shard_map/ppermute | solution.py:180
  686.6 12.3 %collective-permute-start.53 = (bf16[256,768]{1,0:T(8,128)(2,1)}, bf16[256,768]{1,0:T(8,128)(2,1)}, u32[]{:S(2)}, u32[]{:S(2)}) collective-permute-start(bf16[256,768]{1,0:T(8,128)(2,1)} %get-tuple-element.217), channel_id=1, source_target_pairs={{0,4},{4,0},{8,12},{12,8},{16,20},{20,16},{24,28},{28,24},{1,5},{5... | collective-permute-start | bytes 1179656 | tf_op jit(solution)/shard_map/ppermute | solution.py:174
  690.8 18.7 %collective-permute-start.55 = (bf16[256,768]{1,0:T(8,128)(2,1)}, bf16[256,768]{1,0:T(8,128)(2,1)}, u32[]{:S(2)}, u32[]{:S(2)}) collective-permute-start(bf16[256,768]{1,0:T(8,128)(2,1)} %get-tuple-element.220), channel_id=1, source_target_pairs={{0,4},{4,0},{8,12},{12,8},{16,20},{20,16},{24,28},{28,24},{1,5},{5... | collective-permute-start | bytes 1179656 | tf_op jit(solution)/shard_map/ppermute | solution.py:174
  700.8 13.5 %collective-permute-start.54 = (bf16[256,768]{1,0:T(8,128)(2,1)}, bf16[256,768]{1,0:T(8,128)(2,1)}, u32[]{:S(2)}, u32[]{:S(2)}) collective-permute-start(bf16[256,768]{1,0:T(8,128)(2,1)} %fusion.134), channel_id=1, source_target_pairs={{0,8},{4,12},{8,16},{12,20},{16,24},{20,28},{24,0},{28,4},{1,9},{5... | collective-permute-start | bytes 1179656 | tf_op jit(solution)/shard_map/ppermute | solution.py:183
  706.3 16.2 %collective-permute-start.63 = (bf16[256,1024]{0,1:T(8,128)(2,1)}, bf16[256,1024]{0,1:T(8,128)(2,1)}, u32[]{:S(2)}, u32[]{:S(2)}) collective-permute-start(bf16[256,1024]{0,1:T(8,128)(2,1)} %get-tuple-element.247), channel_id=1, source_target_pairs={{0,4},{4,0},{8,12},{12,8},{16,20},{20,16},{24,28},{28,24},{1,5},{5... | collective-permute-start | bytes 1572872 | tf_op jit(solution)/shard_map/ppermute | solution.py:174
  708.6 11.8 %collective-permute-start.62 = (bf16[256,512]{0,1:T(8,128)(2,1)}, bf16[256,512]{0,1:T(8,128)(2,1)}, u32[]{:S(2)}, u32[]{:S(2)}) collective-permute-start(bf16[256,512]{0,1:T(8,128)(2,1)} %fusion.143), channel_id=1, source_target_pairs={{0,8},{4,12},{8,16},{12,20},{16,24},{20,28},{24,0},{28,4},{1,9},{5... | collective-permute-start | bytes 786440 | tf_op jit(solution)/shard_map/ppermute | solution.py:183
  709.5 18.2 %collective-permute-start.57 = (bf16[256,768]{1,0:T(8,128)(2,1)}, bf16[256,768]{1,0:T(8,128)(2,1)}, u32[]{:S(2)}, u32[]{:S(2)}) collective-permute-start(bf16[256,768]{1,0:T(8,128)(2,1)} %get-tuple-element.219), channel_id=1, source_target_pairs={{0,4},{4,0},{8,12},{12,8},{16,20},{20,16},{24,28},{28,24},{1,5},{5... | collective-permute-start | bytes 1179656 | tf_op jit(solution)/shard_map/ppermute | solution.py:174
  716.4 11.9 %collective-permute-start.56 = (bf16[256,768]{1,0:T(8,128)(2,1)}, bf16[256,768]{1,0:T(8,128)(2,1)}, u32[]{:S(2)}, u32[]{:S(2)}) collective-permute-start(bf16[256,768]{1,0:T(8,128)(2,1)} %fusion.133), channel_id=1, source_target_pairs={{0,8},{4,12},{8,16},{12,20},{16,24},{20,28},{24,0},{28,4},{1,9},{5... | collective-permute-start | bytes 1179656 | tf_op jit(solution)/shard_map/ppermute | solution.py:183
  723.6 26.5 %collective-permute-start.42 = (bf16[256,2048]{1,0:T(8,128)(2,1)}, bf16[256,2048]{1,0:T(8,128)(2,1)}, u32[]{:S(2)}, u32[]{:S(2)}) collective-permute-start(bf16[256,2048]{1,0:T(8,128)(2,1)} %get-tuple-element.186), channel_id=1, source_target_pairs={{0,1},{1,0},{2,3},{3,2},{4,5},{5,4},{6,7},{7,6},{8,9},{9,8},{10,11... | collective-permute-start | bytes 3145736 | tf_op jit(solution)/shard_map/ppermute | solution.py:180
  723.7 26.4 %collective-permute-start.43 = (bf16[256,2048]{1,0:T(8,128)(2,1)}, bf16[256,2048]{1,0:T(8,128)(2,1)}, u32[]{:S(2)}, u32[]{:S(2)}) collective-permute-start(bf16[256,2048]{1,0:T(8,128)(2,1)} %get-tuple-element.186), channel_id=1, source_target_pairs={{0,2},{1,3},{2,0},{3,1},{4,6},{5,7},{6,4},{7,5},{8,10},{9,11},{10,... | collective-permute-start | bytes 3145736 | tf_op jit(solution)/shard_map/ppermute | solution.py:177
  727.7 24.7 %collective-permute-start.59 = (bf16[256,768]{1,0:T(8,128)(2,1)}, bf16[256,768]{1,0:T(8,128)(2,1)}, u32[]{:S(2)}, u32[]{:S(2)}) collective-permute-start(bf16[256,768]{1,0:T(8,128)(2,1)} %get-tuple-element.218), channel_id=1, source_target_pairs={{0,4},{4,0},{8,12},{12,8},{16,20},{20,16},{24,28},{28,24},{1,5},{5... | collective-permute-start | bytes 1179656 | tf_op jit(solution)/shard_map/ppermute | solution.py:174
  730.4 22.1 %collective-permute-start.58 = (bf16[256,768]{1,0:T(8,128)(2,1)}, bf16[256,768]{1,0:T(8,128)(2,1)}, u32[]{:S(2)}, u32[]{:S(2)}) collective-permute-start(bf16[256,768]{1,0:T(8,128)(2,1)} %fusion.131), channel_id=1, source_target_pairs={{0,8},{4,12},{8,16},{12,20},{16,24},{20,28},{24,0},{28,4},{1,9},{5... | collective-permute-start | bytes 1179656 | tf_op jit(solution)/shard_map/ppermute | solution.py:183
  735.1 37.0 %collective-permute-start.49 = (bf16[256,2048]{1,0:T(8,128)(2,1)}, bf16[256,2048]{1,0:T(8,128)(2,1)}, u32[]{:S(2)}, u32[]{:S(2)}) collective-permute-start(bf16[256,2048]{1,0:T(8,128)(2,1)} %add_convert_fusion.1), channel_id=1, source_target_pairs={{0,2},{1,3},{2,0},{3,1},{4,6},{5,7},{6,4},{7,5},{8,10},{9,11},{10,... | collective-permute-start | bytes 3145736 | tf_op jit(solution)/shard_map/ppermute | solution.py:177
  750.1 57.9 %collective-permute-start.44 = (bf16[256,2048]{1,0:T(8,128)(2,1)}, bf16[256,2048]{1,0:T(8,128)(2,1)}, u32[]{:S(2)}, u32[]{:S(2)}) collective-permute-start(bf16[256,2048]{1,0:T(8,128)(2,1)} %collective-permute-done.43), channel_id=1, source_target_pairs={{0,1},{1,0},{2,3},{3,2},{4,5},{5,4},{6,7},{7,6},{8,9},{9,8},{10,11... | collective-permute-start | bytes 3145736 | tf_op jit(solution)/shard_map/ppermute | solution.py:180
  755.4 31.9 %collective-permute-start.60 = (f32[256]{0:T(256)}, f32[256]{0:T(256)S(1)}, u32[]{:S(2)}, u32[]{:S(2)}) collective-permute-start(f32[256]{0:T(256)} %get-tuple-element.216), channel_id=1, source_target_pairs={{0,1},{1,0},{2,3},{3,2},{4,5},{5,4},{6,7},{7,6},{8,9},{9,8},{10,11... | collective-permute-start | bytes 3080 | tf_op jit(solution)/shard_map/ppermute | solution.py:180
  757.3 31.2 %collective-permute-start.64 = (bf16[256,1024]{0,1:T(8,128)(2,1)S(1)}, bf16[256,1024]{0,1:T(8,128)(2,1)S(1)}, u32[]{:S(2)}, u32[]{:S(2)}) collective-permute-start(bf16[256,1024]{0,1:T(8,128)(2,1)S(1)} %get-tuple-element.249), channel_id=1, source_target_pairs={{0,4},{4,0},{8,12},{12,8},{16,20},{20,16},{24,28},{28,24},{1,5},{5... | collective-permute-start | bytes 1572872 | tf_op jit(solution)/shard_map/ppermute | solution.py:174
  781.0 31.7 %collective-permute-start.50 = (bf16[256,2048]{1,0:T(8,128)(2,1)}, bf16[256,2048]{1,0:T(8,128)(2,1)S(1)}, u32[]{:S(2)}, u32[]{:S(2)}) collective-permute-start(bf16[256,2048]{1,0:T(8,128)(2,1)} %get-tuple-element.184), channel_id=1, source_target_pairs={{0,1},{1,0},{2,3},{3,2},{4,5},{5,4},{6,7},{7,6},{8,9},{9,8},{10,11... | collective-permute-start | bytes 3145736 | tf_op jit(solution)/shard_map/ppermute | solution.py:180
  781.1 31.7 %collective-permute-start.51 = (bf16[256,2048]{1,0:T(8,128)(2,1)}, bf16[256,2048]{1,0:T(8,128)(2,1)}, u32[]{:S(2)}, u32[]{:S(2)}) collective-permute-start(bf16[256,2048]{1,0:T(8,128)(2,1)} %get-tuple-element.184), channel_id=1, source_target_pairs={{0,2},{1,3},{2,0},{3,1},{4,6},{5,7},{6,4},{7,5},{8,10},{9,11},{10,... | collective-permute-start | bytes 3145736 | tf_op jit(solution)/shard_map/ppermute | solution.py:177
  788.0 19.0 %collective-permute-start.61 = (f32[256]{0:T(256)S(1)}, f32[256]{0:T(256)S(1)}, u32[]{:S(2)}, u32[]{:S(2)}) collective-permute-start(f32[256]{0:T(256)S(1)} %add.687), channel_id=1, source_target_pairs={{0,2},{1,3},{2,0},{3,1},{4,6},{5,7},{6,4},{7,5},{8,10},{9,11},{10,... | collective-permute-start | bytes 3080 | tf_op jit(solution)/shard_map/ppermute | solution.py:177
  789.5 18.1 %collective-permute-start.65 = (f32[256]{0:T(256)S(1)}, f32[256]{0:T(256)S(1)}, u32[]{:S(2)}, u32[]{:S(2)}) collective-permute-start(f32[256]{0:T(256)S(1)} %get-tuple-element.222), channel_id=1, source_target_pairs={{0,1},{1,0},{2,3},{3,2},{4,5},{5,4},{6,7},{7,6},{8,9},{9,8},{10,11... | collective-permute-start | bytes 3080 | tf_op jit(solution)/shard_map/ppermute | solution.py:180
  (138 other events, 1218.4 us)
Sparse Core Ops, SparseCore 0:
  71.8 151.3 all-gather.2
  237.5 92.5 all-gather.4
  429.5 97.3 reduce-scatter.2
  549.9 93.2 reduce-scatter.4

commit v4 on v2

v4 whole, which is shorter than its diff:
```python
from functools import partial
import math

import jax
import jax.numpy as jnp
from jax import lax
from jax.sharding import PartitionSpec as P

HD = 64
GROUP = 4
epsilon = 1e-05
BF = jnp.bfloat16
F32 = jnp.float32


def rope_tables(segment_row, head_size):
    length = segment_row.shape[0]
    places = jnp.arange(length, dtype=jnp.int32)
    boundary = jnp.concatenate([jnp.ones((1,), dtype=bool), segment_row[1:] != segment_row[:-1]])
    starts = lax.cummax(jnp.where(boundary, places, 0), axis=0)
    position = (places - starts).astype(jnp.float32)
    half_size = head_size // 2
    exponent = jnp.arange(half_size, dtype=jnp.float32) * 2.0 / head_size
    inverse = 1.0 / 500000.0**exponent
    wavelen = 2.0 * math.pi / inverse
    smooth = (8192.0 / wavelen - 1.0) / 3.0
    scaled = jnp.where(
        wavelen < 2048.0,
        inverse,
        jnp.where(
            wavelen > 8192.0, inverse / 32.0, (1.0 - smooth) * inverse / 32.0 + smooth * inverse
        ),
    )
    angles = position[:, None] * scaled[None, :]
    cosine_table = jnp.cos(angles)
    sine_table = jnp.sin(angles)
    return (
        jnp.concatenate([cosine_table, cosine_table], axis=-1),
        jnp.concatenate([sine_table, sine_table], axis=-1),
    )


def rotate(values, cosine_table, sine_table):
    half_size = values.shape[-1] // 2
    turned = jnp.concatenate([-values[..., half_size:], values[..., :half_size]], axis=-1)
    return values * cosine_table + turned * sine_table


def dot_rows(left, right, out=F32):
    return lax.dot_general(
        left, right, (((0,), (0,)), ((), ())), preferred_element_type=F32
    ).astype(out)


def dot_cols(left, right, out=F32):
    return lax.dot_general(
        left, right, (((1,), (1,)), ((), ())), preferred_element_type=F32
    ).astype(out)


def dot(left, right, out=F32):
    return jnp.dot(left, right, preferred_element_type=F32).astype(out)


def tie(value, *others):
    return lax.optimization_barrier((value, *others))[0]


def inverse_root(values):
    return lax.rsqrt(jnp.mean(values * values, axis=-1, keepdims=True) + epsilon)


def spans(length):
    rows = length // 4
    most = length // 2
    for start in range(0, length, rows):
        first = max(0, start - most + 1) // rows * rows
        yield start, rows, first, start + rows


def block_scores(query_block, key_block, segment_row, start, first):
    rows, keys = query_block.shape[0], key_block.shape[0]
    scores = jnp.einsum("qkgd,skd->kgqs", query_block, key_block, preferred_element_type=F32)
    row_ids = start + jnp.arange(rows, dtype=jnp.int32)
    col_ids = first + jnp.arange(keys, dtype=jnp.int32)
    same_doc = segment_row[start : start + rows][:, None] == segment_row[first : first + keys][None, :]
    allowed = same_doc & (col_ids[None, :] <= row_ids[:, None])
    return jnp.where(allowed, scores, -1000000000.0)


def attend_forward(query_seq, key_seq, value_seq, segment_row):
    length, kv_local, head_size = key_seq.shape
    grouped = query_seq.reshape(length, kv_local, -1, head_size)
    mixed_parts = []
    total_parts = []
    for start, rows, first, last in spans(length):
        query_block = grouped[start : start + rows]
        scores = block_scores(query_block, key_seq[first:last], segment_row, start, first)
        row_max = jnp.max(scores, axis=-1, keepdims=True)
        log_total = jnp.log(jnp.sum(jnp.exp(scores - row_max), axis=-1, keepdims=True)) + row_max
        soft_low = jnp.exp(scores - log_total).astype(BF)
        mixed_block = jnp.einsum(
            "kgqs,skd->qkgd", soft_low, value_seq[first:last], preferred_element_type=F32
        )
        mixed_parts.append(mixed_block.reshape(rows, -1).astype(BF))
        total_parts.append(log_total)
    return (jnp.concatenate(mixed_parts, axis=0), total_parts)


def block_backward(query_block, key_block, value_block, log_total, grad_block, segment_row, start, first):
    scores = block_scores(query_block, key_block, segment_row, start, first)
    soft_weights = jnp.exp(scores - log_total)
    soft_grad = jnp.einsum("qkgd,skd->kgqs", grad_block, value_block, preferred_element_type=F32)
    score_grad = (
        soft_weights * (soft_grad - jnp.sum(soft_weights * soft_grad, axis=-1, keepdims=True))
    ).astype(BF)
    query_part = jnp.einsum("kgqs,skd->qkgd", score_grad, key_block, preferred_element_type=F32)
    key_part = jnp.einsum("kgqs,qkgd->skd", score_grad, query_block, preferred_element_type=F32)
    value_part = jnp.einsum(
        "kgqs,qkgd->skd", soft_weights.astype(BF), grad_block, preferred_element_type=F32
    )
    return query_part * query_block.shape[-1] ** (-0.5), key_part, value_part


def shards(
    dp_size,
    tensor_size,
    tokens,
    segment_ids,
    attn_gain,
    query_weight,
    key_weight,
    value_weight,
    output_weight,
    ffn_gain,
    gate_weight,
    up_weight,
    down_weight,
    cotangent,
):
    groups = dp_size // 2
    dp_index = lax.axis_index("dp")
    z_index, y_index = dp_index // 2, dp_index % 2
    t_index = lax.axis_index("tensor")
    token_count, width = tokens.shape
    rows = query_weight.shape[0]
    quarter = token_count // tensor_size
    half_quarter = quarter // 2

    def swap_y(value):
        return lax.ppermute(value, "dp", [(i, i ^ 1) for i in range(dp_size)])

    def swap_x(value):
        return lax.ppermute(value, "tensor", [(i, i ^ 2) for i in range(tensor_size)])

    def swap_core(value):
        return lax.ppermute(value, "tensor", [(i, i ^ 1) for i in range(tensor_size)])

    def hop(value):
        return lax.ppermute(value, "dp", [(i, (i + 2) % dp_size) for i in range(dp_size)])

    def my_half(value, axis, mine):
        size = value.shape[axis] // 2
        which = y_index if mine else 1 - y_index
        return lax.dynamic_slice_in_dim(value, which * size, size, axis)

    def relative(value):
        return jnp.concatenate(
            [
                lax.dynamic_slice_in_dim(value, (t_index ^ j) * quarter, quarter, 0)
                for j in range(tensor_size)
            ],
            axis=0,
        )

    def absolute(pieces, dtype):
        whole = jnp.zeros((quarter * tensor_size, pieces[0].shape[1]), dtype)
        for j, piece in enumerate(pieces):
            whole = lax.dynamic_update_slice(
                whole, piece.astype(dtype), ((t_index ^ j) * quarter, 0)
            )
        return whole

    z_groups = [[i for i in range(dp_size) if i % 2 == side] for side in range(2)]

    def gather_z(value):
        return lax.all_gather(value, "dp", axis_index_groups=z_groups, axis=0, tiled=True)

    def scatter_z(value):
        return lax.psum_scatter(
            value, "dp", axis_index_groups=z_groups, scatter_dimension=0, tiled=True
        )

    def by_y(mine, got, axis):
        return jnp.where(
            y_index == 0,
            jnp.concatenate([mine, got], axis=axis),
            jnp.concatenate([got, mine], axis=axis),
        )

    def pair_rows(mine, got):
        size = mine.shape[0]
        whole = jnp.zeros((2 * size, mine.shape[1]), BF)
        whole = lax.dynamic_update_slice(whole, mine, (y_index * size, 0))
        return lax.dynamic_update_slice(whole, got, ((1 - y_index) * size, 0))

    def interleave(mine, other):
        mine = mine.reshape(groups, 1, rows, -1)
        other = other.reshape(groups, 1, rows, -1)
        return by_y(mine, other, 1).reshape(2 * groups * rows, -1)

    attn_scale = attn_gain.astype(F32)[:, None]
    ffn_scale = ffn_gain.astype(F32)[:, None]

    def scaled(weight, scale):
        return (weight.astype(F32) * scale).astype(BF)

    q_cols, kv_cols = query_weight.shape[1], key_weight.shape[1]
    qkv_cols = q_cols + 2 * kv_cols
    hidden_units = gate_weight.shape[1] // 2
    first_units = hidden_units * 3 // 8
    part_units = (first_units, hidden_units - first_units)
    trio = (scaled(gate_weight, ffn_scale), scaled(up_weight, ffn_scale), down_weight.T)

    def trio_part(side, part):
        start = side * hidden_units + part * first_units
        return jnp.concatenate(
            [lax.dynamic_slice_in_dim(weight, start, part_units[part], 1) for weight in trio], axis=1
        )

    attn_local = jnp.concatenate(
        [
            scaled(jnp.concatenate([query_weight, key_weight, value_weight], axis=1), attn_scale),
            output_weight.T,
        ],
        axis=1,
    )
    attn_z = gather_z(attn_local)
    send_a = tie(trio_part(1 - y_index, 0), attn_local)
    got_a = swap_y(send_a)
    got_b = swap_y(tie(trio_part(1 - y_index, 1), got_a))
    pair_a = pair_rows(trio_part(y_index, 0), got_a)
    pair_b = pair_rows(trio_part(y_index, 1), got_b)
    full_a = gather_z(tie(pair_a, attn_local))
    full_b = gather_z(tie(pair_b, pair_a))
    qkv_z, out_z = attn_z[:, :qkv_cols], attn_z[:, qkv_cols:]
    qkv_other = swap_y(tie(qkv_z, pair_b))
    out_other = swap_y(tie(out_z, qkv_other))
    qkv_full = interleave(qkv_z, qkv_other)
    out_full = interleave(out_z, out_other)

    tokens_float = tokens.astype(F32)
    token_root = inverse_root(tokens_float)
    normed = (tokens_float * token_root).astype(BF)
    qkv_raw = dot(normed, qkv_full)
    segment_row = segment_ids[0]
    cosine_table, sine_table = rope_tables(segment_row, HD)
    cosine_wide, sine_wide = cosine_table[:, None, :], sine_table[:, None, :]
    query_raw = qkv_raw[:, :q_cols].reshape(token_count, -1, HD)
    key_raw = qkv_raw[:, q_cols : q_cols + kv_cols].reshape(token_count, -1, HD)
    value_seq = qkv_raw[:, q_cols + kv_cols :].astype(BF).reshape(token_count, -1, HD)
    query_low = (rotate(query_raw, cosine_wide, sine_wide) * HD ** (-0.5)).astype(BF)
    key_low = rotate(key_raw, cosine_wide, sine_wide).astype(BF)
    mixed, log_total = attend_forward(query_low, key_low, value_seq, segment_row)
    mixed_rel = relative(mixed)
    attn_part = dot_cols(mixed_rel, out_full, BF)

    def two_way(first, second):
        return first.astype(F32) + second.astype(F32)

    def scatter_tensor(part):
        send = jnp.concatenate([part[quarter : 2 * quarter], part[3 * quarter :]], axis=0)
        got = swap_core(send)
        keep = two_way(part[:quarter], got[:quarter])
        pass_on = two_way(part[2 * quarter : 3 * quarter], got[quarter:]).astype(BF)
        return keep + swap_x(pass_on).astype(F32)

    def gather_tensor(piece):
        from_core = swap_core(piece)
        from_x = swap_x(piece)
        from_both = swap_core(from_x)
        return [piece, from_core, from_x, from_both]

    def my_quarter(value):
        return lax.dynamic_slice_in_dim(value, t_index * quarter, quarter, 0)

    tokens_quarter = my_quarter(tokens).astype(F32)
    hidden = tokens_quarter + scatter_tensor(attn_part)
    hidden_root = inverse_root(hidden)
    n_two = (hidden * hidden_root).astype(BF)

    first, second = n_two[:half_quarter], n_two[half_quarter:]
    top = jnp.concatenate([first, swap_x(first)], axis=0)
    low = jnp.concatenate([second, swap_y(second)], axis=0)
    top, low = lax.optimization_barrier((top, low))
    n_held = jnp.concatenate([top, swap_y(top), low, swap_x(low)], axis=0)
    n_held = tie(n_held, full_a)
    n_all = jnp.concatenate([n_held, swap_core(n_held)], axis=0)

    def quarter_of(value, other):
        return lax.dynamic_slice_in_dim(value, (t_index ^ other) * quarter, quarter, 0)

    cot_own, cot_x = quarter_of(cotangent, 0), quarter_of(cotangent, 2)
    cot_y = swap_y(tie(cot_own, n_held))
    cot_yx = swap_x(cot_y)
    cot_held = jnp.concatenate(
        [v[:half_quarter] for v in (cot_own, cot_x, cot_y, cot_yx)]
        + [v[half_quarter:] for v in (cot_own, cot_y, cot_x, cot_yx)],
        axis=0,
    )
    cot_all = jnp.concatenate([cot_held, swap_core(cot_held)], axis=0)

    side_rows = 4 * quarter

    def pair_sends(part, got):
        def kept(start):
            return two_way(part[start : start + quarter], got[start : start + quarter])

        keeps = (kept(0), kept(2 * quarter))
        return keeps, (kept(quarter).astype(BF), kept(3 * quarter).astype(BF))

    def pair_pass(keeps, sends):
        top_sum = keeps[0] + swap_y(sends[0]).astype(F32)
        low_sum = keeps[1] + swap_x(sends[1]).astype(F32)
        passes = (top_sum[half_quarter:].astype(BF), low_sum[half_quarter:].astype(BF))
        return (top_sum[:half_quarter], low_sum[:half_quarter]), passes

    def pair_sum(keeps, passes):
        return jnp.concatenate(
            [keeps[0] + swap_x(passes[0]).astype(F32), keeps[1] + swap_y(passes[1]).astype(F32)],
            axis=0,
        )

    def units(full, rows_all):
        count = full.shape[1] // 3
        gu = dot(rows_all, full[:, : 2 * count], BF)
        gate_values = gu[:, :count].astype(F32)
        up_values = gu[:, count:].astype(F32)
        sig = jax.nn.sigmoid(gate_values)
        silu = gate_values * sig
        return gate_values, up_values, sig, silu, (silu * up_values).astype(BF)

    def units_grad(full, parts, cot_rows):
        gate_values, up_values, sig, silu, _ = parts
        active_grad = dot(cot_rows, full[:, full.shape[1] // 3 * 2 :])
        gate_grad = active_grad * up_values * (sig * (1.0 + gate_values * (1.0 - sig)))
        return jnp.concatenate([gate_grad.astype(BF), (active_grad * silu).astype(BF)], axis=1)

    parts_a = units(full_a, n_all)
    active_a = parts_a[-1]
    down_grad_a = dot_rows(cot_all, active_a, BF)
    down_block_a = scatter_z(down_grad_a)
    gu_grad_a = units_grad(full_a, parts_a, tie(cot_all, down_grad_a))
    gu_weight_grad_a = dot_rows(n_all, gu_grad_a, BF)
    gu_block_a = scatter_z(gu_weight_grad_a)
    gu_a, gu_b = (v[:, : 2 * n] for v, n in zip((full_a, full_b), part_units))
    down_a, down_b = (v[:, 2 * n :] for v, n in zip((full_a, full_b), part_units))
    e_part_a = dot_cols(tie(gu_grad_a, gu_weight_grad_a), gu_a, BF)
    ffn_part_a = dot_cols(tie(active_a, e_part_a), down_a, BF)

    parts_b = units(full_b, tie(n_all, ffn_part_a))
    active_b = parts_b[-1]
    gu_grad_b = units_grad(full_b, parts_b, cot_all)
    own, other = slice(0, side_rows), slice(side_rows, 2 * side_rows)
    e_cross = (dot_cols(gu_grad_b[other], gu_b) + e_part_a[other].astype(F32)).astype(BF)
    e_got = swap_core(e_cross)
    e_part = dot_cols(tie(gu_grad_b, e_cross)[own], gu_b) + e_part_a[own].astype(F32)
    e_part = e_part.astype(BF)
    down_grad_b = dot_rows(cot_all, tie(active_b, e_part, down_block_a), BF)
    down_block_b = scatter_z(down_grad_b)
    e_keeps, e_sends = pair_sends(tie(e_part, e_cross), e_got)
    gu_weight_grad_b = dot_rows(n_all, tie(gu_grad_b, down_grad_b, *e_sends), BF)
    gu_block_b = scatter_z(gu_weight_grad_b)
    ffn_cross = dot_cols(tie(active_b, gu_weight_grad_b)[other], down_b)
    ffn_cross = (ffn_cross + ffn_part_a[other].astype(F32)).astype(BF)
    ffn_got = swap_core(ffn_cross)
    e_keeps, e_passes = pair_pass(tuple(tie(v, ffn_cross) for v in e_keeps), e_sends)
    ffn_part = dot_cols(tie(active_b, *e_passes)[own], down_b)
    ffn_part = (ffn_part + ffn_part_a[own].astype(F32)).astype(BF)
    e_two = pair_sum(tuple(tie(v, ffn_part) for v in e_keeps), e_passes)
    n_hidden = hidden * hidden_root
    cot_quarter = my_quarter(cotangent).astype(F32)
    hidden_grad = cot_quarter + hidden_root * (
        e_two - n_hidden * jnp.mean(e_two * n_hidden, axis=-1, keepdims=True)
    )
    hidden_low = jnp.concatenate(gather_tensor(hidden_grad.astype(BF)), axis=0)

    ffn_keeps, ffn_sends = pair_sends(ffn_part, ffn_got)
    ffn_sends = tuple(tie(v, hidden_low) for v in ffn_sends)
    ffn_keeps, ffn_passes = pair_pass(ffn_keeps, ffn_sends)
    layer_quarter = (hidden + pair_sum(ffn_keeps, ffn_passes)).astype(BF)
    layer_output = absolute(gather_tensor(layer_quarter), BF)

    def ring_step(received, block, step):
        return hop((received.astype(F32) + block(step + 1)).astype(BF))

    def ring_end(received, block):
        return received.astype(F32) + block(groups)

    mixed_grad_rel = dot(hidden_low, out_full, BF)
    out_weight_grad = dot_rows(hidden_low, tie(mixed_rel, mixed_grad_rel), BF)
    cut = out_weight_grad.reshape(groups, 2, rows, -1)
    out_mine = lax.dynamic_index_in_dim(cut, y_index, 1, keepdims=False)
    out_sent = swap_y(lax.dynamic_index_in_dim(cut, 1 - y_index, 1, keepdims=False))
    out_both = two_way(out_mine, out_sent).astype(BF).reshape(groups * rows, -1)
    out_block = scatter_z(out_both)
    out_grad = out_block.astype(F32).T
    mixed_grad = absolute(
        [mixed_grad_rel[j * quarter : (j + 1) * quarter] for j in range(tensor_size)], BF
    )
    gates = (
        ffn_sends + (out_weight_grad,),
        (gu_block_a,),
        ffn_passes + (out_both,),
        (layer_quarter, down_block_b),
    )
    grouped = query_low.reshape(token_count, -1, GROUP, HD)
    grad_grouped = mixed_grad.reshape(token_count, -1, GROUP, HD)
    key_grad = jnp.zeros(key_low.shape, F32)
    value_grad = jnp.zeros(value_seq.shape, F32)
    core_index, half_rows = t_index % 2, token_count // 2
    qkv_grad_parts, e_one_parts, query_parts = [], [], []
    for number, ((start, size, first_key, last), log_part, gate) in enumerate(
        zip(reversed(list(spans(token_count))), reversed(log_total), gates)
    ):
        grad_block = tie(grad_grouped[start : start + size], *gate)
        if number == 2:
            grad_block = tie(grad_block, e_one_parts[0])
        query_part, key_part, value_part = block_backward(
            grouped[start : start + size],
            key_low[first_key:last],
            value_seq[first_key:last],
            log_part,
            grad_block,
            segment_row,
            start,
            first_key,
        )
        key_grad = key_grad.at[first_key:last].add(key_part)
        value_grad = value_grad.at[first_key:last].add(value_part)
        query_parts.insert(0, query_part)
        if number % 2 == 1:
            span = slice(start, start + half_rows)
            cosine_span, sine_span = cosine_wide[span], -sine_wide[span]
            query_grad = jnp.concatenate(query_parts, axis=0).reshape(half_rows, -1, HD)
            qkv_grad_part = jnp.concatenate(
                [
                    rotate(query_grad, cosine_span, sine_span).reshape(half_rows, -1),
                    rotate(key_grad[span], cosine_span, sine_span).reshape(half_rows, -1),
                    value_grad[span].reshape(half_rows, -1),
                ],
                axis=1,
            ).astype(BF)
            query_parts = []
            qkv_grad_parts.insert(0, qkv_grad_part)
            if number == 1:
                e_one_parts.append(dot_cols(qkv_grad_part, qkv_full, BF))
    qkv_weight_grad = dot_rows(normed, jnp.concatenate(qkv_grad_parts, axis=0), BF)
    e_one_parts.append(dot_cols(tie(qkv_grad_parts[0], qkv_weight_grad), qkv_full, BF))

    def tokens_rows(part, start):
        size = part.shape[0] // 2

        def mine(value, base):
            return lax.dynamic_slice_in_dim(value, base + core_index * size, size, 0)

        got = swap_core(lax.dynamic_slice_in_dim(part, (1 - core_index) * size, size, 0))
        chip_sum = two_way(mine(part, 0), got).astype(BF)
        e_one = two_way(chip_sum, swap_x(chip_sum))
        grad_rows = lax.dynamic_slice_in_dim(
            hidden_low, (t_index ^ (start // quarter + core_index)) * quarter, size, 0
        ).astype(F32)
        root = mine(token_root, start)
        n_one = mine(tokens, start).astype(F32) * root
        own = grad_rows + root * (e_one - n_one * jnp.mean(e_one * n_one, axis=-1, keepdims=True))
        own = own.astype(BF)
        other = swap_core(own)
        return jnp.where(
            core_index == 0,
            jnp.concatenate([own, other], axis=0),
            jnp.concatenate([other, own], axis=0),
        ).astype(F32)

    tokens_grad = jnp.concatenate(
        [tokens_rows(e_one_parts[1], 0), tokens_rows(e_one_parts[0], half_rows)], axis=0
    )

    qkv_cut = qkv_weight_grad.reshape(groups, 2, rows, -1)

    def qkv_pick(side):
        def pick(back):
            start = ((z_index - back) % groups, side, 0, 0)
            return lax.dynamic_slice(qkv_cut, start, (1, 1, rows, qkv_cols))[0, 0]

        return pick

    qkv_mine, qkv_other_y = qkv_pick(y_index), qkv_pick(1 - y_index)
    qkv_sent = [swap_y(qkv_other_y(back)) for back in range(1, groups + 1)]

    def qkv_part(back):
        return two_way(qkv_mine(back), qkv_sent[back - 1])

    qkv_run = hop(qkv_part(1).astype(BF))
    for step in range(1, groups - 1):
        qkv_run = ring_step(qkv_run, qkv_part, step)
    qkv_block = ring_end(qkv_run, qkv_part)

    def trade(block):
        mine = my_half(block, 0, True)
        return mine, swap_y(my_half(block, 0, False))

    traded = [
        [trade(tie(block, last)) for block, last in zip(pair, (layer_quarter, qkv_weight_grad))]
        for pair in ((gu_block_a, gu_block_b), (down_block_a, down_block_b))
    ]

    def all_units(pairs, place):
        def side(which):
            return jnp.concatenate(
                [pair[which][:, place * n : (place + 1) * n] for pair, n in zip(pairs, part_units)],
                axis=1,
            )

        return by_y(side(0), side(1), 1).astype(F32)

    gate_g, up_g = all_units(traded[0], 0), all_units(traded[0], 1)
    down_weight_grad = all_units(traded[1], 0).T

    attn_gain_part = jnp.sum(
        qkv_block * jnp.concatenate([query_weight, key_weight, value_weight], axis=1).astype(F32),
        axis=1,
    )
    ffn_gain_part = jnp.sum(
        gate_g * gate_weight.astype(F32) + up_g * up_weight.astype(F32), axis=1
    )

    def sum_tensor(value):
        value = value + swap_core(value)
        return value + swap_x(value)

    attn_gain_grad, ffn_gain_grad = sum_tensor(jnp.stack([attn_gain_part, ffn_gain_part]))
    qkv_out = qkv_block * attn_scale
    return (
        layer_output,
        tokens_grad,
        attn_gain_grad,
        qkv_out[:, :q_cols],
        qkv_out[:, q_cols : q_cols + kv_cols],
        qkv_out[:, q_cols + kv_cols :],
        out_grad,
        ffn_gain_grad,
        gate_g * ffn_scale,
        up_g * ffn_scale,
        down_weight_grad,
    )


def solution(mesh):
    return jax.shard_map(
        partial(shards, mesh.shape["dp"], mesh.shape["tensor"]),
        mesh=mesh,
        in_specs=(
            P("dp", None),
            P("dp", None),
            P("dp"),
            P("dp", "tensor"),
            P("dp", "tensor"),
            P("dp", "tensor"),
            P("tensor", "dp"),
            P("dp"),
            P("dp", "tensor"),
            P("dp", "tensor"),
            P("tensor", "dp"),
            P("dp", None),
        ),
        out_specs=(
            P("dp", None),
            P("dp", None),
            P("dp"),
            P("dp", "tensor"),
            P("dp", "tensor"),
            P("dp", "tensor"),
            P("tensor", "dp"),
            P("dp"),
            P("dp", "tensor"),
            P("dp", "tensor"),
            P("tensor", "dp"),
        ),
        check_vma=False,
    )
```

time: 853 us -> 756 us (0.89)
  waiting for transfers between devices: 411 us -> 302 us
  matrix products: 183 us -> 208 us
  local copies, waits for them, and re-layouts: 86.4 us -> 75.4 us
    all_gather x2 -> x3, waiting for transfers between devices: 83.6 us -> 11.1 us  [gather_z(): lax.all_gather(value, 'dp', axis_index_groups=z_groups, axis=0, tiled=True)]
    ppermute x6 -> x3, waiting for transfers between devices: 31.1 us -> 0.98 us  [hop(): lax.ppermute(value, 'dp', [(i, (i + 2) % dp_size) for i in range(dp_size)])]
    unnamed x313 -> x298, local copies, waits for them, and re-layouts: 51.8 us -> 35.1 us
    dot_general x4 -> x9, matrix products: 45.8 us -> 60.1 us  [dot_cols(): lax.dot_general(left, right, (((1,), (1,)), ((), ())), preferred_element_...]
    ppermute x21 -> x20, waiting for transfers between devices: 182 us -> 195 us  [swap_y(): return lax.ppermute(value, 'dp', [(i, i ^ 1) for i in range(dp_size)])]
    concatenate x12 -> x15, other arithmetic: 6.17 us -> 18 us  [the longest x1 4.28 us: shards(): jnp.concatenate([tokens_rows(e_one_parts[1], 0), tokens_rows(e_one_parts[...]
    ppermute x14 -> x13, waiting for transfers between devices: 99.9 us -> 88.8 us  [swap_x(): lax.ppermute(value, 'tensor', [(i, i ^ 2) for i in range(tensor_size)])]
    add x2 -> x8, other arithmetic: 1.11 us -> 12.1 us  [the longest x2 7.4 us: pair_pass(): top_sum = keeps[0] + swap_y(sends[0]).astype(F32)]
  transfers between devices with their start and end apart: 61 -> 58, of which waited for: 33 -> 29; matrix products, arithmetic and copies ran while one was open for 34% -> 48% of each run, Pallas kernels for 0% -> 0%
where the time goes in v4:
time: 756 us; the launch traced here: 750 us
  waiting for transfers between devices  302 us (40%)
  matrix products  208 us (28%)
  other arithmetic  103 us (14%)
  local copies, waits for them, and re-layouts  75.4 us (10%)
  starting transfers between devices  45.1 us (6%)
  between operations  17 us (2%)
    ppermute x20, waiting for transfers between devices, swap_y(): return lax.ppermute(value, 'dp', [(i, i ^ 1) for i in range(dp_size)])  195 us
    ppermute x13, waiting for transfers between devices, swap_x(): lax.ppermute(value, 'tensor', [(i, i ^ 2) for i in range(tensor_size)])  88.8 us
    dot_general x9, matrix products, dot_cols(): lax.dot_general(left, right, (((1,), (1,)), ((), ())), preferred_element_...  60.1 us
    dot_general x6, matrix products, dot(): return jnp.dot(left, right, preferred_element_type=F32).astype(out)  57.7 us
    dot_general x6, matrix products, dot_rows(): lax.dot_general(left, right, (((0,), (0,)), ((), ())), preferred_element_...  56.2 us
    unnamed x298, local copies, waits for them, and re-layouts  35.1 us
    ppermute x20, starting transfers between devices, swap_y(): return lax.ppermute(value, 'dp', [(i, i ^ 1) for i in range(dp_size)])  27.5 us
    ppermute x13, starting transfers between devices, swap_x(): lax.ppermute(value, 'tensor', [(i, i ^ 2) for i in range(tensor_size)])  15.3 us
  transfers between devices with their start and end apart: 58, of which 29 were waited for; matrix products, arithmetic and copies ran while one was open for 48% of the time, Pallas kernels for 0%

profile of v4, /device:TPU:0, one launch (start us, length us, event | category | flops | bytes accessed | tf_op | source)
XLA Modules:
  0.0 750.1 jit_solution(519489216737231312)
XLA Ops:
  16.6 3.0 collective-permute-start
  22.9 10.3 %collective-permute-done = bf16[256,1152]{1,0:T(8,128)(2,1)} collective-permute-done((bf16[256,1152]{1,0:T(8,128)(2,1)}, bf16[256,1152]{1,0:T(8,128)(2,1)}, u32[]{:S(2)}, u32[]{:S(2)}) %collective-permute-start) | collective-permute-done | bytes 589856 | tf_op jit(solution)/shard_map/ppermute | solution.py:151
  38.4 18.0 %collective-permute-done.1 = bf16[256,1920]{1,0:T(8,128)(2,1)} collective-permute-done((bf16[256,1920]{1,0:T(8,128)(2,1)}, bf16[256,1920]{1,0:T(8,128)(2,1)}, u32[]{:S(2)}, u32[]{:S(2)}) %collective-permute-start.1) | collective-permute-done | bytes 983072 | tf_op jit(solution)/shard_map/ppermute | solution.py:151
  57.8 11.0 %all-gather.4.cloned.1.call-done = bf16[1024,1280]{1,0:T(8,128)(2,1)} async-done(((bf16[256,1280]{1,0:T(8,128)(2,1)}), bf16[1024,1280]{1,0:T(8,128)(2,1)}) %all-gather.4.cloned.1.call-update) | async-done | bytes 2621456 | tf_op jit(solution)/shard_map/all_gather | solution.py:187
  68.8 2.7 slice.787
  80.4 27.3 %collective-permute-done.2 = bf16[1024,768]{1,0:T(8,128)(2,1)} collective-permute-done((bf16[1024,768]{1,0:T(8,128)(2,1)}, bf16[1024,768]{1,0:T(8,128)(2,1)}, u32[]{:S(2)}, u32[]{:S(2)}) %collective-permute-start.2) | collective-permute-done | bytes 1572896 | tf_op jit(solution)/shard_map/ppermute | solution.py:151
  107.8 3.7 maximum_select_fusion
  111.9 3.8 fusion.164
  133.6 7.4 collective-permute-done.3
  144.2 4.1 collective-permute-done.4
  150.2 23.8 %collective-permute-done.5 = bf16[256,2048]{1,0:T(8,128)(2,1)S(1)} collective-permute-done((bf16[256,2048]{1,0:T(8,128)(2,1)S(1)}, bf16[256,2048]{1,0:T(8,128)(2,1)S(1)}, u32[]{:S(2)}, u32[]{:S(2)}) %collective-permute-start.5) | collective-permute-done | bytes 1048608 | tf_op jit(solution)/shard_map/ppermute | solution.py:154
  178.2 10.1 %collective-permute-done.7 = bf16[128,2048]{1,0:T(8,128)(2,1)S(1)} collective-permute-done((bf16[128,2048]{1,0:T(8,128)(2,1)S(1)}, bf16[128,2048]{1,0:T(8,128)(2,1)S(1)}, u32[]{:S(2)}, u32[]{:S(2)}) %collective-permute-start.7) | collective-permute-done | bytes 524320 | tf_op jit(solution)/shard_map/ppermute | solution.py:151
  192.9 20.1 %collective-permute-done.8 = bf16[256,2048]{1,0:T(8,128)(2,1)} collective-permute-done((bf16[256,2048]{1,0:T(8,128)(2,1)S(1)}, bf16[256,2048]{1,0:T(8,128)(2,1)}, u32[]{:S(2)}, u32[]{:S(2)}) %collective-permute-start.8) | collective-permute-done | bytes 1048608 | tf_op jit(solution)/shard_map/ppermute | solution.py:151
  213.4 3.6 pad_maximum_fusion.1
  218.3 20.9 %collective-permute-done.11 = bf16[256,2048]{1,0:T(8,128)(2,1)S(1)} collective-permute-done((bf16[256,2048]{1,0:T(8,128)(2,1)S(1)}, bf16[256,2048]{1,0:T(8,128)(2,1)S(1)}, u32[]{:S(2)}, u32[]{:S(2)}) %collective-permute-start.11) | collective-permute-done | bytes 1048608 | tf_op jit(solution)/shard_map/ppermute | solution.py:151
  244.5 2.7 constant_dynamic-update-slice_fusion.1
  248.0 12.6 %collective-permute-done.12 = bf16[256,2048]{1,0:T(8,128)(2,1)S(1)} collective-permute-done((bf16[256,2048]{1,0:T(8,128)(2,1)S(1)}, bf16[256,2048]{1,0:T(8,128)(2,1)S(1)}, u32[]{:S(2)}, u32[]{:S(2)}) %collective-permute-start.12) | collective-permute-done | bytes 1048608 | tf_op jit(solution)/shard_map/ppermute | solution.py:154
  265.2 3.4 copy-done.122
  268.9 10.1 %convolution_convert_fusion.5 = bf16[2048,768]{0,1:T(8,128)(2,1)S(1)} fusion(bf16[2048,2048]{1,0:T(8,128)(2,1)S(1)} %constant_dynamic-update-slice_fusion, bf16[2048,1152]{1,0:T(8,128)(2,1)} %all-gather.6.cloned.1.call-done), kind=kOutput, calls=%fused_computation.72 | convolution fusion | flops 6444023808 | bytes 14680064 | tf_op jit(solution)/shard_map/dot_general | solution.py:62
  280.0 2.6 constant_dynamic-update-slice_fusion.2
  282.6 9.2 %convolution_convert_fusion.12 = bf16[2048,384]{1,0:T(8,128)(2,1)} fusion(bf16[2048,2048]{1,0:T(8,128)(2,1)} %constant_dynamic-update-slice_fusion.2, bf16[2048,384]{0,1:T(8,128)(2,1)S(1)} %fusion.33), kind=kOutput, calls=%fused_computation.90 | convolution fusion | flops 3222011904 | bytes 11534336 | tf_op jit(solution)/shard_map/dot_general | solution.py:50
  292.1 8.8 %fusion.35 = (bf16[2048,384]{0,1:T(8,128)(2,1)S(1)}, bf16[2048,384]{0,1:T(8,128)(2,1)S(1)}) fusion(bf16[2048,768]{0,1:T(8,128)(2,1)S(1)} %convolution_convert_fusion.5, bf16[2048,2048]{1,0:T(8,128)(2,1)} %constant_dynamic-update-slice_fusion.2, bf16[2048,1152]{1,0:T(8,128)(2,1)} %all-gather.6.cloned.1.call-done), kind=kOutput, calls=%fused_computation.78 | convolution fusion | flops 3233021952 | bytes 16252928 | tf_op jit(solution)/shard_map/dot_general | solution.py:62
  302.5 10.4 %convolution_convert_fusion.7 = bf16[2048,768]{1,0:T(8,128)(2,1)} fusion(bf16[2048,2048]{1,0:T(8,128)(2,1)} %copy-done.53, bf16[2048,384]{0,1:T(8,128)(2,1)S(1)} %get-tuple-element.222, bf16[2048,384]{0,1:T(8,128)(2,1)S(1)} %get-tuple-element.221), kind=kOutput, calls=%fused_computation.74 | convolution fusion | flops 6450315264 | bytes 14680064 | tf_op jit(solution)/shard_map/dot_general | solution.py:50
  315.1 11.0 %convolution_convert_fusion.1 = bf16[2048,2048]{1,0:T(8,128)(2,1)} fusion(bf16[2048,768]{0,1:T(8,128)(2,1)S(1)} %pad_maximum_fusion.3, bf16[2048,1152]{1,0:T(8,128)(2,1)} %all-gather.6.cloned.1.call-done), kind=kOutput, calls=%fused_computation.12 | convolution fusion | flops 6446645248 | bytes 14680064 | tf_op jit(solution)/shard_map/dot_general | solution.py:56
  326.1 8.2 %convolution_convert_fusion = bf16[2048,2048]{1,0:T(8,128)(2,1)} fusion(bf16[2048,384]{0,1:T(8,128)(2,1)S(1)} %copy-done.60, bf16[2048,1152]{1,0:T(8,128)(2,1)} %all-gather.6.cloned.1.call-done), kind=kOutput, calls=%fused_computation.11 | convolution fusion | flops 3225419776 | bytes 11534336 | tf_op jit(solution)/shard_map/dot_general | solution.py:56
  334.5 17.5 %convolution_convert_fusion.3 = bf16[2048,1280]{0,1:T(8,128)(2,1)} fusion(bf16[2048,2048]{1,0:T(8,128)(2,1)} %copy-done.53, bf16[2048,1920]{1,0:T(8,128)(2,1)} %all-gather.8.cloned.1.call-done), kind=kOutput, calls=%fused_computation.14 | convolution fusion | flops 10740039680 | bytes 18874368 | tf_op jit(solution)/shard_map/dot_general | solution.py:62
  352.0 12.5 %fusion.12 = (bf16[2048,640]{0,1:T(8,128)(2,1)S(1)}, bf16[2048,640]{0,1:T(8,128)(2,1)S(1)}, bf16[2048,640]{0,1:T(8,128)(2,1)}) fusion(bf16[2048,1280]{0,1:T(8,128)(2,1)} %convolution_convert_fusion.3, bf16[2048,2048]{1,0:T(8,128)(2,1)} %constant_dynamic-update-slice_fusion.2, bf16[2048,1920]{1,0:T(8,128)(2,1)S(1)} %copy-done.132), kind=kOutput, calls=%fused_computation.40 | convolution fusion | flops 5390991360 | bytes 24117248 | tf_op jit(solution)/shard_map/dot_general | solution.py:62
  364.5 9.1 %add_convert_fusion.3 = bf16[1024,2048]{1,0:T(8,128)(2,1)} fusion(bf16[2048,2048]{1,0:T(8,128)(2,1)} %convolution_convert_fusion.1, bf16[2048,1920]{1,0:T(8,128)(2,1)S(1)} %copy-done.132, bf16[2048,640]{0,1:T(8,128)(2,1)S(1)} %get-tuple-element.211, bf16[2048,640]{0,1:T(8,128)(2,1)S(1)} %get-tuple-element.212), kind=kOutput, calls=%fused_computation.7 | convolution fusion | flops 5380243456 | bytes 18874368 | tf_op jit(solution)/shard_map/dot_general | solution.py:56
  377.3 8.8 %add_convert_fusion.2 = bf16[1024,2048]{1,0:T(8,128)(2,1)} fusion(bf16[2048,2048]{1,0:T(8,128)(2,1)} %convolution_convert_fusion.1, bf16[2048,1920]{1,0:T(8,128)(2,1)S(1)} %copy-done.132, bf16[2048,1280]{0,1:T(8,128)(2,1)S(1)} %pad_maximum_fusion), kind=kOutput, calls=%fused_computation.6 | convolution fusion | flops 5375000576 | bytes 16252928 | tf_op jit(solution)/shard_map/dot_general | solution.py:56
  386.1 11.1 %convolution_convert_fusion.8 = bf16[2048,640]{1,0:T(8,128)(2,1)} fusion(bf16[2048,2048]{1,0:T(8,128)(2,1)} %constant_dynamic-update-slice_fusion.2, bf16[2048,640]{0,1:T(8,128)(2,1)} %get-tuple-element.165), kind=kOutput, calls=%fused_computation.75 | convolution fusion | flops 5370019840 | bytes 13631488 | tf_op jit(solution)/shard_map/dot_general | solution.py:50
  397.3 7.0 convert_add_fusion.6
  406.8 16.9 %convolution_convert_fusion.2 = bf16[2048,1280]{1,0:T(8,128)(2,1)} fusion(bf16[2048,2048]{1,0:T(8,128)(2,1)} %copy-done.53, bf16[2048,1280]{0,1:T(8,128)(2,1)} %copy-done.28), kind=kOutput, calls=%fused_computation.13 | convolution fusion | flops 10740039680 | bytes 18874368 | tf_op jit(solution)/shard_map/dot_general | solution.py:50
  423.7 9.0 %add_convert_fusion.1 = bf16[1024,2048]{1,0:T(8,128)(2,1)} fusion(bf16[2048,2048]{1,0:T(8,128)(2,1)} %convolution_convert_fusion, bf16[2048,1920]{1,0:T(8,128)(2,1)} %all-gather.8.cloned.1.call-done, bf16[2048,640]{0,1:T(8,128)(2,1)} %get-tuple-element.165), kind=kOutput, calls=%fused_computation.5 | convolution fusion | flops 2690646016 | bytes 12320768 | tf_op jit(solution)/shard_map/dot_general | solution.py:56
  438.4 7.8 %add_convert_fusion = bf16[1024,2048]{1,0:T(8,128)(2,1)} fusion(bf16[2048,2048]{1,0:T(8,128)(2,1)} %convolution_convert_fusion, bf16[2048,1920]{1,0:T(8,128)(2,1)} %all-gather.8.cloned.1.call-done, bf16[2048,640]{0,1:T(8,128)(2,1)S(1)} %copy-done.134), kind=kOutput, calls=%fused_computation.4 | convolution fusion | flops 2690646016 | bytes 12320768 | tf_op jit(solution)/shard_map/dot_general | solution.py:56
  446.4 3.7 collective-permute-done.18
  454.3 22.2 %collective-permute-done.21 = bf16[256,2048]{1,0:T(8,128)(2,1)S(1)} collective-permute-done((bf16[256,2048]{1,0:T(8,128)(2,1)S(1)}, bf16[256,2048]{1,0:T(8,128)(2,1)S(1)}, u32[]{:S(2)}, u32[]{:S(2)}) %collective-permute-start.21) | collective-permute-done | bytes 1048608 | tf_op jit(solution)/shard_map/ppermute | solution.py:154
  479.3 5.0 convolution_convert_fusion.13
  484.3 4.0 convolution_convert_fusion.9
  491.0 24.0 %collective-permute-done.30 = bf16[4,256,512]{2,1,0:T(8,128)(2,1)} collective-permute-done((bf16[4,256,512]{2,1,0:T(8,128)(2,1)S(1)}, bf16[4,256,512]{2,1,0:T(8,128)(2,1)}, u32[]{:S(2)}, u32[]{:S(2)}) %collective-permute-start.30) | collective-permute-done | bytes 1048608 | tf_op jit(solution)/shard_map/ppermute | solution.py:151
  521.0 3.9 pad_maximum_fusion.2
  525.0 3.2 add_convert_fusion.10
  534.3 18.4 %collective-permute-done.23 = bf16[256,2048]{1,0:T(8,128)(2,1)} collective-permute-done((bf16[256,2048]{1,0:T(8,128)(2,1)}, bf16[256,2048]{1,0:T(8,128)(2,1)}, u32[]{:S(2)}, u32[]{:S(2)}) %collective-permute-start.23) | collective-permute-done | bytes 1048608 | tf_op jit(solution)/shard_map/ppermute | solution.py:151
  552.7 5.1 convert_add_fusion.4
  559.2 4.4 fusion.2
  563.6 6.0 fusion.4
  569.6 2.7 fusion.84
  583.4 9.8 %collective-permute-done.24 = bf16[128,2048]{1,0:T(8,128)(2,1)S(1)} collective-permute-done((bf16[128,2048]{1,0:T(8,128)(2,1)S(1)}, bf16[128,2048]{1,0:T(8,128)(2,1)S(1)}, u32[]{:S(2)}, u32[]{:S(2)}) %collective-permute-start.24) | collective-permute-done | bytes 524320 | tf_op jit(solution)/shard_map/ppermute | solution.py:154
  593.4 2.6 convert_add_fusion.3
  605.0 3.1 collective-permute-done.26
  608.2 2.5 broadcast_in_dim.48
  623.3 4.5 convolution_convert_fusion.6
  637.7 9.0 %collective-permute-done.37 = bf16[256,768]{1,0:T(8,128)(2,1)} collective-permute-done((bf16[256,768]{1,0:T(8,128)(2,1)}, bf16[256,768]{1,0:T(8,128)(2,1)}, u32[]{:S(2)}, u32[]{:S(2)}) %collective-permute-start.37) | collective-permute-done | bytes 393248 | tf_op jit(solution)/shard_map/ppermute | solution.py:151
  651.7 5.9 collective-permute-done.49
  658.0 6.4 collective-permute-done.39
  667.2 2.6 convert_bitcast_fusion
  669.9 2.9 copy.68
  680.0 3.7 collective-permute-done.41
  687.5 14.7 %collective-permute-done.32 = bf16[256,2048]{1,0:T(8,128)(2,1)} collective-permute-done((bf16[256,2048]{1,0:T(8,128)(2,1)S(1)}, bf16[256,2048]{1,0:T(8,128)(2,1)}, u32[]{:S(2)}, u32[]{:S(2)}) %collective-permute-start.32) | collective-permute-done | bytes 1048608 | tf_op jit(solution)/shard_map/ppermute | solution.py:154
  702.2 2.4 multiply_reduce_fusion.1
  704.7 4.0 add_convert_fusion.6
  718.2 2.4 maximum_select_fusion.2
  720.7 2.6 maximum_select_fusion.3
  723.4 9.9 %collective-permute-done.45 = bf16[256,1280]{1,0:T(8,128)(2,1)S(1)} collective-permute-done((bf16[256,1280]{1,0:T(8,128)(2,1)S(1)}, bf16[256,1280]{1,0:T(8,128)(2,1)S(1)}, u32[]{:S(2)}, u32[]{:S(2)}) %collective-permute-start.45) | collective-permute-done | bytes 655392 | tf_op jit(solution)/shard_map/ppermute | solution.py:151
  734.6 4.3 maximum_convert_fusion
  (579 shorter events, 188.5 us)
Async XLA Ops:
  7.2 61.6 %all-gather.4.cloned.1.call-start = ((), (), s32[]{:S(2)}) async-start(), calls=%async_computation.5 | async-start | bytes 3276800 | tf_op jit(solution)/shard_map/all_gather | solution.py:187
  11.2 205.7 %all-gather.6.cloned.1.call-start = ((), (), s32[]{:S(2)}) async-start(), calls=%async_computation.6 | async-start | bytes 5898240 | tf_op jit(solution)/shard_map/all_gather | solution.py:187
  16.6 16.6 %collective-permute-start = (bf16[256,1152]{1,0:T(8,128)(2,1)}, bf16[256,1152]{1,0:T(8,128)(2,1)}, u32[]{:S(2)}, u32[]{:S(2)}) collective-permute-start(bf16[256,1152]{1,0:T(8,128)(2,1)} %pad_maximum_fusion.15), channel_id=1, source_target_pairs={{0,4},{4,0},{8,12},{12,8},{16,20},{20,16},{24,28},{28,24},{1,5},{5... | collective-permute-start | bytes 1769480 | tf_op jit(solution)/shard_map/ppermute | solution.py:151
  33.2 23.2 %collective-permute-start.1 = (bf16[256,1920]{1,0:T(8,128)(2,1)}, bf16[256,1920]{1,0:T(8,128)(2,1)}, u32[]{:S(2)}, u32[]{:S(2)}) collective-permute-start(bf16[256,1920]{1,0:T(8,128)(2,1)} %pad_maximum_fusion.12), channel_id=1, source_target_pairs={{0,4},{4,0},{8,12},{12,8},{16,20},{20,16},{24,28},{28,24},{1,5},{5... | collective-permute-start | bytes 2949128 | tf_op jit(solution)/shard_map/ppermute | solution.py:151
  71.5 36.3 %collective-permute-start.2 = (bf16[1024,768]{1,0:T(8,128)(2,1)}, bf16[1024,768]{1,0:T(8,128)(2,1)}, u32[]{:S(2)}, u32[]{:S(2)}) collective-permute-start(bf16[1024,768]{1,0:T(8,128)(2,1)} %slice.787), channel_id=1, source_target_pairs={{0,4},{4,0},{8,12},{12,8},{16,20},{20,16},{24,28},{28,24},{1,5},{5... | collective-permute-start | bytes 4718600 | tf_op jit(solution)/shard_map/ppermute | solution.py:151
  73.3 38.2 %copy-start.125 = (f32[1024]{0:T(1024)}, f32[1024]{0:T(1024)S(1)}, u32[]{:S(2)}) copy-start(f32[1024]{0:T(1024)S(1)} %add_rsqrt_fusion) | copy-start | bytes 12292
  73.4 57.0 %copy-start.37 = (pred[256,256]{0,1:T(8,128)(4,1)}, pred[256,256]{0,1:T(8,128)(4,1)S(1)}, u32[]{:S(2)}) copy-start(pred[256,256]{0,1:T(8,128)(4,1)S(1)} %fusion.124) | copy-start | bytes 196612
  73.5 47.7 %copy-start.21 = (pred[256,512]{0,1:T(8,128)(4,1)}, pred[256,512]{0,1:T(8,128)(4,1)S(1)}, u32[]{:S(2)}) copy-start(pred[256,512]{0,1:T(8,128)(4,1)S(1)} %fusion.114) | copy-start | bytes 393220
  74.2 50.4 %copy-start.14 = (pred[256,768]{0,1:T(8,128)(4,1)}, pred[256,768]{0,1:T(8,128)(4,1)S(1)}, u32[]{:S(2)}) copy-start(pred[256,768]{0,1:T(8,128)(4,1)S(1)} %get-tuple-element.338) | copy-start | bytes 589828
  74.2 56.7 %copy-start.16 = (pred[256,768]{0,1:T(8,128)(4,1)}, pred[256,768]{0,1:T(8,128)(4,1)S(1)}, u32[]{:S(2)}) copy-start(pred[256,768]{0,1:T(8,128)(4,1)S(1)} %get-tuple-element.339) | copy-start | bytes 589828
  79.1 255.3 %all-gather.8.cloned.1.call-start = ((), (), s32[]{:S(2)}) async-start(), calls=%async_computation.7 | async-start | bytes 9830400 | tf_op jit(solution)/shard_map/all_gather | solution.py:187
  117.1 23.9 %collective-permute-start.3 = (bf16[1024,512]{1,0:T(8,128)(2,1)S(1)}, bf16[1024,512]{1,0:T(8,128)(2,1)S(1)}, u32[]{:S(2)}, u32[]{:S(2)}) collective-permute-start(bf16[1024,512]{1,0:T(8,128)(2,1)S(1)} %slice.807), channel_id=1, source_target_pairs={{0,4},{4,0},{8,12},{12,8},{16,20},{20,16},{24,28},{28,24},{1,5},{5... | collective-permute-start | bytes 3145736 | tf_op jit(solution)/shard_map/ppermute | solution.py:151
  144.2 4.2 collective-permute-start.4
  148.8 25.3 %collective-permute-start.5 = (bf16[256,2048]{1,0:T(8,128)(2,1)S(1)}, bf16[256,2048]{1,0:T(8,128)(2,1)S(1)}, u32[]{:S(2)}, u32[]{:S(2)}) collective-permute-start(bf16[256,2048]{1,0:T(8,128)(2,1)S(1)} %add_convert_fusion.13), channel_id=1, source_target_pairs={{0,2},{1,3},{2,0},{3,1},{4,6},{5,7},{6,4},{7,5},{8,10},{9,11},{10,... | collective-permute-start | bytes 3145736 | tf_op jit(solution)/shard_map/ppermute | solution.py:154
  175.1 13.2 %collective-permute-start.7 = (bf16[128,2048]{1,0:T(8,128)(2,1)S(1)}, bf16[128,2048]{1,0:T(8,128)(2,1)S(1)}, u32[]{:S(2)}, u32[]{:S(2)}) collective-permute-start(bf16[128,2048]{1,0:T(8,128)(2,1)S(1)} %get-tuple-element.256), channel_id=1, source_target_pairs={{0,4},{4,0},{8,12},{12,8},{16,20},{20,16},{24,28},{28,24},{1,5},{5... | collective-permute-start | bytes 1572872 | tf_op jit(solution)/shard_map/ppermute | solution.py:151
  176.7 12.8 %collective-permute-start.6 = (bf16[128,2048]{1,0:T(8,128)(2,1)S(1)}, bf16[128,2048]{1,0:T(8,128)(2,1)S(1)}, u32[]{:S(2)}, u32[]{:S(2)}) collective-permute-start(bf16[128,2048]{1,0:T(8,128)(2,1)S(1)} %get-tuple-element.257), channel_id=1, source_target_pairs={{0,2},{1,3},{2,0},{3,1},{4,6},{5,7},{6,4},{7,5},{8,10},{9,11},{10,... | collective-permute-start | bytes 1572872 | tf_op jit(solution)/shard_map/ppermute | solution.py:154
  189.6 23.4 %collective-permute-start.8 = (bf16[256,2048]{1,0:T(8,128)(2,1)S(1)}, bf16[256,2048]{1,0:T(8,128)(2,1)}, u32[]{:S(2)}, u32[]{:S(2)}) collective-permute-start(bf16[256,2048]{1,0:T(8,128)(2,1)S(1)} %pad_maximum_fusion.8), channel_id=1, source_target_pairs={{0,4},{4,0},{8,12},{12,8},{16,20},{20,16},{24,28},{28,24},{1,5},{5... | collective-permute-start | bytes 3145736 | tf_op jit(solution)/shard_map/ppermute | solution.py:151
  190.2 23.2 %collective-permute-start.9 = (bf16[256,2048]{1,0:T(8,128)(2,1)S(1)}, bf16[256,2048]{1,0:T(8,128)(2,1)}, u32[]{:S(2)}, u32[]{:S(2)}) collective-permute-start(bf16[256,2048]{1,0:T(8,128)(2,1)S(1)} %pad_maximum_fusion.9), channel_id=1, source_target_pairs={{0,2},{1,3},{2,0},{3,1},{4,6},{5,7},{6,4},{7,5},{8,10},{9,11},{10,... | collective-permute-start | bytes 3145736 | tf_op jit(solution)/shard_map/ppermute | solution.py:154
  191.6 194.5 %reduce-scatter.6.cloned.1.call-start = ((), (), s32[]{:S(2)}) async-start(), calls=%async_computation.8 | async-start | bytes 1966080 | tf_op jit(solution)/shard_map/reduce_scatter | solution.py:190
  216.9 22.2 %collective-permute-start.11 = (bf16[256,2048]{1,0:T(8,128)(2,1)S(1)}, bf16[256,2048]{1,0:T(8,128)(2,1)S(1)}, u32[]{:S(2)}, u32[]{:S(2)}) collective-permute-start(bf16[256,2048]{1,0:T(8,128)(2,1)S(1)} %constant_dynamic-slice_fusion.10), channel_id=1, source_target_pairs={{0,4},{4,0},{8,12},{12,8},{16,20},{20,16},{24,28},{28,24},{1,5},{5... | collective-permute-start | bytes 3145736 | tf_op jit(solution)/shard_map/ppermute | solution.py:151
  239.2 21.5 %collective-permute-start.12 = (bf16[256,2048]{1,0:T(8,128)(2,1)S(1)}, bf16[256,2048]{1,0:T(8,128)(2,1)S(1)}, u32[]{:S(2)}, u32[]{:S(2)}) collective-permute-start(bf16[256,2048]{1,0:T(8,128)(2,1)S(1)} %collective-permute-done.11), channel_id=1, source_target_pairs={{0,2},{1,3},{2,0},{3,1},{4,6},{5,7},{6,4},{7,5},{8,10},{9,11},{10,... | collective-permute-start | bytes 3145736 | tf_op jit(solution)/shard_map/ppermute | solution.py:154
  244.5 24.1 %collective-permute-start.10 = (bf16[1024,2048]{1,0:T(8,128)(2,1)}, bf16[1024,2048]{1,0:T(8,128)(2,1)S(1)}, u32[]{:S(2)}, u32[]{:S(2)}) collective-permute-start(bf16[1024,2048]{1,0:T(8,128)(2,1)} %pad_maximum_fusion.1), channel_id=1, source_target_pairs={{0,1},{1,0},{2,3},{3,2},{4,5},{5,4},{6,7},{7,6},{8,9},{9,8},{10,11... | collective-permute-start | bytes 12582920 | tf_op jit(solution)/shard_map/ppermute | solution.py:157
  265.0 15.0 %collective-permute-start.13 = (bf16[1024,2048]{1,0:T(8,128)(2,1)}, bf16[1024,2048]{1,0:T(8,128)(2,1)S(1)}, u32[]{:S(2)}, u32[]{:S(2)}) collective-permute-start(bf16[1024,2048]{1,0:T(8,128)(2,1)} %get-tuple-element.248), channel_id=1, source_target_pairs={{0,1},{1,0},{2,3},{3,2},{4,5},{5,4},{6,7},{7,6},{8,9},{9,8},{10,11... | collective-permute-start | bytes 12582920 | tf_op jit(solution)/shard_map/ppermute | solution.py:157
  291.8 229.1 %reduce-scatter.10.cloned.1.call-start = ((), (), s32[]{:S(2)}) async-start(), calls=%async_computation.10 | async-start | bytes 3932160 | tf_op jit(solution)/shard_map/reduce_scatter | solution.py:190
  334.4 279.8 %reduce-scatter.8.cloned.1.call-start = ((), (), s32[]{:S(2)}) async-start(), calls=%async_computation.9 | async-start | bytes 3276800 | tf_op jit(solution)/shard_map/reduce_scatter | solution.py:190
  373.6 23.7 %collective-permute-start.14 = (bf16[1024,2048]{1,0:T(8,128)(2,1)}, bf16[1024,2048]{1,0:T(8,128)(2,1)}, u32[]{:S(2)}, u32[]{:S(2)}) collective-permute-start(bf16[1024,2048]{1,0:T(8,128)(2,1)} %add_convert_fusion.3), channel_id=1, source_target_pairs={{0,1},{1,0},{2,3},{3,2},{4,5},{5,4},{6,7},{7,6},{8,9},{9,8},{10,11... | collective-permute-start | bytes 12582920 | tf_op jit(solution)/shard_map/ppermute | solution.py:157
  397.2 238.7 %reduce-scatter.14.cloned.1.call-start = ((), (), s32[]{:S(2)}) async-start(), calls=%async_computation.12 | async-start | bytes 1310720 | tf_op jit(solution)/shard_map/reduce_scatter | solution.py:190
  404.3 28.4 %collective-permute-start.16 = (bf16[256,2048]{1,0:T(8,128)(2,1)}, bf16[256,2048]{1,0:T(8,128)(2,1)}, u32[]{:S(2)}, u32[]{:S(2)}) collective-permute-start(bf16[256,2048]{1,0:T(8,128)(2,1)} %get-tuple-element.218), channel_id=1, source_target_pairs={{0,2},{1,3},{2,0},{3,1},{4,6},{5,7},{6,4},{7,5},{8,10},{9,11},{10,... | collective-permute-start | bytes 3145736 | tf_op jit(solution)/shard_map/ppermute | solution.py:154
  406.0 28.4 %collective-permute-start.15 = (bf16[256,2048]{1,0:T(8,128)(2,1)S(1)}, bf16[256,2048]{1,0:T(8,128)(2,1)}, u32[]{:S(2)}, u32[]{:S(2)}) collective-permute-start(bf16[256,2048]{1,0:T(8,128)(2,1)S(1)} %get-tuple-element.219), channel_id=1, source_target_pairs={{0,4},{4,0},{8,12},{12,8},{16,20},{20,16},{24,28},{28,24},{1,5},{5... | collective-permute-start | bytes 3145736 | tf_op jit(solution)/shard_map/ppermute | solution.py:151
  436.7 13.3 %collective-permute-start.18 = (bf16[128,2048]{1,0:T(8,128)(2,1)S(1)}, bf16[128,2048]{1,0:T(8,128)(2,1)S(1)}, u32[]{:S(2)}, u32[]{:S(2)}) collective-permute-start(bf16[128,2048]{1,0:T(8,128)(2,1)S(1)} %slice.1061), channel_id=1, source_target_pairs={{0,2},{1,3},{2,0},{3,1},{4,6},{5,7},{6,4},{7,5},{8,10},{9,11},{10,... | collective-permute-start | bytes 1572872 | tf_op jit(solution)/shard_map/ppermute | solution.py:154
  437.4 12.9 %collective-permute-start.19 = (bf16[128,2048]{1,0:T(8,128)(2,1)S(1)}, bf16[128,2048]{1,0:T(8,128)(2,1)S(1)}, u32[]{:S(2)}, u32[]{:S(2)}) collective-permute-start(bf16[128,2048]{1,0:T(8,128)(2,1)S(1)} %slice.1060), channel_id=1, source_target_pairs={{0,4},{4,0},{8,12},{12,8},{16,20},{20,16},{24,28},{28,24},{1,5},{5... | collective-permute-start | bytes 1572872 | tf_op jit(solution)/shard_map/ppermute | solution.py:151
  452.8 23.7 %collective-permute-start.21 = (bf16[256,2048]{1,0:T(8,128)(2,1)S(1)}, bf16[256,2048]{1,0:T(8,128)(2,1)S(1)}, u32[]{:S(2)}, u32[]{:S(2)}) collective-permute-start(bf16[256,2048]{1,0:T(8,128)(2,1)S(1)} %add_convert_fusion.9), channel_id=1, source_target_pairs={{0,2},{1,3},{2,0},{3,1},{4,6},{5,7},{6,4},{7,5},{8,10},{9,11},{10,... | collective-permute-start | bytes 3145736 | tf_op jit(solution)/shard_map/ppermute | solution.py:154
  454.3 22.4 %collective-permute-start.20 = (bf16[256,2048]{1,0:T(8,128)(2,1)S(1)}, bf16[256,2048]{1,0:T(8,128)(2,1)}, u32[]{:S(2)}, u32[]{:S(2)}) collective-permute-start(bf16[256,2048]{1,0:T(8,128)(2,1)S(1)} %add_convert_fusion.9), channel_id=1, source_target_pairs={{0,1},{1,0},{2,3},{3,2},{4,5},{5,4},{6,7},{7,6},{8,9},{9,8},{10,11... | collective-permute-start | bytes 3145736 | tf_op jit(solution)/shard_map/ppermute | solution.py:157
  476.5 2.8 collective-permute-start.22
  489.7 25.4 %collective-permute-start.30 = (bf16[4,256,512]{2,1,0:T(8,128)(2,1)S(1)}, bf16[4,256,512]{2,1,0:T(8,128)(2,1)}, u32[]{:S(2)}, u32[]{:S(2)}) collective-permute-start(bf16[4,256,512]{2,1,0:T(8,128)(2,1)S(1)} %dynamic-slice_bitcast_fusion), channel_id=1, source_target_pairs={{0,4},{4,0},{8,12},{12,8},{16,20},{20,16},{24,28},{28,24},{1,5},{5... | collective-permute-start | bytes 3145736 | tf_op jit(solution)/shard_map/ppermute | solution.py:151
  491.0 33.9 %collective-permute-start.17 = (bf16[1024,2048]{1,0:T(8,128)(2,1)}, bf16[1024,2048]{1,0:T(8,128)(2,1)}, u32[]{:S(2)}, u32[]{:S(2)}) collective-permute-start(bf16[1024,2048]{1,0:T(8,128)(2,1)} %add_convert_fusion.1), channel_id=1, source_target_pairs={{0,1},{1,0},{2,3},{3,2},{4,5},{5,4},{6,7},{7,6},{8,9},{9,8},{10,11... | collective-permute-start | bytes 12582920 | tf_op jit(solution)/shard_map/ppermute | solution.py:157
  518.2 197.3 %reduce-scatter.12.cloned.1.call-start = ((), (), s32[]{:S(2)}) async-start(), calls=%async_computation.11 | async-start | bytes 6553600 | tf_op jit(solution)/shard_map/reduce_scatter | solution.py:190
  520.9 38.2 %copy-start.83 = (bf16[256,512]{0,1:T(8,128)(2,1)}, bf16[256,512]{0,1:T(8,128)(2,1)S(1)}, u32[]{:S(2)}) copy-start(bf16[256,512]{0,1:T(8,128)(2,1)S(1)} %get-tuple-element.243) | copy-start | bytes 786436
  528.2 24.5 %collective-permute-start.23 = (bf16[256,2048]{1,0:T(8,128)(2,1)}, bf16[256,2048]{1,0:T(8,128)(2,1)}, u32[]{:S(2)}, u32[]{:S(2)}) collective-permute-start(bf16[256,2048]{1,0:T(8,128)(2,1)} %add_convert_fusion.10), channel_id=1, source_target_pairs={{0,4},{4,0},{8,12},{12,8},{16,20},{20,16},{24,28},{28,24},{1,5},{5... | collective-permute-start | bytes 3145736 | tf_op jit(solution)/shard_map/ppermute | solution.py:151
  557.8 35.5 %collective-permute-start.25 = (bf16[256,2048]{1,0:T(8,128)(2,1)}, bf16[256,2048]{1,0:T(8,128)(2,1)}, u32[]{:S(2)}, u32[]{:S(2)}) collective-permute-start(bf16[256,2048]{1,0:T(8,128)(2,1)} %get-tuple-element.169), channel_id=1, source_target_pairs={{0,2},{1,3},{2,0},{3,1},{4,6},{5,7},{6,4},{7,5},{8,10},{9,11},{10,... | collective-permute-start | bytes 3145736 | tf_op jit(solution)/shard_map/ppermute | solution.py:154
  575.1 18.1 %collective-permute-start.24 = (bf16[128,2048]{1,0:T(8,128)(2,1)S(1)}, bf16[128,2048]{1,0:T(8,128)(2,1)S(1)}, u32[]{:S(2)}, u32[]{:S(2)}) collective-permute-start(bf16[128,2048]{1,0:T(8,128)(2,1)S(1)} %slice.1059), channel_id=1, source_target_pairs={{0,2},{1,3},{2,0},{3,1},{4,6},{5,7},{6,4},{7,5},{8,10},{9,11},{10,... | collective-permute-start | bytes 1572872 | tf_op jit(solution)/shard_map/ppermute | solution.py:154
  583.3 21.2 %collective-permute-start.34 = (bf16[256,2048]{1,0:T(8,128)(2,1)S(1)}, bf16[256,2048]{1,0:T(8,128)(2,1)S(1)}, u32[]{:S(2)}, u32[]{:S(2)}) collective-permute-start(bf16[256,2048]{1,0:T(8,128)(2,1)S(1)} %constant_dynamic-slice_fusion.8), channel_id=1, source_target_pairs={{0,1},{1,0},{2,3},{3,2},{4,5},{5,4},{6,7},{7,6},{8,9},{9,8},{10,11... | collective-permute-start | bytes 3145736 | tf_op jit(solution)/shard_map/ppermute | solution.py:157
  596.1 12.0 %collective-permute-start.26 = (bf16[128,2048]{1,0:T(8,128)(2,1)S(1)}, bf16[128,2048]{1,0:T(8,128)(2,1)S(1)}, u32[]{:S(2)}, u32[]{:S(2)}) collective-permute-start(bf16[128,2048]{1,0:T(8,128)(2,1)S(1)} %slice.1058), channel_id=1, source_target_pairs={{0,4},{4,0},{8,12},{12,8},{16,20},{20,16},{24,28},{28,24},{1,5},{5... | collective-permute-start | bytes 1572872 | tf_op jit(solution)/shard_map/ppermute | solution.py:151
  612.4 63.4 %collective-permute-start.27 = (bf16[256,2048]{1,0:T(8,128)(2,1)}, bf16[256,2048]{1,0:T(8,128)(2,1)}, u32[]{:S(2)}, u32[]{:S(2)}) collective-permute-start(bf16[256,2048]{1,0:T(8,128)(2,1)} %get-tuple-element.208), channel_id=1, source_target_pairs={{0,1},{1,0},{2,3},{3,2},{4,5},{5,4},{6,7},{7,6},{8,9},{9,8},{10,11... | collective-permute-start | bytes 3145736 | tf_op jit(solution)/shard_map/ppermute | solution.py:157
  612.4 72.7 %collective-permute-start.28 = (bf16[256,2048]{1,0:T(8,128)(2,1)}, bf16[256,2048]{1,0:T(8,128)(2,1)}, u32[]{:S(2)}, u32[]{:S(2)}) collective-permute-start(bf16[256,2048]{1,0:T(8,128)(2,1)} %get-tuple-element.208), channel_id=1, source_target_pairs={{0,2},{1,3},{2,0},{3,1},{4,6},{5,7},{6,4},{7,5},{8,10},{9,11},{10,... | collective-permute-start | bytes 3145736 | tf_op jit(solution)/shard_map/ppermute | solution.py:154
  629.8 20.2 %collective-permute-start.31 = (bf16[256,2048]{1,0:T(8,128)(2,1)S(1)}, bf16[256,2048]{1,0:T(8,128)(2,1)S(1)}, u32[]{:S(2)}, u32[]{:S(2)}) collective-permute-start(bf16[256,2048]{1,0:T(8,128)(2,1)S(1)} %constant_dynamic-slice_fusion.9), channel_id=1, source_target_pairs={{0,1},{1,0},{2,3},{3,2},{4,5},{5,4},{6,7},{7,6},{8,9},{9,8},{10,11... | collective-permute-start | bytes 3145736 | tf_op jit(solution)/shard_map/ppermute | solution.py:157
  630.9 18.5 %collective-permute-start.48 = (bf16[256,384]{1,0:T(8,128)(2,1)}, bf16[256,384]{1,0:T(8,128)(2,1)}, u32[]{:S(2)}, u32[]{:S(2)}) collective-permute-start(bf16[256,384]{1,0:T(8,128)(2,1)} %get-tuple-element.287), channel_id=1, source_target_pairs={{0,4},{4,0},{8,12},{12,8},{16,20},{20,16},{24,28},{28,24},{1,5},{5... | collective-permute-start | bytes 589832 | tf_op jit(solution)/shard_map/ppermute | solution.py:151
  633.6 13.2 %collective-permute-start.37 = (bf16[256,768]{1,0:T(8,128)(2,1)}, bf16[256,768]{1,0:T(8,128)(2,1)}, u32[]{:S(2)}, u32[]{:S(2)}) collective-permute-start(bf16[256,768]{1,0:T(8,128)(2,1)} %get-tuple-element.230), channel_id=1, source_target_pairs={{0,4},{4,0},{8,12},{12,8},{16,20},{20,16},{24,28},{28,24},{1,5},{5... | collective-permute-start | bytes 1179656 | tf_op jit(solution)/shard_map/ppermute | solution.py:151
  646.7 10.8 %collective-permute-start.49 = (bf16[256,640]{1,0:T(8,128)(2,1)}, bf16[256,640]{1,0:T(8,128)(2,1)S(1)}, u32[]{:S(2)}, u32[]{:S(2)}) collective-permute-start(bf16[256,640]{1,0:T(8,128)(2,1)} %get-tuple-element.277), channel_id=1, source_target_pairs={{0,4},{4,0},{8,12},{12,8},{16,20},{20,16},{24,28},{28,24},{1,5},{5... | collective-permute-start | bytes 983048 | tf_op jit(solution)/shard_map/ppermute | solution.py:151
  649.5 14.9 %collective-permute-start.39 = (bf16[256,768]{1,0:T(8,128)(2,1)}, bf16[256,768]{1,0:T(8,128)(2,1)S(1)}, u32[]{:S(2)}, u32[]{:S(2)}) collective-permute-start(bf16[256,768]{1,0:T(8,128)(2,1)} %get-tuple-element.233), channel_id=1, source_target_pairs={{0,4},{4,0},{8,12},{12,8},{16,20},{20,16},{24,28},{28,24},{1,5},{5... | collective-permute-start | bytes 1179656 | tf_op jit(solution)/shard_map/ppermute | solution.py:151
  650.0 15.9 %collective-permute-start.38 = (bf16[256,768]{1,0:T(8,128)(2,1)S(1)}, bf16[256,768]{1,0:T(8,128)(2,1)S(1)}, u32[]{:S(2)}, u32[]{:S(2)}) collective-permute-start(bf16[256,768]{1,0:T(8,128)(2,1)S(1)} %fusion.110), channel_id=1, source_target_pairs={{0,8},{4,12},{8,16},{12,20},{16,24},{20,28},{24,0},{28,4},{1,9},{5... | collective-permute-start | bytes 1179656 | tf_op jit(solution)/shard_map/ppermute | solution.py:160
  657.5 30.0 %collective-permute-start.35 = (bf16[256,2048]{1,0:T(8,128)(2,1)S(1)}, bf16[256,2048]{1,0:T(8,128)(2,1)S(1)}, u32[]{:S(2)}, u32[]{:S(2)}) collective-permute-start(bf16[256,2048]{1,0:T(8,128)(2,1)S(1)} %add_convert_fusion.5), channel_id=1, source_target_pairs={{0,2},{1,3},{2,0},{3,1},{4,6},{5,7},{6,4},{7,5},{8,10},{9,11},{10,... | collective-permute-start | bytes 3145736 | tf_op jit(solution)/shard_map/ppermute | solution.py:154
  664.4 9.9 %collective-permute-start.44 = (bf16[256,768]{1,0:T(8,128)(2,1)}, bf16[256,768]{1,0:T(8,128)(2,1)}, u32[]{:S(2)}, u32[]{:S(2)}) collective-permute-start(bf16[256,768]{1,0:T(8,128)(2,1)} %constant_dynamic-slice_fusion.7), channel_id=1, source_target_pairs={{0,4},{4,0},{8,12},{12,8},{16,20},{20,16},{24,28},{28,24},{1,5},{5... | collective-permute-start | bytes 1179656 | tf_op jit(solution)/shard_map/ppermute | solution.py:151
  666.7 35.5 %collective-permute-start.32 = (bf16[256,2048]{1,0:T(8,128)(2,1)S(1)}, bf16[256,2048]{1,0:T(8,128)(2,1)}, u32[]{:S(2)}, u32[]{:S(2)}) collective-permute-start(bf16[256,2048]{1,0:T(8,128)(2,1)S(1)} %add_convert_fusion.7), channel_id=1, source_target_pairs={{0,2},{1,3},{2,0},{3,1},{4,6},{5,7},{6,4},{7,5},{8,10},{9,11},{10,... | collective-permute-start | bytes 3145736 | tf_op jit(solution)/shard_map/ppermute | solution.py:154
  674.3 9.3 %collective-permute-start.41 = (bf16[256,768]{1,0:T(8,128)(2,1)}, bf16[256,768]{1,0:T(8,128)(2,1)S(1)}, u32[]{:S(2)}, u32[]{:S(2)}) collective-permute-start(bf16[256,768]{1,0:T(8,128)(2,1)} %get-tuple-element.232), channel_id=1, source_target_pairs={{0,4},{4,0},{8,12},{12,8},{16,20},{20,16},{24,28},{28,24},{1,5},{5... | collective-permute-start | bytes 1179656 | tf_op jit(solution)/shard_map/ppermute | solution.py:151
  675.8 10.3 %collective-permute-start.40 = (bf16[256,768]{1,0:T(8,128)(2,1)S(1)}, bf16[256,768]{1,0:T(8,128)(2,1)S(1)}, u32[]{:S(2)}, u32[]{:S(2)}) collective-permute-start(bf16[256,768]{1,0:T(8,128)(2,1)S(1)} %fusion.109), channel_id=1, source_target_pairs={{0,8},{4,12},{8,16},{12,20},{16,24},{20,28},{24,0},{28,4},{1,9},{5... | collective-permute-start | bytes 1179656 | tf_op jit(solution)/shard_map/ppermute | solution.py:160
  683.6 27.9 %collective-permute-start.43 = (bf16[256,768]{1,0:T(8,128)(2,1)}, bf16[256,768]{1,0:T(8,128)(2,1)S(1)}, u32[]{:S(2)}, u32[]{:S(2)}) collective-permute-start(bf16[256,768]{1,0:T(8,128)(2,1)} %get-tuple-element.231), channel_id=1, source_target_pairs={{0,4},{4,0},{8,12},{12,8},{16,20},{20,16},{24,28},{28,24},{1,5},{5... | collective-permute-start | bytes 1179656 | tf_op jit(solution)/shard_map/ppermute | solution.py:151
  685.1 29.3 %collective-permute-start.29 = (bf16[256,2048]{1,0:T(8,128)(2,1)}, bf16[256,2048]{1,0:T(8,128)(2,1)S(1)}, u32[]{:S(2)}, u32[]{:S(2)}) collective-permute-start(bf16[256,2048]{1,0:T(8,128)(2,1)} %collective-permute-done.28), channel_id=1, source_target_pairs={{0,1},{1,0},{2,3},{3,2},{4,5},{5,4},{6,7},{7,6},{8,9},{9,8},{10,11... | collective-permute-start | bytes 3145736 | tf_op jit(solution)/shard_map/ppermute | solution.py:157
  687.2 24.3 %collective-permute-start.42 = (bf16[256,768]{1,0:T(8,128)(2,1)S(1)}, bf16[256,768]{1,0:T(8,128)(2,1)S(1)}, u32[]{:S(2)}, u32[]{:S(2)}) collective-permute-start(bf16[256,768]{1,0:T(8,128)(2,1)S(1)} %fusion.107), channel_id=1, source_target_pairs={{0,8},{4,12},{8,16},{12,20},{16,24},{20,28},{24,0},{28,4},{1,9},{5... | collective-permute-start | bytes 1179656 | tf_op jit(solution)/shard_map/ppermute | solution.py:160
  708.7 9.5 %collective-permute-start.33 = (bf16[256,2048]{1,0:T(8,128)(2,1)}, bf16[256,2048]{1,0:T(8,128)(2,1)S(1)}, u32[]{:S(2)}, u32[]{:S(2)}) collective-permute-start(bf16[256,2048]{1,0:T(8,128)(2,1)} %get-tuple-element.213), channel_id=1, source_target_pairs={{0,1},{1,0},{2,3},{3,2},{4,5},{5,4},{6,7},{7,6},{8,9},{9,8},{10,11... | collective-permute-start | bytes 3145736 | tf_op jit(solution)/shard_map/ppermute | solution.py:157
  711.0 9.7 %collective-permute-start.36 = (bf16[256,2048]{1,0:T(8,128)(2,1)S(1)}, bf16[256,2048]{1,0:T(8,128)(2,1)}, u32[]{:S(2)}, u32[]{:S(2)}) collective-permute-start(bf16[256,2048]{1,0:T(8,128)(2,1)S(1)} %get-tuple-element.214), channel_id=1, source_target_pairs={{0,1},{1,0},{2,3},{3,2},{4,5},{5,4},{6,7},{7,6},{8,9},{9,8},{10,11... | collective-permute-start | bytes 3145736 | tf_op jit(solution)/shard_map/ppermute | solution.py:157
  716.6 16.7 %collective-permute-start.45 = (bf16[256,1280]{1,0:T(8,128)(2,1)S(1)}, bf16[256,1280]{1,0:T(8,128)(2,1)S(1)}, u32[]{:S(2)}, u32[]{:S(2)}) collective-permute-start(bf16[256,1280]{1,0:T(8,128)(2,1)S(1)} %constant_dynamic-slice_fusion.6), channel_id=1, source_target_pairs={{0,4},{4,0},{8,12},{12,8},{16,20},{20,16},{24,28},{28,24},{1,5},{5... | collective-permute-start | bytes 1966088 | tf_op jit(solution)/shard_map/ppermute | solution.py:151
  734.5 4.4 collective-permute-start.46
  738.8 3.7 collective-permute-start.47
  (135 other events, 1200.3 us)
Sparse Core Ops, SparseCore 0:
  11.3 57.4 all-gather.3
  79.2 87.2 all-gather.5
  191.7 139.5 all-gather.7
  333.5 33.5 reduce-scatter.5
  369.3 59.2 reduce-scatter.9
  430.7 52.1 reduce-scatter.7
  518.3 25.7 reduce-scatter.13
  546.4 92.2 reduce-scatter.11

commit v5 on v4

--- a/solution.py
+++ b/solution.py
@@ -238,16 +238,22 @@
     attn_z = gather_z(attn_local)
     send_a = tie(trio_part(1 - y_index, 0), attn_local)
     got_a = swap_y(send_a)
+    pair_a = pair_rows(trio_part(y_index, 0), got_a)
+    full_a = gather_z(tie(pair_a, attn_local))
     got_b = swap_y(tie(trio_part(1 - y_index, 1), got_a))
-    pair_a = pair_rows(trio_part(y_index, 0), got_a)
     pair_b = pair_rows(trio_part(y_index, 1), got_b)
-    full_a = gather_z(tie(pair_a, attn_local))
     full_b = gather_z(tie(pair_b, pair_a))
     qkv_z, out_z = attn_z[:, :qkv_cols], attn_z[:, qkv_cols:]
     qkv_other = swap_y(tie(qkv_z, pair_b))
     out_other = swap_y(tie(out_z, qkv_other))
     qkv_full = interleave(qkv_z, qkv_other)
     out_full = interleave(out_z, out_other)
+
+    def quarter_of(value, other):
+        return lax.dynamic_slice_in_dim(value, (t_index ^ other) * quarter, quarter, 0)
+
+    cot_own, cot_x = quarter_of(cotangent, 0), quarter_of(cotangent, 2)
+    cot_pair = swap_y(tie(jnp.concatenate([cot_own, cot_x], axis=0), out_other))
 
     tokens_float = tokens.astype(F32)
     token_root = inverse_root(tokens_float)
@@ -297,18 +303,15 @@
     n_held = tie(n_held, full_a)
     n_all = jnp.concatenate([n_held, swap_core(n_held)], axis=0)
 
-    def quarter_of(value, other):
-        return lax.dynamic_slice_in_dim(value, (t_index ^ other) * quarter, quarter, 0)
-
-    cot_own, cot_x = quarter_of(cotangent, 0), quarter_of(cotangent, 2)
-    cot_y = swap_y(tie(cot_own, n_held))
-    cot_yx = swap_x(cot_y)
+    cot_pair = tie(cot_pair, n_two)
+    cot_y, cot_yx = cot_pair[:quarter], cot_pair[quarter:]
     cot_held = jnp.concatenate(
         [v[:half_quarter] for v in (cot_own, cot_x, cot_y, cot_yx)]
         + [v[half_quarter:] for v in (cot_own, cot_y, cot_x, cot_yx)],
         axis=0,
     )
     cot_all = jnp.concatenate([cot_held, swap_core(cot_held)], axis=0)
+
 
     side_rows = 4 * quarter
 
@@ -385,14 +388,24 @@
     )
     hidden_low = jnp.concatenate(gather_tensor(hidden_grad.astype(BF)), axis=0)
 
-    ffn_keeps, ffn_sends = pair_sends(ffn_part, ffn_got)
-    ffn_sends = tuple(tie(v, hidden_low) for v in ffn_sends)
-    ffn_keeps, ffn_passes = pair_pass(ffn_keeps, ffn_sends)
-    layer_quarter = (hidden + pair_sum(ffn_keeps, ffn_passes)).astype(BF)
-    layer_output = absolute(gather_tensor(layer_quarter), BF)
-
-    def ring_step(received, block, step):
-        return hop((received.astype(F32) + block(step + 1)).astype(BF))
+    def pair_rows_of(part, got, blocks):
+        return jnp.concatenate(
+            [
+                two_way(
+                    part[i * half_quarter : (i + 1) * half_quarter],
+                    got[i * half_quarter : (i + 1) * half_quarter],
+                )
+                for i in blocks
+            ],
+            axis=0,
+        )
+
+    ffn_send = pair_rows_of(ffn_part, ffn_got, (2, 5, 3, 7)).astype(BF)
+    ffn_keep = pair_rows_of(ffn_part, ffn_got, (0, 4, 1, 6))
+    hidden_low = tie(hidden_low, ffn_send)
+    ffn_sum = ffn_keep + swap_y(ffn_send).astype(F32)
+    ffn_pass = ffn_sum[quarter:].astype(BF)
+    layer_quarter = (hidden + ffn_sum[:quarter] + swap_x(ffn_pass).astype(F32)).astype(BF)
 
     def ring_end(received, block):
         return received.astype(F32) + block(groups)
@@ -401,24 +414,38 @@
     out_weight_grad = dot_rows(hidden_low, tie(mixed_rel, mixed_grad_rel), BF)
     cut = out_weight_grad.reshape(groups, 2, rows, -1)
     out_mine = lax.dynamic_index_in_dim(cut, y_index, 1, keepdims=False)
-    out_sent = swap_y(lax.dynamic_index_in_dim(cut, 1 - y_index, 1, keepdims=False))
+    out_send = lax.dynamic_index_in_dim(cut, 1 - y_index, 1, keepdims=False)
+    out_sent = swap_y(tie(out_send, ffn_pass))
     out_both = two_way(out_mine, out_sent).astype(BF).reshape(groups * rows, -1)
-    out_block = scatter_z(out_both)
+    out_block = scatter_z(tie(out_both, gu_block_b))
     out_grad = out_block.astype(F32).T
     mixed_grad = absolute(
         [mixed_grad_rel[j * quarter : (j + 1) * quarter] for j in range(tensor_size)], BF
     )
+    def trade(block):
+        return my_half(block, 0, True), swap_y(my_half(block, 0, False))
+
+    gu_trade_a, down_trade_a = trade(gu_block_a), trade(down_block_a)
+    down_trade_b, gu_trade_b = trade(tie(down_block_b, mixed_grad_rel)), trade(gu_block_b)
     gates = (
-        ffn_sends + (out_weight_grad,),
-        (gu_block_a,),
-        ffn_passes + (out_both,),
+        (out_weight_grad,),
+        (gu_block_a, ffn_pass),
         (layer_quarter, down_block_b),
-    )
+        (out_sent, gu_block_b, gu_trade_a[1], down_trade_a[1], down_trade_b[1]),
+    )
+    core_index, half_rows = t_index % 2, token_count // 2
+
+    def core_rows(value, base, which):
+        return lax.dynamic_slice_in_dim(value, base + which * quarter, quarter, 0)
+
+    def chip_rows(part):
+        got = swap_core(core_rows(part, 0, 1 - core_index))
+        return two_way(core_rows(part, 0, core_index), got).astype(BF)
+
     grouped = query_low.reshape(token_count, -1, GROUP, HD)
     grad_grouped = mixed_grad.reshape(token_count, -1, GROUP, HD)
     key_grad = jnp.zeros(key_low.shape, F32)
     value_grad = jnp.zeros(value_seq.shape, F32)
-    core_index, half_rows = t_index % 2, token_count // 2
     qkv_grad_parts, e_one_parts, query_parts = [], [], []
     for number, ((start, size, first_key, last), log_part, gate) in enumerate(
         zip(reversed(list(spans(token_count))), reversed(log_total), gates)
@@ -426,6 +453,9 @@
         grad_block = tie(grad_grouped[start : start + size], *gate)
         if number == 2:
             grad_block = tie(grad_block, e_one_parts[0])
+        if number == 3:
+            chip_late = chip_rows(e_one_parts[0])
+            grad_block = tie(grad_block, chip_late)
         query_part, key_part, value_part = block_backward(
             grouped[start : start + size],
             key_low[first_key:last],
@@ -458,63 +488,65 @@
     qkv_weight_grad = dot_rows(normed, jnp.concatenate(qkv_grad_parts, axis=0), BF)
     e_one_parts.append(dot_cols(tie(qkv_grad_parts[0], qkv_weight_grad), qkv_full, BF))
 
-    def tokens_rows(part, start):
-        size = part.shape[0] // 2
-
-        def mine(value, base):
-            return lax.dynamic_slice_in_dim(value, base + core_index * size, size, 0)
-
-        got = swap_core(lax.dynamic_slice_in_dim(part, (1 - core_index) * size, size, 0))
-        chip_sum = two_way(mine(part, 0), got).astype(BF)
-        e_one = two_way(chip_sum, swap_x(chip_sum))
+    chip_early = chip_rows(e_one_parts[1])
+
+    qkv_cut = qkv_weight_grad.reshape(groups, 2, rows, -1)
+
+    def qkv_pick(side):
+        def pick(back):
+            start = ((z_index - back) % groups, side, 0, 0)
+            return lax.dynamic_slice(qkv_cut, start, (1, 1, rows, qkv_cols))[0, 0]
+
+        return pick
+
+    qkv_mine, qkv_other_y = qkv_pick(y_index), qkv_pick(1 - y_index)
+    qkv_sent = [swap_y(qkv_other_y(back)) for back in range(1, groups + 1)]
+
+    def qkv_part(back):
+        return two_way(qkv_mine(back), qkv_sent[back - 1])
+
+    def tokens_rows(chip_sum, chip_other, start):
+        e_one = two_way(chip_sum, chip_other)
         grad_rows = lax.dynamic_slice_in_dim(
-            hidden_low, (t_index ^ (start // quarter + core_index)) * quarter, size, 0
+            hidden_low, (t_index ^ (start // quarter + core_index)) * quarter, quarter, 0
         ).astype(F32)
-        root = mine(token_root, start)
-        n_one = mine(tokens, start).astype(F32) * root
+        root = core_rows(token_root, start, core_index)
+        n_one = core_rows(tokens, start, core_index).astype(F32) * root
         own = grad_rows + root * (e_one - n_one * jnp.mean(e_one * n_one, axis=-1, keepdims=True))
         own = own.astype(BF)
-        other = swap_core(own)
+        return own, swap_core(own)
+
+    def core_order(own, other):
         return jnp.where(
             core_index == 0,
             jnp.concatenate([own, other], axis=0),
             jnp.concatenate([other, own], axis=0),
         ).astype(F32)
 
+    late_other, early_other = swap_x(chip_late), swap_x(chip_early)
+    layer_x = swap_x(layer_quarter)
+    layer_output = absolute(
+        [layer_quarter, swap_core(layer_quarter), layer_x, swap_core(tie(layer_x, qkv_weight_grad))],
+        BF,
+    )
+    qkv_send = tie(qkv_part(1).astype(BF), chip_early, out_block, gu_trade_b[1])
+    qkv_runs = []
+    for step in range(1, groups):
+        qkv_runs.append(hop(qkv_send))
+        if step == 1:
+            late_rows = tokens_rows(chip_late, tie(late_other, qkv_send), half_rows)
+        if step < groups - 1:
+            qkv_send = (qkv_runs[-1].astype(F32) + qkv_part(step + 1)).astype(BF)
+            if step == 1:
+                early_rows = tokens_rows(chip_early, tie(early_other, qkv_send), 0)
+    qkv_block = ring_end(qkv_runs[-1], qkv_part)
     tokens_grad = jnp.concatenate(
-        [tokens_rows(e_one_parts[1], 0), tokens_rows(e_one_parts[0], half_rows)], axis=0
-    )
-
-    qkv_cut = qkv_weight_grad.reshape(groups, 2, rows, -1)
-
-    def qkv_pick(side):
-        def pick(back):
-            start = ((z_index - back) % groups, side, 0, 0)
-            return lax.dynamic_slice(qkv_cut, start, (1, 1, rows, qkv_cols))[0, 0]
-
-        return pick
-
-    qkv_mine, qkv_other_y = qkv_pick(y_index), qkv_pick(1 - y_index)
-    qkv_sent = [swap_y(qkv_other_y(back)) for back in range(1, groups + 1)]
-
-    def qkv_part(back):
-        return two_way(qkv_mine(back), qkv_sent[back - 1])
-
-    qkv_run = hop(qkv_part(1).astype(BF))
-    for step in range(1, groups - 1):
-        qkv_run = ring_step(qkv_run, qkv_part, step)
-    qkv_block = ring_end(qkv_run, qkv_part)
-
-    def trade(block):
-        mine = my_half(block, 0, True)
-        return mine, swap_y(my_half(block, 0, False))
-
-    traded = [
-        [trade(tie(block, last)) for block, last in zip(pair, (layer_quarter, qkv_weight_grad))]
-        for pair in ((gu_block_a, gu_block_b), (down_block_a, down_block_b))
-    ]
+        [core_order(*early_rows), core_order(tie(late_rows[0], qkv_send), late_rows[1])], axis=0
+    )
 
     def all_units(pairs, place):
+        pairs = [(mine, tie(got, qkv_send)) for mine, got in pairs]
+
         def side(which):
             return jnp.concatenate(
                 [pair[which][:, place * n : (place + 1) * n] for pair, n in zip(pairs, part_units)],
@@ -523,8 +555,8 @@
 
         return by_y(side(0), side(1), 1).astype(F32)
 
-    gate_g, up_g = all_units(traded[0], 0), all_units(traded[0], 1)
-    down_weight_grad = all_units(traded[1], 0).T
+    gate_g, up_g = all_units((gu_trade_a, gu_trade_b), 0), all_units((gu_trade_a, gu_trade_b), 1)
+    down_weight_grad = all_units((down_trade_a, down_trade_b), 0).T
 
     attn_gain_part = jnp.sum(
         qkv_block * jnp.concatenate([query_weight, key_weight, value_weight], axis=1).astype(F32),

time: 756 us -> 700 us (0.926)
  waiting for transfers between devices: 302 us -> 227 us
  local copies, waits for them, and re-layouts: 75.4 us -> 95.2 us
  starting transfers between devices: 45.1 us -> 36.4 us
  other arithmetic: 103 us -> 111 us
    ppermute x20 -> x19, waiting for transfers between devices: 195 us -> 149 us  [swap_y(): return lax.ppermute(value, 'dp', [(i, i ^ 1) for i in range(dp_size)])]
    ppermute x13 -> x11, waiting for transfers between devices: 88.8 us -> 52.1 us  [swap_x(): lax.ppermute(value, 'tensor', [(i, i ^ 2) for i in range(tensor_size)])]
    unnamed x298 -> x338, local copies, waits for them, and re-layouts: 35.1 us -> 49.3 us
    ppermute x3, waiting for transfers between devices: 0.98 us -> 10.7 us  [hop(): lax.ppermute(value, 'dp', [(i, (i + 2) % dp_size) for i in range(dp_size)])]
    ppermute x20 -> x19, starting transfers between devices: 27.5 us -> 22.8 us  [swap_y(): return lax.ppermute(value, 'dp', [(i, i ^ 1) for i in range(dp_size)])]
    ppermute x13 -> x11, starting transfers between devices: 15.3 us -> 11.3 us  [swap_x(): lax.ppermute(value, 'tensor', [(i, i ^ 2) for i in range(tensor_size)])]
  transfers between devices with their start and end apart: 58 -> 55, of which waited for: 29 -> 25; matrix products, arithmetic and copies ran while one was open for 48% -> 54% of each run, Pallas kernels for 0% -> 0%
where the time goes in v5:
time: 700 us; the launch traced here: 694 us
  waiting for transfers between devices  227 us (32%)
  matrix products  208 us (30%)
  other arithmetic  111 us (16%)
  local copies, waits for them, and re-layouts  95.2 us (14%)
  starting transfers between devices  36.4 us (5%)
  between operations  17 us (2%)
    ppermute x19, waiting for transfers between devices, swap_y(): return lax.ppermute(value, 'dp', [(i, i ^ 1) for i in range(dp_size)])  149 us
    dot_general x9, matrix products, dot_cols(): lax.dot_general(left, right, (((1,), (1,)), ((), ())), preferred_element_...  60.3 us
    dot_general x6, matrix products, dot_rows(): lax.dot_general(left, right, (((0,), (0,)), ((), ())), preferred_element_...  57.3 us
    dot_general x6, matrix products, dot(): return jnp.dot(left, right, preferred_element_type=F32).astype(out)  54.8 us
    ppermute x11, waiting for transfers between devices, swap_x(): lax.ppermute(value, 'tensor', [(i, i ^ 2) for i in range(tensor_size)])  52.1 us
    unnamed x338, local copies, waits for them, and re-layouts  49.3 us
    ppermute x19, starting transfers between devices, swap_y(): return lax.ppermute(value, 'dp', [(i, i ^ 1) for i in range(dp_size)])  22.8 us
  transfers between devices with their start and end apart: 55, of which 25 were waited for; matrix products, arithmetic and copies ran while one was open for 54% of the time, Pallas kernels for 0%

profile of v5, /device:TPU:0, one launch (start us, length us, event | category | flops | bytes accessed | tf_op | source)
XLA Modules:
  0.0 693.6 jit_solution(6341182091749366511)
XLA Ops:
  15.9 3.0 collective-permute-start
  24.7 7.8 %collective-permute-done = bf16[256,1152]{1,0:T(8,128)(2,1)} collective-permute-done((bf16[256,1152]{1,0:T(8,128)(2,1)}, bf16[256,1152]{1,0:T(8,128)(2,1)}, u32[]{:S(2)}, u32[]{:S(2)}) %collective-permute-start) | collective-permute-done | bytes 589856 | tf_op jit(solution)/shard_map/ppermute | solution.py:151
  39.3 16.2 %collective-permute-done.1 = bf16[256,1920]{1,0:T(8,128)(2,1)} collective-permute-done((bf16[256,1920]{1,0:T(8,128)(2,1)S(1)}, bf16[256,1920]{1,0:T(8,128)(2,1)}, u32[]{:S(2)}, u32[]{:S(2)}) %collective-permute-start.1) | collective-permute-done | bytes 983072 | tf_op jit(solution)/shard_map/ppermute | solution.py:151
  57.9 11.0 %all-gather.4.cloned.1.call-done = bf16[1024,1280]{1,0:T(8,128)(2,1)} async-done(((bf16[256,1280]{1,0:T(8,128)(2,1)}), bf16[1024,1280]{1,0:T(8,128)(2,1)}) %all-gather.4.cloned.1.call-update) | async-done | bytes 2621456 | tf_op jit(solution)/shard_map/all_gather | solution.py:187
  79.5 27.0 %collective-permute-done.2 = bf16[1024,768]{1,0:T(8,128)(2,1)} collective-permute-done((bf16[1024,768]{1,0:T(8,128)(2,1)S(1)}, bf16[1024,768]{1,0:T(8,128)(2,1)}, u32[]{:S(2)}, u32[]{:S(2)}) %collective-permute-start.2) | collective-permute-done | bytes 1572896 | tf_op jit(solution)/shard_map/ppermute | solution.py:151
  106.5 2.6 maximum_select_fusion
  109.7 3.8 fusion.165
  132.0 7.6 %collective-permute-done.3 = bf16[1024,512]{1,0:T(8,128)(2,1)S(1)} collective-permute-done((bf16[1024,512]{1,0:T(8,128)(2,1)S(1)}, bf16[1024,512]{1,0:T(8,128)(2,1)S(1)}, u32[]{:S(2)}, u32[]{:S(2)}) %collective-permute-start.3) | collective-permute-done | bytes 1048608 | tf_op jit(solution)/shard_map/ppermute | solution.py:151
  143.0 4.1 collective-permute-done.4
  158.3 15.5 %collective-permute-done.5 = bf16[256,2048]{1,0:T(8,128)(2,1)} collective-permute-done((bf16[256,2048]{1,0:T(8,128)(2,1)S(1)}, bf16[256,2048]{1,0:T(8,128)(2,1)}, u32[]{:S(2)}, u32[]{:S(2)}) %collective-permute-start.5) | collective-permute-done | bytes 1048608 | tf_op jit(solution)/shard_map/ppermute | solution.py:154
  173.8 3.4 multiply_reduce_fusion.3
  178.0 22.2 %collective-permute-done.11 = bf16[512,2048]{1,0:T(8,128)(2,1)S(1)} collective-permute-done((bf16[512,2048]{1,0:T(8,128)(2,1)}, bf16[512,2048]{1,0:T(8,128)(2,1)S(1)}, u32[]{:S(2)}, u32[]{:S(2)}) %collective-permute-start.11) | collective-permute-done | bytes 2097184 | tf_op jit(solution)/shard_map/ppermute | solution.py:151
  205.1 8.1 %collective-permute-done.7 = bf16[128,2048]{1,0:T(8,128)(2,1)S(1)} collective-permute-done((bf16[128,2048]{1,0:T(8,128)(2,1)S(1)}, bf16[128,2048]{1,0:T(8,128)(2,1)S(1)}, u32[]{:S(2)}, u32[]{:S(2)}) %collective-permute-start.7) | collective-permute-done | bytes 524320 | tf_op jit(solution)/shard_map/ppermute | solution.py:151
  219.5 18.4 %collective-permute-done.8 = bf16[256,2048]{1,0:T(8,128)(2,1)S(1)} collective-permute-done((bf16[256,2048]{1,0:T(8,128)(2,1)S(1)}, bf16[256,2048]{1,0:T(8,128)(2,1)S(1)}, u32[]{:S(2)}, u32[]{:S(2)}) %collective-permute-start.8) | collective-permute-done | bytes 1048608 | tf_op jit(solution)/shard_map/ppermute | solution.py:151
  238.3 2.7 pad_maximum_fusion.1
  241.8 2.5 dynamic-slice_dynamic-update-slice_fusion.2
  248.2 3.1 copy-done.136
  251.3 2.5 constant_dynamic-update-slice_fusion.2
  253.8 3.2 copy-done.137
  257.4 10.1 %convolution_convert_fusion.5 = bf16[2048,768]{0,1:T(8,128)(2,1)S(1)} fusion(bf16[2048,2048]{1,0:T(8,128)(2,1)S(1)} %constant_dynamic-update-slice_fusion, bf16[2048,1152]{1,0:T(8,128)(2,1)} %all-gather.6.cloned.1.call-done), kind=kOutput, calls=%fused_computation.73 | convolution fusion | flops 6444023808 | bytes 14680064 | tf_op jit(solution)/shard_map/dot_general | solution.py:62
  269.6 9.1 %convolution_convert_fusion.12 = bf16[2048,384]{1,0:T(8,128)(2,1)} fusion(bf16[2048,2048]{1,0:T(8,128)(2,1)} %copy-done.137, bf16[2048,384]{0,1:T(8,128)(2,1)S(1)} %fusion.33), kind=kOutput, calls=%fused_computation.91 | convolution fusion | flops 3222011904 | bytes 11534336 | tf_op jit(solution)/shard_map/dot_general | solution.py:50
  279.0 8.7 %fusion.35 = (bf16[2048,384]{0,1:T(8,128)(2,1)S(1)}, bf16[2048,384]{0,1:T(8,128)(2,1)S(1)}) fusion(bf16[2048,768]{0,1:T(8,128)(2,1)S(1)} %convolution_convert_fusion.5, bf16[2048,2048]{1,0:T(8,128)(2,1)} %copy-done.137, bf16[2048,1152]{1,0:T(8,128)(2,1)} %all-gather.6.cloned.1.call-done), kind=kOutput, calls=%fused_computation.79 | convolution fusion | flops 3233021952 | bytes 16252928 | tf_op jit(solution)/shard_map/dot_general | solution.py:62
  289.4 10.4 %convolution_convert_fusion.7 = bf16[2048,768]{1,0:T(8,128)(2,1)} fusion(bf16[2048,2048]{1,0:T(8,128)(2,1)} %copy-done.71, bf16[2048,384]{0,1:T(8,128)(2,1)S(1)} %get-tuple-element.246, bf16[2048,384]{0,1:T(8,128)(2,1)S(1)} %get-tuple-element.245), kind=kOutput, calls=%fused_computation.75 | convolution fusion | flops 6450315264 | bytes 14680064 | tf_op jit(solution)/shard_map/dot_general | solution.py:50
  302.0 11.1 %convolution_convert_fusion.1 = bf16[2048,2048]{1,0:T(8,128)(2,1)} fusion(bf16[2048,768]{0,1:T(8,128)(2,1)S(1)} %pad_maximum_fusion.3, bf16[2048,1152]{1,0:T(8,128)(2,1)} %all-gather.6.cloned.1.call-done), kind=kOutput, calls=%fused_computation.12 | convolution fusion | flops 6446645248 | bytes 14680064 | tf_op jit(solution)/shard_map/dot_general | solution.py:56
  313.0 8.3 %convolution_convert_fusion = bf16[2048,2048]{1,0:T(8,128)(2,1)} fusion(bf16[2048,384]{0,1:T(8,128)(2,1)S(1)} %copy-done.82, bf16[2048,1152]{1,0:T(8,128)(2,1)} %all-gather.6.cloned.1.call-done), kind=kOutput, calls=%fused_computation.11 | convolution fusion | flops 3225419776 | bytes 11534336 | tf_op jit(solution)/shard_map/dot_general | solution.py:56
  321.4 17.2 %convolution_convert_fusion.3 = bf16[2048,1280]{0,1:T(8,128)(2,1)} fusion(bf16[2048,2048]{1,0:T(8,128)(2,1)} %copy-done.71, bf16[2048,1920]{1,0:T(8,128)(2,1)} %all-gather.8.cloned.1.call-done), kind=kOutput, calls=%fused_computation.14 | convolution fusion | flops 10740039680 | bytes 18874368 | tf_op jit(solution)/shard_map/dot_general | solution.py:62
  338.6 12.5 %fusion.12 = (bf16[2048,640]{0,1:T(8,128)(2,1)S(1)}, bf16[2048,640]{0,1:T(8,128)(2,1)S(1)}, bf16[2048,640]{0,1:T(8,128)(2,1)}) fusion(bf16[2048,1280]{0,1:T(8,128)(2,1)} %convolution_convert_fusion.3, bf16[2048,2048]{1,0:T(8,128)(2,1)} %copy-done.137, bf16[2048,1920]{1,0:T(8,128)(2,1)S(1)} %copy-done.152), kind=kOutput, calls=%fused_computation.40 | convolution fusion | flops 5390991360 | bytes 24117248 | tf_op jit(solution)/shard_map/dot_general | solution.py:62
  351.2 9.1 %add_convert_fusion.3 = bf16[1024,2048]{1,0:T(8,128)(2,1)} fusion(bf16[2048,2048]{1,0:T(8,128)(2,1)} %convolution_convert_fusion.1, bf16[2048,1920]{1,0:T(8,128)(2,1)S(1)} %copy-done.152, bf16[2048,640]{0,1:T(8,128)(2,1)S(1)} %get-tuple-element.229, bf16[2048,640]{0,1:T(8,128)(2,1)S(1)} %get-tuple-element.230), kind=kOutput, calls=%fused_computation.7 | convolution fusion | flops 5380243456 | bytes 18874368 | tf_op jit(solution)/shard_map/dot_general | solution.py:56
  363.4 8.8 %add_convert_fusion.2 = bf16[1024,2048]{1,0:T(8,128)(2,1)} fusion(bf16[2048,2048]{1,0:T(8,128)(2,1)} %convolution_convert_fusion.1, bf16[2048,1920]{1,0:T(8,128)(2,1)S(1)} %copy-done.152, bf16[2048,1280]{0,1:T(8,128)(2,1)S(1)} %pad_maximum_fusion), kind=kOutput, calls=%fused_computation.6 | convolution fusion | flops 5375000576 | bytes 16252928 | tf_op jit(solution)/shard_map/dot_general | solution.py:56
  372.3 11.1 %convolution_convert_fusion.8 = bf16[2048,640]{1,0:T(8,128)(2,1)} fusion(bf16[2048,2048]{1,0:T(8,128)(2,1)} %copy-done.137, bf16[2048,640]{0,1:T(8,128)(2,1)} %get-tuple-element.175), kind=kOutput, calls=%fused_computation.76 | convolution fusion | flops 5370019840 | bytes 13631488 | tf_op jit(solution)/shard_map/dot_general | solution.py:50
  383.5 7.1 %convert_add_fusion.4 = (f32[256,2048]{1,0:T(8,128)}, bf16[256,2048]{1,0:T(8,128)(2,1)}, bf16[256,2048]{1,0:T(8,128)(2,1)S(1)}, f32[256,2048]{1,0:T(8,128)S(1)}) fusion(bf16[1024,2048]{1,0:T(8,128)(2,1)} %collective-permute-done.13, bf16[1024,2048]{1,0:T(8,128)(2,1)} %add_convert_fusion.2), kind=kLoop, calls=%fused_computation.144 | loop fusion | flops 7340032 | bytes 14680064 | tf_op jit(solution)/shard_map/add | solution.py:275
  392.5 17.0 %convolution_convert_fusion.2 = bf16[2048,1280]{1,0:T(8,128)(2,1)} fusion(bf16[2048,2048]{1,0:T(8,128)(2,1)} %copy-done.71, bf16[2048,1280]{0,1:T(8,128)(2,1)} %copy-done.32), kind=kOutput, calls=%fused_computation.13 | convolution fusion | flops 10740039680 | bytes 18874368 | tf_op jit(solution)/shard_map/dot_general | solution.py:50
  409.5 9.5 %add_convert_fusion.1 = bf16[1024,2048]{1,0:T(8,128)(2,1)} fusion(bf16[2048,2048]{1,0:T(8,128)(2,1)} %convolution_convert_fusion, bf16[2048,1920]{1,0:T(8,128)(2,1)} %all-gather.8.cloned.1.call-done, bf16[2048,640]{0,1:T(8,128)(2,1)} %get-tuple-element.175), kind=kOutput, calls=%fused_computation.5 | convolution fusion | flops 2690646016 | bytes 12320768 | tf_op jit(solution)/shard_map/dot_general | solution.py:56
  424.7 7.5 %add_convert_fusion = bf16[1024,2048]{1,0:T(8,128)(2,1)} fusion(bf16[2048,2048]{1,0:T(8,128)(2,1)} %convolution_convert_fusion, bf16[2048,1920]{1,0:T(8,128)(2,1)} %all-gather.8.cloned.1.call-done, bf16[2048,640]{0,1:T(8,128)(2,1)S(1)} %copy-done.154), kind=kOutput, calls=%fused_computation.4 | convolution fusion | flops 2690646016 | bytes 12320768 | tf_op jit(solution)/shard_map/dot_general | solution.py:56
  432.3 5.1 collective-permute-done.21
  441.0 23.5 %collective-permute-done.24 = bf16[256,2048]{1,0:T(8,128)(2,1)} collective-permute-done((bf16[256,2048]{1,0:T(8,128)(2,1)S(1)}, bf16[256,2048]{1,0:T(8,128)(2,1)}, u32[]{:S(2)}, u32[]{:S(2)}) %collective-permute-start.24) | collective-permute-done | bytes 1048608 | tf_op jit(solution)/shard_map/ppermute | solution.py:154
  472.3 2.6 pad_maximum_fusion.2
  474.9 7.1 %add_convert_fusion.15 = (bf16[128,2048]{1,0:T(8,128)(2,1)S(1)}, bf16[128,2048]{1,0:T(8,128)(2,1)S(1)}, bf16[128,2048]{1,0:T(8,128)(2,1)S(1)}, bf16[128,2048]{1,...) fusion(bf16[1024,2048]{1,0:T(8,128)(2,1)} %collective-permute-do, ...), kind=kLoop, calls=%fused_computation.233 | loop fusion | flops 7340032 | bytes 14680064 | tf_op jit(solution)/shard_map/convert.21
  484.3 2.4 convolution_convert_fusion.13
  486.7 3.8 convolution_convert_fusion.9
  491.8 4.4 fusion.2
  496.2 4.3 fusion.4
  508.1 2.7 dynamic-slice_bitcast_fusion
  512.2 20.0 %collective-permute-done.17 = bf16[512,2048]{1,0:T(8,128)(2,1)} collective-permute-done((bf16[512,2048]{1,0:T(8,128)(2,1)}, bf16[512,2048]{1,0:T(8,128)(2,1)}, u32[]{:S(2)}, u32[]{:S(2)}) %collective-permute-start.17) | collective-permute-done | bytes 2097184 | tf_op jit(solution)/shard_map/ppermute | solution.py:151
  532.3 2.9 maximum_add_fusion
  538.1 4.4 fusion.5
  542.5 4.3 fusion.7
  556.4 2.9 collective-permute-done.18
  559.9 2.9 constant_dynamic-update-slice_fusion.10
  571.9 2.5 fusion.56
  576.8 2.9 fusion.87
  586.6 5.8 convolution_convert_fusion.6
  599.8 2.5 constant_dynamic-update-slice_fusion.8
  609.5 5.8 collective-permute-done.34
  617.3 12.2 %collective-permute-done.35 = bf16[256,1280]{1,0:T(8,128)(2,1)} collective-permute-done((bf16[256,1280]{1,0:T(8,128)(2,1)S(1)}, bf16[256,1280]{1,0:T(8,128)(2,1)}, u32[]{:S(2)}, u32[]{:S(2)}) %collective-permute-start.35) | collective-permute-done | bytes 655392 | tf_op jit(solution)/shard_map/ppermute | solution.py:151
  630.6 2.5 constant_dynamic-update-slice_fusion.3
  637.9 3.6 collective-permute-done.36
  644.9 2.4 multiply_reduce_fusion.1
  647.4 4.2 add_convert_fusion.5
  657.6 2.4 convert_multiply_fusion.10
  660.0 6.4 collective-permute-done.43
  675.4 3.4 maximum_select_fusion.2
  678.8 3.4 maximum_select_fusion.3
  682.2 4.3 maximum_convert_fusion
  (611 shorter events, 196.5 us)
Async XLA Ops:
  7.2 61.7 %all-gather.4.cloned.1.call-start = ((), (), s32[]{:S(2)}) async-start(), calls=%async_computation.5 | async-start | bytes 3276800 | tf_op jit(solution)/shard_map/all_gather | solution.py:187
  11.2 229.8 %all-gather.6.cloned.1.call-start = ((), (), s32[]{:S(2)}) async-start(), calls=%async_computation.6 | async-start | bytes 5898240 | tf_op jit(solution)/shard_map/all_gather | solution.py:187
  15.9 16.6 %collective-permute-start = (bf16[256,1152]{1,0:T(8,128)(2,1)}, bf16[256,1152]{1,0:T(8,128)(2,1)}, u32[]{:S(2)}, u32[]{:S(2)}) collective-permute-start(bf16[256,1152]{1,0:T(8,128)(2,1)} %pad_maximum_fusion.17), channel_id=1, source_target_pairs={{0,4},{4,0},{8,12},{12,8},{16,20},{20,16},{24,28},{28,24},{1,5},{5... | collective-permute-start | bytes 1769480 | tf_op jit(solution)/shard_map/ppermute | solution.py:151
  32.6 23.0 %collective-permute-start.1 = (bf16[256,1920]{1,0:T(8,128)(2,1)S(1)}, bf16[256,1920]{1,0:T(8,128)(2,1)}, u32[]{:S(2)}, u32[]{:S(2)}) collective-permute-start(bf16[256,1920]{1,0:T(8,128)(2,1)S(1)} %pad_maximum_fusion.14), channel_id=1, source_target_pairs={{0,4},{4,0},{8,12},{12,8},{16,20},{20,16},{24,28},{28,24},{1,5},{5... | collective-permute-start | bytes 2949128 | tf_op jit(solution)/shard_map/ppermute | solution.py:151
  36.0 36.8 %copy-start.88 = (f32[1024,32]{0,1:T(8,128)}, f32[1024,32]{0,1:T(8,128)S(1)}, u32[]{:S(2)}) copy-start(f32[1024,32]{0,1:T(8,128)S(1)} %get-tuple-element.320) | copy-start | bytes 393220
  36.0 36.8 %copy-start.90 = (f32[1024,32]{0,1:T(8,128)}, f32[1024,32]{0,1:T(8,128)S(1)}, u32[]{:S(2)}) copy-start(f32[1024,32]{0,1:T(8,128)S(1)} %get-tuple-element.321) | copy-start | bytes 393220
  39.3 34.5 %slice-start.5 = ((s32[1,1024]{1,0:T(1,128)}), s32[1,512]{1,0:T(1,128)S(1)}, s32[]{:S(2)}) async-start(s32[1,1024]{1,0:T(1,128)} %param.29), calls=%async_computation.18 | async-start | bytes 4096 | tf_op jit(solution)/shard_map/slice | solution.py:86
  39.3 34.5 %copy-start.147 = (s32[1,256]{1,0:T(1,128)S(1)}, s32[1,256]{1,0:T(1,128)}, u32[]{:S(2)}) copy-start(s32[1,256]{1,0:T(1,128)} %get-tuple-element.325) | copy-start | bytes 3076
  70.4 36.1 %collective-permute-start.2 = (bf16[1024,768]{1,0:T(8,128)(2,1)S(1)}, bf16[1024,768]{1,0:T(8,128)(2,1)}, u32[]{:S(2)}, u32[]{:S(2)}) collective-permute-start(bf16[1024,768]{1,0:T(8,128)(2,1)S(1)} %slice.816), channel_id=1, source_target_pairs={{0,4},{4,0},{8,12},{12,8},{16,20},{20,16},{24,28},{28,24},{1,5},{5... | collective-permute-start | bytes 4718600 | tf_op jit(solution)/shard_map/ppermute | solution.py:151
  73.6 35.5 %copy-start.140 = (f32[1024]{0:T(1024)}, f32[1024]{0:T(1024)S(1)}, u32[]{:S(2)}) copy-start(f32[1024]{0:T(1024)S(1)} %add_rsqrt_fusion) | copy-start | bytes 12292
  73.8 54.9 %copy-start.47 = (pred[256,256]{0,1:T(8,128)(4,1)}, pred[256,256]{0,1:T(8,128)(4,1)S(1)}, u32[]{:S(2)}) copy-start(pred[256,256]{0,1:T(8,128)(4,1)S(1)} %fusion.125) | copy-start | bytes 196612
  74.0 46.0 %copy-start.27 = (pred[256,512]{0,1:T(8,128)(4,1)}, pred[256,512]{0,1:T(8,128)(4,1)S(1)}, u32[]{:S(2)}) copy-start(pred[256,512]{0,1:T(8,128)(4,1)S(1)} %fusion.115) | copy-start | bytes 393220
  74.7 48.6 %copy-start.16 = (pred[256,768]{0,1:T(8,128)(4,1)}, pred[256,768]{0,1:T(8,128)(4,1)S(1)}, u32[]{:S(2)}) copy-start(pred[256,768]{0,1:T(8,128)(4,1)S(1)} %get-tuple-element.364) | copy-start | bytes 589828
  74.7 55.0 %copy-start.18 = (pred[256,768]{0,1:T(8,128)(4,1)}, pred[256,768]{0,1:T(8,128)(4,1)S(1)}, u32[]{:S(2)}) copy-start(pred[256,768]{0,1:T(8,128)(4,1)S(1)} %get-tuple-element.365) | copy-start | bytes 589828
  78.2 243.2 %all-gather.8.cloned.1.call-start = ((), (), s32[]{:S(2)}) async-start(), calls=%async_computation.7 | async-start | bytes 9830400 | tf_op jit(solution)/shard_map/all_gather | solution.py:187
  115.7 23.9 %collective-permute-start.3 = (bf16[1024,512]{1,0:T(8,128)(2,1)S(1)}, bf16[1024,512]{1,0:T(8,128)(2,1)S(1)}, u32[]{:S(2)}, u32[]{:S(2)}) collective-permute-start(bf16[1024,512]{1,0:T(8,128)(2,1)S(1)} %slice.836), channel_id=1, source_target_pairs={{0,4},{4,0},{8,12},{12,8},{16,20},{20,16},{24,28},{28,24},{1,5},{5... | collective-permute-start | bytes 3145736 | tf_op jit(solution)/shard_map/ppermute | solution.py:151
  142.9 4.2 collective-permute-start.4
  148.5 25.3 %collective-permute-start.5 = (bf16[256,2048]{1,0:T(8,128)(2,1)S(1)}, bf16[256,2048]{1,0:T(8,128)(2,1)}, u32[]{:S(2)}, u32[]{:S(2)}) collective-permute-start(bf16[256,2048]{1,0:T(8,128)(2,1)S(1)} %add_convert_fusion.11), channel_id=1, source_target_pairs={{0,2},{1,3},{2,0},{3,1},{4,6},{5,7},{6,4},{7,5},{8,10},{9,11},{10,... | collective-permute-start | bytes 3145736 | tf_op jit(solution)/shard_map/ppermute | solution.py:154
  152.7 47.6 %collective-permute-start.11 = (bf16[512,2048]{1,0:T(8,128)(2,1)}, bf16[512,2048]{1,0:T(8,128)(2,1)S(1)}, u32[]{:S(2)}, u32[]{:S(2)}) collective-permute-start(bf16[512,2048]{1,0:T(8,128)(2,1)} %pad_maximum_fusion.5), channel_id=1, source_target_pairs={{0,4},{4,0},{8,12},{12,8},{16,20},{20,16},{24,28},{28,24},{1,5},{5... | collective-permute-start | bytes 6291464 | tf_op jit(solution)/shard_map/ppermute | solution.py:151
  158.2 214.0 %reduce-scatter.6.cloned.1.call-start = ((), (), s32[]{:S(2)}) async-start(), calls=%async_computation.8 | async-start | bytes 1966080 | tf_op jit(solution)/shard_map/reduce_scatter | solution.py:190
  200.3 12.9 %collective-permute-start.7 = (bf16[128,2048]{1,0:T(8,128)(2,1)S(1)}, bf16[128,2048]{1,0:T(8,128)(2,1)S(1)}, u32[]{:S(2)}, u32[]{:S(2)}) collective-permute-start(bf16[128,2048]{1,0:T(8,128)(2,1)S(1)} %get-tuple-element.282), channel_id=1, source_target_pairs={{0,4},{4,0},{8,12},{12,8},{16,20},{20,16},{24,28},{28,24},{1,5},{5... | collective-permute-start | bytes 1572872 | tf_op jit(solution)/shard_map/ppermute | solution.py:151
  202.0 12.7 %collective-permute-start.6 = (bf16[128,2048]{1,0:T(8,128)(2,1)S(1)}, bf16[128,2048]{1,0:T(8,128)(2,1)S(1)}, u32[]{:S(2)}, u32[]{:S(2)}) collective-permute-start(bf16[128,2048]{1,0:T(8,128)(2,1)S(1)} %get-tuple-element.283), channel_id=1, source_target_pairs={{0,2},{1,3},{2,0},{3,1},{4,6},{5,7},{6,4},{7,5},{8,10},{9,11},{10,... | collective-permute-start | bytes 1572872 | tf_op jit(solution)/shard_map/ppermute | solution.py:154
  214.7 23.2 %collective-permute-start.8 = (bf16[256,2048]{1,0:T(8,128)(2,1)S(1)}, bf16[256,2048]{1,0:T(8,128)(2,1)S(1)}, u32[]{:S(2)}, u32[]{:S(2)}) collective-permute-start(bf16[256,2048]{1,0:T(8,128)(2,1)S(1)} %pad_maximum_fusion.10), channel_id=1, source_target_pairs={{0,4},{4,0},{8,12},{12,8},{16,20},{20,16},{24,28},{28,24},{1,5},{5... | collective-permute-start | bytes 3145736 | tf_op jit(solution)/shard_map/ppermute | solution.py:151
  215.2 23.1 %collective-permute-start.9 = (bf16[256,2048]{1,0:T(8,128)(2,1)S(1)}, bf16[256,2048]{1,0:T(8,128)(2,1)S(1)}, u32[]{:S(2)}, u32[]{:S(2)}) collective-permute-start(bf16[256,2048]{1,0:T(8,128)(2,1)S(1)} %pad_maximum_fusion.11), channel_id=1, source_target_pairs={{0,2},{1,3},{2,0},{3,1},{4,6},{5,7},{6,4},{7,5},{8,10},{9,11},{10,... | collective-permute-start | bytes 3145736 | tf_op jit(solution)/shard_map/ppermute | solution.py:154
  219.5 28.6 %collective-permute-start.12 = (bf16[1024,2048]{1,0:T(8,128)(2,1)}, bf16[1024,2048]{1,0:T(8,128)(2,1)}, u32[]{:S(2)}, u32[]{:S(2)}) collective-permute-start(bf16[1024,2048]{1,0:T(8,128)(2,1)} %get-tuple-element.260), channel_id=1, source_target_pairs={{0,1},{1,0},{2,3},{3,2},{4,5},{5,4},{6,7},{7,6},{8,9},{9,8},{10,11... | collective-permute-start | bytes 12582920 | tf_op jit(solution)/shard_map/ppermute | solution.py:157
  241.0 12.8 %collective-permute-start.10 = (bf16[1024,2048]{1,0:T(8,128)(2,1)}, bf16[1024,2048]{1,0:T(8,128)(2,1)S(1)}, u32[]{:S(2)}, u32[]{:S(2)}) collective-permute-start(bf16[1024,2048]{1,0:T(8,128)(2,1)} %pad_maximum_fusion.1), channel_id=1, source_target_pairs={{0,1},{1,0},{2,3},{3,2},{4,5},{5,4},{6,7},{7,6},{8,9},{9,8},{10,11... | collective-permute-start | bytes 12582920 | tf_op jit(solution)/shard_map/ppermute | solution.py:157
  278.8 190.2 %reduce-scatter.10.cloned.1.call-start = ((), (), s32[]{:S(2)}) async-start(), calls=%async_computation.10 | async-start | bytes 3932160 | tf_op jit(solution)/shard_map/reduce_scatter | solution.py:190
  321.3 183.4 %reduce-scatter.12.cloned.1.call-start = ((), (), s32[]{:S(2)}) async-start(), calls=%async_computation.11 | async-start | bytes 3276800 | tf_op jit(solution)/shard_map/reduce_scatter | solution.py:190
  360.2 23.2 %collective-permute-start.13 = (bf16[1024,2048]{1,0:T(8,128)(2,1)}, bf16[1024,2048]{1,0:T(8,128)(2,1)}, u32[]{:S(2)}, u32[]{:S(2)}) collective-permute-start(bf16[1024,2048]{1,0:T(8,128)(2,1)} %add_convert_fusion.3), channel_id=1, source_target_pairs={{0,1},{1,0},{2,3},{3,2},{4,5},{5,4},{6,7},{7,6},{8,9},{9,8},{10,11... | collective-permute-start | bytes 12582920 | tf_op jit(solution)/shard_map/ppermute | solution.py:157
  383.4 196.3 %reduce-scatter.8.cloned.1.call-start = ((), (), s32[]{:S(2)}) async-start(), calls=%async_computation.9 | async-start | bytes 6553600 | tf_op jit(solution)/shard_map/reduce_scatter | solution.py:190
  390.5 28.5 %collective-permute-start.15 = (bf16[256,2048]{1,0:T(8,128)(2,1)}, bf16[256,2048]{1,0:T(8,128)(2,1)}, u32[]{:S(2)}, u32[]{:S(2)}) collective-permute-start(bf16[256,2048]{1,0:T(8,128)(2,1)} %get-tuple-element.242), channel_id=1, source_target_pairs={{0,2},{1,3},{2,0},{3,1},{4,6},{5,7},{6,4},{7,5},{8,10},{9,11},{10,... | collective-permute-start | bytes 3145736 | tf_op jit(solution)/shard_map/ppermute | solution.py:154
  391.2 29.6 %collective-permute-start.14 = (bf16[256,2048]{1,0:T(8,128)(2,1)S(1)}, bf16[256,2048]{1,0:T(8,128)(2,1)}, u32[]{:S(2)}, u32[]{:S(2)}) collective-permute-start(bf16[256,2048]{1,0:T(8,128)(2,1)S(1)} %get-tuple-element.243), channel_id=1, source_target_pairs={{0,4},{4,0},{8,12},{12,8},{16,20},{20,16},{24,28},{28,24},{1,5},{5... | collective-permute-start | bytes 3145736 | tf_op jit(solution)/shard_map/ppermute | solution.py:151
  419.0 55.8 %collective-permute-start.16 = (bf16[1024,2048]{1,0:T(8,128)(2,1)}, bf16[1024,2048]{1,0:T(8,128)(2,1)}, u32[]{:S(2)}, u32[]{:S(2)}) collective-permute-start(bf16[1024,2048]{1,0:T(8,128)(2,1)} %add_convert_fusion.1), channel_id=1, source_target_pairs={{0,1},{1,0},{2,3},{3,2},{4,5},{5,4},{6,7},{7,6},{8,9},{9,8},{10,11... | collective-permute-start | bytes 12582920 | tf_op jit(solution)/shard_map/ppermute | solution.py:157
  423.1 14.4 %collective-permute-start.21 = (bf16[128,2048]{1,0:T(8,128)(2,1)S(1)}, bf16[128,2048]{1,0:T(8,128)(2,1)S(1)}, u32[]{:S(2)}, u32[]{:S(2)}) collective-permute-start(bf16[128,2048]{1,0:T(8,128)(2,1)S(1)} %slice.1097), channel_id=1, source_target_pairs={{0,2},{1,3},{2,0},{3,1},{4,6},{5,7},{6,4},{7,5},{8,10},{9,11},{10,... | collective-permute-start | bytes 1572872 | tf_op jit(solution)/shard_map/ppermute | solution.py:154
  424.6 14.0 %collective-permute-start.22 = (bf16[128,2048]{1,0:T(8,128)(2,1)S(1)}, bf16[128,2048]{1,0:T(8,128)(2,1)S(1)}, u32[]{:S(2)}, u32[]{:S(2)}) collective-permute-start(bf16[128,2048]{1,0:T(8,128)(2,1)S(1)} %slice.1096), channel_id=1, source_target_pairs={{0,4},{4,0},{8,12},{12,8},{16,20},{20,16},{24,28},{28,24},{1,5},{5... | collective-permute-start | bytes 1572872 | tf_op jit(solution)/shard_map/ppermute | solution.py:151
  439.8 24.7 %collective-permute-start.24 = (bf16[256,2048]{1,0:T(8,128)(2,1)S(1)}, bf16[256,2048]{1,0:T(8,128)(2,1)}, u32[]{:S(2)}, u32[]{:S(2)}) collective-permute-start(bf16[256,2048]{1,0:T(8,128)(2,1)S(1)} %add_convert_fusion.8), channel_id=1, source_target_pairs={{0,2},{1,3},{2,0},{3,1},{4,6},{5,7},{6,4},{7,5},{8,10},{9,11},{10,... | collective-permute-start | bytes 3145736 | tf_op jit(solution)/shard_map/ppermute | solution.py:154
  441.0 31.3 %collective-permute-start.23 = (bf16[256,2048]{1,0:T(8,128)(2,1)S(1)}, bf16[256,2048]{1,0:T(8,128)(2,1)}, u32[]{:S(2)}, u32[]{:S(2)}) collective-permute-start(bf16[256,2048]{1,0:T(8,128)(2,1)S(1)} %add_convert_fusion.8), channel_id=1, source_target_pairs={{0,1},{1,0},{2,3},{3,2},{4,5},{5,4},{6,7},{7,6},{8,9},{9,8},{10,11... | collective-permute-start | bytes 3145736 | tf_op jit(solution)/shard_map/ppermute | solution.py:157
  464.5 7.8 %collective-permute-start.25 = (bf16[256,2048]{1,0:T(8,128)(2,1)}, bf16[256,2048]{1,0:T(8,128)(2,1)}, u32[]{:S(2)}, u32[]{:S(2)}) collective-permute-start(bf16[256,2048]{1,0:T(8,128)(2,1)} %collective-permute-done.24), channel_id=1, source_target_pairs={{0,1},{1,0},{2,3},{3,2},{4,5},{5,4},{6,7},{7,6},{8,9},{9,8},{10,11... | collective-permute-start | bytes 3145736 | tf_op jit(solution)/shard_map/ppermute | solution.py:157
  468.3 111.4 %collective-permute-start.28 = (bf16[256,384]{1,0:T(8,128)(2,1)}, bf16[256,384]{1,0:T(8,128)(2,1)}, u32[]{:S(2)}, u32[]{:S(2)}) collective-permute-start(bf16[256,384]{1,0:T(8,128)(2,1)} %get-tuple-element.313), channel_id=1, source_target_pairs={{0,4},{4,0},{8,12},{12,8},{16,20},{20,16},{24,28},{28,24},{1,5},{5... | collective-permute-start | bytes 589832 | tf_op jit(solution)/shard_map/ppermute | solution.py:151
  468.9 161.7 %reduce-scatter.14.cloned.1.call-start = ((), (), s32[]{:S(2)}) async-start(), calls=%async_computation.12 | async-start | bytes 1310720 | tf_op jit(solution)/shard_map/reduce_scatter | solution.py:190
  470.7 109.0 %collective-permute-start.27 = (bf16[256,768]{1,0:T(8,128)(2,1)}, bf16[256,768]{1,0:T(8,128)(2,1)}, u32[]{:S(2)}, u32[]{:S(2)}) collective-permute-start(bf16[256,768]{1,0:T(8,128)(2,1)} %constant_dynamic-slice_fusion.9), channel_id=1, source_target_pairs={{0,4},{4,0},{8,12},{12,8},{16,20},{20,16},{24,28},{28,24},{1,5},{5... | collective-permute-start | bytes 1179656 | tf_op jit(solution)/shard_map/ppermute | solution.py:151
  483.4 48.8 %collective-permute-start.17 = (bf16[512,2048]{1,0:T(8,128)(2,1)}, bf16[512,2048]{1,0:T(8,128)(2,1)}, u32[]{:S(2)}, u32[]{:S(2)}) collective-permute-start(bf16[512,2048]{1,0:T(8,128)(2,1)} %pad_maximum_fusion.6), channel_id=1, source_target_pairs={{0,4},{4,0},{8,12},{12,8},{16,20},{20,16},{24,28},{28,24},{1,5},{5... | collective-permute-start | bytes 6291464 | tf_op jit(solution)/shard_map/ppermute | solution.py:151
  506.9 72.8 %collective-permute-start.29 = (bf16[256,640]{1,0:T(8,128)(2,1)}, bf16[256,640]{1,0:T(8,128)(2,1)}, u32[]{:S(2)}, u32[]{:S(2)}) collective-permute-start(bf16[256,640]{1,0:T(8,128)(2,1)} %get-tuple-element.303), channel_id=1, source_target_pairs={{0,4},{4,0},{8,12},{12,8},{16,20},{20,16},{24,28},{28,24},{1,5},{5... | collective-permute-start | bytes 983048 | tf_op jit(solution)/shard_map/ppermute | solution.py:151
  536.3 23.0 %collective-permute-start.18 = (bf16[256,2048]{1,0:T(8,128)(2,1)}, bf16[256,2048]{1,0:T(8,128)(2,1)}, u32[]{:S(2)}, u32[]{:S(2)}) collective-permute-start(bf16[256,2048]{1,0:T(8,128)(2,1)} %slice.1095), channel_id=1, source_target_pairs={{0,2},{1,3},{2,0},{3,1},{4,6},{5,7},{6,4},{7,5},{8,10},{9,11},{10,... | collective-permute-start | bytes 3145736 | tf_op jit(solution)/shard_map/ppermute | solution.py:154
  537.5 34.1 %collective-permute-start.26 = (bf16[4,256,512]{2,1,0:T(8,128)(2,1)}, bf16[4,256,512]{2,1,0:T(8,128)(2,1)}, u32[]{:S(2)}, u32[]{:S(2)}) collective-permute-start(bf16[4,256,512]{2,1,0:T(8,128)(2,1)} %dynamic-slice_bitcast_fusion), channel_id=1, source_target_pairs={{0,4},{4,0},{8,12},{12,8},{16,20},{20,16},{24,28},{28,24},{1,5},{5... | collective-permute-start | bytes 3145736 | tf_op jit(solution)/shard_map/ppermute | solution.py:151
  559.3 10.0 %collective-permute-start.30 = (bf16[256,2048]{1,0:T(8,128)(2,1)S(1)}, bf16[256,2048]{1,0:T(8,128)(2,1)S(1)}, u32[]{:S(2)}, u32[]{:S(2)}) collective-permute-start(bf16[256,2048]{1,0:T(8,128)(2,1)S(1)} %constant_dynamic-slice_fusion.6), channel_id=1, source_target_pairs={{0,1},{1,0},{2,3},{3,2},{4,5},{5,4},{6,7},{7,6},{8,9},{9,8},{10,11... | collective-permute-start | bytes 3145736 | tf_op jit(solution)/shard_map/ppermute | solution.py:157
  569.4 30.4 %collective-permute-start.20 = (bf16[256,2048]{1,0:T(8,128)(2,1)}, bf16[256,2048]{1,0:T(8,128)(2,1)}, u32[]{:S(2)}, u32[]{:S(2)}) collective-permute-start(bf16[256,2048]{1,0:T(8,128)(2,1)} %get-tuple-element.226), channel_id=1, source_target_pairs={{0,2},{1,3},{2,0},{3,1},{4,6},{5,7},{6,4},{7,5},{8,10},{9,11},{10,... | collective-permute-start | bytes 3145736 | tf_op jit(solution)/shard_map/ppermute | solution.py:154
  571.5 25.9 %collective-permute-start.19 = (bf16[256,2048]{1,0:T(8,128)(2,1)}, bf16[256,2048]{1,0:T(8,128)(2,1)}, u32[]{:S(2)}, u32[]{:S(2)}) collective-permute-start(bf16[256,2048]{1,0:T(8,128)(2,1)} %get-tuple-element.226), channel_id=1, source_target_pairs={{0,1},{1,0},{2,3},{3,2},{4,5},{5,4},{6,7},{7,6},{8,9},{9,8},{10,11... | collective-permute-start | bytes 3145736 | tf_op jit(solution)/shard_map/ppermute | solution.py:157
  595.7 9.7 %collective-permute-start.32 = (bf16[256,2048]{1,0:T(8,128)(2,1)S(1)}, bf16[256,2048]{1,0:T(8,128)(2,1)}, u32[]{:S(2)}, u32[]{:S(2)}) collective-permute-start(bf16[256,2048]{1,0:T(8,128)(2,1)S(1)} %constant_dynamic-slice_fusion.5), channel_id=1, source_target_pairs={{0,1},{1,0},{2,3},{3,2},{4,5},{5,4},{6,7},{7,6},{8,9},{9,8},{10,11... | collective-permute-start | bytes 3145736 | tf_op jit(solution)/shard_map/ppermute | solution.py:157
  597.0 36.1 %collective-permute-start.39 = (bf16[256,2048]{1,0:T(8,128)(2,1)S(1)}, bf16[256,2048]{1,0:T(8,128)(2,1)S(1)}, u32[]{:S(2)}, u32[]{:S(2)}) collective-permute-start(bf16[256,2048]{1,0:T(8,128)(2,1)S(1)} %add_convert_fusion.7), channel_id=1, source_target_pairs={{0,2},{1,3},{2,0},{3,1},{4,6},{5,7},{6,4},{7,5},{8,10},{9,11},{10,... | collective-permute-start | bytes 3145736 | tf_op jit(solution)/shard_map/ppermute | solution.py:154
  603.3 12.0 %collective-permute-start.34 = (bf16[256,768]{1,0:T(8,128)(2,1)S(1)}, bf16[256,768]{1,0:T(8,128)(2,1)S(1)}, u32[]{:S(2)}, u32[]{:S(2)}) collective-permute-start(bf16[256,768]{1,0:T(8,128)(2,1)S(1)} %get-tuple-element.259), channel_id=1, source_target_pairs={{0,4},{4,0},{8,12},{12,8},{16,20},{20,16},{24,28},{28,24},{1,5},{5... | collective-permute-start | bytes 1179656 | tf_op jit(solution)/shard_map/ppermute | solution.py:151
  604.5 26.1 %collective-permute-start.31 = (bf16[256,2048]{1,0:T(8,128)(2,1)}, bf16[256,2048]{1,0:T(8,128)(2,1)}, u32[]{:S(2)}, u32[]{:S(2)}) collective-permute-start(bf16[256,2048]{1,0:T(8,128)(2,1)} %collective-permute-done.20), channel_id=1, source_target_pairs={{0,1},{1,0},{2,3},{3,2},{4,5},{5,4},{6,7},{7,6},{8,9},{9,8},{10,11... | collective-permute-start | bytes 3145736 | tf_op jit(solution)/shard_map/ppermute | solution.py:157
  604.5 24.9 %collective-permute-start.35 = (bf16[256,1280]{1,0:T(8,128)(2,1)S(1)}, bf16[256,1280]{1,0:T(8,128)(2,1)}, u32[]{:S(2)}, u32[]{:S(2)}) collective-permute-start(bf16[256,1280]{1,0:T(8,128)(2,1)S(1)} %constant_dynamic-slice_fusion.4), channel_id=1, source_target_pairs={{0,4},{4,0},{8,12},{12,8},{16,20},{20,16},{24,28},{28,24},{1,5},{5... | collective-permute-start | bytes 1966088 | tf_op jit(solution)/shard_map/ppermute | solution.py:151
  607.1 37.8 %collective-permute-start.33 = (bf16[256,2048]{1,0:T(8,128)(2,1)S(1)}, bf16[256,2048]{1,0:T(8,128)(2,1)}, u32[]{:S(2)}, u32[]{:S(2)}) collective-permute-start(bf16[256,2048]{1,0:T(8,128)(2,1)S(1)} %add_convert_fusion.6), channel_id=1, source_target_pairs={{0,2},{1,3},{2,0},{3,1},{4,6},{5,7},{6,4},{7,5},{8,10},{9,11},{10,... | collective-permute-start | bytes 3145736 | tf_op jit(solution)/shard_map/ppermute | solution.py:154
  615.3 22.6 %collective-permute-start.37 = (bf16[256,768]{1,0:T(8,128)(2,1)}, bf16[256,768]{1,0:T(8,128)(2,1)}, u32[]{:S(2)}, u32[]{:S(2)}) collective-permute-start(bf16[256,768]{1,0:T(8,128)(2,1)} %get-tuple-element.258), channel_id=1, source_target_pairs={{0,4},{4,0},{8,12},{12,8},{16,20},{20,16},{24,28},{28,24},{1,5},{5... | collective-permute-start | bytes 1179656 | tf_op jit(solution)/shard_map/ppermute | solution.py:151
  629.5 22.7 %collective-permute-start.41 = (bf16[256,768]{1,0:T(8,128)(2,1)}, bf16[256,768]{1,0:T(8,128)(2,1)}, u32[]{:S(2)}, u32[]{:S(2)}) collective-permute-start(bf16[256,768]{1,0:T(8,128)(2,1)} %get-tuple-element.257), channel_id=1, source_target_pairs={{0,4},{4,0},{8,12},{12,8},{16,20},{20,16},{24,28},{28,24},{1,5},{5... | collective-permute-start | bytes 1179656 | tf_op jit(solution)/shard_map/ppermute | solution.py:151
  630.6 10.9 %collective-permute-start.36 = (bf16[256,768]{1,0:T(8,128)(2,1)}, bf16[256,768]{1,0:T(8,128)(2,1)S(1)}, u32[]{:S(2)}, u32[]{:S(2)}) collective-permute-start(bf16[256,768]{1,0:T(8,128)(2,1)} %fusion.111), channel_id=1, source_target_pairs={{0,8},{4,12},{8,16},{12,20},{16,24},{20,28},{24,0},{28,4},{1,9},{5... | collective-permute-start | bytes 1179656 | tf_op jit(solution)/shard_map/ppermute | solution.py:160
  633.1 27.0 %collective-permute-start.44 = (bf16[256,768]{1,0:T(8,128)(2,1)}, bf16[256,768]{1,0:T(8,128)(2,1)S(1)}, u32[]{:S(2)}, u32[]{:S(2)}) collective-permute-start(bf16[256,768]{1,0:T(8,128)(2,1)} %get-tuple-element.256), channel_id=1, source_target_pairs={{0,4},{4,0},{8,12},{12,8},{16,20},{20,16},{24,28},{28,24},{1,5},{5... | collective-permute-start | bytes 1179656 | tf_op jit(solution)/shard_map/ppermute | solution.py:151
  642.8 10.1 %collective-permute-start.40 = (bf16[256,768]{1,0:T(8,128)(2,1)S(1)}, bf16[256,768]{1,0:T(8,128)(2,1)S(1)}, u32[]{:S(2)}, u32[]{:S(2)}) collective-permute-start(bf16[256,768]{1,0:T(8,128)(2,1)S(1)} %fusion.110), channel_id=1, source_target_pairs={{0,8},{4,12},{8,16},{12,20},{16,24},{20,28},{24,0},{28,4},{1,9},{5... | collective-permute-start | bytes 1179656 | tf_op jit(solution)/shard_map/ppermute | solution.py:160
  651.6 23.8 %collective-permute-start.38 = (bf16[256,2048]{1,0:T(8,128)(2,1)}, bf16[256,2048]{1,0:T(8,128)(2,1)}, u32[]{:S(2)}, u32[]{:S(2)}) collective-permute-start(bf16[256,2048]{1,0:T(8,128)(2,1)} %get-tuple-element.231), channel_id=1, source_target_pairs={{0,1},{1,0},{2,3},{3,2},{4,5},{5,4},{6,7},{7,6},{8,9},{9,8},{10,11... | collective-permute-start | bytes 3145736 | tf_op jit(solution)/shard_map/ppermute | solution.py:157
  651.7 27.2 %collective-permute-start.42 = (bf16[256,2048]{1,0:T(8,128)(2,1)}, bf16[256,2048]{1,0:T(8,128)(2,1)}, u32[]{:S(2)}, u32[]{:S(2)}) collective-permute-start(bf16[256,2048]{1,0:T(8,128)(2,1)} %get-tuple-element.194), channel_id=1, source_target_pairs={{0,1},{1,0},{2,3},{3,2},{4,5},{5,4},{6,7},{7,6},{8,9},{9,8},{10,11... | collective-permute-start | bytes 3145736 | tf_op jit(solution)/shard_map/ppermute | solution.py:157
  654.2 12.2 %collective-permute-start.43 = (bf16[256,768]{1,0:T(8,128)(2,1)S(1)}, bf16[256,768]{1,0:T(8,128)(2,1)S(1)}, u32[]{:S(2)}, u32[]{:S(2)}) collective-permute-start(bf16[256,768]{1,0:T(8,128)(2,1)S(1)} %fusion.108), channel_id=1, source_target_pairs={{0,8},{4,12},{8,16},{12,20},{16,24},{20,28},{24,0},{28,4},{1,9},{5... | collective-permute-start | bytes 1179656 | tf_op jit(solution)/shard_map/ppermute | solution.py:160
  667.8 3.4 collective-permute-start.45
  671.2 3.7 collective-permute-start.46
  (152 other events, 933.9 us)
Sparse Core Ops, SparseCore 0:
  11.3 57.5 all-gather.3
  78.3 87.2 all-gather.5
  167.1 139.4 all-gather.7
  308.8 33.5 reduce-scatter.5
  344.6 59.2 reduce-scatter.9
  406.0 52.1 reduce-scatter.11
  469.0 92.7 reduce-scatter.7
  579.8 25.2 reduce-scatter.13

commit v6 on v5

--- a/solution.py
+++ b/solution.py
@@ -429,9 +429,9 @@
     down_trade_b, gu_trade_b = trade(tie(down_block_b, mixed_grad_rel)), trade(gu_block_b)
     gates = (
         (out_weight_grad,),
-        (gu_block_a, ffn_pass),
-        (layer_quarter, down_block_b),
-        (out_sent, gu_block_b, gu_trade_a[1], down_trade_a[1], down_trade_b[1]),
+        (gu_block_a,),
+        (ffn_pass, down_block_b),
+        (layer_quarter, out_sent, gu_block_b, gu_trade_a[1], down_trade_a[1], down_trade_b[1]),
     )
     core_index, half_rows = t_index % 2, token_count // 2
 
@@ -529,7 +529,7 @@
         [layer_quarter, swap_core(layer_quarter), layer_x, swap_core(tie(layer_x, qkv_weight_grad))],
         BF,
     )
-    qkv_send = tie(qkv_part(1).astype(BF), chip_early, out_block, gu_trade_b[1])
+    qkv_send = tie(qkv_part(1).astype(BF), chip_early, out_block)
     qkv_runs = []
     for step in range(1, groups):
         qkv_runs.append(hop(qkv_send))
@@ -538,11 +538,12 @@
         if step < groups - 1:
             qkv_send = (qkv_runs[-1].astype(F32) + qkv_part(step + 1)).astype(BF)
             if step == 1:
+                qkv_send = tie(qkv_send, gu_trade_b[1])
                 early_rows = tokens_rows(chip_early, tie(early_other, qkv_send), 0)
-    qkv_block = ring_end(qkv_runs[-1], qkv_part)
     tokens_grad = jnp.concatenate(
         [core_order(*early_rows), core_order(tie(late_rows[0], qkv_send), late_rows[1])], axis=0
     )
+    qkv_block = ring_end(tie(qkv_runs[-1], tokens_grad), qkv_part)
 
     def all_units(pairs, place):
         pairs = [(mine, tie(got, qkv_send)) for mine, got in pairs]

time: 700 us -> 688 us (0.983)
  waiting for transfers between devices: 227 us -> 216 us
  other arithmetic: 111 us -> 104 us
    ppermute x19, waiting for transfers between devices: 149 us -> 123 us  [swap_y(): return lax.ppermute(value, 'dp', [(i, i ^ 1) for i in range(dp_size)])]
    ppermute x11, waiting for transfers between devices: 52.1 us -> 70.5 us  [swap_x(): lax.ppermute(value, 'tensor', [(i, i ^ 2) for i in range(tensor_size)])]
    unnamed x338 -> x330, local copies, waits for them, and re-layouts: 49.3 us -> 49.7 us
  transfers between devices with their start and end apart: 55 -> 55, of which waited for: 25 -> 23; matrix products, arithmetic and copies ran while one was open for 54% -> 55% of each run, Pallas kernels for 0% -> 0%
where the time goes in v6:
time: 688 us; the launch traced here: 682 us
  waiting for transfers between devices  216 us (31%)
  matrix products  211 us (31%)
  other arithmetic  104 us (15%)
  local copies, waits for them, and re-layouts  95.9 us (14%)
  starting transfers between devices  37.5 us (5%)
  between operations  17.1 us (2%)
    ppermute x19, waiting for transfers between devices, swap_y(): return lax.ppermute(value, 'dp', [(i, i ^ 1) for i in range(dp_size)])  123 us
    ppermute x11, waiting for transfers between devices, swap_x(): lax.ppermute(value, 'tensor', [(i, i ^ 2) for i in range(tensor_size)])  70.5 us
    dot_general x9, matrix products, dot_cols(): lax.dot_general(left, right, (((1,), (1,)), ((), ())), preferred_element_...  60.3 us
    dot_general x6, matrix products, dot_rows(): lax.dot_general(left, right, (((0,), (0,)), ((), ())), preferred_element_...  57.2 us
    dot_general x6, matrix products, dot(): return jnp.dot(left, right, preferred_element_type=F32).astype(out)  54.7 us
    unnamed x330, local copies, waits for them, and re-layouts  49.7 us
    ppermute x19, starting transfers between devices, swap_y(): return lax.ppermute(value, 'dp', [(i, i ^ 1) for i in range(dp_size)])  22.8 us
  transfers between devices with their start and end apart: 55, of which 23 were waited for; matrix products, arithmetic and copies ran while one was open for 55% of the time, Pallas kernels for 0%

profile of v6, /device:TPU:0, one launch (start us, length us, event | category | flops | bytes accessed | tf_op | source)
XLA Modules:
  0.0 681.8 jit_solution(244884582142884074)
XLA Ops:
  15.9 3.0 collective-permute-start
  24.7 7.9 %collective-permute-done = bf16[256,1152]{1,0:T(8,128)(2,1)} collective-permute-done((bf16[256,1152]{1,0:T(8,128)(2,1)}, bf16[256,1152]{1,0:T(8,128)(2,1)}, u32[]{:S(2)}, u32[]{:S(2)}) %collective-permute-start) | collective-permute-done | bytes 589856 | tf_op jit(solution)/shard_map/ppermute | solution.py:151
  39.4 16.2 %collective-permute-done.1 = bf16[256,1920]{1,0:T(8,128)(2,1)} collective-permute-done((bf16[256,1920]{1,0:T(8,128)(2,1)S(1)}, bf16[256,1920]{1,0:T(8,128)(2,1)}, u32[]{:S(2)}, u32[]{:S(2)}) %collective-permute-start.1) | collective-permute-done | bytes 983072 | tf_op jit(solution)/shard_map/ppermute | solution.py:151
  57.9 11.0 %all-gather.4.cloned.1.call-done = bf16[1024,1280]{1,0:T(8,128)(2,1)} async-done(((bf16[256,1280]{1,0:T(8,128)(2,1)}), bf16[1024,1280]{1,0:T(8,128)(2,1)}) %all-gather.4.cloned.1.call-update) | async-done | bytes 2621456 | tf_op jit(solution)/shard_map/all_gather | solution.py:187
  79.5 27.0 %collective-permute-done.2 = bf16[1024,768]{1,0:T(8,128)(2,1)} collective-permute-done((bf16[1024,768]{1,0:T(8,128)(2,1)S(1)}, bf16[1024,768]{1,0:T(8,128)(2,1)}, u32[]{:S(2)}, u32[]{:S(2)}) %collective-permute-start.2) | collective-permute-done | bytes 1572896 | tf_op jit(solution)/shard_map/ppermute | solution.py:151
  106.5 2.6 maximum_select_fusion
  109.6 3.8 fusion.165
  132.0 7.7 %collective-permute-done.3 = bf16[1024,512]{1,0:T(8,128)(2,1)S(1)} collective-permute-done((bf16[1024,512]{1,0:T(8,128)(2,1)S(1)}, bf16[1024,512]{1,0:T(8,128)(2,1)S(1)}, u32[]{:S(2)}, u32[]{:S(2)}) %collective-permute-start.3) | collective-permute-done | bytes 1048608 | tf_op jit(solution)/shard_map/ppermute | solution.py:151
  140.0 2.4 convolution_convert_fusion.4
  143.0 4.1 collective-permute-done.4
  158.2 15.6 %collective-permute-done.5 = bf16[256,2048]{1,0:T(8,128)(2,1)} collective-permute-done((bf16[256,2048]{1,0:T(8,128)(2,1)S(1)}, bf16[256,2048]{1,0:T(8,128)(2,1)}, u32[]{:S(2)}, u32[]{:S(2)}) %collective-permute-start.5) | collective-permute-done | bytes 1048608 | tf_op jit(solution)/shard_map/ppermute | solution.py:154
  173.8 3.4 multiply_reduce_fusion.3
  178.0 22.3 %collective-permute-done.11 = bf16[512,2048]{1,0:T(8,128)(2,1)S(1)} collective-permute-done((bf16[512,2048]{1,0:T(8,128)(2,1)}, bf16[512,2048]{1,0:T(8,128)(2,1)S(1)}, u32[]{:S(2)}, u32[]{:S(2)}) %collective-permute-start.11) | collective-permute-done | bytes 2097184 | tf_op jit(solution)/shard_map/ppermute | solution.py:151
  205.0 8.2 %collective-permute-done.7 = bf16[128,2048]{1,0:T(8,128)(2,1)S(1)} collective-permute-done((bf16[128,2048]{1,0:T(8,128)(2,1)S(1)}, bf16[128,2048]{1,0:T(8,128)(2,1)S(1)}, u32[]{:S(2)}, u32[]{:S(2)}) %collective-permute-start.7) | collective-permute-done | bytes 524320 | tf_op jit(solution)/shard_map/ppermute | solution.py:151
  219.5 18.4 %collective-permute-done.8 = bf16[256,2048]{1,0:T(8,128)(2,1)S(1)} collective-permute-done((bf16[256,2048]{1,0:T(8,128)(2,1)S(1)}, bf16[256,2048]{1,0:T(8,128)(2,1)S(1)}, u32[]{:S(2)}, u32[]{:S(2)}) %collective-permute-start.8) | collective-permute-done | bytes 1048608 | tf_op jit(solution)/shard_map/ppermute | solution.py:151
  238.3 2.7 pad_maximum_fusion.1
  241.8 2.5 dynamic-slice_dynamic-update-slice_fusion.2
  248.1 3.1 copy-done.132
  251.2 2.5 constant_dynamic-update-slice_fusion.2
  253.7 3.3 copy-done.133
  257.3 10.1 %convolution_convert_fusion.5 = bf16[2048,768]{0,1:T(8,128)(2,1)S(1)} fusion(bf16[2048,2048]{1,0:T(8,128)(2,1)S(1)} %constant_dynamic-update-slice_fusion, bf16[2048,1152]{1,0:T(8,128)(2,1)} %all-gather.6.cloned.1.call-done), kind=kOutput, calls=%fused_computation.73 | convolution fusion | flops 6444023808 | bytes 14680064 | tf_op jit(solution)/shard_map/dot_general | solution.py:62
  269.5 9.2 %convolution_convert_fusion.12 = bf16[2048,384]{1,0:T(8,128)(2,1)} fusion(bf16[2048,2048]{1,0:T(8,128)(2,1)} %copy-done.133, bf16[2048,384]{0,1:T(8,128)(2,1)S(1)} %fusion.33), kind=kOutput, calls=%fused_computation.91 | convolution fusion | flops 3222011904 | bytes 11534336 | tf_op jit(solution)/shard_map/dot_general | solution.py:50
  279.0 8.7 %fusion.35 = (bf16[2048,384]{0,1:T(8,128)(2,1)S(1)}, bf16[2048,384]{0,1:T(8,128)(2,1)S(1)}) fusion(bf16[2048,768]{0,1:T(8,128)(2,1)S(1)} %convolution_convert_fusion.5, bf16[2048,2048]{1,0:T(8,128)(2,1)} %copy-done.133, bf16[2048,1152]{1,0:T(8,128)(2,1)} %all-gather.6.cloned.1.call-done), kind=kOutput, calls=%fused_computation.79 | convolution fusion | flops 3233021952 | bytes 16252928 | tf_op jit(solution)/shard_map/dot_general | solution.py:62
  289.3 10.4 %convolution_convert_fusion.7 = bf16[2048,768]{1,0:T(8,128)(2,1)} fusion(bf16[2048,2048]{1,0:T(8,128)(2,1)} %copy-done.69, bf16[2048,384]{0,1:T(8,128)(2,1)S(1)} %get-tuple-element.250, bf16[2048,384]{0,1:T(8,128)(2,1)S(1)} %get-tuple-element.249), kind=kOutput, calls=%fused_computation.75 | convolution fusion | flops 6450315264 | bytes 14680064 | tf_op jit(solution)/shard_map/dot_general | solution.py:50
  301.9 11.1 %convolution_convert_fusion.1 = bf16[2048,2048]{1,0:T(8,128)(2,1)} fusion(bf16[2048,768]{0,1:T(8,128)(2,1)S(1)} %pad_maximum_fusion.3, bf16[2048,1152]{1,0:T(8,128)(2,1)} %all-gather.6.cloned.1.call-done), kind=kOutput, calls=%fused_computation.12 | convolution fusion | flops 6446645248 | bytes 14680064 | tf_op jit(solution)/shard_map/dot_general | solution.py:56
  312.9 8.3 %convolution_convert_fusion = bf16[2048,2048]{1,0:T(8,128)(2,1)} fusion(bf16[2048,384]{0,1:T(8,128)(2,1)S(1)} %copy-done.77, bf16[2048,1152]{1,0:T(8,128)(2,1)} %all-gather.6.cloned.1.call-done), kind=kOutput, calls=%fused_computation.11 | convolution fusion | flops 3225419776 | bytes 11534336 | tf_op jit(solution)/shard_map/dot_general | solution.py:56
  321.3 17.2 %convolution_convert_fusion.3 = bf16[2048,1280]{0,1:T(8,128)(2,1)} fusion(bf16[2048,2048]{1,0:T(8,128)(2,1)} %copy-done.69, bf16[2048,1920]{1,0:T(8,128)(2,1)} %all-gather.8.cloned.1.call-done), kind=kOutput, calls=%fused_computation.14 | convolution fusion | flops 10740039680 | bytes 18874368 | tf_op jit(solution)/shard_map/dot_general | solution.py:62
  338.5 12.5 %fusion.12 = (bf16[2048,640]{0,1:T(8,128)(2,1)S(1)}, bf16[2048,640]{0,1:T(8,128)(2,1)S(1)}, bf16[2048,640]{0,1:T(8,128)(2,1)}) fusion(bf16[2048,1280]{0,1:T(8,128)(2,1)} %convolution_convert_fusion.3, bf16[2048,2048]{1,0:T(8,128)(2,1)} %copy-done.133, bf16[2048,1920]{1,0:T(8,128)(2,1)S(1)} %copy-done.148), kind=kOutput, calls=%fused_computation.40 | convolution fusion | flops 5390991360 | bytes 24117248 | tf_op jit(solution)/shard_map/dot_general | solution.py:62
  351.1 9.1 %add_convert_fusion.3 = bf16[1024,2048]{1,0:T(8,128)(2,1)} fusion(bf16[2048,2048]{1,0:T(8,128)(2,1)} %convolution_convert_fusion.1, bf16[2048,1920]{1,0:T(8,128)(2,1)S(1)} %copy-done.148, bf16[2048,640]{0,1:T(8,128)(2,1)S(1)} %get-tuple-element.233, bf16[2048,640]{0,1:T(8,128)(2,1)S(1)} %get-tuple-element.234), kind=kOutput, calls=%fused_computation.7 | convolution fusion | flops 5380243456 | bytes 18874368 | tf_op jit(solution)/shard_map/dot_general | solution.py:56
  361.0 2.3 copy-done.30
  363.3 8.8 %add_convert_fusion.2 = bf16[1024,2048]{1,0:T(8,128)(2,1)} fusion(bf16[2048,2048]{1,0:T(8,128)(2,1)} %convolution_convert_fusion.1, bf16[2048,1920]{1,0:T(8,128)(2,1)S(1)} %copy-done.148, bf16[2048,1280]{0,1:T(8,128)(2,1)S(1)} %pad_maximum_fusion), kind=kOutput, calls=%fused_computation.6 | convolution fusion | flops 5375000576 | bytes 16252928 | tf_op jit(solution)/shard_map/dot_general | solution.py:56
  372.2 11.1 %convolution_convert_fusion.8 = bf16[2048,640]{1,0:T(8,128)(2,1)} fusion(bf16[2048,2048]{1,0:T(8,128)(2,1)} %copy-done.133, bf16[2048,640]{0,1:T(8,128)(2,1)} %get-tuple-element.177), kind=kOutput, calls=%fused_computation.76 | convolution fusion | flops 5370019840 | bytes 13631488 | tf_op jit(solution)/shard_map/dot_general | solution.py:50
  383.3 7.1 %convert_add_fusion.4 = (f32[256,2048]{1,0:T(8,128)}, bf16[256,2048]{1,0:T(8,128)(2,1)}, bf16[256,2048]{1,0:T(8,128)(2,1)S(1)}, f32[256,2048]{1,0:T(8,128)S(1)}) fusion(bf16[1024,2048]{1,0:T(8,128)(2,1)} %collective-permute-done.13, bf16[1024,2048]{1,0:T(8,128)(2,1)} %add_convert_fusion.2), kind=kLoop, calls=%fused_computation.144 | loop fusion | flops 7340032 | bytes 14680064 | tf_op jit(solution)/shard_map/add | solution.py:275
  392.4 17.0 %convolution_convert_fusion.2 = bf16[2048,1280]{1,0:T(8,128)(2,1)} fusion(bf16[2048,2048]{1,0:T(8,128)(2,1)} %copy-done.69, bf16[2048,1280]{0,1:T(8,128)(2,1)} %copy-done.30), kind=kOutput, calls=%fused_computation.13 | convolution fusion | flops 10740039680 | bytes 18874368 | tf_op jit(solution)/shard_map/dot_general | solution.py:50
  409.4 9.5 %add_convert_fusion.1 = bf16[1024,2048]{1,0:T(8,128)(2,1)} fusion(bf16[2048,2048]{1,0:T(8,128)(2,1)} %convolution_convert_fusion, bf16[2048,1920]{1,0:T(8,128)(2,1)} %all-gather.8.cloned.1.call-done, bf16[2048,640]{0,1:T(8,128)(2,1)} %get-tuple-element.177), kind=kOutput, calls=%fused_computation.5 | convolution fusion | flops 2690646016 | bytes 12320768 | tf_op jit(solution)/shard_map/dot_general | solution.py:56
  420.6 2.3 convert_add_fusion.5
  424.7 7.5 %add_convert_fusion = bf16[1024,2048]{1,0:T(8,128)(2,1)} fusion(bf16[2048,2048]{1,0:T(8,128)(2,1)} %convolution_convert_fusion, bf16[2048,1920]{1,0:T(8,128)(2,1)} %all-gather.8.cloned.1.call-done, bf16[2048,640]{0,1:T(8,128)(2,1)S(1)} %copy-done.150), kind=kOutput, calls=%fused_computation.4 | convolution fusion | flops 2690646016 | bytes 12320768 | tf_op jit(solution)/shard_map/dot_general | solution.py:56
  432.2 5.2 collective-permute-done.21
  440.9 23.5 %collective-permute-done.24 = bf16[256,2048]{1,0:T(8,128)(2,1)} collective-permute-done((bf16[256,2048]{1,0:T(8,128)(2,1)S(1)}, bf16[256,2048]{1,0:T(8,128)(2,1)}, u32[]{:S(2)}, u32[]{:S(2)}) %collective-permute-start.24) | collective-permute-done | bytes 1048608 | tf_op jit(solution)/shard_map/ppermute | solution.py:154
  467.6 2.4 pad_maximum_fusion.2
  470.7 6.9 %add_convert_fusion.15 = (bf16[128,2048]{1,0:T(8,128)(2,1)S(1)}, bf16[128,2048]{1,0:T(8,128)(2,1)S(1)}, bf16[128,2048]{1,0:T(8,128)(2,1)S(1)}, bf16[128,2048]{1,...) fusion(bf16[1024,2048]{1,0:T(8,128)(2,1)} %collective-permute-do, ...), kind=kLoop, calls=%fused_computation.233 | loop fusion | flops 7340032 | bytes 14680064 | tf_op jit(solution)/shard_map/convert.21
  480.0 2.4 convolution_convert_fusion.13
  482.4 3.8 convolution_convert_fusion.9
  489.3 3.2 fusion.4
  492.5 3.0 convolution_bitcast_fusion.3
  495.6 4.4 convolution_bitcast_fusion.1
  500.1 5.6 constant_dynamic-update-slice_fusion.6
  507.7 4.4 fusion.5
  512.2 4.3 fusion.7
  536.2 3.7 maximum_add_fusion
  550.0 14.7 %collective-permute-done.18 = bf16[256,2048]{1,0:T(8,128)(2,1)} collective-permute-done((bf16[256,2048]{1,0:T(8,128)(2,1)S(1)}, bf16[256,2048]{1,0:T(8,128)(2,1)}, u32[]{:S(2)}, u32[]{:S(2)}) %collective-permute-start.18) | collective-permute-done | bytes 1048608 | tf_op jit(solution)/shard_map/ppermute | solution.py:154
  565.3 2.9 constant_dynamic-update-slice_fusion.10
  582.4 5.7 convolution_convert_fusion.6
  596.3 2.5 constant_dynamic-update-slice_fusion.8
  606.3 5.5 collective-permute-done.34
  613.8 2.5 constant_dynamic-update-slice_fusion.3
  616.3 2.8 collective-permute-done.39
  625.5 8.9 %collective-permute-done.37 = bf16[256,1280]{1,0:T(8,128)(2,1)} collective-permute-done((bf16[256,1280]{1,0:T(8,128)(2,1)}, bf16[256,1280]{1,0:T(8,128)(2,1)}, u32[]{:S(2)}, u32[]{:S(2)}) %collective-permute-start.37) | collective-permute-done | bytes 655392 | tf_op jit(solution)/shard_map/ppermute | solution.py:151
  634.6 6.1 collective-permute-done.33
  640.7 2.4 multiply_reduce_fusion.1
  643.2 3.2 add_convert_fusion.5
  650.4 2.4 convert_multiply_fusion.10
  655.9 4.3 maximum_convert_fusion
  660.2 5.5 collective-permute-done.43
  (603 shorter events, 192.9 us)
Async XLA Ops:
  7.2 61.7 %all-gather.4.cloned.1.call-start = ((), (), s32[]{:S(2)}) async-start(), calls=%async_computation.5 | async-start | bytes 3276800 | tf_op jit(solution)/shard_map/all_gather | solution.py:187
  11.2 229.7 %all-gather.6.cloned.1.call-start = ((), (), s32[]{:S(2)}) async-start(), calls=%async_computation.6 | async-start | bytes 5898240 | tf_op jit(solution)/shard_map/all_gather | solution.py:187
  15.9 16.6 %collective-permute-start = (bf16[256,1152]{1,0:T(8,128)(2,1)}, bf16[256,1152]{1,0:T(8,128)(2,1)}, u32[]{:S(2)}, u32[]{:S(2)}) collective-permute-start(bf16[256,1152]{1,0:T(8,128)(2,1)} %pad_maximum_fusion.17), channel_id=1, source_target_pairs={{0,4},{4,0},{8,12},{12,8},{16,20},{20,16},{24,28},{28,24},{1,5},{5... | collective-permute-start | bytes 1769480 | tf_op jit(solution)/shard_map/ppermute | solution.py:151
  32.6 23.0 %collective-permute-start.1 = (bf16[256,1920]{1,0:T(8,128)(2,1)S(1)}, bf16[256,1920]{1,0:T(8,128)(2,1)}, u32[]{:S(2)}, u32[]{:S(2)}) collective-permute-start(bf16[256,1920]{1,0:T(8,128)(2,1)S(1)} %pad_maximum_fusion.14), channel_id=1, source_target_pairs={{0,4},{4,0},{8,12},{12,8},{16,20},{20,16},{24,28},{28,24},{1,5},{5... | collective-permute-start | bytes 2949128 | tf_op jit(solution)/shard_map/ppermute | solution.py:151
  36.0 36.8 %copy-start.83 = (f32[1024,32]{0,1:T(8,128)}, f32[1024,32]{0,1:T(8,128)S(1)}, u32[]{:S(2)}) copy-start(f32[1024,32]{0,1:T(8,128)S(1)} %get-tuple-element.324) | copy-start | bytes 393220
  36.0 36.8 %copy-start.85 = (f32[1024,32]{0,1:T(8,128)}, f32[1024,32]{0,1:T(8,128)S(1)}, u32[]{:S(2)}) copy-start(f32[1024,32]{0,1:T(8,128)S(1)} %get-tuple-element.325) | copy-start | bytes 393220
  39.3 34.4 %slice-start.5 = ((s32[1,1024]{1,0:T(1,128)}), s32[1,512]{1,0:T(1,128)S(1)}, s32[]{:S(2)}) async-start(s32[1,1024]{1,0:T(1,128)} %param.29), calls=%async_computation.18 | async-start | bytes 4096 | tf_op jit(solution)/shard_map/slice | solution.py:86
  39.3 34.4 %copy-start.143 = (s32[1,256]{1,0:T(1,128)S(1)}, s32[1,256]{1,0:T(1,128)}, u32[]{:S(2)}) copy-start(s32[1,256]{1,0:T(1,128)} %get-tuple-element.329) | copy-start | bytes 3076
  70.4 36.1 %collective-permute-start.2 = (bf16[1024,768]{1,0:T(8,128)(2,1)S(1)}, bf16[1024,768]{1,0:T(8,128)(2,1)}, u32[]{:S(2)}, u32[]{:S(2)}) collective-permute-start(bf16[1024,768]{1,0:T(8,128)(2,1)S(1)} %slice.816), channel_id=1, source_target_pairs={{0,4},{4,0},{8,12},{12,8},{16,20},{20,16},{24,28},{28,24},{1,5},{5... | collective-permute-start | bytes 4718600 | tf_op jit(solution)/shard_map/ppermute | solution.py:151
  73.6 35.5 %copy-start.136 = (f32[1024]{0:T(1024)}, f32[1024]{0:T(1024)S(1)}, u32[]{:S(2)}) copy-start(f32[1024]{0:T(1024)S(1)} %add_rsqrt_fusion) | copy-start | bytes 12292
  73.7 54.9 %copy-start.45 = (pred[256,256]{0,1:T(8,128)(4,1)}, pred[256,256]{0,1:T(8,128)(4,1)S(1)}, u32[]{:S(2)}) copy-start(pred[256,256]{0,1:T(8,128)(4,1)S(1)} %fusion.125) | copy-start | bytes 196612
  73.9 46.0 %copy-start.25 = (pred[256,512]{0,1:T(8,128)(4,1)}, pred[256,512]{0,1:T(8,128)(4,1)S(1)}, u32[]{:S(2)}) copy-start(pred[256,512]{0,1:T(8,128)(4,1)S(1)} %fusion.115) | copy-start | bytes 393220
  74.6 48.6 %copy-start.14 = (pred[256,768]{0,1:T(8,128)(4,1)}, pred[256,768]{0,1:T(8,128)(4,1)S(1)}, u32[]{:S(2)}) copy-start(pred[256,768]{0,1:T(8,128)(4,1)S(1)} %get-tuple-element.368) | copy-start | bytes 589828
  74.6 55.0 %copy-start.16 = (pred[256,768]{0,1:T(8,128)(4,1)}, pred[256,768]{0,1:T(8,128)(4,1)S(1)}, u32[]{:S(2)}) copy-start(pred[256,768]{0,1:T(8,128)(4,1)S(1)} %get-tuple-element.369) | copy-start | bytes 589828
  78.2 243.1 %all-gather.8.cloned.1.call-start = ((), (), s32[]{:S(2)}) async-start(), calls=%async_computation.7 | async-start | bytes 9830400 | tf_op jit(solution)/shard_map/all_gather | solution.py:187
  115.7 23.9 %collective-permute-start.3 = (bf16[1024,512]{1,0:T(8,128)(2,1)S(1)}, bf16[1024,512]{1,0:T(8,128)(2,1)S(1)}, u32[]{:S(2)}, u32[]{:S(2)}) collective-permute-start(bf16[1024,512]{1,0:T(8,128)(2,1)S(1)} %slice.836), channel_id=1, source_target_pairs={{0,4},{4,0},{8,12},{12,8},{16,20},{20,16},{24,28},{28,24},{1,5},{5... | collective-permute-start | bytes 3145736 | tf_op jit(solution)/shard_map/ppermute | solution.py:151
  142.9 4.2 collective-permute-start.4
  148.5 25.3 %collective-permute-start.5 = (bf16[256,2048]{1,0:T(8,128)(2,1)S(1)}, bf16[256,2048]{1,0:T(8,128)(2,1)}, u32[]{:S(2)}, u32[]{:S(2)}) collective-permute-start(bf16[256,2048]{1,0:T(8,128)(2,1)S(1)} %add_convert_fusion.11), channel_id=1, source_target_pairs={{0,2},{1,3},{2,0},{3,1},{4,6},{5,7},{6,4},{7,5},{8,10},{9,11},{10,... | collective-permute-start | bytes 3145736 | tf_op jit(solution)/shard_map/ppermute | solution.py:154
  152.7 47.6 %collective-permute-start.11 = (bf16[512,2048]{1,0:T(8,128)(2,1)}, bf16[512,2048]{1,0:T(8,128)(2,1)S(1)}, u32[]{:S(2)}, u32[]{:S(2)}) collective-permute-start(bf16[512,2048]{1,0:T(8,128)(2,1)} %pad_maximum_fusion.5), channel_id=1, source_target_pairs={{0,4},{4,0},{8,12},{12,8},{16,20},{20,16},{24,28},{28,24},{1,5},{5... | collective-permute-start | bytes 6291464 | tf_op jit(solution)/shard_map/ppermute | solution.py:151
  158.2 214.0 %reduce-scatter.6.cloned.1.call-start = ((), (), s32[]{:S(2)}) async-start(), calls=%async_computation.8 | async-start | bytes 1966080 | tf_op jit(solution)/shard_map/reduce_scatter | solution.py:190
  200.3 12.9 %collective-permute-start.7 = (bf16[128,2048]{1,0:T(8,128)(2,1)S(1)}, bf16[128,2048]{1,0:T(8,128)(2,1)S(1)}, u32[]{:S(2)}, u32[]{:S(2)}) collective-permute-start(bf16[128,2048]{1,0:T(8,128)(2,1)S(1)} %get-tuple-element.286), channel_id=1, source_target_pairs={{0,4},{4,0},{8,12},{12,8},{16,20},{20,16},{24,28},{28,24},{1,5},{5... | collective-permute-start | bytes 1572872 | tf_op jit(solution)/shard_map/ppermute | solution.py:151
  201.9 12.7 %collective-permute-start.6 = (bf16[128,2048]{1,0:T(8,128)(2,1)S(1)}, bf16[128,2048]{1,0:T(8,128)(2,1)S(1)}, u32[]{:S(2)}, u32[]{:S(2)}) collective-permute-start(bf16[128,2048]{1,0:T(8,128)(2,1)S(1)} %get-tuple-element.287), channel_id=1, source_target_pairs={{0,2},{1,3},{2,0},{3,1},{4,6},{5,7},{6,4},{7,5},{8,10},{9,11},{10,... | collective-permute-start | bytes 1572872 | tf_op jit(solution)/shard_map/ppermute | solution.py:154
  214.7 23.2 %collective-permute-start.8 = (bf16[256,2048]{1,0:T(8,128)(2,1)S(1)}, bf16[256,2048]{1,0:T(8,128)(2,1)S(1)}, u32[]{:S(2)}, u32[]{:S(2)}) collective-permute-start(bf16[256,2048]{1,0:T(8,128)(2,1)S(1)} %pad_maximum_fusion.10), channel_id=1, source_target_pairs={{0,4},{4,0},{8,12},{12,8},{16,20},{20,16},{24,28},{28,24},{1,5},{5... | collective-permute-start | bytes 3145736 | tf_op jit(solution)/shard_map/ppermute | solution.py:151
  215.1 23.1 %collective-permute-start.9 = (bf16[256,2048]{1,0:T(8,128)(2,1)S(1)}, bf16[256,2048]{1,0:T(8,128)(2,1)S(1)}, u32[]{:S(2)}, u32[]{:S(2)}) collective-permute-start(bf16[256,2048]{1,0:T(8,128)(2,1)S(1)} %pad_maximum_fusion.11), channel_id=1, source_target_pairs={{0,2},{1,3},{2,0},{3,1},{4,6},{5,7},{6,4},{7,5},{8,10},{9,11},{10,... | collective-permute-start | bytes 3145736 | tf_op jit(solution)/shard_map/ppermute | solution.py:154
  219.5 28.6 %collective-permute-start.12 = (bf16[1024,2048]{1,0:T(8,128)(2,1)}, bf16[1024,2048]{1,0:T(8,128)(2,1)}, u32[]{:S(2)}, u32[]{:S(2)}) collective-permute-start(bf16[1024,2048]{1,0:T(8,128)(2,1)} %get-tuple-element.264), channel_id=1, source_target_pairs={{0,1},{1,0},{2,3},{3,2},{4,5},{5,4},{6,7},{7,6},{8,9},{9,8},{10,11... | collective-permute-start | bytes 12582920 | tf_op jit(solution)/shard_map/ppermute | solution.py:157
  240.9 12.8 %collective-permute-start.10 = (bf16[1024,2048]{1,0:T(8,128)(2,1)}, bf16[1024,2048]{1,0:T(8,128)(2,1)S(1)}, u32[]{:S(2)}, u32[]{:S(2)}) collective-permute-start(bf16[1024,2048]{1,0:T(8,128)(2,1)} %pad_maximum_fusion.1), channel_id=1, source_target_pairs={{0,1},{1,0},{2,3},{3,2},{4,5},{5,4},{6,7},{7,6},{8,9},{9,8},{10,11... | collective-permute-start | bytes 12582920 | tf_op jit(solution)/shard_map/ppermute | solution.py:157
  278.7 213.8 %reduce-scatter.10.cloned.1.call-start = ((), (), s32[]{:S(2)}) async-start(), calls=%async_computation.10 | async-start | bytes 3932160 | tf_op jit(solution)/shard_map/reduce_scatter | solution.py:190
  321.2 208.9 %reduce-scatter.12.cloned.1.call-start = ((), (), s32[]{:S(2)}) async-start(), calls=%async_computation.11 | async-start | bytes 3276800 | tf_op jit(solution)/shard_map/reduce_scatter | solution.py:190
  360.1 23.2 %collective-permute-start.13 = (bf16[1024,2048]{1,0:T(8,128)(2,1)}, bf16[1024,2048]{1,0:T(8,128)(2,1)}, u32[]{:S(2)}, u32[]{:S(2)}) collective-permute-start(bf16[1024,2048]{1,0:T(8,128)(2,1)} %add_convert_fusion.3), channel_id=1, source_target_pairs={{0,1},{1,0},{2,3},{3,2},{4,5},{5,4},{6,7},{7,6},{8,9},{9,8},{10,11... | collective-permute-start | bytes 12582920 | tf_op jit(solution)/shard_map/ppermute | solution.py:157
  383.3 192.2 %reduce-scatter.8.cloned.1.call-start = ((), (), s32[]{:S(2)}) async-start(), calls=%async_computation.9 | async-start | bytes 6553600 | tf_op jit(solution)/shard_map/reduce_scatter | solution.py:190
  390.4 28.5 %collective-permute-start.15 = (bf16[256,2048]{1,0:T(8,128)(2,1)}, bf16[256,2048]{1,0:T(8,128)(2,1)}, u32[]{:S(2)}, u32[]{:S(2)}) collective-permute-start(bf16[256,2048]{1,0:T(8,128)(2,1)} %get-tuple-element.246), channel_id=1, source_target_pairs={{0,2},{1,3},{2,0},{3,1},{4,6},{5,7},{6,4},{7,5},{8,10},{9,11},{10,... | collective-permute-start | bytes 3145736 | tf_op jit(solution)/shard_map/ppermute | solution.py:154
  391.0 29.5 %collective-permute-start.14 = (bf16[256,2048]{1,0:T(8,128)(2,1)S(1)}, bf16[256,2048]{1,0:T(8,128)(2,1)}, u32[]{:S(2)}, u32[]{:S(2)}) collective-permute-start(bf16[256,2048]{1,0:T(8,128)(2,1)S(1)} %get-tuple-element.247), channel_id=1, source_target_pairs={{0,4},{4,0},{8,12},{12,8},{16,20},{20,16},{24,28},{28,24},{1,5},{5... | collective-permute-start | bytes 3145736 | tf_op jit(solution)/shard_map/ppermute | solution.py:151
  418.9 51.2 %collective-permute-start.16 = (bf16[1024,2048]{1,0:T(8,128)(2,1)}, bf16[1024,2048]{1,0:T(8,128)(2,1)}, u32[]{:S(2)}, u32[]{:S(2)}) collective-permute-start(bf16[1024,2048]{1,0:T(8,128)(2,1)} %add_convert_fusion.1), channel_id=1, source_target_pairs={{0,1},{1,0},{2,3},{3,2},{4,5},{5,4},{6,7},{7,6},{8,9},{9,8},{10,11... | collective-permute-start | bytes 12582920 | tf_op jit(solution)/shard_map/ppermute | solution.py:157
  423.0 14.4 %collective-permute-start.21 = (bf16[128,2048]{1,0:T(8,128)(2,1)S(1)}, bf16[128,2048]{1,0:T(8,128)(2,1)S(1)}, u32[]{:S(2)}, u32[]{:S(2)}) collective-permute-start(bf16[128,2048]{1,0:T(8,128)(2,1)S(1)} %slice.1097), channel_id=1, source_target_pairs={{0,2},{1,3},{2,0},{3,1},{4,6},{5,7},{6,4},{7,5},{8,10},{9,11},{10,... | collective-permute-start | bytes 1572872 | tf_op jit(solution)/shard_map/ppermute | solution.py:154
  424.6 14.0 %collective-permute-start.22 = (bf16[128,2048]{1,0:T(8,128)(2,1)S(1)}, bf16[128,2048]{1,0:T(8,128)(2,1)S(1)}, u32[]{:S(2)}, u32[]{:S(2)}) collective-permute-start(bf16[128,2048]{1,0:T(8,128)(2,1)S(1)} %slice.1096), channel_id=1, source_target_pairs={{0,4},{4,0},{8,12},{12,8},{16,20},{20,16},{24,28},{28,24},{1,5},{5... | collective-permute-start | bytes 1572872 | tf_op jit(solution)/shard_map/ppermute | solution.py:151
  439.7 24.7 %collective-permute-start.24 = (bf16[256,2048]{1,0:T(8,128)(2,1)S(1)}, bf16[256,2048]{1,0:T(8,128)(2,1)}, u32[]{:S(2)}, u32[]{:S(2)}) collective-permute-start(bf16[256,2048]{1,0:T(8,128)(2,1)S(1)} %add_convert_fusion.8), channel_id=1, source_target_pairs={{0,2},{1,3},{2,0},{3,1},{4,6},{5,7},{6,4},{7,5},{8,10},{9,11},{10,... | collective-permute-start | bytes 3145736 | tf_op jit(solution)/shard_map/ppermute | solution.py:154
  440.9 26.7 %collective-permute-start.23 = (bf16[256,2048]{1,0:T(8,128)(2,1)S(1)}, bf16[256,2048]{1,0:T(8,128)(2,1)}, u32[]{:S(2)}, u32[]{:S(2)}) collective-permute-start(bf16[256,2048]{1,0:T(8,128)(2,1)S(1)} %add_convert_fusion.8), channel_id=1, source_target_pairs={{0,1},{1,0},{2,3},{3,2},{4,5},{5,4},{6,7},{7,6},{8,9},{9,8},{10,11... | collective-permute-start | bytes 3145736 | tf_op jit(solution)/shard_map/ppermute | solution.py:157
  464.4 3.2 collective-permute-start.25
  467.5 146.3 %reduce-scatter.14.cloned.1.call-start = ((), (), s32[]{:S(2)}) async-start(), calls=%async_computation.12 | async-start | bytes 1310720 | tf_op jit(solution)/shard_map/reduce_scatter | solution.py:190
  479.1 57.1 %collective-permute-start.17 = (bf16[512,2048]{1,0:T(8,128)(2,1)}, bf16[512,2048]{1,0:T(8,128)(2,1)}, u32[]{:S(2)}, u32[]{:S(2)}) collective-permute-start(bf16[512,2048]{1,0:T(8,128)(2,1)} %pad_maximum_fusion.6), channel_id=1, source_target_pairs={{0,4},{4,0},{8,12},{12,8},{16,20},{20,16},{24,28},{28,24},{1,5},{5... | collective-permute-start | bytes 6291464 | tf_op jit(solution)/shard_map/ppermute | solution.py:151
  524.0 10.4 %collective-permute-start.30 = (bf16[256,2048]{1,0:T(8,128)(2,1)}, bf16[256,2048]{1,0:T(8,128)(2,1)}, u32[]{:S(2)}, u32[]{:S(2)}) collective-permute-start(bf16[256,2048]{1,0:T(8,128)(2,1)} %constant_dynamic-slice_fusion.6), channel_id=1, source_target_pairs={{0,1},{1,0},{2,3},{3,2},{4,5},{5,4},{6,7},{7,6},{8,9},{9,8},{10,11... | collective-permute-start | bytes 3145736 | tf_op jit(solution)/shard_map/ppermute | solution.py:157
  526.3 49.2 %collective-permute-start.28 = (bf16[256,384]{1,0:T(8,128)(2,1)}, bf16[256,384]{1,0:T(8,128)(2,1)}, u32[]{:S(2)}, u32[]{:S(2)}) collective-permute-start(bf16[256,384]{1,0:T(8,128)(2,1)} %get-tuple-element.317), channel_id=1, source_target_pairs={{0,4},{4,0},{8,12},{12,8},{16,20},{20,16},{24,28},{28,24},{1,5},{5... | collective-permute-start | bytes 589832 | tf_op jit(solution)/shard_map/ppermute | solution.py:151
  529.0 46.5 %collective-permute-start.27 = (bf16[256,768]{1,0:T(8,128)(2,1)}, bf16[256,768]{1,0:T(8,128)(2,1)}, u32[]{:S(2)}, u32[]{:S(2)}) collective-permute-start(bf16[256,768]{1,0:T(8,128)(2,1)} %constant_dynamic-slice_fusion.9), channel_id=1, source_target_pairs={{0,4},{4,0},{8,12},{12,8},{16,20},{20,16},{24,28},{28,24},{1,5},{5... | collective-permute-start | bytes 1179656 | tf_op jit(solution)/shard_map/ppermute | solution.py:151
  532.2 43.3 %collective-permute-start.29 = (bf16[256,640]{1,0:T(8,128)(2,1)}, bf16[256,640]{1,0:T(8,128)(2,1)}, u32[]{:S(2)}, u32[]{:S(2)}) collective-permute-start(bf16[256,640]{1,0:T(8,128)(2,1)} %get-tuple-element.307), channel_id=1, source_target_pairs={{0,4},{4,0},{8,12},{12,8},{16,20},{20,16},{24,28},{28,24},{1,5},{5... | collective-permute-start | bytes 983048 | tf_op jit(solution)/shard_map/ppermute | solution.py:151
  540.0 24.7 %collective-permute-start.18 = (bf16[256,2048]{1,0:T(8,128)(2,1)S(1)}, bf16[256,2048]{1,0:T(8,128)(2,1)}, u32[]{:S(2)}, u32[]{:S(2)}) collective-permute-start(bf16[256,2048]{1,0:T(8,128)(2,1)S(1)} %slice.1095), channel_id=1, source_target_pairs={{0,2},{1,3},{2,0},{3,1},{4,6},{5,7},{6,4},{7,5},{8,10},{9,11},{10,... | collective-permute-start | bytes 3145736 | tf_op jit(solution)/shard_map/ppermute | solution.py:154
  541.5 30.4 %collective-permute-start.26 = (bf16[4,256,512]{2,1,0:T(8,128)(2,1)S(1)}, bf16[4,256,512]{2,1,0:T(8,128)(2,1)S(1)}, u32[]{:S(2)}, u32[]{:S(2)}) collective-permute-start(bf16[4,256,512]{2,1,0:T(8,128)(2,1)S(1)} %dynamic-slice_bitcast_fusion), channel_id=1, source_target_pairs={{0,4},{4,0},{8,12},{12,8},{16,20},{20,16},{24,28},{28,24},{1,5},{5... | collective-permute-start | bytes 3145736 | tf_op jit(solution)/shard_map/ppermute | solution.py:151
  570.2 26.1 %collective-permute-start.20 = (bf16[256,2048]{1,0:T(8,128)(2,1)}, bf16[256,2048]{1,0:T(8,128)(2,1)}, u32[]{:S(2)}, u32[]{:S(2)}) collective-permute-start(bf16[256,2048]{1,0:T(8,128)(2,1)} %get-tuple-element.230), channel_id=1, source_target_pairs={{0,2},{1,3},{2,0},{3,1},{4,6},{5,7},{6,4},{7,5},{8,10},{9,11},{10,... | collective-permute-start | bytes 3145736 | tf_op jit(solution)/shard_map/ppermute | solution.py:154
  571.9 22.1 %collective-permute-start.19 = (bf16[256,2048]{1,0:T(8,128)(2,1)}, bf16[256,2048]{1,0:T(8,128)(2,1)}, u32[]{:S(2)}, u32[]{:S(2)}) collective-permute-start(bf16[256,2048]{1,0:T(8,128)(2,1)} %get-tuple-element.230), channel_id=1, source_target_pairs={{0,1},{1,0},{2,3},{3,2},{4,5},{5,4},{6,7},{7,6},{8,9},{9,8},{10,11... | collective-permute-start | bytes 3145736 | tf_op jit(solution)/shard_map/ppermute | solution.py:157
  591.5 11.2 %collective-permute-start.32 = (bf16[256,2048]{1,0:T(8,128)(2,1)S(1)}, bf16[256,2048]{1,0:T(8,128)(2,1)}, u32[]{:S(2)}, u32[]{:S(2)}) collective-permute-start(bf16[256,2048]{1,0:T(8,128)(2,1)S(1)} %constant_dynamic-slice_fusion.5), channel_id=1, source_target_pairs={{0,1},{1,0},{2,3},{3,2},{4,5},{5,4},{6,7},{7,6},{8,9},{9,8},{10,11... | collective-permute-start | bytes 3145736 | tf_op jit(solution)/shard_map/ppermute | solution.py:157
  593.0 26.0 %collective-permute-start.39 = (bf16[256,2048]{1,0:T(8,128)(2,1)S(1)}, bf16[256,2048]{1,0:T(8,128)(2,1)S(1)}, u32[]{:S(2)}, u32[]{:S(2)}) collective-permute-start(bf16[256,2048]{1,0:T(8,128)(2,1)S(1)} %add_convert_fusion.7), channel_id=1, source_target_pairs={{0,2},{1,3},{2,0},{3,1},{4,6},{5,7},{6,4},{7,5},{8,10},{9,11},{10,... | collective-permute-start | bytes 3145736 | tf_op jit(solution)/shard_map/ppermute | solution.py:154
  599.8 12.0 %collective-permute-start.34 = (bf16[256,768]{1,0:T(8,128)(2,1)S(1)}, bf16[256,768]{1,0:T(8,128)(2,1)S(1)}, u32[]{:S(2)}, u32[]{:S(2)}) collective-permute-start(bf16[256,768]{1,0:T(8,128)(2,1)S(1)} %get-tuple-element.263), channel_id=1, source_target_pairs={{0,4},{4,0},{8,12},{12,8},{16,20},{20,16},{24,28},{28,24},{1,5},{5... | collective-permute-start | bytes 1179656 | tf_op jit(solution)/shard_map/ppermute | solution.py:151
  601.0 20.6 %collective-permute-start.36 = (bf16[256,768]{1,0:T(8,128)(2,1)}, bf16[256,768]{1,0:T(8,128)(2,1)}, u32[]{:S(2)}, u32[]{:S(2)}) collective-permute-start(bf16[256,768]{1,0:T(8,128)(2,1)} %get-tuple-element.262), channel_id=1, source_target_pairs={{0,4},{4,0},{8,12},{12,8},{16,20},{20,16},{24,28},{28,24},{1,5},{5... | collective-permute-start | bytes 1179656 | tf_op jit(solution)/shard_map/ppermute | solution.py:151
  601.8 12.0 %collective-permute-start.31 = (bf16[256,2048]{1,0:T(8,128)(2,1)}, bf16[256,2048]{1,0:T(8,128)(2,1)}, u32[]{:S(2)}, u32[]{:S(2)}) collective-permute-start(bf16[256,2048]{1,0:T(8,128)(2,1)} %collective-permute-done.20), channel_id=1, source_target_pairs={{0,1},{1,0},{2,3},{3,2},{4,5},{5,4},{6,7},{7,6},{8,9},{9,8},{10,11... | collective-permute-start | bytes 3145736 | tf_op jit(solution)/shard_map/ppermute | solution.py:157
  604.4 36.3 %collective-permute-start.33 = (bf16[256,2048]{1,0:T(8,128)(2,1)S(1)}, bf16[256,2048]{1,0:T(8,128)(2,1)}, u32[]{:S(2)}, u32[]{:S(2)}) collective-permute-start(bf16[256,2048]{1,0:T(8,128)(2,1)S(1)} %add_convert_fusion.6), channel_id=1, source_target_pairs={{0,2},{1,3},{2,0},{3,1},{4,6},{5,7},{6,4},{7,5},{8,10},{9,11},{10,... | collective-permute-start | bytes 3145736 | tf_op jit(solution)/shard_map/ppermute | solution.py:154
  611.8 22.6 %collective-permute-start.37 = (bf16[256,1280]{1,0:T(8,128)(2,1)}, bf16[256,1280]{1,0:T(8,128)(2,1)}, u32[]{:S(2)}, u32[]{:S(2)}) collective-permute-start(bf16[256,1280]{1,0:T(8,128)(2,1)} %constant_dynamic-slice_fusion.4), channel_id=1, source_target_pairs={{0,4},{4,0},{8,12},{12,8},{16,20},{20,16},{24,28},{28,24},{1,5},{5... | collective-permute-start | bytes 1966088 | tf_op jit(solution)/shard_map/ppermute | solution.py:151
  613.8 10.4 %collective-permute-start.35 = (bf16[256,768]{1,0:T(8,128)(2,1)}, bf16[256,768]{1,0:T(8,128)(2,1)S(1)}, u32[]{:S(2)}, u32[]{:S(2)}) collective-permute-start(bf16[256,768]{1,0:T(8,128)(2,1)} %fusion.111), channel_id=1, source_target_pairs={{0,8},{4,12},{8,16},{12,20},{16,24},{20,28},{24,0},{28,4},{1,9},{5... | collective-permute-start | bytes 1179656 | tf_op jit(solution)/shard_map/ppermute | solution.py:160
  619.1 27.9 %collective-permute-start.41 = (bf16[256,768]{1,0:T(8,128)(2,1)}, bf16[256,768]{1,0:T(8,128)(2,1)S(1)}, u32[]{:S(2)}, u32[]{:S(2)}) collective-permute-start(bf16[256,768]{1,0:T(8,128)(2,1)} %get-tuple-element.261), channel_id=1, source_target_pairs={{0,4},{4,0},{8,12},{12,8},{16,20},{20,16},{24,28},{28,24},{1,5},{5... | collective-permute-start | bytes 1179656 | tf_op jit(solution)/shard_map/ppermute | solution.py:151
  621.6 44.1 %collective-permute-start.44 = (bf16[256,768]{1,0:T(8,128)(2,1)}, bf16[256,768]{1,0:T(8,128)(2,1)S(1)}, u32[]{:S(2)}, u32[]{:S(2)}) collective-permute-start(bf16[256,768]{1,0:T(8,128)(2,1)} %get-tuple-element.260), channel_id=1, source_target_pairs={{0,4},{4,0},{8,12},{12,8},{16,20},{20,16},{24,28},{28,24},{1,5},{5... | collective-permute-start | bytes 1179656 | tf_op jit(solution)/shard_map/ppermute | solution.py:151
  634.4 12.6 %collective-permute-start.40 = (bf16[256,768]{1,0:T(8,128)(2,1)S(1)}, bf16[256,768]{1,0:T(8,128)(2,1)S(1)}, u32[]{:S(2)}, u32[]{:S(2)}) collective-permute-start(bf16[256,768]{1,0:T(8,128)(2,1)S(1)} %fusion.110), channel_id=1, source_target_pairs={{0,8},{4,12},{8,16},{12,20},{16,24},{20,28},{24,0},{28,4},{1,9},{5... | collective-permute-start | bytes 1179656 | tf_op jit(solution)/shard_map/ppermute | solution.py:160
  646.4 7.5 %collective-permute-start.38 = (bf16[256,2048]{1,0:T(8,128)(2,1)S(1)}, bf16[256,2048]{1,0:T(8,128)(2,1)S(1)}, u32[]{:S(2)}, u32[]{:S(2)}) collective-permute-start(bf16[256,2048]{1,0:T(8,128)(2,1)S(1)} %get-tuple-element.235), channel_id=1, source_target_pairs={{0,1},{1,0},{2,3},{3,2},{4,5},{5,4},{6,7},{7,6},{8,9},{9,8},{10,11... | collective-permute-start | bytes 3145736 | tf_op jit(solution)/shard_map/ppermute | solution.py:157
  646.5 8.4 %collective-permute-start.42 = (bf16[256,2048]{1,0:T(8,128)(2,1)S(1)}, bf16[256,2048]{1,0:T(8,128)(2,1)S(1)}, u32[]{:S(2)}, u32[]{:S(2)}) collective-permute-start(bf16[256,2048]{1,0:T(8,128)(2,1)S(1)} %get-tuple-element.197), channel_id=1, source_target_pairs={{0,1},{1,0},{2,3},{3,2},{4,5},{5,4},{6,7},{7,6},{8,9},{9,8},{10,11... | collective-permute-start | bytes 3145736 | tf_op jit(solution)/shard_map/ppermute | solution.py:157
  652.8 12.9 %collective-permute-start.43 = (bf16[256,768]{1,0:T(8,128)(2,1)S(1)}, bf16[256,768]{1,0:T(8,128)(2,1)S(1)}, u32[]{:S(2)}, u32[]{:S(2)}) collective-permute-start(bf16[256,768]{1,0:T(8,128)(2,1)S(1)} %fusion.108), channel_id=1, source_target_pairs={{0,8},{4,12},{8,16},{12,20},{16,24},{20,28},{24,0},{28,4},{1,9},{5... | collective-permute-start | bytes 1179656 | tf_op jit(solution)/shard_map/ppermute | solution.py:160
  667.1 3.4 collective-permute-start.45
  670.5 3.7 collective-permute-start.46
  (148 other events, 932.5 us)
Sparse Core Ops, SparseCore 0:
  11.3 57.4 all-gather.3
  78.3 87.2 all-gather.5
  167.1 139.4 all-gather.7
  308.8 33.5 reduce-scatter.5
  344.6 59.2 reduce-scatter.9
  406.0 52.1 reduce-scatter.11
  467.7 91.9 reduce-scatter.7
  575.6 24.8 reduce-scatter.13

commit v7 on v6

--- a/solution.py
+++ b/solution.py
@@ -303,7 +303,7 @@
     n_held = tie(n_held, full_a)
     n_all = jnp.concatenate([n_held, swap_core(n_held)], axis=0)
 
-    cot_pair = tie(cot_pair, n_two)
+    cot_pair = tie(cot_pair, top, low)
     cot_y, cot_yx = cot_pair[:quarter], cot_pair[quarter:]
     cot_held = jnp.concatenate(
         [v[:half_quarter] for v in (cot_own, cot_x, cot_y, cot_yx)]

time: 688 us -> 686 us (level)
    unnamed x330 -> x326, local copies, waits for them, and re-layouts: 49.7 us -> 47.1 us
  transfers between devices with their start and end apart: 55 -> 55, of which waited for: 23 -> 21; matrix products, arithmetic and copies ran while one was open for 55% -> 55% of each run, Pallas kernels for 0% -> 0%
where the time goes in v7:
time: 686 us; the launch traced here: 679 us
  waiting for transfers between devices  214 us (31%)
  matrix products  211 us (31%)
  other arithmetic  103 us (15%)
  local copies, waits for them, and re-layouts  93.3 us (14%)
  starting transfers between devices  40.8 us (6%)
  between operations  17.1 us (2%)
    ppermute x19, waiting for transfers between devices, swap_y(): return lax.ppermute(value, 'dp', [(i, i ^ 1) for i in range(dp_size)])  118 us
    ppermute x11, waiting for transfers between devices, swap_x(): lax.ppermute(value, 'tensor', [(i, i ^ 2) for i in range(tensor_size)])  73.6 us
    dot_general x9, matrix products, dot_cols(): lax.dot_general(left, right, (((1,), (1,)), ((), ())), preferred_element_...  59.8 us
    dot_general x6, matrix products, dot_rows(): lax.dot_general(left, right, (((0,), (0,)), ((), ())), preferred_element_...  57.3 us
    dot_general x6, matrix products, dot(): return jnp.dot(left, right, preferred_element_type=F32).astype(out)  54.9 us
    unnamed x326, local copies, waits for them, and re-layouts  47.1 us
    ppermute x19, starting transfers between devices, swap_y(): return lax.ppermute(value, 'dp', [(i, i ^ 1) for i in range(dp_size)])  26 us
  transfers between devices with their start and end apart: 55, of which 21 were waited for; matrix products, arithmetic and copies ran while one was open for 55% of the time, Pallas kernels for 0%

profile of v7, /device:TPU:0, one launch (start us, length us, event | category | flops | bytes accessed | tf_op | source)
XLA Modules:
  0.0 679.3 jit_solution(5210720702578404672)
XLA Ops:
  15.9 3.0 collective-permute-start
  24.8 7.8 %collective-permute-done = bf16[256,1152]{1,0:T(8,128)(2,1)} collective-permute-done((bf16[256,1152]{1,0:T(8,128)(2,1)}, bf16[256,1152]{1,0:T(8,128)(2,1)}, u32[]{:S(2)}, u32[]{:S(2)}) %collective-permute-start) | collective-permute-done | bytes 589856 | tf_op jit(solution)/shard_map/ppermute | solution.py:151
  39.3 16.2 %collective-permute-done.1 = bf16[256,1920]{1,0:T(8,128)(2,1)} collective-permute-done((bf16[256,1920]{1,0:T(8,128)(2,1)S(1)}, bf16[256,1920]{1,0:T(8,128)(2,1)}, u32[]{:S(2)}, u32[]{:S(2)}) %collective-permute-start.1) | collective-permute-done | bytes 983072 | tf_op jit(solution)/shard_map/ppermute | solution.py:151
  57.8 11.0 %all-gather.4.cloned.1.call-done = bf16[1024,1280]{1,0:T(8,128)(2,1)} async-done(((bf16[256,1280]{1,0:T(8,128)(2,1)}), bf16[1024,1280]{1,0:T(8,128)(2,1)}) %all-gather.4.cloned.1.call-update) | async-done | bytes 2621456 | tf_op jit(solution)/shard_map/all_gather | solution.py:187
  79.5 27.0 %collective-permute-done.2 = bf16[1024,768]{1,0:T(8,128)(2,1)} collective-permute-done((bf16[1024,768]{1,0:T(8,128)(2,1)S(1)}, bf16[1024,768]{1,0:T(8,128)(2,1)}, u32[]{:S(2)}, u32[]{:S(2)}) %collective-permute-start.2) | collective-permute-done | bytes 1572896 | tf_op jit(solution)/shard_map/ppermute | solution.py:151
  106.5 2.6 maximum_select_fusion
  109.7 3.8 fusion.165
  132.1 7.6 %collective-permute-done.3 = bf16[1024,512]{1,0:T(8,128)(2,1)S(1)} collective-permute-done((bf16[1024,512]{1,0:T(8,128)(2,1)S(1)}, bf16[1024,512]{1,0:T(8,128)(2,1)S(1)}, u32[]{:S(2)}, u32[]{:S(2)}) %collective-permute-start.3) | collective-permute-done | bytes 1048608 | tf_op jit(solution)/shard_map/ppermute | solution.py:151
  140.0 2.4 convolution_convert_fusion.4
  142.8 4.1 collective-permute-done.4
  152.2 20.5 %collective-permute-done.5 = bf16[256,2048]{1,0:T(8,128)(2,1)S(1)} collective-permute-done((bf16[256,2048]{1,0:T(8,128)(2,1)S(1)}, bf16[256,2048]{1,0:T(8,128)(2,1)S(1)}, u32[]{:S(2)}, u32[]{:S(2)}) %collective-permute-start.5) | collective-permute-done | bytes 1048608 | tf_op jit(solution)/shard_map/ppermute | solution.py:154
  180.9 28.6 %collective-permute-done.7 = bf16[128,2048]{1,0:T(8,128)(2,1)} collective-permute-done((bf16[128,2048]{1,0:T(8,128)(2,1)S(1)}, bf16[128,2048]{1,0:T(8,128)(2,1)}, u32[]{:S(2)}, u32[]{:S(2)}) %collective-permute-start.7) | collective-permute-done | bytes 524320 | tf_op jit(solution)/shard_map/ppermute | solution.py:151
  220.5 15.4 %collective-permute-done.8 = bf16[256,2048]{1,0:T(8,128)(2,1)S(1)} collective-permute-done((bf16[256,2048]{1,0:T(8,128)(2,1)S(1)}, bf16[256,2048]{1,0:T(8,128)(2,1)S(1)}, u32[]{:S(2)}, u32[]{:S(2)}) %collective-permute-start.8) | collective-permute-done | bytes 1048608 | tf_op jit(solution)/shard_map/ppermute | solution.py:151
  237.2 2.7 pad_maximum_fusion.1
  240.7 2.5 dynamic-slice_dynamic-update-slice_fusion.2
  247.1 3.1 copy-done.130
  250.2 2.5 constant_dynamic-update-slice_fusion.2
  252.7 3.2 copy-done.131
  256.3 10.0 %convolution_convert_fusion.5 = bf16[2048,768]{0,1:T(8,128)(2,1)S(1)} fusion(bf16[2048,2048]{1,0:T(8,128)(2,1)S(1)} %constant_dynamic-update-slice_fusion, bf16[2048,1152]{1,0:T(8,128)(2,1)} %all-gather.6.cloned.1.call-done), kind=kOutput, calls=%fused_computation.73 | convolution fusion | flops 6444023808 | bytes 14680064 | tf_op jit(solution)/shard_map/dot_general | solution.py:62
  268.5 9.2 %convolution_convert_fusion.12 = bf16[2048,384]{1,0:T(8,128)(2,1)} fusion(bf16[2048,2048]{1,0:T(8,128)(2,1)} %copy-done.131, bf16[2048,384]{0,1:T(8,128)(2,1)S(1)} %fusion.33), kind=kOutput, calls=%fused_computation.91 | convolution fusion | flops 3222011904 | bytes 11534336 | tf_op jit(solution)/shard_map/dot_general | solution.py:50
  278.0 8.6 %fusion.35 = (bf16[2048,384]{0,1:T(8,128)(2,1)S(1)}, bf16[2048,384]{0,1:T(8,128)(2,1)S(1)}) fusion(bf16[2048,768]{0,1:T(8,128)(2,1)S(1)} %convolution_convert_fusion.5, bf16[2048,2048]{1,0:T(8,128)(2,1)} %copy-done.131, bf16[2048,1152]{1,0:T(8,128)(2,1)} %all-gather.6.cloned.1.call-done), kind=kOutput, calls=%fused_computation.79 | convolution fusion | flops 3233021952 | bytes 16252928 | tf_op jit(solution)/shard_map/dot_general | solution.py:62
  288.3 10.4 %convolution_convert_fusion.7 = bf16[2048,768]{1,0:T(8,128)(2,1)} fusion(bf16[2048,2048]{1,0:T(8,128)(2,1)} %copy-done.68, bf16[2048,384]{0,1:T(8,128)(2,1)S(1)} %get-tuple-element.250, bf16[2048,384]{0,1:T(8,128)(2,1)S(1)} %get-tuple-element.249), kind=kOutput, calls=%fused_computation.75 | convolution fusion | flops 6450315264 | bytes 14680064 | tf_op jit(solution)/shard_map/dot_general | solution.py:50
  300.8 11.1 %convolution_convert_fusion.1 = bf16[2048,2048]{1,0:T(8,128)(2,1)} fusion(bf16[2048,768]{0,1:T(8,128)(2,1)S(1)} %pad_maximum_fusion.3, bf16[2048,1152]{1,0:T(8,128)(2,1)} %all-gather.6.cloned.1.call-done), kind=kOutput, calls=%fused_computation.12 | convolution fusion | flops 6446645248 | bytes 14680064 | tf_op jit(solution)/shard_map/dot_general | solution.py:56
  311.9 8.2 %convolution_convert_fusion = bf16[2048,2048]{1,0:T(8,128)(2,1)} fusion(bf16[2048,384]{0,1:T(8,128)(2,1)S(1)} %copy-done.75, bf16[2048,1152]{1,0:T(8,128)(2,1)} %all-gather.6.cloned.1.call-done), kind=kOutput, calls=%fused_computation.11 | convolution fusion | flops 3225419776 | bytes 11534336 | tf_op jit(solution)/shard_map/dot_general | solution.py:56
  320.3 17.4 %convolution_convert_fusion.3 = bf16[2048,1280]{0,1:T(8,128)(2,1)} fusion(bf16[2048,2048]{1,0:T(8,128)(2,1)} %copy-done.68, bf16[2048,1920]{1,0:T(8,128)(2,1)} %all-gather.8.cloned.1.call-done), kind=kOutput, calls=%fused_computation.14 | convolution fusion | flops 10740039680 | bytes 18874368 | tf_op jit(solution)/shard_map/dot_general | solution.py:62
  337.7 12.5 %fusion.12 = (bf16[2048,640]{0,1:T(8,128)(2,1)S(1)}, bf16[2048,640]{0,1:T(8,128)(2,1)S(1)}, bf16[2048,640]{0,1:T(8,128)(2,1)}) fusion(bf16[2048,1280]{0,1:T(8,128)(2,1)} %convolution_convert_fusion.3, bf16[2048,2048]{1,0:T(8,128)(2,1)} %copy-done.131, bf16[2048,1920]{1,0:T(8,128)(2,1)S(1)} %copy-done.146), kind=kOutput, calls=%fused_computation.40 | convolution fusion | flops 5390991360 | bytes 24117248 | tf_op jit(solution)/shard_map/dot_general | solution.py:62
  350.2 9.1 %add_convert_fusion.3 = bf16[1024,2048]{1,0:T(8,128)(2,1)} fusion(bf16[2048,2048]{1,0:T(8,128)(2,1)} %convolution_convert_fusion.1, bf16[2048,1920]{1,0:T(8,128)(2,1)S(1)} %copy-done.146, bf16[2048,640]{0,1:T(8,128)(2,1)S(1)} %get-tuple-element.233, bf16[2048,640]{0,1:T(8,128)(2,1)S(1)} %get-tuple-element.234), kind=kOutput, calls=%fused_computation.7 | convolution fusion | flops 5380243456 | bytes 18874368 | tf_op jit(solution)/shard_map/dot_general | solution.py:56
  360.2 2.3 copy-done.30
  362.5 8.8 %add_convert_fusion.2 = bf16[1024,2048]{1,0:T(8,128)(2,1)} fusion(bf16[2048,2048]{1,0:T(8,128)(2,1)} %convolution_convert_fusion.1, bf16[2048,1920]{1,0:T(8,128)(2,1)S(1)} %copy-done.146, bf16[2048,1280]{0,1:T(8,128)(2,1)S(1)} %pad_maximum_fusion), kind=kOutput, calls=%fused_computation.6 | convolution fusion | flops 5375000576 | bytes 16252928 | tf_op jit(solution)/shard_map/dot_general | solution.py:56
  371.3 11.2 %convolution_convert_fusion.8 = bf16[2048,640]{1,0:T(8,128)(2,1)} fusion(bf16[2048,2048]{1,0:T(8,128)(2,1)} %copy-done.131, bf16[2048,640]{0,1:T(8,128)(2,1)} %get-tuple-element.177), kind=kOutput, calls=%fused_computation.76 | convolution fusion | flops 5370019840 | bytes 13631488 | tf_op jit(solution)/shard_map/dot_general | solution.py:50
  382.6 7.0 %convert_add_fusion.4 = (f32[256,2048]{1,0:T(8,128)}, bf16[256,2048]{1,0:T(8,128)(2,1)}, bf16[256,2048]{1,0:T(8,128)(2,1)S(1)}, f32[256,2048]{1,0:T(8,128)S(1)}) fusion(bf16[1024,2048]{1,0:T(8,128)(2,1)} %collective-permute-done.13, bf16[1024,2048]{1,0:T(8,128)(2,1)} %add_convert_fusion.2), kind=kLoop, calls=%fused_computation.144 | loop fusion | flops 7340032 | bytes 14680064 | tf_op jit(solution)/shard_map/add | solution.py:275
  390.9 17.0 %convolution_convert_fusion.2 = bf16[2048,1280]{1,0:T(8,128)(2,1)} fusion(bf16[2048,2048]{1,0:T(8,128)(2,1)} %copy-done.68, bf16[2048,1280]{0,1:T(8,128)(2,1)} %copy-done.30), kind=kOutput, calls=%fused_computation.13 | convolution fusion | flops 10740039680 | bytes 18874368 | tf_op jit(solution)/shard_map/dot_general | solution.py:50
  407.8 9.1 %add_convert_fusion.1 = bf16[1024,2048]{1,0:T(8,128)(2,1)} fusion(bf16[2048,2048]{1,0:T(8,128)(2,1)} %convolution_convert_fusion, bf16[2048,1920]{1,0:T(8,128)(2,1)} %all-gather.8.cloned.1.call-done, bf16[2048,640]{0,1:T(8,128)(2,1)} %get-tuple-element.177), kind=kOutput, calls=%fused_computation.5 | convolution fusion | flops 2690646016 | bytes 12320768 | tf_op jit(solution)/shard_map/dot_general | solution.py:56
  418.5 2.3 convert_add_fusion.5
  423.9 7.4 %add_convert_fusion = bf16[1024,2048]{1,0:T(8,128)(2,1)} fusion(bf16[2048,2048]{1,0:T(8,128)(2,1)} %convolution_convert_fusion, bf16[2048,1920]{1,0:T(8,128)(2,1)} %all-gather.8.cloned.1.call-done, bf16[2048,640]{0,1:T(8,128)(2,1)S(1)} %copy-done.148), kind=kOutput, calls=%fused_computation.4 | convolution fusion | flops 2690646016 | bytes 12320768 | tf_op jit(solution)/shard_map/dot_general | solution.py:56
  431.4 4.0 collective-permute-done.21
  438.4 23.9 %collective-permute-done.24 = bf16[256,2048]{1,0:T(8,128)(2,1)} collective-permute-done((bf16[256,2048]{1,0:T(8,128)(2,1)S(1)}, bf16[256,2048]{1,0:T(8,128)(2,1)}, u32[]{:S(2)}, u32[]{:S(2)}) %collective-permute-start.24) | collective-permute-done | bytes 1048608 | tf_op jit(solution)/shard_map/ppermute | solution.py:154
  463.1 2.3 pad_maximum_fusion.9
  465.5 2.4 pad_maximum_fusion.2
  468.6 6.4 add_convert_fusion.15
  477.9 2.4 convolution_convert_fusion.13
  480.3 3.8 convolution_convert_fusion.9
  487.2 3.2 fusion.4
  490.4 3.0 convolution_bitcast_fusion.3
  493.5 4.4 convolution_bitcast_fusion.1
  498.0 5.6 constant_dynamic-update-slice_fusion.6
  505.7 4.4 fusion.5
  510.1 4.3 fusion.7
  534.3 3.6 maximum_add_fusion
  547.8 14.8 %collective-permute-done.18 = bf16[256,2048]{1,0:T(8,128)(2,1)} collective-permute-done((bf16[256,2048]{1,0:T(8,128)(2,1)S(1)}, bf16[256,2048]{1,0:T(8,128)(2,1)}, u32[]{:S(2)}, u32[]{:S(2)}) %collective-permute-start.18) | collective-permute-done | bytes 1048608 | tf_op jit(solution)/shard_map/ppermute | solution.py:154
  563.1 2.9 constant_dynamic-update-slice_fusion.10
  580.0 5.7 convolution_convert_fusion.6
  591.8 2.3 constant_dynamic-update-slice_fusion.9
  594.1 2.5 constant_dynamic-update-slice_fusion.8
  603.8 5.8 collective-permute-done.34
  611.5 2.5 constant_dynamic-update-slice_fusion.3
  614.0 2.6 collective-permute-done.39
  623.2 9.0 %collective-permute-done.37 = bf16[256,1280]{1,0:T(8,128)(2,1)} collective-permute-done((bf16[256,1280]{1,0:T(8,128)(2,1)}, bf16[256,1280]{1,0:T(8,128)(2,1)}, u32[]{:S(2)}, u32[]{:S(2)}) %collective-permute-start.37) | collective-permute-done | bytes 655392 | tf_op jit(solution)/shard_map/ppermute | solution.py:151
  632.4 5.8 collective-permute-done.33
  638.2 2.4 multiply_reduce_fusion.1
  640.7 3.2 add_convert_fusion.5
  647.9 2.4 convert_multiply_fusion.10
  653.5 4.3 maximum_convert_fusion
  657.8 5.5 collective-permute-done.43
  (599 shorter events, 190.9 us)
Async XLA Ops:
  7.2 61.7 %all-gather.4.cloned.1.call-start = ((), (), s32[]{:S(2)}) async-start(), calls=%async_computation.5 | async-start | bytes 3276800 | tf_op jit(solution)/shard_map/all_gather | solution.py:187
  11.2 228.7 %all-gather.6.cloned.1.call-start = ((), (), s32[]{:S(2)}) async-start(), calls=%async_computation.6 | async-start | bytes 5898240 | tf_op jit(solution)/shard_map/all_gather | solution.py:187
  15.9 16.6 %collective-permute-start = (bf16[256,1152]{1,0:T(8,128)(2,1)}, bf16[256,1152]{1,0:T(8,128)(2,1)}, u32[]{:S(2)}, u32[]{:S(2)}) collective-permute-start(bf16[256,1152]{1,0:T(8,128)(2,1)} %pad_maximum_fusion.17), channel_id=1, source_target_pairs={{0,4},{4,0},{8,12},{12,8},{16,20},{20,16},{24,28},{28,24},{1,5},{5... | collective-permute-start | bytes 1769480 | tf_op jit(solution)/shard_map/ppermute | solution.py:151
  32.6 23.0 %collective-permute-start.1 = (bf16[256,1920]{1,0:T(8,128)(2,1)S(1)}, bf16[256,1920]{1,0:T(8,128)(2,1)}, u32[]{:S(2)}, u32[]{:S(2)}) collective-permute-start(bf16[256,1920]{1,0:T(8,128)(2,1)S(1)} %pad_maximum_fusion.14), channel_id=1, source_target_pairs={{0,4},{4,0},{8,12},{12,8},{16,20},{20,16},{24,28},{28,24},{1,5},{5... | collective-permute-start | bytes 2949128 | tf_op jit(solution)/shard_map/ppermute | solution.py:151
  36.0 36.8 %copy-start.81 = (f32[1024,32]{0,1:T(8,128)}, f32[1024,32]{0,1:T(8,128)S(1)}, u32[]{:S(2)}) copy-start(f32[1024,32]{0,1:T(8,128)S(1)} %get-tuple-element.324) | copy-start | bytes 393220
  36.0 36.8 %copy-start.83 = (f32[1024,32]{0,1:T(8,128)}, f32[1024,32]{0,1:T(8,128)S(1)}, u32[]{:S(2)}) copy-start(f32[1024,32]{0,1:T(8,128)S(1)} %get-tuple-element.325) | copy-start | bytes 393220
  39.3 34.5 %slice-start.5 = ((s32[1,1024]{1,0:T(1,128)}), s32[1,512]{1,0:T(1,128)S(1)}, s32[]{:S(2)}) async-start(s32[1,1024]{1,0:T(1,128)} %param.29), calls=%async_computation.18 | async-start | bytes 4096 | tf_op jit(solution)/shard_map/slice | solution.py:86
  70.4 36.1 %collective-permute-start.2 = (bf16[1024,768]{1,0:T(8,128)(2,1)S(1)}, bf16[1024,768]{1,0:T(8,128)(2,1)}, u32[]{:S(2)}, u32[]{:S(2)}) collective-permute-start(bf16[1024,768]{1,0:T(8,128)(2,1)S(1)} %slice.816), channel_id=1, source_target_pairs={{0,4},{4,0},{8,12},{12,8},{16,20},{20,16},{24,28},{28,24},{1,5},{5... | collective-permute-start | bytes 4718600 | tf_op jit(solution)/shard_map/ppermute | solution.py:151
  73.6 35.5 %copy-start.134 = (f32[1024]{0:T(1024)}, f32[1024]{0:T(1024)S(1)}, u32[]{:S(2)}) copy-start(f32[1024]{0:T(1024)S(1)} %add_rsqrt_fusion) | copy-start | bytes 12292
  73.8 55.0 %copy-start.44 = (pred[256,256]{0,1:T(8,128)(4,1)}, pred[256,256]{0,1:T(8,128)(4,1)S(1)}, u32[]{:S(2)}) copy-start(pred[256,256]{0,1:T(8,128)(4,1)S(1)} %fusion.125) | copy-start | bytes 196612
  74.0 46.1 %copy-start.25 = (pred[256,512]{0,1:T(8,128)(4,1)}, pred[256,512]{0,1:T(8,128)(4,1)S(1)}, u32[]{:S(2)}) copy-start(pred[256,512]{0,1:T(8,128)(4,1)S(1)} %fusion.115) | copy-start | bytes 393220
  74.7 48.7 %copy-start.14 = (pred[256,768]{0,1:T(8,128)(4,1)}, pred[256,768]{0,1:T(8,128)(4,1)S(1)}, u32[]{:S(2)}) copy-start(pred[256,768]{0,1:T(8,128)(4,1)S(1)} %get-tuple-element.368) | copy-start | bytes 589828
  74.7 54.7 %copy-start.16 = (pred[256,768]{0,1:T(8,128)(4,1)}, pred[256,768]{0,1:T(8,128)(4,1)S(1)}, u32[]{:S(2)}) copy-start(pred[256,768]{0,1:T(8,128)(4,1)S(1)} %get-tuple-element.369) | copy-start | bytes 589828
  78.2 242.0 %all-gather.8.cloned.1.call-start = ((), (), s32[]{:S(2)}) async-start(), calls=%async_computation.7 | async-start | bytes 9830400 | tf_op jit(solution)/shard_map/all_gather | solution.py:187
  115.7 23.9 %collective-permute-start.3 = (bf16[1024,512]{1,0:T(8,128)(2,1)S(1)}, bf16[1024,512]{1,0:T(8,128)(2,1)S(1)}, u32[]{:S(2)}, u32[]{:S(2)}) collective-permute-start(bf16[1024,512]{1,0:T(8,128)(2,1)S(1)} %slice.836), channel_id=1, source_target_pairs={{0,4},{4,0},{8,12},{12,8},{16,20},{20,16},{24,28},{28,24},{1,5},{5... | collective-permute-start | bytes 3145736 | tf_op jit(solution)/shard_map/ppermute | solution.py:151
  142.7 4.2 collective-permute-start.4
  147.4 25.3 %collective-permute-start.5 = (bf16[256,2048]{1,0:T(8,128)(2,1)S(1)}, bf16[256,2048]{1,0:T(8,128)(2,1)S(1)}, u32[]{:S(2)}, u32[]{:S(2)}) collective-permute-start(bf16[256,2048]{1,0:T(8,128)(2,1)S(1)} %add_convert_fusion.11), channel_id=1, source_target_pairs={{0,2},{1,3},{2,0},{3,1},{4,6},{5,7},{6,4},{7,5},{8,10},{9,11},{10,... | collective-permute-start | bytes 3145736 | tf_op jit(solution)/shard_map/ppermute | solution.py:154
  150.6 63.6 %collective-permute-start.11 = (bf16[512,2048]{1,0:T(8,128)(2,1)}, bf16[512,2048]{1,0:T(8,128)(2,1)S(1)}, u32[]{:S(2)}, u32[]{:S(2)}) collective-permute-start(bf16[512,2048]{1,0:T(8,128)(2,1)} %pad_maximum_fusion.5), channel_id=1, source_target_pairs={{0,4},{4,0},{8,12},{12,8},{16,20},{20,16},{24,28},{28,24},{1,5},{5... | collective-permute-start | bytes 6291464 | tf_op jit(solution)/shard_map/ppermute | solution.py:151
  175.1 34.4 %collective-permute-start.7 = (bf16[128,2048]{1,0:T(8,128)(2,1)S(1)}, bf16[128,2048]{1,0:T(8,128)(2,1)}, u32[]{:S(2)}, u32[]{:S(2)}) collective-permute-start(bf16[128,2048]{1,0:T(8,128)(2,1)S(1)} %get-tuple-element.286), channel_id=1, source_target_pairs={{0,4},{4,0},{8,12},{12,8},{16,20},{20,16},{24,28},{28,24},{1,5},{5... | collective-permute-start | bytes 1572872 | tf_op jit(solution)/shard_map/ppermute | solution.py:151
  176.8 33.9 %collective-permute-start.6 = (bf16[128,2048]{1,0:T(8,128)(2,1)S(1)}, bf16[128,2048]{1,0:T(8,128)(2,1)}, u32[]{:S(2)}, u32[]{:S(2)}) collective-permute-start(bf16[128,2048]{1,0:T(8,128)(2,1)S(1)} %get-tuple-element.287), channel_id=1, source_target_pairs={{0,2},{1,3},{2,0},{3,1},{4,6},{5,7},{6,4},{7,5},{8,10},{9,11},{10,... | collective-permute-start | bytes 1572872 | tf_op jit(solution)/shard_map/ppermute | solution.py:154
  178.9 192.4 %reduce-scatter.6.cloned.1.call-start = ((), (), s32[]{:S(2)}) async-start(), calls=%async_computation.8 | async-start | bytes 1966080 | tf_op jit(solution)/shard_map/reduce_scatter | solution.py:190
  180.9 35.0 %copy-start.19 = (bf16[1024,2048]{1,0:T(8,128)(2,1)S(1)}, bf16[1024,2048]{1,0:T(8,128)(2,1)}, u32[]{:S(2)}) copy-start(bf16[1024,2048]{1,0:T(8,128)(2,1)} %param.39) | copy-start | bytes 12582916
  211.8 24.1 %collective-permute-start.8 = (bf16[256,2048]{1,0:T(8,128)(2,1)S(1)}, bf16[256,2048]{1,0:T(8,128)(2,1)S(1)}, u32[]{:S(2)}, u32[]{:S(2)}) collective-permute-start(bf16[256,2048]{1,0:T(8,128)(2,1)S(1)} %pad_maximum_fusion.10), channel_id=1, source_target_pairs={{0,4},{4,0},{8,12},{12,8},{16,20},{20,16},{24,28},{28,24},{1,5},{5... | collective-permute-start | bytes 3145736 | tf_op jit(solution)/shard_map/ppermute | solution.py:151
  213.5 23.8 %collective-permute-start.9 = (bf16[256,2048]{1,0:T(8,128)(2,1)S(1)}, bf16[256,2048]{1,0:T(8,128)(2,1)S(1)}, u32[]{:S(2)}, u32[]{:S(2)}) collective-permute-start(bf16[256,2048]{1,0:T(8,128)(2,1)S(1)} %pad_maximum_fusion.11), channel_id=1, source_target_pairs={{0,2},{1,3},{2,0},{3,1},{4,6},{5,7},{6,4},{7,5},{8,10},{9,11},{10,... | collective-permute-start | bytes 3145736 | tf_op jit(solution)/shard_map/ppermute | solution.py:154
  220.5 26.6 %collective-permute-start.12 = (bf16[1024,2048]{1,0:T(8,128)(2,1)}, bf16[1024,2048]{1,0:T(8,128)(2,1)}, u32[]{:S(2)}, u32[]{:S(2)}) collective-permute-start(bf16[1024,2048]{1,0:T(8,128)(2,1)} %get-tuple-element.264), channel_id=1, source_target_pairs={{0,1},{1,0},{2,3},{3,2},{4,5},{5,4},{6,7},{7,6},{8,9},{9,8},{10,11... | collective-permute-start | bytes 12582920 | tf_op jit(solution)/shard_map/ppermute | solution.py:157
  239.9 12.8 %collective-permute-start.10 = (bf16[1024,2048]{1,0:T(8,128)(2,1)}, bf16[1024,2048]{1,0:T(8,128)(2,1)S(1)}, u32[]{:S(2)}, u32[]{:S(2)}) collective-permute-start(bf16[1024,2048]{1,0:T(8,128)(2,1)} %pad_maximum_fusion.1), channel_id=1, source_target_pairs={{0,1},{1,0},{2,3},{3,2},{4,5},{5,4},{6,7},{7,6},{8,9},{9,8},{10,11... | collective-permute-start | bytes 12582920 | tf_op jit(solution)/shard_map/ppermute | solution.py:157
  277.7 212.7 %reduce-scatter.10.cloned.1.call-start = ((), (), s32[]{:S(2)}) async-start(), calls=%async_computation.10 | async-start | bytes 3932160 | tf_op jit(solution)/shard_map/reduce_scatter | solution.py:190
  320.2 207.7 %reduce-scatter.12.cloned.1.call-start = ((), (), s32[]{:S(2)}) async-start(), calls=%async_computation.11 | async-start | bytes 3276800 | tf_op jit(solution)/shard_map/reduce_scatter | solution.py:190
  359.3 23.3 %collective-permute-start.13 = (bf16[1024,2048]{1,0:T(8,128)(2,1)}, bf16[1024,2048]{1,0:T(8,128)(2,1)}, u32[]{:S(2)}, u32[]{:S(2)}) collective-permute-start(bf16[1024,2048]{1,0:T(8,128)(2,1)} %add_convert_fusion.3), channel_id=1, source_target_pairs={{0,1},{1,0},{2,3},{3,2},{4,5},{5,4},{6,7},{7,6},{8,9},{9,8},{10,11... | collective-permute-start | bytes 12582920 | tf_op jit(solution)/shard_map/ppermute | solution.py:157
  382.5 190.5 %reduce-scatter.8.cloned.1.call-start = ((), (), s32[]{:S(2)}) async-start(), calls=%async_computation.9 | async-start | bytes 6553600 | tf_op jit(solution)/shard_map/reduce_scatter | solution.py:190
  389.6 27.3 %collective-permute-start.15 = (bf16[256,2048]{1,0:T(8,128)(2,1)}, bf16[256,2048]{1,0:T(8,128)(2,1)}, u32[]{:S(2)}, u32[]{:S(2)}) collective-permute-start(bf16[256,2048]{1,0:T(8,128)(2,1)} %get-tuple-element.246), channel_id=1, source_target_pairs={{0,2},{1,3},{2,0},{3,1},{4,6},{5,7},{6,4},{7,5},{8,10},{9,11},{10,... | collective-permute-start | bytes 3145736 | tf_op jit(solution)/shard_map/ppermute | solution.py:154
  390.2 28.3 %collective-permute-start.14 = (bf16[256,2048]{1,0:T(8,128)(2,1)S(1)}, bf16[256,2048]{1,0:T(8,128)(2,1)}, u32[]{:S(2)}, u32[]{:S(2)}) collective-permute-start(bf16[256,2048]{1,0:T(8,128)(2,1)S(1)} %get-tuple-element.247), channel_id=1, source_target_pairs={{0,4},{4,0},{8,12},{12,8},{16,20},{20,16},{24,28},{28,24},{1,5},{5... | collective-permute-start | bytes 3145736 | tf_op jit(solution)/shard_map/ppermute | solution.py:151
  416.9 51.1 %collective-permute-start.16 = (bf16[1024,2048]{1,0:T(8,128)(2,1)}, bf16[1024,2048]{1,0:T(8,128)(2,1)}, u32[]{:S(2)}, u32[]{:S(2)}) collective-permute-start(bf16[1024,2048]{1,0:T(8,128)(2,1)} %add_convert_fusion.1), channel_id=1, source_target_pairs={{0,1},{1,0},{2,3},{3,2},{4,5},{5,4},{6,7},{7,6},{8,9},{9,8},{10,11... | collective-permute-start | bytes 12582920 | tf_op jit(solution)/shard_map/ppermute | solution.py:157
  421.0 14.4 %collective-permute-start.21 = (bf16[128,2048]{1,0:T(8,128)(2,1)S(1)}, bf16[128,2048]{1,0:T(8,128)(2,1)S(1)}, u32[]{:S(2)}, u32[]{:S(2)}) collective-permute-start(bf16[128,2048]{1,0:T(8,128)(2,1)S(1)} %slice.1097), channel_id=1, source_target_pairs={{0,2},{1,3},{2,0},{3,1},{4,6},{5,7},{6,4},{7,5},{8,10},{9,11},{10,... | collective-permute-start | bytes 1572872 | tf_op jit(solution)/shard_map/ppermute | solution.py:154
  422.1 14.1 %collective-permute-start.22 = (bf16[128,2048]{1,0:T(8,128)(2,1)S(1)}, bf16[128,2048]{1,0:T(8,128)(2,1)S(1)}, u32[]{:S(2)}, u32[]{:S(2)}) collective-permute-start(bf16[128,2048]{1,0:T(8,128)(2,1)S(1)} %slice.1096), channel_id=1, source_target_pairs={{0,4},{4,0},{8,12},{12,8},{16,20},{20,16},{24,28},{28,24},{1,5},{5... | collective-permute-start | bytes 1572872 | tf_op jit(solution)/shard_map/ppermute | solution.py:151
  437.3 25.0 %collective-permute-start.24 = (bf16[256,2048]{1,0:T(8,128)(2,1)S(1)}, bf16[256,2048]{1,0:T(8,128)(2,1)}, u32[]{:S(2)}, u32[]{:S(2)}) collective-permute-start(bf16[256,2048]{1,0:T(8,128)(2,1)S(1)} %add_convert_fusion.8), channel_id=1, source_target_pairs={{0,2},{1,3},{2,0},{3,1},{4,6},{5,7},{6,4},{7,5},{8,10},{9,11},{10,... | collective-permute-start | bytes 3145736 | tf_op jit(solution)/shard_map/ppermute | solution.py:154
  438.4 27.1 %collective-permute-start.23 = (bf16[256,2048]{1,0:T(8,128)(2,1)S(1)}, bf16[256,2048]{1,0:T(8,128)(2,1)}, u32[]{:S(2)}, u32[]{:S(2)}) collective-permute-start(bf16[256,2048]{1,0:T(8,128)(2,1)S(1)} %add_convert_fusion.8), channel_id=1, source_target_pairs={{0,1},{1,0},{2,3},{3,2},{4,5},{5,4},{6,7},{7,6},{8,9},{9,8},{10,11... | collective-permute-start | bytes 3145736 | tf_op jit(solution)/shard_map/ppermute | solution.py:157
  462.3 3.2 collective-permute-start.25
  465.4 146.1 %reduce-scatter.14.cloned.1.call-start = ((), (), s32[]{:S(2)}) async-start(), calls=%async_computation.12 | async-start | bytes 1310720 | tf_op jit(solution)/shard_map/reduce_scatter | solution.py:190
  476.5 57.8 %collective-permute-start.17 = (bf16[512,2048]{1,0:T(8,128)(2,1)}, bf16[512,2048]{1,0:T(8,128)(2,1)}, u32[]{:S(2)}, u32[]{:S(2)}) collective-permute-start(bf16[512,2048]{1,0:T(8,128)(2,1)} %pad_maximum_fusion.6), channel_id=1, source_target_pairs={{0,4},{4,0},{8,12},{12,8},{16,20},{20,16},{24,28},{28,24},{1,5},{5... | collective-permute-start | bytes 6291464 | tf_op jit(solution)/shard_map/ppermute | solution.py:151
  522.0 10.6 %collective-permute-start.30 = (bf16[256,2048]{1,0:T(8,128)(2,1)}, bf16[256,2048]{1,0:T(8,128)(2,1)}, u32[]{:S(2)}, u32[]{:S(2)}) collective-permute-start(bf16[256,2048]{1,0:T(8,128)(2,1)} %constant_dynamic-slice_fusion.6), channel_id=1, source_target_pairs={{0,1},{1,0},{2,3},{3,2},{4,5},{5,4},{6,7},{7,6},{8,9},{9,8},{10,11... | collective-permute-start | bytes 3145736 | tf_op jit(solution)/shard_map/ppermute | solution.py:157
  524.1 49.0 %collective-permute-start.28 = (bf16[256,384]{1,0:T(8,128)(2,1)}, bf16[256,384]{1,0:T(8,128)(2,1)}, u32[]{:S(2)}, u32[]{:S(2)}) collective-permute-start(bf16[256,384]{1,0:T(8,128)(2,1)} %get-tuple-element.317), channel_id=1, source_target_pairs={{0,4},{4,0},{8,12},{12,8},{16,20},{20,16},{24,28},{28,24},{1,5},{5... | collective-permute-start | bytes 589832 | tf_op jit(solution)/shard_map/ppermute | solution.py:151
  527.1 46.0 %collective-permute-start.27 = (bf16[256,768]{1,0:T(8,128)(2,1)}, bf16[256,768]{1,0:T(8,128)(2,1)}, u32[]{:S(2)}, u32[]{:S(2)}) collective-permute-start(bf16[256,768]{1,0:T(8,128)(2,1)} %constant_dynamic-slice_fusion.9), channel_id=1, source_target_pairs={{0,4},{4,0},{8,12},{12,8},{16,20},{20,16},{24,28},{28,24},{1,5},{5... | collective-permute-start | bytes 1179656 | tf_op jit(solution)/shard_map/ppermute | solution.py:151
  530.0 43.1 %collective-permute-start.29 = (bf16[256,640]{1,0:T(8,128)(2,1)}, bf16[256,640]{1,0:T(8,128)(2,1)}, u32[]{:S(2)}, u32[]{:S(2)}) collective-permute-start(bf16[256,640]{1,0:T(8,128)(2,1)} %get-tuple-element.307), channel_id=1, source_target_pairs={{0,4},{4,0},{8,12},{12,8},{16,20},{20,16},{24,28},{28,24},{1,5},{5... | collective-permute-start | bytes 983048 | tf_op jit(solution)/shard_map/ppermute | solution.py:151
  538.1 24.5 %collective-permute-start.18 = (bf16[256,2048]{1,0:T(8,128)(2,1)S(1)}, bf16[256,2048]{1,0:T(8,128)(2,1)}, u32[]{:S(2)}, u32[]{:S(2)}) collective-permute-start(bf16[256,2048]{1,0:T(8,128)(2,1)S(1)} %slice.1095), channel_id=1, source_target_pairs={{0,2},{1,3},{2,0},{3,1},{4,6},{5,7},{6,4},{7,5},{8,10},{9,11},{10,... | collective-permute-start | bytes 3145736 | tf_op jit(solution)/shard_map/ppermute | solution.py:154
  539.6 29.9 %collective-permute-start.26 = (bf16[4,256,512]{2,1,0:T(8,128)(2,1)S(1)}, bf16[4,256,512]{2,1,0:T(8,128)(2,1)S(1)}, u32[]{:S(2)}, u32[]{:S(2)}) collective-permute-start(bf16[4,256,512]{2,1,0:T(8,128)(2,1)S(1)} %dynamic-slice_bitcast_fusion), channel_id=1, source_target_pairs={{0,4},{4,0},{8,12},{12,8},{16,20},{20,16},{24,28},{28,24},{1,5},{5... | collective-permute-start | bytes 3145736 | tf_op jit(solution)/shard_map/ppermute | solution.py:151
  568.1 26.1 %collective-permute-start.20 = (bf16[256,2048]{1,0:T(8,128)(2,1)}, bf16[256,2048]{1,0:T(8,128)(2,1)}, u32[]{:S(2)}, u32[]{:S(2)}) collective-permute-start(bf16[256,2048]{1,0:T(8,128)(2,1)} %get-tuple-element.230), channel_id=1, source_target_pairs={{0,2},{1,3},{2,0},{3,1},{4,6},{5,7},{6,4},{7,5},{8,10},{9,11},{10,... | collective-permute-start | bytes 3145736 | tf_op jit(solution)/shard_map/ppermute | solution.py:154
  569.5 22.3 %collective-permute-start.19 = (bf16[256,2048]{1,0:T(8,128)(2,1)}, bf16[256,2048]{1,0:T(8,128)(2,1)}, u32[]{:S(2)}, u32[]{:S(2)}) collective-permute-start(bf16[256,2048]{1,0:T(8,128)(2,1)} %get-tuple-element.230), channel_id=1, source_target_pairs={{0,1},{1,0},{2,3},{3,2},{4,5},{5,4},{6,7},{7,6},{8,9},{9,8},{10,11... | collective-permute-start | bytes 3145736 | tf_op jit(solution)/shard_map/ppermute | solution.py:157
  589.1 11.5 %collective-permute-start.32 = (bf16[256,2048]{1,0:T(8,128)(2,1)S(1)}, bf16[256,2048]{1,0:T(8,128)(2,1)}, u32[]{:S(2)}, u32[]{:S(2)}) collective-permute-start(bf16[256,2048]{1,0:T(8,128)(2,1)S(1)} %constant_dynamic-slice_fusion.5), channel_id=1, source_target_pairs={{0,1},{1,0},{2,3},{3,2},{4,5},{5,4},{6,7},{7,6},{8,9},{9,8},{10,11... | collective-permute-start | bytes 3145736 | tf_op jit(solution)/shard_map/ppermute | solution.py:157
  590.6 26.0 %collective-permute-start.39 = (bf16[256,2048]{1,0:T(8,128)(2,1)S(1)}, bf16[256,2048]{1,0:T(8,128)(2,1)S(1)}, u32[]{:S(2)}, u32[]{:S(2)}) collective-permute-start(bf16[256,2048]{1,0:T(8,128)(2,1)S(1)} %add_convert_fusion.7), channel_id=1, source_target_pairs={{0,2},{1,3},{2,0},{3,1},{4,6},{5,7},{6,4},{7,5},{8,10},{9,11},{10,... | collective-permute-start | bytes 3145736 | tf_op jit(solution)/shard_map/ppermute | solution.py:154
  597.6 12.0 %collective-permute-start.34 = (bf16[256,768]{1,0:T(8,128)(2,1)S(1)}, bf16[256,768]{1,0:T(8,128)(2,1)S(1)}, u32[]{:S(2)}, u32[]{:S(2)}) collective-permute-start(bf16[256,768]{1,0:T(8,128)(2,1)S(1)} %get-tuple-element.263), channel_id=1, source_target_pairs={{0,4},{4,0},{8,12},{12,8},{16,20},{20,16},{24,28},{28,24},{1,5},{5... | collective-permute-start | bytes 1179656 | tf_op jit(solution)/shard_map/ppermute | solution.py:151
  598.7 20.9 %collective-permute-start.36 = (bf16[256,768]{1,0:T(8,128)(2,1)}, bf16[256,768]{1,0:T(8,128)(2,1)}, u32[]{:S(2)}, u32[]{:S(2)}) collective-permute-start(bf16[256,768]{1,0:T(8,128)(2,1)} %get-tuple-element.262), channel_id=1, source_target_pairs={{0,4},{4,0},{8,12},{12,8},{16,20},{20,16},{24,28},{28,24},{1,5},{5... | collective-permute-start | bytes 1179656 | tf_op jit(solution)/shard_map/ppermute | solution.py:151
  599.7 11.9 %collective-permute-start.31 = (bf16[256,2048]{1,0:T(8,128)(2,1)}, bf16[256,2048]{1,0:T(8,128)(2,1)}, u32[]{:S(2)}, u32[]{:S(2)}) collective-permute-start(bf16[256,2048]{1,0:T(8,128)(2,1)} %collective-permute-done.20), channel_id=1, source_target_pairs={{0,1},{1,0},{2,3},{3,2},{4,5},{5,4},{6,7},{7,6},{8,9},{9,8},{10,11... | collective-permute-start | bytes 3145736 | tf_op jit(solution)/shard_map/ppermute | solution.py:157
  602.2 36.0 %collective-permute-start.33 = (bf16[256,2048]{1,0:T(8,128)(2,1)S(1)}, bf16[256,2048]{1,0:T(8,128)(2,1)}, u32[]{:S(2)}, u32[]{:S(2)}) collective-permute-start(bf16[256,2048]{1,0:T(8,128)(2,1)S(1)} %add_convert_fusion.6), channel_id=1, source_target_pairs={{0,2},{1,3},{2,0},{3,1},{4,6},{5,7},{6,4},{7,5},{8,10},{9,11},{10,... | collective-permute-start | bytes 3145736 | tf_op jit(solution)/shard_map/ppermute | solution.py:154
  609.6 22.6 %collective-permute-start.37 = (bf16[256,1280]{1,0:T(8,128)(2,1)}, bf16[256,1280]{1,0:T(8,128)(2,1)}, u32[]{:S(2)}, u32[]{:S(2)}) collective-permute-start(bf16[256,1280]{1,0:T(8,128)(2,1)} %constant_dynamic-slice_fusion.4), channel_id=1, source_target_pairs={{0,4},{4,0},{8,12},{12,8},{16,20},{20,16},{24,28},{28,24},{1,5},{5... | collective-permute-start | bytes 1966088 | tf_op jit(solution)/shard_map/ppermute | solution.py:151
  611.5 10.4 %collective-permute-start.35 = (bf16[256,768]{1,0:T(8,128)(2,1)}, bf16[256,768]{1,0:T(8,128)(2,1)S(1)}, u32[]{:S(2)}, u32[]{:S(2)}) collective-permute-start(bf16[256,768]{1,0:T(8,128)(2,1)} %fusion.111), channel_id=1, source_target_pairs={{0,8},{4,12},{8,16},{12,20},{16,24},{20,28},{24,0},{28,4},{1,9},{5... | collective-permute-start | bytes 1179656 | tf_op jit(solution)/shard_map/ppermute | solution.py:160
  616.6 27.9 %collective-permute-start.41 = (bf16[256,768]{1,0:T(8,128)(2,1)}, bf16[256,768]{1,0:T(8,128)(2,1)S(1)}, u32[]{:S(2)}, u32[]{:S(2)}) collective-permute-start(bf16[256,768]{1,0:T(8,128)(2,1)} %get-tuple-element.261), channel_id=1, source_target_pairs={{0,4},{4,0},{8,12},{12,8},{16,20},{20,16},{24,28},{28,24},{1,5},{5... | collective-permute-start | bytes 1179656 | tf_op jit(solution)/shard_map/ppermute | solution.py:151
  619.6 43.7 %collective-permute-start.44 = (bf16[256,768]{1,0:T(8,128)(2,1)}, bf16[256,768]{1,0:T(8,128)(2,1)S(1)}, u32[]{:S(2)}, u32[]{:S(2)}) collective-permute-start(bf16[256,768]{1,0:T(8,128)(2,1)} %get-tuple-element.260), channel_id=1, source_target_pairs={{0,4},{4,0},{8,12},{12,8},{16,20},{20,16},{24,28},{28,24},{1,5},{5... | collective-permute-start | bytes 1179656 | tf_op jit(solution)/shard_map/ppermute | solution.py:151
  632.2 12.3 %collective-permute-start.40 = (bf16[256,768]{1,0:T(8,128)(2,1)S(1)}, bf16[256,768]{1,0:T(8,128)(2,1)S(1)}, u32[]{:S(2)}, u32[]{:S(2)}) collective-permute-start(bf16[256,768]{1,0:T(8,128)(2,1)S(1)} %fusion.110), channel_id=1, source_target_pairs={{0,8},{4,12},{8,16},{12,20},{16,24},{20,28},{24,0},{28,4},{1,9},{5... | collective-permute-start | bytes 1179656 | tf_op jit(solution)/shard_map/ppermute | solution.py:160
  644.0 7.5 %collective-permute-start.38 = (bf16[256,2048]{1,0:T(8,128)(2,1)S(1)}, bf16[256,2048]{1,0:T(8,128)(2,1)S(1)}, u32[]{:S(2)}, u32[]{:S(2)}) collective-permute-start(bf16[256,2048]{1,0:T(8,128)(2,1)S(1)} %get-tuple-element.235), channel_id=1, source_target_pairs={{0,1},{1,0},{2,3},{3,2},{4,5},{5,4},{6,7},{7,6},{8,9},{9,8},{10,11... | collective-permute-start | bytes 3145736 | tf_op jit(solution)/shard_map/ppermute | solution.py:157
  644.0 8.4 %collective-permute-start.42 = (bf16[256,2048]{1,0:T(8,128)(2,1)S(1)}, bf16[256,2048]{1,0:T(8,128)(2,1)S(1)}, u32[]{:S(2)}, u32[]{:S(2)}) collective-permute-start(bf16[256,2048]{1,0:T(8,128)(2,1)S(1)} %get-tuple-element.197), channel_id=1, source_target_pairs={{0,1},{1,0},{2,3},{3,2},{4,5},{5,4},{6,7},{7,6},{8,9},{9,8},{10,11... | collective-permute-start | bytes 3145736 | tf_op jit(solution)/shard_map/ppermute | solution.py:157
  650.4 12.9 %collective-permute-start.43 = (bf16[256,768]{1,0:T(8,128)(2,1)S(1)}, bf16[256,768]{1,0:T(8,128)(2,1)S(1)}, u32[]{:S(2)}, u32[]{:S(2)}) collective-permute-start(bf16[256,768]{1,0:T(8,128)(2,1)S(1)} %fusion.108), channel_id=1, source_target_pairs={{0,8},{4,12},{8,16},{12,20},{16,24},{20,28},{24,0},{28,4},{1,9},{5... | collective-permute-start | bytes 1179656 | tf_op jit(solution)/shard_map/ppermute | solution.py:160
  664.6 3.4 collective-permute-start.45
  668.0 3.7 collective-permute-start.46
  (146 other events, 940.9 us)
Sparse Core Ops, SparseCore 0:
  11.3 57.4 all-gather.3
  78.3 87.1 all-gather.5
  179.1 138.6 all-gather.7
  319.9 33.5 reduce-scatter.5
  355.7 59.2 reduce-scatter.9
  417.1 52.1 reduce-scatter.11
  471.6 93.3 reduce-scatter.7
  573.2 25.9 reduce-scatter.13
